TPU v7x, 32 devices: a whole 2x2x4 slice. The times are simulated.
32 devices in a mesh: groups: 2 (over y), seq: 8 (over z, x), dp: 2 (over core).
Axes of the slice: x: 2, y: 2, z: 4, core: 2. Of those that a mesh axis runs over, the one named last changes fastest.
Arguments:
- history_item_index: int32 [4, 8192], P(('groups', 'dp'), 'seq'), parts along dimension 0, may hold values from 0 to 4095
- log_head_retention: float32 [4, 8, 8192], P(('groups', 'dp'), None, 'seq'), parts along dimension 0, may hold values from -1.5 to 0
- user_history_length: int32 [4], P(('groups', 'dp')), parts along dimension 0, may hold values from 2048 to 8192, as said below
- candidate_item_index: int32 [4, 512], P(('groups', 'dp'), 'seq'), parts along dimension 0, may hold values from 0 to 4095
- item_stored_row: int32 [4096], replicated, may hold values from 0 to 4095, each once
- item_embedding_table: bfloat16 [4096, 512], P('dp'), may hold values from -6 to 6
- head_score_scale: float32 [8], replicated, may hold values from 0.2 to 4
- history_query_key_value_weight: bfloat16 [512, 1536], replicated, may hold values from -0.25 to 0.25
- history_output_weight: bfloat16 [512, 512], replicated, may hold values from -0.25 to 0.25
- candidate_key_value_weight: bfloat16 [512, 1024], replicated, may hold values from -0.25 to 0.25
- candidate_query_weight: bfloat16 [512, 512], replicated, may hold values from -0.25 to 0.25
- candidate_output_weight: bfloat16 [512, 512], replicated, may hold values from -0.25 to 0.25
Outputs:
- history_out: float32 [4, 8192, 512], P(('groups', 'dp'), 'seq'), parts along dimension 0
- cand_out: float32 [4, 512, 512], P(('groups', 'dp'), 'seq'), parts along dimension 0
There are 2 independent parts, one for each index of `groups`. A program takes and returns all parts, laid end to end along the dimension named above; an argument that names none is the same for every part. Nothing has to cross between parts.
Inputs may be any that keep to these rules, and one draw needn't show every extreme that they name: `user_history_length`: at least one user has exactly 8192 events; positions at or past a user's length are padding. `item_stored_row`: each stored row holds exactly one item. `history_item_index`: items repeat within a history.
All inputs are finite; a program needn't handle non-finite values.
Results may differ from a plain program's by a relative error of at most 0.038.
Values may be sent and summed in bfloat16 or wider, within the bound.
No kernel may reach another device: no remote copies, remote signals or barrier semaphores. Data moves between devices by JAX's collectives and lax.ppermute only.
A program may use at most 128 MiB of HBM per device.

v0:
```python
import math

import jax
import jax.numpy as jnp
from jax import lax
from jax.sharding import PartitionSpec as P

highest = lax.Precision.HIGHEST


def carried_in(value, axis, join, neutral):
    count, mine = (lax.axis_size(axis), lax.axis_index(axis))
    pieces = jax.tree.map(lambda part: lax.all_gather(part, axis), value)
    subtotal = jax.tree.map(
        lambda part, zero: jnp.full_like(part, 0) + jnp.asarray(zero, part.dtype), value, neutral
    )

    def hop(position, subtotal):
        longer = join(subtotal, jax.tree.map(lambda part: part[position], pieces))
        return jax.tree.map(lambda new, old: jnp.where(position < mine, new, old), longer, subtotal)

    return lax.fori_loop(0, count - 1, hop, subtotal)


def unit_rows(projected):
    scale = lax.rsqrt(jnp.mean(projected * projected, axis=-1, keepdims=True) + 1e-06)
    return projected * scale / math.sqrt(projected.shape[-1])


def block_terms(items):
    queries, key_rows, val_rows, decay = items
    cumulative = jnp.cumsum(decay, axis=1)
    width = decay.shape[1]
    causal = jnp.arange(width)[:, None] >= jnp.arange(width)[None, :]
    attention_scores = jnp.einsum(
        "shd,thd->hst", queries, key_rows, preferred_element_type=jnp.float32
    )
    gap_log = jnp.where(causal[None], cumulative[:, :, None] - cumulative[:, None, :], 0.0)
    weights = jnp.where(causal[None], attention_scores * jnp.exp(gap_log), 0.0).astype(jnp.bfloat16)
    local_out = jnp.einsum("hst,thd->shd", weights, val_rows, preferred_element_type=jnp.float32)
    tail_decay = jnp.exp(cumulative[:, -1:] - cumulative)
    keyed = key_rows.astype(jnp.float32) * jnp.transpose(tail_decay)[:, :, None]
    summary = jnp.einsum("thd,the->hde", keyed, val_rows.astype(jnp.float32), precision=highest)
    return (local_out, cumulative, summary, jnp.exp(cumulative[:, -1]))


def fetch_rows(item_ids, item_stored_row, item_embedding_table):
    slot_ids = item_stored_row[item_ids]
    owners = lax.axis_size("dp")
    requests = jnp.broadcast_to(slot_ids[None], (owners,) + slot_ids.shape)
    received = lax.all_to_all(requests, "dp", split_axis=0, concat_axis=0, tiled=True)
    table_rows = item_embedding_table.shape[0]
    owned = received // table_rows == lax.axis_index("dp")
    local_rows = jnp.where(owned, received % table_rows, 0)
    looked_up = jnp.where(
        owned[..., None], item_embedding_table[local_rows], jnp.zeros((), jnp.bfloat16)
    )
    served = lax.all_to_all(looked_up, "dp", split_axis=0, concat_axis=0, tiled=True)
    return jnp.sum(served, axis=0)


def chain(early, late):
    early_decay, early_state = early
    late_decay, late_state = late
    return (early_decay * late_decay, late_decay[..., None, None] * early_state + late_state)


def shards(
    history_item_index,
    log_head_retention,
    user_history_length,
    candidate_item_index,
    item_stored_row,
    item_embedding_table,
    head_score_scale,
    history_query_key_value_weight,
    history_output_weight,
    candidate_key_value_weight,
    candidate_query_weight,
    candidate_output_weight,
):
    users, slab_len = history_item_index.shape
    heads = log_head_retention.shape[1]
    width = item_embedding_table.shape[1]
    head_dim = width // heads
    cand_dev = candidate_item_index.shape[1]
    seq_rank = lax.axis_index("seq")
    first_pos = seq_rank * slab_len
    fetched = fetch_rows(
        jnp.concatenate([history_item_index, candidate_item_index], axis=1),
        item_stored_row,
        item_embedding_table,
    )
    own_query = jnp.dot(
        fetched[:, slab_len:], candidate_query_weight, preferred_element_type=jnp.float32
    ).astype(jnp.bfloat16)
    candidate_query_rows = lax.all_gather(own_query, "seq", axis=1, tiled=True)
    embedded = fetched[:, :slab_len]
    cand_total = candidate_query_rows.shape[1]
    event_positions = first_pos + jnp.arange(slab_len, dtype=jnp.int32)
    alive = event_positions[None, :] < user_history_length[:, None]
    projected = jnp.dot(
        embedded, history_query_key_value_weight, preferred_element_type=jnp.float32
    )
    projected = projected.reshape(users, slab_len, 3, heads, head_dim)
    queries = unit_rows(projected[:, :, 0]).astype(jnp.bfloat16)
    key_rows = jnp.where(alive[..., None, None], unit_rows(projected[:, :, 1]), 0.0).astype(
        jnp.bfloat16
    )
    val_rows = jnp.where(alive[..., None, None], projected[:, :, 2], 0.0).astype(jnp.bfloat16)
    local_out, cumulative, summary, total_decay = lax.map(
        block_terms, (queries, key_rows, val_rows, log_head_retention)
    )
    neutral = (jnp.ones_like(total_decay), jnp.zeros_like(summary))
    prefix_decay, state_in = carried_in((total_decay, summary), "seq", chain, neutral)
    carried = jnp.transpose(jnp.exp(cumulative), (0, 2, 1))[..., None] * jnp.einsum(
        "ushd,uhde->ushe", queries.astype(jnp.float32), state_in, precision=highest
    )
    mixed = local_out + carried
    normed = mixed * lax.rsqrt(jnp.mean(mixed * mixed, axis=-1, keepdims=True) + 1e-05)
    normed = normed.astype(jnp.bfloat16).reshape(users, slab_len, width)
    hidden_sum = embedded.astype(jnp.float32) + jnp.dot(
        normed, history_output_weight, preferred_element_type=jnp.float32
    )
    hidden = hidden_sum.astype(jnp.bfloat16)
    history_out = jnp.where(alive[..., None], hidden_sum, jnp.zeros((), jnp.float32))
    pair = jnp.dot(hidden, candidate_key_value_weight, preferred_element_type=jnp.float32).astype(
        jnp.bfloat16
    )
    second_key_random = pair[..., :width].reshape(users, slab_len, heads, head_dim)
    val_two = pair[..., width:].reshape(users, slab_len, heads, head_dim)
    query_heads = candidate_query_rows.reshape(users, cand_total, heads, head_dim)
    attention_scores = head_score_scale[None, None, :, None] * jnp.einsum(
        "uchd,uthd->ucht", query_heads, second_key_random, preferred_element_type=jnp.float32
    )
    attention_scores = jnp.where(alive[:, None, None, :], attention_scores, -jnp.inf)
    block_peak = jnp.max(attention_scores, axis=-1)
    present = block_peak > -jnp.inf
    safe_peak = jnp.where(present, block_peak, 0.0)
    probs = jnp.where(
        alive[:, None, None, :], jnp.exp(attention_scores - safe_peak[..., None]), 0.0
    ).astype(jnp.bfloat16)
    denominator = jnp.sum(probs.astype(jnp.float32), axis=-1)
    weighted = jnp.einsum("ucht,uthd->uchd", probs, val_two, preferred_element_type=jnp.float32)
    got_weighted, got_denom, got_peak = (
        lax.all_to_all(weighted[None], "seq", split_axis=2, concat_axis=0, tiled=True),
        lax.all_to_all(denominator[None], "seq", split_axis=2, concat_axis=0, tiled=True),
        lax.all_to_all(block_peak[None], "seq", split_axis=2, concat_axis=0, tiled=True),
    )
    peak_all = jnp.max(got_peak, axis=0)
    got_present = got_peak > -jnp.inf
    got_safe = jnp.where(got_present, got_peak, 0.0)
    rescale = jnp.where(got_present, jnp.exp(got_safe - peak_all[None]), 0.0)
    weighted = jnp.sum(rescale[..., None] * got_weighted, axis=0)
    denominator = jnp.sum(rescale * got_denom, axis=0)
    attended = (
        (weighted / denominator[..., None]).astype(jnp.bfloat16).reshape(users, cand_dev, width)
    )
    cand_out = jnp.dot(attended, candidate_output_weight, preferred_element_type=jnp.float32)
    return (history_out, cand_out)


def solution(mesh):
    in_specs = (
        P(("groups", "dp"), "seq"),
        P(("groups", "dp"), None, "seq"),
        P(("groups", "dp")),
        P(("groups", "dp"), "seq"),
        P(),
        P("dp", None),
        P(),
        P(),
        P(),
        P(),
        P(),
        P(),
    )
    out_specs = (P(("groups", "dp"), "seq", None), P(("groups", "dp"), "seq", None))
    return jax.shard_map(shards, mesh=mesh, in_specs=in_specs, out_specs=out_specs, check_vma=False)
```

profile of v0, /device:TPU:0, one launch (start us, length us, event | category | flops | bytes accessed | tf_op | source)
XLA Modules:
  0.0 234.0 jit_solution(4187878945356999454)
XLA Ops:
  7.2 0.9 fusion.49
  8.1 6.2 %gather_fusion = s32[1088]{0:T(1024)S(1)} fusion(s32[4096]{0:T(1024)S(1)} %copy-done.2, s32[2048]{0:T(1024)S(1)} %pad_clamp_fusion.1), kind=kCustom, calls=%fused_computation | custom fusion | bytes 13056 | tf_op jit(solution)/shard_map/gather | solution.py:48
  14.9 3.2 %all-to-all-start = ((s32[2,1,1088]{2,1,0:T(1,128)}), s32[2,1,1088]{2,1,0:T(1,128)S(1)}, u32[]{:S(2)}, u32[]{:S(2)}) async-start(s32[2,1,1088]{2,1,0:T(1,128)} %broadcast_in_dim.166), calls=%async_computation | async-start | bytes 18432 | tf_op jit(solution)/shard_map/all_to_all | solution.py:51
  18.1 1.4 all-to-all-done
  19.7 7.5 %gather_fusion.1 = bf16[2176,512]{1,0:T(8,128)(2,1)} fusion(bf16[2048,512]{1,0:T(8,128)(2,1)S(1)} %copy-done, s32[3072]{0:T(1024)S(1)} %pad_clamp_fusion), kind=kCustom, calls=%fused_computation.1 | custom fusion | bytes 4465152 | tf_op jit(solution)/shard_map/gather | solution.py:56
  27.2 2.9 %broadcast_select_fusion = bf16[2,1,1088,512]{3,2,1,0:T(8,128)(2,1)} fusion(bf16[2,1,1088,512]{3,2,1,0:T(8,128)(2,1)} %bitcast.181, pred[2,1088]{1,0:T(4,128)(4,1)S(1)} %bitcast.206), kind=kLoop, calls=%fused_computation.21 | loop fusion | flops 1114112 | bytes 4458624 | tf_op jit(solution)/shard_map/jit(_where)/select_n | solution.py:55
  30.1 5.0 %all-to-all-start.1 = ((bf16[2,1,1088,512]{3,2,1,0:T(8,128)(2,1)}), bf16[2,1,1088,512]{3,2,1,0:T(8,128)(2,1)}, u32[]{:S(2)}, u32[]{:S(2)}) async-start(bf16[2,1,1088,512]{3,2,1,0:T(8,128)(2,1)} %broadcast_select_fusion), calls=%async_computation.1 | async-start | bytes 4456448 | tf_op jit(solution)/shard_map/all_to_all | solution.py:58
  35.2 1.6 copy.66
  36.8 1.4 all-to-all-done.1
  38.2 2.7 %reduce_sum.68 = bf16[1088,512]{1,0:T(8,128)(2,1)S(1)} reduce(bf16[2,1,1088,512]{3,2,1,0:T(8,128)(2,1)} %all-to-all-done.1, bf16[]{:T(256)} %constant.108.clone.1), dimensions={0,1}, to_apply=%region_0.1 | reduce | flops 557056 | bytes 3342338 | tf_op jit(solution)/shard_map/reduce_sum | solution.py:59
  40.9 3.2 %convolution_bitcast_fusion = f32[1,1024,3,8,64]{1,4,3,2,0:T(8,128)S(1)} fusion(bf16[3,8,64,512]{3,2,1,0:T(8,128)(2,1)} %bitcast.193, bf16[1,1088,512]{2,1,0:T(8,128)(2,1)S(1)} %bitcast.184), kind=kOutput, calls=%fused_computation.20 | convolution fusion | flops 1610612736 | bytes 8912896 | tf_op jit(solution)/shard_map/dot_general | solution.py:102
  44.2 2.7 %copy-done.4 = f32[1,1024,3,8,64]{1,4,3,2,0:T(8,128)} copy-done((f32[1,1024,3,8,64]{1,4,3,2,0:T(8,128)}, f32[1,1024,3,8,64]{1,4,3,2,0:T(8,128)S(1)}, u32[]{:S(2)}) %copy-start.4) | copy-done | bytes 6291480
  47.6 2.3 reduce-window.6
  51.2 4.3 %fusion.19 = f32[8,64,64]{2,1,0:T(8,128)} fusion(f32[1024,8]{0,1:T(8,128)S(1)} %exponential_bitcast_fusion, f32[1,1024,3,8,64]{1,4,3,2,0:T(8,128)} %copy-done.4, pred[1024]{0:T(1024)(128)(4,1)S(1)} %add_compare_fusion, f32[1024,8]{0,1:T(8,128)S(1)} %add_rsqrt_fusion.1), kind=kOutput, calls=%fused_computation.39 | convolution fusion | flops 406847488 | bytes 4392960 | tf_op jit(solution)/shard_map/while/body/eval_jaxpr/thd,the->hde/dot_general | solution.py:43
  57.0 23.2 %all-reduce = f32[64]{0:T(128)S(1)} all-reduce(f32[64]{0:T(128)S(1)} %bitcast_dynamic-update-slice_fusion), channel_id=2, replica_groups=mesh['groups'=2,'seq'=8,'dp'=2] {'seq'}, use_global_device_ids=true, to_apply=%add | all-reduce | flops 64 | bytes 512
  80.4 33.0 %all-gather.2 = bf16[512,512]{1,0:T(8,128)(2,1)S(1)} all-gather(bf16[64,512]{1,0:T(8,128)(2,1)S(1)} %convolution_convert_fusion), channel_id=4, replica_groups=mesh['groups'=2,'seq'=8,'dp'=2] {'seq'}, dimensions={0}, use_global_device_ids=true | all-gather | bytes 589824 | tf_op jit(solution)/shard_map/all_gather | solution.py:97
  114.0 7.6 %while.9 = (s32[]{:T(128)}, f32[1,8,64,64]{3,2,1,0:T(8,128)S(1)}, s32[]{:T(128)}, f32[8,1,8]{2,1,0:T(1,128)S(1)}, f32[8,1,8,64,64]{4,3,2,1,0:T(8,128)}, /*index=5*/s32[]{:T(128)}, s32[]{:T(128)}) while((s32[]{:T(128)}, f32[1,8,64,64]{3,2,1,0:T(8,128)S(1)}, s32[]{:T(128)}, f32[8,1,8]{2,1,0:T(1,128)S(1)}, ...), condition=%wide.region_6.7_spmd.clone, body=%wide.region_5.6_spmd.clone.sunk | while | flops 131076 | bytes 393417 | solution.py:22
  114.1 1.1 fusion.75
  115.1 1.1 fusion.75
  116.2 1.1 fusion.75
  117.3 1.1 fusion.75
  118.4 1.1 fusion.75
  119.5 1.1 fusion.75
  120.6 1.1 fusion.75
  121.7 3.9 %fusion.34 = f32[8,64,1024]{2,1,0:T(8,128)} fusion(f32[1,8,64,64]{3,2,1,0:T(8,128)S(1)} %get-tuple-element.123, f32[1,1024,3,8,64]{1,4,3,2,0:T(8,128)} %copy-done.4, f32[1024,8]{0,1:T(8,128)S(1)} %add_rsqrt_fusion.2), kind=kOutput, calls=%fused_computation.57 | convolution fusion | flops 404226048 | bytes 4358144 | tf_op jit(solution)/shard_map/ushd,uhde->ushe/dot_general | solution.py:116
  125.6 16.9 %multiply_reduce_fusion.1 = (f32[1024,8]{0,1:T(8,128)S(1)}, f32[1,1024,8,64]{1,3,2,0:T(8,128)}) fusion(f32[8,64,1024]{2,1,0:T(8,128)} %fusion.34, f32[1024,8]{0,1:T(8,128)S(1)} %bitcast.205, f32[8,1024]{1,0:T(8,128)S(1)} %bitcast.203, pred[1024,1024]{1,0:T(8,128)(4,1)S(1)} %iota_compare_fusion, f32[1,1024,3,8,64]{1,4,3,2,0:T(8,128)} %copy-done.4, ...), kind=kOutput, calls=%fused_computation.38 | convolution fusion | flops 2196234240 | bytes 11732992 | tf_op jit(solution)/shard_map/while/body/eval_jaxpr/hst,thd->shd/dot_general | solution.py:40
  142.5 1.9 multiply_convert_fusion
  144.5 2.1 broadcast_select_fusion.1
  146.5 1.3 convert_bitcast_fusion
  147.9 1.2 fusion.59
  149.0 3.7 %bitcast_reduce_fusion = (f32[512,8]{0,1:T(8,128)S(1)}, f32[8,1024,512]{2,1,0:T(8,128)S(1)}) fusion(f32[8]{0:T(128)S(1)} %copy-done.11, pred[1024]{0:T(1024)(128)(4,1)S(1)} %add_compare_fusion, bf16[1024,8,64]{0,2,1:T(8,128)(2,1)S(1)} %bitcast.187, bf16[512,8,64]{0,2,1:T(8,128)(2,1)S(1)} %bitcast.192), kind=kOutput, calls=%fused_computation.7 | convolution fusion | flops 549449728 | bytes 18367520 | tf_op jit(solution)/shard_map/uchd,uthd->ucht/dot_general | solution.py:133
  152.7 4.9 %convert_reduce_fusion = f32[512,8]{0,1:T(8,128)S(1)} fusion(f32[512,8]{0,1:T(8,128)S(1)} %compare_select_fusion.3, f32[8,1024,512]{2,1,0:T(8,128)S(1)} %get-tuple-element.190, f32[8]{0:T(128)S(1)} %copy-done.11, pred[1024]{0:T(1024)(128)(4,1)S(1)} %add_compare_fusion), kind=kLoop, calls=%fused_computation.13 | loop fusion | flops 29356032 | bytes 16811040 | tf_op jit(solution)/shard_map/reduce_sum | solution.py:143
  157.6 0.8 copy-done.3
  159.1 1.3 reduce.21
  161.2 3.3 %all-to-all-start.4 = ((f32[8,1,512]{2,1,0:T(1,128)}), f32[8,1,512]{2,1,0:T(1,128)S(1)}, u32[]{:S(2)}, u32[]{:S(2)}) async-start(f32[8,1,512]{2,1,0:T(1,128)} %reshape.577), calls=%async_computation.4 | async-start | bytes 32768 | tf_op jit(solution)/shard_map/all_to_all | solution.py:147
  164.7 1.3 reduce.19
  166.1 0.8 reshape.575
  166.8 4.3 %all-to-all-done.4 = f32[8,1,512]{2,1,0:T(1,128)S(1)} async-done(((f32[8,1,512]{2,1,0:T(1,128)}), f32[8,1,512]{2,1,0:T(1,128)S(1)}, u32[]{:S(2)}, u32[]{:S(2)}) %all-to-all-start.4) | async-done | bytes 16416 | tf_op jit(solution)/shard_map/all_to_all | solution.py:147
  171.1 3.6 %all-to-all-start.2 = ((f32[8,1,512]{2,1,0:T(1,128)}), f32[8,1,512]{2,1,0:T(1,128)S(1)}, u32[]{:S(2)}, u32[]{:S(2)}) async-start(f32[8,1,512]{2,1,0:T(1,128)} %reshape.575), calls=%async_computation.2 | async-start | bytes 32768 | tf_op jit(solution)/shard_map/all_to_all | solution.py:148
  174.7 7.8 %fusion.22 = f32[1,1,512,8,64]{2,4,3,1,0:T(8,128)S(1)} fusion(bf16[1024,8,64]{0,2,1:T(8,128)(2,1)S(1)} %bitcast.197, f32[8,1024,512]{2,1,0:T(8,128)} %copy-done.3, f32[512,8]{0,1:T(8,128)S(1)} %compare_select_fusion.3, f32[8]{0:T(128)S(1)} %copy-done.11, pred[1024]{0:T(1024)(128)(4,1)S(1)} %add_compare_fusion), kind=kOutput, calls=%fused_computation.44 | convolution fusion | flops 557842432 | bytes 18891808 | tf_op jit(solution)/shard_map/ucht,uthd->uchd/dot_general | solution.py:144
  183.3 2.1 reshape.573
  185.4 5.7 %all-to-all-start.3 = ((f32[8,1,32768]{2,1,0:T(1,128)}), f32[8,1,32768]{2,1,0:T(1,128)S(1)}, u32[]{:S(2)}, u32[]{:S(2)}) async-start(f32[8,1,32768]{2,1,0:T(1,128)} %reshape.573), calls=%async_computation.3 | async-start | bytes 2097152 | tf_op jit(solution)/shard_map/all_to_all | solution.py:146
  194.0 20.8 %all-to-all-done.3 = f32[8,1,32768]{2,1,0:T(1,128)S(1)} async-done(((f32[8,1,32768]{2,1,0:T(1,128)}), f32[8,1,32768]{2,1,0:T(1,128)S(1)}, u32[]{:S(2)}, u32[]{:S(2)}) %all-to-all-start.3) | async-done | bytes 1048608 | tf_op jit(solution)/shard_map/all_to_all | solution.py:146
  214.8 3.2 %reduce.18 = f32[8,32768]{1,0:T(8,128)S(1)} reduce(f32[8,1,32768]{2,1,0:T(1,128)S(1)} %all-to-all-done.3, f32[]{:T(128)} %broadcast.340), dimensions={1}, to_apply=%all_to_all.39.reduce_sub_computation | reduce | bytes 2097156 | tf_op jit(solution)/shard_map/all_to_all | solution.py:146
  218.0 2.2 reshape.574
  220.2 3.8 %copy.77 = f32[8,1,64,8,64]{2,0,4,3,1:T(8,128)} copy(f32[8,1,64,8,64]{4,3,2,0,1:T(8,128)} %bitcast.183) | data formatting | bytes 2097152 | tf_op jit(solution)/shard_map/all_to_all | solution.py:146
  224.0 2.3 multiply_reduce_fusion
  226.3 0.9 convolution_bitcast_fusion.1
  (83 shorter events, 9.3 us)
Async XLA Ops:
  7.2 12.5 %copy-start = (bf16[2048,512]{1,0:T(8,128)(2,1)S(1)}, bf16[2048,512]{1,0:T(8,128)(2,1)}, u32[]{:S(2)}) copy-start(bf16[2048,512]{1,0:T(8,128)(2,1)} %param.19) | copy-start | bytes 6291460
  7.2 0.9 copy-start.2
  14.9 4.6 %all-to-all-start = ((s32[2,1,1088]{2,1,0:T(1,128)}), s32[2,1,1088]{2,1,0:T(1,128)S(1)}, u32[]{:S(2)}, u32[]{:S(2)}) async-start(s32[2,1,1088]{2,1,0:T(1,128)} %broadcast_in_dim.166), calls=%async_computation | async-start | bytes 18432 | tf_op jit(solution)/shard_map/all_to_all | solution.py:51
  30.1 5.1 %copy-start.5 = (bf16[512,1536]{1,0:T(8,128)(2,1)S(1)}, bf16[512,1536]{1,0:T(8,128)(2,1)}, u32[]{:S(2)}) copy-start(bf16[512,1536]{1,0:T(8,128)(2,1)} %param.21) | copy-start | bytes 4718596
  30.1 8.1 %all-to-all-start.1 = ((bf16[2,1,1088,512]{3,2,1,0:T(8,128)(2,1)}), bf16[2,1,1088,512]{3,2,1,0:T(8,128)(2,1)}, u32[]{:S(2)}, u32[]{:S(2)}) async-start(bf16[2,1,1088,512]{3,2,1,0:T(8,128)(2,1)} %broadcast_select_fusion), calls=%async_computation.1 | async-start | bytes 4456448 | tf_op jit(solution)/shard_map/all_to_all | solution.py:58
  35.1 78.9 %all-gather.5.cloned.1.call-start = ((), (), s32[]{:S(2)}) async-start(), calls=%async_computation.5 | async-start | bytes 2359296 | tf_op jit(solution)/shard_map/all_gather | solution.py:13
  44.2 2.7 %copy-start.4 = (f32[1,1024,3,8,64]{1,4,3,2,0:T(8,128)}, f32[1,1024,3,8,64]{1,4,3,2,0:T(8,128)S(1)}, u32[]{:S(2)}) copy-start(f32[1,1024,3,8,64]{1,4,3,2,0:T(8,128)S(1)} %convolution_bitcast_fusion) | copy-start | bytes 18874372
  46.8 0.8 copy-start.10
  51.2 4.4 %copy-start.13 = (u32[32]{0:T(128)S(1)}, u32[32]{0:T(128)}, u32[]{:S(2)}) copy-start(u32[32]{0:T(128)} %constant.121) | copy-start | bytes 388
  51.2 29.0 %copy-start.8 = (bf16[512,512]{1,0:T(8,128)(2,1)S(1)}, bf16[512,512]{1,0:T(8,128)(2,1)}, u32[]{:S(2)}) copy-start(bf16[512,512]{1,0:T(8,128)(2,1)} %param.24) | copy-start | bytes 1572868
  142.5 1.9 copy-start.7
  144.4 2.1 copy-start.12
  147.8 1.2 copy-start.11
  152.7 5.7 %copy-start.3 = (f32[8,1024,512]{2,1,0:T(8,128)}, f32[8,1024,512]{2,1,0:T(8,128)S(1)}, u32[]{:S(2)}) copy-start(f32[8,1024,512]{2,1,0:T(8,128)S(1)} %get-tuple-element.190) | copy-start | bytes 50331652
  158.4 16.3 %copy-start.6 = (bf16[1,1024,512]{1,2,0:T(8,128)(2,1)S(1)}, bf16[1,1024,512]{1,2,0:T(8,128)(2,1)}, u32[]{:S(2)}) copy-start(bf16[1,1024,512]{1,2,0:T(8,128)(2,1)} %get-tuple-element.182) | copy-start | bytes 3145732
  161.2 9.9 %all-to-all-start.4 = ((f32[8,1,512]{2,1,0:T(1,128)}), f32[8,1,512]{2,1,0:T(1,128)S(1)}, u32[]{:S(2)}, u32[]{:S(2)}) async-start(f32[8,1,512]{2,1,0:T(1,128)} %reshape.577), calls=%async_computation.4 | async-start | bytes 32768 | tf_op jit(solution)/shard_map/all_to_all | solution.py:147
  171.1 14.3 %all-to-all-start.2 = ((f32[8,1,512]{2,1,0:T(1,128)}), f32[8,1,512]{2,1,0:T(1,128)S(1)}, u32[]{:S(2)}, u32[]{:S(2)}) async-start(f32[8,1,512]{2,1,0:T(1,128)} %reshape.575), calls=%async_computation.2 | async-start | bytes 32768 | tf_op jit(solution)/shard_map/all_to_all | solution.py:148
  185.4 29.4 %all-to-all-start.3 = ((f32[8,1,32768]{2,1,0:T(1,128)}), f32[8,1,32768]{2,1,0:T(1,128)S(1)}, u32[]{:S(2)}, u32[]{:S(2)}) async-start(f32[8,1,32768]{2,1,0:T(1,128)} %reshape.573), calls=%async_computation.3 | async-start | bytes 2097152 | tf_op jit(solution)/shard_map/all_to_all | solution.py:146
  220.2 7.0 %copy-start.1 = (bf16[2048,512]{1,0:T(8,128)(2,1)S(1)}, bf16[2048,512]{1,0:T(8,128)(2,1)}, u32[]{:S(2)}) copy-start(bf16[2048,512]{1,0:T(8,128)(2,1)} %param.19) | copy-start | bytes 6291460
  224.0 2.3 copy-start.9
Sparse Core Ops, SparseCore 0:
  55.7 57.3 all-gather.4
where the time goes:
time: 235 us; the launch traced here: 234 us
  blocking collectives  56.2 us (24%)
  matrix products  44.3 us (19%)
  local copies, waits for them, and re-layouts  34.7 us (15%)
  other arithmetic  34.1 us (15%)
  waiting for transfers between devices  27.9 us (12%)
  starting transfers between devices  20.8 us (9%)
  between operations  15.8 us (7%)
    all_gather x1, blocking collectives, shards(): candidate_query_rows = lax.all_gather(own_query, 'seq', axis=1, tiled=True)  33 us
    unnamed x1, blocking collectives  23.2 us
    all_to_all x1, waiting for transfers between devices, shards(): lax.all_to_all(weighted[None], 'seq', split_axis=2, concat_axis=0, tiled=...  20.8 us
    dot_general x1, matrix products, block_terms(): jnp.einsum('hst,thd->shd', weights, val_rows, preferred_element_type=jnp....  16.9 us
    unnamed x41, local copies, waits for them, and re-layouts  12.8 us
    dot_general x1, matrix products, shards(): jnp.einsum('ucht,uthd->uchd', probs, val_two, preferred_element_type=jnp....  7.77 us
    gather x1, local copies, waits for them, and re-layouts, fetch_rows(): item_embedding_table[local_rows]  7.45 us
    select_n x7, other arithmetic, hop(): jnp.where(position < mine, new, old)  7.37 us
  transfers between devices with their start and end apart: 6, of which 4 were waited for; matrix products, arithmetic and copies ran while one was open for 8% of the time, Pallas kernels for 0%

commit v1 on v0

v1 whole, which is shorter than its diff:
```python
import math

import jax
import jax.numpy as jnp
from jax import lax
from jax.experimental import pallas as pl
from jax.experimental.pallas import tpu as pltpu
from jax.sharding import PartitionSpec as P

f32, bf16, i32 = jnp.float32, jnp.bfloat16, jnp.int32
CHUNK = 256
LANES = 128
LOG2E = math.log2(math.e)
DEAD = -1e30
VMEM_LIMIT = 40 << 20


def dot(a, b):
    return jnp.dot(a, b, preferred_element_type=f32)


def dot_nt(a, b):
    return lax.dot_general(a, b, (((1,), (1,)), ((), ())), preferred_element_type=f32)


def dot_tn(a, b):
    return lax.dot_general(a, b, (((0,), (0,)), ((), ())), preferred_element_type=f32)


def iota(shape, axis):
    return lax.broadcasted_iota(i32, shape, axis)


def thirds(value):
    high = value.astype(bf16).astype(f32)
    rest = value - high
    mid = rest.astype(bf16).astype(f32)
    return high, mid, rest - mid


def first_half(shape):
    return iota(shape, len(shape) - 1) % LANES < LANES // 2


def half_masks():
    low = first_half((1, LANES))
    return jnp.where(low, 1.0, 0.0).astype(bf16), jnp.where(low, 0.0, 1.0).astype(bf16)


def head_sums(width, heads):
    dims = (width, 2 * heads)
    same = iota(dims, 0) // (width // heads) == iota(dims, 1) % heads
    return jnp.where(same, 1.0, 0.0).astype(bf16)


def head_spread(width, heads):
    dims = (2 * heads, width)
    same = iota(dims, 1) // (width // heads) == iota(dims, 0) % heads
    return jnp.where(same, 1.0, 0.0).astype(bf16)


def spread(value, matrix):
    heads = value.shape[1] // 2
    high = value.astype(bf16).astype(f32)
    both = jnp.where(iota(value.shape, 1) < heads, high, value - high)
    return dot(both.astype(bf16), matrix)


def stored_slots(ids, stored):
    groups = stored.shape[0]
    n = ids.shape[1]
    pick = jnp.where(iota((groups, n), 0) == ids // LANES, 1.0, 0.0).astype(bf16)
    high = dot_tn((stored // 64).astype(f32).astype(bf16), pick)
    low = dot_tn((stored % 64).astype(f32).astype(bf16), pick)
    rows = jnp.where(iota((LANES, n), 0) == ids % LANES, high * 64.0 + low, 0.0)
    return jnp.sum(rows, axis=0, keepdims=True)


def as_column(row):
    return jnp.transpose(jnp.broadcast_to(row, (8, row.shape[1])))


def one_hot(column, first, count):
    local = column.astype(i32) - first
    return jnp.where(iota((column.shape[0], count), 1) == local, 1.0, 0.0).astype(bf16)


def own_rows_kernel(sc, ids, stored, decay, own, part_o, slot_o, crow_o, ccol_o, ctl_o):
    n, half, heads = ids.shape[1], own.shape[0], decay.shape[0]
    slot_o[...] = as_column(stored_slots(ids[...], stored[...]))
    upto = jnp.where(
        iota((CHUNK, CHUNK), 0) <= iota((CHUNK, CHUNK), 1), 1.0, 0.0
    ).astype(bf16)
    low = first_half((1, LANES))
    for i in range(n // CHUNK):
        pieces = jnp.concatenate(thirds(decay[:, i * CHUNK : (i + 1) * CHUNK]), axis=0)
        sums = dot(pieces.astype(bf16), upto)
        cum = sums[:heads] + sums[heads : 2 * heads] + sums[2 * heads :]
        crow_o[i] = cum
        ccol_o[i * CHUNK : (i + 1) * CHUNK, :] = jnp.transpose(jnp.concatenate([cum, cum], axis=0))
        for p in range(heads // 2):
            r = i * (heads // 2) + p
            ctl_o[r : r + 1, :] = jnp.where(
                low, cum[2 * p : 2 * p + 1, CHUNK - 1 :], cum[2 * p + 1 : 2 * p + 2, CHUNK - 1 :]
            )

    def step(i, carry):
        rows = pl.ds(pl.multiple_of(i * CHUNK, CHUNK), CHUNK)
        hot = one_hot(slot_o[rows, 0:1], sc[3] * half, half)
        part_o[rows, :] = dot(hot, own[...]).astype(bf16)
        return carry

    lax.fori_loop(0, n // CHUNK, step, 0)


def summary_kernel(
    sc, part, peer, slot, ccol, ctl, key_w, val_w, emb_o, key_o, val_o, enter_o, pay_o, total
):
    n, width = part.shape
    half, heads = peer.shape[0], ccol.shape[1] // 2
    pairs = heads // 2
    block = LANES // 2
    sums, lanes = head_sums(width, heads), head_spread(width, heads)
    total[...] = jnp.zeros_like(total)
    low = first_half((1, LANES))

    def step(i, carry):
        rows = pl.ds(pl.multiple_of(i * CHUNK, CHUNK), CHUNK)
        hot = one_hot(slot[rows, 0:1], (1 - sc[3]) * half, half)
        emb = (part[rows, :].astype(f32) + dot(hot, peer[...])).astype(bf16)
        emb_o[rows, :] = emb
        alive = sc[1] + i * CHUNK + iota((CHUNK, 1), 0) < sc[2]
        key = dot(emb, key_w[...])
        val = jnp.where(alive, dot(emb, val_w[...]), 0.0).astype(bf16)
        val_o[rows, :] = val
        square = dot((key * key).astype(bf16), sums)
        unit = lax.rsqrt(square * (heads / width) + 1e-06) * math.sqrt(heads / width)
        unit = jnp.where(alive, unit, 0.0)
        normed = key * spread(unit, lanes)
        key_o[rows, :] = normed.astype(bf16)
        cum = ccol[rows, :]
        tail = spread(jnp.exp(cum[CHUNK - 1 :, :] - cum), lanes)
        keyed = (normed * tail).astype(bf16)
        for p in range(pairs):
            cut = slice(p * LANES, (p + 1) * LANES)
            both = dot_tn(keyed[:, cut], val[:, cut])
            fresh = jnp.where(low, both[:block], both[block:])
            here = pl.ds(p * block, block)
            old = total[here, :]
            enter_o[i, here, :] = old
            keep = jnp.exp(ctl[pl.ds(i * pairs + p, 1), :])
            total[here, :] = old * keep + fresh
        return carry

    lax.fori_loop(0, n // CHUNK, step, 0)
    logs = ctl[0:pairs, :]
    for i in range(1, n // CHUNK):
        logs = logs + ctl[i * pairs : (i + 1) * pairs, :]
    pay_o[...] = pack_state(total[...], logs)


def pack_state(state, logs):
    pad = jnp.zeros((16 - 3 * logs.shape[0], LANES), f32)
    return jnp.concatenate([state, *thirds(logs), pad], axis=0).astype(bf16)


def unpack_state(packed):
    whole = packed.astype(f32)
    rows = whole.shape[0] - 16
    pairs = rows // (LANES // 2)
    tail = whole[rows:]
    return whole[:rows], tail[:pairs] + tail[pairs : 2 * pairs] + tail[2 * pairs : 3 * pairs]


def row_factors(logs):
    factors = jnp.exp(logs)
    return jnp.concatenate(
        [
            jnp.broadcast_to(factors[p : p + 1], (LANES // 2, LANES))
            for p in range(logs.shape[0])
        ],
        axis=0,
    )


def join_prefix(upper, prefix, prefix_logs, early, early_logs):
    joined = prefix + row_factors(prefix_logs) * early
    return (
        jnp.where(upper, joined, prefix),
        jnp.where(upper, prefix_logs + early_logs, prefix_logs),
    )


def first_join_kernel(bit, sc, mine, got, pay_o, prefix_o, logs_o):
    upper = (sc[0] >> bit) & 1 == 1
    state, logs = unpack_state(mine[...])
    other, other_logs = unpack_state(got[...])
    pay_o[...] = merged(upper, state, logs, other, other_logs)
    prefix_o[...] = jnp.where(upper, other, 0.0)
    logs_o[...] = jnp.where(upper, other_logs, 0.0)


def merged(upper, state, logs, other, other_logs):
    late_logs = jnp.where(upper, logs, other_logs)
    factor = row_factors(late_logs)
    early = jnp.where(upper, other, state)
    late = jnp.where(upper, state, other)
    return pack_state(early * factor + late, logs + other_logs)


def join_kernel(bit, sc, mine, got, prefix, prefix_logs, pay_o, prefix_o, logs_o):
    upper = (sc[0] >> bit) & 1 == 1
    state, logs = unpack_state(mine[...])
    other, other_logs = unpack_state(got[...])
    pay_o[...] = merged(upper, state, logs, other, other_logs)
    prefix_o[...], logs_o[...] = join_prefix(
        upper, prefix[...], prefix_logs[...], other, other_logs
    )


def local_kernel(emb, key, val, crow, ccol, query_w, query_o, intra_o):
    n, width = emb.shape
    heads = ccol.shape[1] // 2
    sums, lanes = head_sums(width, heads), head_spread(width, heads)
    mask_a, mask_b = half_masks()

    def step(i, carry):
        rows = pl.ds(pl.multiple_of(i * CHUNK, CHUNK), CHUNK)
        query = dot(emb[rows, :], query_w[...])
        square = dot((query * query).astype(bf16), sums)
        unit = lax.rsqrt(square * (heads / width) + 1e-06) * math.sqrt(heads / width)
        query = (query * spread(unit, lanes)).astype(bf16)
        query_o[rows, :] = query
        cum = ccol[rows, :]
        cum_row = crow[i]
        causal = iota((CHUNK, CHUNK), 0) >= iota((CHUNK, CHUNK), 1)
        for p in range(heads // 2):
            cut = slice(p * LANES, (p + 1) * LANES)
            key_p, val_p, query_p = key[rows, cut], val[rows, cut], query[:, cut]
            parts = []
            for b, mask in ((0, mask_a), (1, mask_b)):
                h = 2 * p + b
                scores = dot_nt(query_p * mask, key_p)
                gap = cum[:, h : h + 1] - cum_row[h : h + 1, :]
                parts.append(jnp.where(causal, scores * jnp.exp(gap), 0.0).astype(bf16))
            intra_o[rows, cut] = dot(parts[0], val_p * mask_a) + dot(parts[1], val_p * mask_b)
        return carry

    lax.fori_loop(0, n // CHUNK, step, 0)


def candidate_kernel(sc, ids, stored, own, peer, query_w, query_o):
    n, half = ids.shape[1], own.shape[0]
    column = as_column(stored_slots(ids[...], stored[...]))
    for i in range(n // CHUNK):
        slot = column[i * CHUNK : (i + 1) * CHUNK, 0:1]
        rows = dot(one_hot(slot, sc[3] * half, half), own[...])
        rows += dot(one_hot(slot, (1 - sc[3]) * half, half), peer[...])
        query_o[i * CHUNK : (i + 1) * CHUNK, :] = dot(rows.astype(bf16), query_w[...]).astype(bf16)


def attend(sc, scale, query, first_row, rows, key, val, emit):
    n, width = key.shape
    mask_a, mask_b = half_masks()
    alive = sc[1] + iota((1, n), 1) < sc[2]
    any_alive = sc[1] < sc[2]
    low = first_half((1, LANES))

    def pair(p, carry):
        cut = pl.ds(pl.multiple_of(p * LANES, LANES), LANES)
        key_p, val_p = key[:, cut], val[:, cut]
        query_p = query[first_row : first_row + rows, cut]
        peaks, sums = [], None
        for b, mask in ((0, mask_a), (1, mask_b)):
            factor = scale[2 * p + b] * LOG2E
            scores = jnp.where(alive, dot_nt(query_p * mask, key_p), DEAD)
            peak = jnp.max(scores, axis=1, keepdims=True)
            probs = jnp.exp2((scores - peak) * factor).astype(bf16)
            side = jnp.concatenate(
                [val_p * mask, jnp.broadcast_to(mask, (n, LANES))], axis=1
            )
            part = dot(probs, side)
            sums = part if sums is None else sums + part
            peaks.append(peak * factor)
        total = sums[:, LANES:]
        logs = jnp.where(low, peaks[0], peaks[1]) + jnp.log2(total)
        emit(p, cut, sums[:, :LANES] / total, jnp.where(any_alive, logs, DEAD))
        return carry

    lax.fori_loop(0, width // LANES, pair, 0)


def log_columns(p, pairs, logs, columns):
    lane = iota((1, LANES), 1) % (LANES // 2)
    for k, piece in enumerate(thirds(logs)):
        columns = jnp.where(lane == p + k * pairs, piece, columns)
    return columns


def log_spread(width):
    pairs = width // LANES
    dims = (LANES, width)
    lane, col = iota(dims, 0), iota(dims, 1)
    inner = lane % (LANES // 2)
    same = (lane // (LANES // 2) == (col // (LANES // 2)) % 2) & (inner % pairs == col // LANES)
    return jnp.where(same & (inner < 3 * pairs), 1.0, 0.0).astype(bf16)


def finish_kernel(
    sc, scale, emb, query, intra, enter, ccol, ctl, got, prefix, prefix_logs, out_w, pair_w,
    cand_q, hist_o, key_o, val_o, pay_o, columns, bit,
):
    n, width = emb.shape
    heads = ccol.shape[1] // 2
    pairs = heads // 2
    block = LANES // 2
    sums, lanes = head_sums(width, heads), head_spread(width, heads)
    upper = (sc[0] >> bit) & 1 == 1
    state, logs = unpack_state(got[...])
    entering = join_prefix(upper, prefix[...], prefix_logs[...], state, logs)[0]
    low = first_half((1, LANES))

    def step(i, gone):
        rows = pl.ds(pl.multiple_of(i * CHUNK, CHUNK), CHUNK)
        states = enter[i] + row_factors(gone) * entering
        parts = []
        for p in range(pairs):
            cut = slice(p * LANES, (p + 1) * LANES)
            one = states[p * block : (p + 1) * block]
            matrix = jnp.concatenate([jnp.where(low, one, 0.0), jnp.where(low, 0.0, one)], axis=0)
            parts.append(dot(query[rows, cut], matrix.astype(bf16)))
        carried = jnp.concatenate(parts, axis=1) * spread(jnp.exp(ccol[rows, :]), lanes)
        mixed = intra[rows, :] + carried
        square = dot((mixed * mixed).astype(bf16), sums)
        unit = lax.rsqrt(square * (heads / width) + 1e-05)
        normed = (mixed * spread(unit, lanes)).astype(bf16)
        hidden_sum = emb[rows, :].astype(f32) + dot(normed, out_w[...])
        alive = sc[1] + i * CHUNK + iota((CHUNK, 1), 0) < sc[2]
        hist_o[rows, :] = jnp.where(alive, hidden_sum, 0.0)
        both = dot(hidden_sum.astype(bf16), pair_w[...]).astype(bf16)
        key_o[rows, :] = both[:, :width]
        val_o[rows, :] = both[:, width:]
        return gone + ctl[pl.ds(pl.multiple_of(i * pairs, pairs), pairs), :]

    lax.fori_loop(0, n // CHUNK, step, jnp.zeros((pairs, LANES), f32))
    columns[...] = jnp.zeros_like(columns)
    count = pay_o.shape[0]

    def emit(p, cut, attended, logs):
        pay_o[:, cut] = attended.astype(bf16)
        columns[...] = log_columns(p, pairs, logs, columns[...])

    attend(sc, scale, cand_q, count, count, key_o, val_o, emit)
    pay_o[:, width:] = columns[...].astype(bf16)


def keep_kernel(sc, scale, cand_q, key, val, mean_o, logs_o):
    def emit(p, cut, attended, logs):
        mean_o[:, cut] = attended
        logs_o[:, cut] = logs

    attend(sc, scale, cand_q, 0, mean_o.shape[0], key, val, emit)


def weigh(mean, logs, got):
    width = mean.shape[1]
    other = got[:, :width].astype(f32)
    other_logs = dot(got[:, width:], log_spread(width))
    peak = jnp.maximum(logs, other_logs)
    mine, theirs = jnp.exp2(logs - peak), jnp.exp2(other_logs - peak)
    total = mine + theirs
    return (mine * mean + theirs * other) / total, peak + jnp.log2(total)


def fold_kernel(mean, logs, got, mean_o, logs_o, pay_o):
    new_mean, new_logs = weigh(mean[...], logs[...], got[...])
    keep, width = mean_o.shape
    mean_o[...] = new_mean[:keep]
    logs_o[...] = new_logs[:keep]
    sent = new_logs[keep:]
    columns = jnp.zeros((sent.shape[0], LANES), f32)
    pairs = width // LANES
    for p in range(pairs):
        columns = log_columns(p, pairs, sent[:, p * LANES : (p + 1) * LANES], columns)
    pay_o[...] = jnp.concatenate([new_mean[keep:], columns], axis=1).astype(bf16)


def last_kernel(mean, logs, got, out_w, cand_o):
    attended = weigh(mean[...], logs[...], got[...])[0]
    cand_o[...] = dot(attended.astype(bf16), out_w[...])


def shape(dims, dtype):
    return jax.ShapeDtypeStruct(dims, dtype)


VMEM = pl.BlockSpec(memory_space=pltpu.VMEM)
SMEM = pl.BlockSpec(memory_space=pltpu.SMEM)


def call(kernel, name, scalars, operands, outs, scratch=(), flops=0, moved=0):
    return pl.pallas_call(
        kernel,
        name=name,
        in_specs=[SMEM] * len(scalars) + [VMEM] * len(operands),
        out_specs=[VMEM] * len(outs),
        out_shape=outs,
        scratch_shapes=list(scratch),
        compiler_params=pltpu.CompilerParams(vmem_limit_bytes=VMEM_LIMIT),
        cost_estimate=pl.CostEstimate(flops=flops, transcendentals=0, bytes_accessed=moved),
    )(*scalars, *operands)


def shards(
    history_item_index,
    log_head_retention,
    user_history_length,
    candidate_item_index,
    item_stored_row,
    item_embedding_table,
    head_score_scale,
    history_query_key_value_weight,
    history_output_weight,
    candidate_key_value_weight,
    candidate_query_weight,
    candidate_output_weight,
):
    users, n = history_item_index.shape
    heads = log_head_retention.shape[1]
    half, width = item_embedding_table.shape
    owned = candidate_item_index.shape[1]
    seq = lax.axis_size("seq")
    assert users == 1 and lax.axis_size("dp") == 2 and seq & (seq - 1) == 0
    pairs = heads // 2
    rows = pairs * LANES // 2
    bits = seq.bit_length() - 1
    cands = owned * seq
    rank = lax.axis_index("seq")

    def swap(value, bit):
        return lax.ppermute(value, "seq", [(j, j ^ (1 << bit)) for j in range(seq)])

    peer = lax.ppermute(item_embedding_table, "dp", [(0, 1), (1, 0)])
    sc = jnp.stack(
        [rank, rank * n, user_history_length[0], lax.axis_index("dp")]
    ).astype(i32)
    stored = item_stored_row.reshape(-1, LANES)
    decay = log_head_retention.reshape(heads, n)
    ids = candidate_item_index
    for bit in reversed(range(bits)):
        ids = jnp.concatenate([ids, swap(ids, bit)], axis=1)

    part, slot, crow, ccol, ctl = call(
        own_rows_kernel, "own_rows", [sc],
        [history_item_index, stored, decay, item_embedding_table],
        [
            shape((n, width), bf16), shape((n, 8), f32), shape((n // CHUNK, heads, CHUNK), f32),
            shape((n, 2 * heads), f32), shape((n // CHUNK * pairs, LANES), f32),
        ],
        flops=2 * n * half * width,
    )
    query_w = history_query_key_value_weight[:, :width]
    key_w = history_query_key_value_weight[:, width : 2 * width]
    val_w = history_query_key_value_weight[:, 2 * width :]
    emb, key, val, enter, pay = call(
        summary_kernel, "summary", [sc],
        [part, peer, slot, ccol, ctl, key_w, val_w],
        [
            shape((n, width), bf16), shape((n, width), bf16), shape((n, width), bf16),
            shape((n // CHUNK, rows, LANES), f32), shape((rows + 16, LANES), bf16),
        ],
        [pltpu.VMEM((rows, LANES), f32)],
        flops=2 * n * half * width,
    )
    query, intra = call(
        local_kernel, "local", [], [emb, key, val, crow, ccol, query_w],
        [shape((n, width), bf16), shape((n, width), f32)],
        flops=2 * n * half * width,
    )
    (cand_q,) = call(
        candidate_kernel, "candidates", [sc],
        [ids, stored, item_embedding_table, peer, candidate_query_weight],
        [shape((cands, width), bf16)],
        flops=2 * cands * 2 * half * width,
    )
    prefix = logs = None
    for bit in range(bits - 1):
        got = swap(pay, bit)
        outs = [shape((rows + 16, LANES), bf16), shape((rows, LANES), f32), shape((pairs, LANES), f32)]
        if bit == 0:
            pay, prefix, logs = call(
                lambda *refs: first_join_kernel(0, *refs), "first_join", [sc], [pay, got], outs
            )
        else:
            pay, prefix, logs = call(
                lambda *refs, bit=bit: join_kernel(bit, *refs), "join", [sc],
                [pay, got, prefix, logs], outs,
            )
    got = swap(pay, bits - 1)
    send = cands // 2
    hist, key_two, val_two, pay = call(
        lambda *refs: finish_kernel(*refs, bit=bits - 1), "finish", [sc, head_score_scale],
        [
            emb, query, intra, enter, ccol, ctl, got, prefix, logs,
            history_output_weight, candidate_key_value_weight, cand_q,
        ],
        [
            shape((n, width), f32), shape((n, width), bf16), shape((n, width), bf16),
            shape((send, width + LANES), bf16),
        ],
        [pltpu.VMEM((send, LANES), f32)],
        flops=2 * n * half * width,
    )
    mean, logs = call(
        keep_kernel, "keep", [sc, head_score_scale], [cand_q, key_two, val_two],
        [shape((send, width), f32), shape((send, width), f32)],
        flops=2 * n * half * width,
    )
    for bit in range(bits - 1):
        got = swap(pay, bit)
        send //= 2
        mean, logs, pay = call(
            fold_kernel, "fold", [], [mean, logs, got],
            [shape((send, width), f32), shape((send, width), f32), shape((send, width + LANES), bf16)],
        )
    got = swap(pay, bits - 1)
    (cand_out,) = call(
        last_kernel, "last", [], [mean, logs, got, candidate_output_weight],
        [shape((owned, width), f32)],
    )
    return hist[None], cand_out[None]


def solution(mesh):
    in_specs = (
        P(("groups", "dp"), "seq"),
        P(("groups", "dp"), None, "seq"),
        P(("groups", "dp")),
        P(("groups", "dp"), "seq"),
        P(),
        P("dp", None),
        P(),
        P(),
        P(),
        P(),
        P(),
        P(),
    )
    out_specs = (P(("groups", "dp"), "seq", None), P(("groups", "dp"), "seq", None))
    return jax.shard_map(shards, mesh=mesh, in_specs=in_specs, out_specs=out_specs, check_vma=False)
```

time: 235 us -> 75.8 us (0.32)
  blocking collectives: 56.2 us -> 0 us
  Pallas kernels: 0 us -> 45.5 us
  matrix products: 44.3 us -> 0 us
  other arithmetic: 34.1 us -> 0.3 us
  local copies, waits for them, and re-layouts: 34.7 us -> 1.52 us
  between operations: 15.8 us -> 1.49 us
  waiting for transfers between devices: 27.9 us -> 13.7 us
  starting transfers between devices: 20.8 us -> 13.1 us
    pallas_call x0 -> x11, Pallas kernels: none -> 45.5 us  [call(): pl.pallas_call(kernel, name=name, in_specs=[SMEM] * len(scalars) + [VMEM]...]
    dot_general x10 -> x0, matrix products: 44.3 us -> none  [the longest x1 16.9 us: block_terms(): jnp.einsum('hst,thd->shd', weights, val_rows, preferred_element_type=jnp....]
    all_gather x1 -> x0, blocking collectives: 33 us -> none  [shards(): candidate_query_rows = lax.all_gather(own_query, 'seq', axis=1, tiled=True)]
    all_to_all x5 -> x0, waiting for transfers between devices: 27.9 us -> none  [the longest x1 20.8 us: shards(): lax.all_to_all(weighted[None], 'seq', split_axis=2, concat_axis=0, tiled=...]
    unnamed x1 -> x0, blocking collectives: 23.2 us -> none
    all_to_all x5 -> x0, starting transfers between devices: 20.8 us -> none  [the longest x1 5.65 us: shards(): lax.all_to_all(weighted[None], 'seq', split_axis=2, concat_axis=0, tiled=...]
    ppermute x0 -> x10, waiting for transfers between devices: none -> 13.7 us  [the longest x9 13.7 us: swap(): return lax.ppermute(value, 'seq', [(j, j ^ 1 << bit) for j in range(seq)])]
    gather x2 -> x0, local copies, waits for them, and re-layouts: 13.6 us -> none  [the longest x1 7.45 us: fetch_rows(): item_embedding_table[local_rows]]
  transfers between devices with their start and end apart: 6 -> 10, of which waited for: 4 -> 4; matrix products, arithmetic and copies ran while one was open for 8% -> 2% of each run, Pallas kernels for 0% -> 40%
where the time goes in v1:
time: 75.8 us; the launch traced here: 75.6 us
  Pallas kernels  45.5 us (60%)
  waiting for transfers between devices  13.7 us (18%)
  starting transfers between devices  13.1 us (17%)
  local copies, waits for them, and re-layouts  1.52 us (2%)
  between operations  1.49 us (2%)
    pallas_call x11, Pallas kernels, call(): pl.pallas_call(kernel, name=name, in_specs=[SMEM] * len(scalars) + [VMEM]...  45.5 us
    ppermute x9, waiting for transfers between devices, swap(): return lax.ppermute(value, 'seq', [(j, j ^ 1 << bit) for j in range(seq)])  13.7 us
    ppermute x9, starting transfers between devices, swap(): return lax.ppermute(value, 'seq', [(j, j ^ 1 << bit) for j in range(seq)])  12.6 us
  transfers between devices with their start and end apart: 10, of which 4 were waited for; matrix products, arithmetic and copies ran while one was open for 2% of the time, Pallas kernels for 40%

profile of v1, /device:TPU:0, one launch (start us, length us, event | category | flops | bytes accessed | tf_op | source)
XLA Modules:
  0.0 75.6 jit_solution(1419018248748696436)
XLA Ops:
  0.6 0.0 copy-start.1
  0.6 0.0 copy-start.9
  0.7 0.0 copy-start.6
  0.7 0.0 copy-start.5
  0.7 0.0 copy-start.7
  0.7 0.5 collective-permute-start
  1.2 3.7 %collective-permute-start.4 = (s32[1,64]{1,0:T(1,128)}, s32[1,64]{1,0:T(1,128)S(1)}, u32[]{:S(2)}, u32[]{:S(2)}) collective-permute-start(s32[1,64]{1,0:T(1,128)} %param.15), channel_id=1, source_target_pairs={{0,8},{2,10},{4,12},{6,14},{8,0},{10,2},{12,4},{14,6},{1,9},{3,11}... | collective-permute-start | bytes 776 | tf_op jit(solution)/shard_map/ppermute | solution.py:441
  5.5 1.5 %fusion = (bf16[512,512]{1,0:T(8,128)(2,1)S(1)}, bf16[512,512]{1,0:T(8,128)(2,1)S(1)}, bf16[512,512]{1,0:T(8,128)(2,1)S(1)}) fusion(bf16[512,1536]{1,0:T(8,128)(2,1)} %param.19), kind=kLoop, calls=%fused_computation.4 | loop fusion | bytes 3145728 | tf_op jit(solution)/shard_map/slice | solution.py:462
  7.0 0.1 pad_add_fusion.2.sc.refs_0_
  7.1 0.0 collective-permute-done.4
  7.1 0.1 pad_add_fusion.3
  7.2 1.6 %collective-permute-start.5 = (s32[1,128]{1,0:T(1,128)S(1)}, s32[1,128]{1,0:T(1,128)S(1)}, u32[]{:S(2)}, u32[]{:S(2)}) collective-permute-start(s32[1,128]{1,0:T(1,128)S(1)} %pad_add_fusion.3), channel_id=1, source_target_pairs={{0,4},{2,6},{4,0},{6,2},{8,12},{10,14},{12,8},{14,10},{1,5},{3,7},... | collective-permute-start | bytes 1544 | tf_op jit(solution)/shard_map/ppermute | solution.py:441
  8.7 0.0 copy-done.1
  8.7 4.3 %own_rows.1 = (bf16[1024,512]{1,0:T(8,128)(2,1)S(1)}, f32[1024,8]{1,0:T(8,128)S(1)}, f32[4,8,256]{2,1,0:T(8,128)S(1)}, f32[1024,16]{1,0:T(8,128)S(1)}, f32[16,128]{1,0:T(8,128)S(1)}) custom-call(s32[4]{0:T(128)S(1)} %pad_add_fusion.2.sc.refs_0_, s32[1,1024]{1,0:T(1,128)S(1)} %copy-done.7, s32[32,128]{1,0:T(8,128)S(1)} %bitcast.8, f32[8,1024]{1,0:T(8,128)S(1)} %bitcast.7, ...), custom_call_target="tpu_custom_call" | custom-call | flops 2147483648 | tf_op jit(solution)/shard_map/own_rows/pallas_call | solution.py:402
  13.1 0.0 collective-permute-done.5
  13.1 0.1 pad_add_fusion.1
  13.2 1.5 %collective-permute-start.6 = (s32[1,256]{1,0:T(1,128)S(1)}, s32[1,256]{1,0:T(1,128)S(1)}, u32[]{:S(2)}, u32[]{:S(2)}) collective-permute-start(s32[1,256]{1,0:T(1,128)S(1)} %pad_add_fusion.1), channel_id=1, source_target_pairs={{0,2},{2,0},{4,6},{6,4},{8,10},{10,8},{12,14},{14,12},{1,3},{3,1},... | collective-permute-start | bytes 3080 | tf_op jit(solution)/shard_map/ppermute | solution.py:441
  14.7 0.0 collective-permute-done.peer
  14.7 8.4 %summary.1 = (bf16[1024,512]{1,0:T(8,128)(2,1)S(1)}, bf16[1024,512]{1,0:T(8,128)(2,1)S(1)}, bf16[1024,512]{1,0:T(8,128)(2,1)S(1)}, f32[4,256,128]{2,1,0:T(8,128)S(1)}, bf16[272,128]{1,0:T(8,128)(2,1)S(1)}) custom-call(s32[4]{0:T(128)S(1)} %pad_add_fusion.2.sc.refs_0_, bf16[1024,512]{1,0:T(8,128)(2,1)S(1)} %get-tuple-element.32.part, ...), custom_call_target="tpu_custom_call" | custom-call | flops 2147483648 | tf_op jit(solution)/shard_map/summary/pallas_call | solution.py:402
  23.0 0.6 collective-permute-start.1
  23.6 0.0 collective-permute-done.6
  23.6 0.1 pad_add_fusion.ids
  23.7 3.7 %collective-permute-done.1.refs_2_ = bf16[272,128]{1,0:T(8,128)(2,1)S(1)} collective-permute-done((bf16[272,128]{1,0:T(8,128)(2,1)S(1)}, bf16[272,128]{1,0:T(8,128)(2,1)S(1)}, u32[]{:S(2)}, u32[]{:S(2)}) %collective-permute-start.1) | collective-permute-done | bytes 69664 | tf_op jit(solution)/shard_map/ppermute | solution.py:441
  27.4 0.6 first_join.1
  28.0 0.5 collective-permute-start.2
  28.5 6.2 %local.1 = (bf16[1024,512]{1,0:T(8,128)(2,1)S(1)}, f32[1024,512]{1,0:T(8,128)S(1)}) custom-call(bf16[1024,512]{1,0:T(8,128)(2,1)S(1)} %get-tuple-element.36.emb.refs_2_, bf16[1024,512]{1,0:T(8,128)(2,1)S(1)} %get-tuple-element.37.key, bf16[1024,512]{1,0:T(8,128)(2,1)S(1)} %get-tuple-element.38.val, f32[4,8,256]{2,1,0:T(8,128)S(1)} %get-tuple-element.39.crow, ...), custom_call_target="tpu_custom_call" | custom-call | flops 2147483648 | tf_op jit(solution)/shard_map/local/pallas_call | solution.py:402
  34.7 0.0 collective-permute-done.2.refs_2_
  34.7 0.6 join.1
  35.3 0.0 copy-start.2
  35.3 0.0 copy-start.4
  35.4 0.0 copy-start.8
  35.4 2.4 %collective-permute-start.3 = (bf16[272,128]{1,0:T(8,128)(2,1)S(1)}, bf16[272,128]{1,0:T(8,128)(2,1)S(1)}, u32[]{:S(2)}, u32[]{:S(2)}) collective-permute-start(bf16[272,128]{1,0:T(8,128)(2,1)S(1)} %get-tuple-element.47), channel_id=1, source_target_pairs={{0,8},{2,10},{4,12},{6,14},{8,0},{10,2},{12,4},{14,6},{1,9},{3,11}... | collective-permute-start | bytes 208904 | tf_op jit(solution)/shard_map/ppermute | solution.py:441
  37.8 4.8 %candidates.1.refs_13_.cand_q = bf16[512,512]{1,0:T(8,128)(2,1)S(1)} custom-call(s32[4]{0:T(128)S(1)} %pad_add_fusion.2.sc.refs_0_, s32[1,512]{1,0:T(1,128)S(1)} %pad_add_fusion.ids, s32[32,128]{1,0:T(8,128)S(1)} %bitcast.9, bf16[2048,512]{1,0:T(8,128)(2,1)S(1)} %copy-done.1, bf16[2048,512]{1,0:T(8,128)(2,1)} %collective-permute-done.peer, ...), custom_call_target="tpu_custom_call" | custom-call | flops 2147483648 | tf_op jit(solution)/shard_map/candidates/pallas_call | solution.py:402
  42.6 0.0 collective-permute-done.3.refs_8_
  42.6 0.0 copy-done.2
  42.6 0.0 copy-done.4
  42.7 12.4 %finish.1 = (f32[1024,512]{1,0:T(8,128)}, bf16[1024,512]{1,0:T(8,128)(2,1)S(1)}, bf16[1024,512]{1,0:T(8,128)(2,1)S(1)}, bf16[256,640]{1,0:T(8,128)(2,1)S(1)}) custom-call(s32[4]{0:T(128)S(1)} %pad_add_fusion.2.sc.refs_0_, f32[8]{0:T(128)S(1)} %copy-done.8, bf16[1024,512]{1,0:T(8,128)(2,1)S(1)} %get-tuple-element.36.emb.refs_2_, ...), custom_call_target="tpu_custom_call" | custom-call | flops 2147483648 | tf_op jit(solution)/shard_map/finish/pallas_call | solution.py:402
  55.0 0.5 collective-permute-start.7
  55.6 6.4 %keep.1 = (f32[256,512]{1,0:T(8,128)S(1)}, f32[256,512]{1,0:T(8,128)S(1)}) custom-call(s32[4]{0:T(128)S(1)} %pad_add_fusion.2.sc.refs_0_, f32[8]{0:T(128)S(1)} %copy-done.8, bf16[512,512]{1,0:T(8,128)(2,1)S(1)} %candidates.1.refs_13_.cand_q, bf16[1024,512]{1,0:T(8,128)(2,1)S(1)} %get-tuple-element.51.key, bf16[1024,512]{1,0:T(8,128)(2,1)S(1)} %get-tuple-element.52.val), custom_call_target="tpu_custom_call" | custom-call | flops 2147483648 | tf_op jit(solution)/shard_map/keep/pallas_call | solution.py:402
  62.0 0.0 copy-start
  62.0 0.1 collective-permute-done.7.got
  62.1 0.5 fold.2
  62.6 1.6 %collective-permute-start.8 = (bf16[128,640]{1,0:T(8,128)(2,1)S(1)}, bf16[128,640]{1,0:T(8,128)(2,1)S(1)}, u32[]{:S(2)}, u32[]{:S(2)}) collective-permute-start(bf16[128,640]{1,0:T(8,128)(2,1)S(1)} %get-tuple-element.58), channel_id=1, source_target_pairs={{0,4},{2,6},{4,0},{6,2},{8,12},{10,14},{12,8},{14,10},{1,5},{3,7},... | collective-permute-start | bytes 491528 | tf_op jit(solution)/shard_map/ppermute | solution.py:441
  64.3 4.6 %collective-permute-done.8.got = bf16[128,640]{1,0:T(8,128)(2,1)S(1)} collective-permute-done((bf16[128,640]{1,0:T(8,128)(2,1)S(1)}, bf16[128,640]{1,0:T(8,128)(2,1)S(1)}, u32[]{:S(2)}, u32[]{:S(2)}) %collective-permute-start.8) | collective-permute-done | bytes 163872 | tf_op jit(solution)/shard_map/ppermute | solution.py:441
  68.9 0.3 fold.3
  69.2 0.2 collective-permute-start.9
  69.4 5.2 %collective-permute-done.9.got = bf16[64,640]{1,0:T(8,128)(2,1)S(1)} collective-permute-done((bf16[64,640]{1,0:T(8,128)(2,1)S(1)}, bf16[64,640]{1,0:T(8,128)(2,1)S(1)}, u32[]{:S(2)}, u32[]{:S(2)}) %collective-permute-start.9) | collective-permute-done | bytes 81952 | tf_op jit(solution)/shard_map/ppermute | solution.py:441
  74.6 1.0 %last.1 = f32[64,512]{1,0:T(8,128)} custom-call(f32[64,512]{1,0:T(8,128)S(1)} %get-tuple-element.59.mean, f32[64,512]{1,0:T(8,128)S(1)} %get-tuple-element.60.logs, bf16[64,640]{1,0:T(8,128)(2,1)S(1)} %collective-permute-done.9.got, bf16[512,512]{1,0:T(8,128)(2,1)S(1)} %copy-done), custom_call_target="tpu_custom_call" | custom-call | tf_op jit(solution)/shard_map/last/pallas_call | solution.py:402
  (8 shorter events, 0.0 us)
Async XLA Ops:
  0.6 8.1 %copy-start.1 = (bf16[2048,512]{1,0:T(8,128)(2,1)S(1)}, bf16[2048,512]{1,0:T(8,128)(2,1)}, u32[]{:S(2)}) copy-start(bf16[2048,512]{1,0:T(8,128)(2,1)} %own.3) | copy-start | bytes 6291460
  0.6 6.4 %copy-start.9 = (s32[1,64]{1,0:T(1,128)S(1)}, s32[1,64]{1,0:T(1,128)}, u32[]{:S(2)}) copy-start(s32[1,64]{1,0:T(1,128)} %param.15) | copy-start | bytes 772
  0.7 8.1 %copy-start.6 = (s32[4096]{0:T(1024)S(1)}, s32[4096]{0:T(1024)}, u32[]{:S(2)}) copy-start(s32[4096]{0:T(1024)} %param.16) | copy-start | bytes 49156
  0.7 8.1 %copy-start.5 = (f32[1,8,1024]{2,1,0:T(8,128)S(1)}, f32[1,8,1024]{2,1,0:T(8,128)}, u32[]{:S(2)}) copy-start(f32[1,8,1024]{2,1,0:T(8,128)} %param.13) | copy-start | bytes 98308
  0.7 8.1 %copy-start.7 = (s32[1,1024]{1,0:T(1,128)S(1)}, s32[1,1024]{1,0:T(1,128)}, u32[]{:S(2)}) copy-start(s32[1,1024]{1,0:T(1,128)} %ids.1) | copy-start | bytes 12292
  0.7 14.0 %collective-permute-start = (bf16[2048,512]{1,0:T(8,128)(2,1)}, bf16[2048,512]{1,0:T(8,128)(2,1)}, u32[]{:S(2)}, u32[]{:S(2)}) collective-permute-start(bf16[2048,512]{1,0:T(8,128)(2,1)} %own.3), channel_id=1, source_target_pairs={{0,1},{1,0},{2,3},{3,2},{4,5},{5,4},{6,7},{7,6},{8,9},{9,8},{10,11... | collective-permute-start | bytes 6291464 | tf_op jit(solution)/shard_map/ppermute | solution.py:443
  1.2 5.9 %collective-permute-start.4 = (s32[1,64]{1,0:T(1,128)}, s32[1,64]{1,0:T(1,128)S(1)}, u32[]{:S(2)}, u32[]{:S(2)}) collective-permute-start(s32[1,64]{1,0:T(1,128)} %param.15), channel_id=1, source_target_pairs={{0,8},{2,10},{4,12},{6,14},{8,0},{10,2},{12,4},{14,6},{1,9},{3,11}... | collective-permute-start | bytes 776 | tf_op jit(solution)/shard_map/ppermute | solution.py:441
  7.2 5.9 %collective-permute-start.5 = (s32[1,128]{1,0:T(1,128)S(1)}, s32[1,128]{1,0:T(1,128)S(1)}, u32[]{:S(2)}, u32[]{:S(2)}) collective-permute-start(s32[1,128]{1,0:T(1,128)S(1)} %pad_add_fusion.3), channel_id=1, source_target_pairs={{0,4},{2,6},{4,0},{6,2},{8,12},{10,14},{12,8},{14,10},{1,5},{3,7},... | collective-permute-start | bytes 1544 | tf_op jit(solution)/shard_map/ppermute | solution.py:441
  13.2 10.5 %collective-permute-start.6 = (s32[1,256]{1,0:T(1,128)S(1)}, s32[1,256]{1,0:T(1,128)S(1)}, u32[]{:S(2)}, u32[]{:S(2)}) collective-permute-start(s32[1,256]{1,0:T(1,128)S(1)} %pad_add_fusion.1), channel_id=1, source_target_pairs={{0,2},{2,0},{4,6},{6,4},{8,10},{10,8},{12,14},{14,12},{1,3},{3,1},... | collective-permute-start | bytes 3080 | tf_op jit(solution)/shard_map/ppermute | solution.py:441
  23.0 4.4 %collective-permute-start.1 = (bf16[272,128]{1,0:T(8,128)(2,1)S(1)}, bf16[272,128]{1,0:T(8,128)(2,1)S(1)}, u32[]{:S(2)}, u32[]{:S(2)}) collective-permute-start(bf16[272,128]{1,0:T(8,128)(2,1)S(1)} %get-tuple-element.43.refs_1_), channel_id=1, source_target_pairs={{0,2},{2,0},{4,6},{6,4},{8,10},{10,8},{12,14},{14,12},{1,3},{3,1},... | collective-permute-start | bytes 208904 | tf_op jit(solution)/shard_map/ppermute | solution.py:441
  28.0 6.7 %collective-permute-start.2 = (bf16[272,128]{1,0:T(8,128)(2,1)S(1)}, bf16[272,128]{1,0:T(8,128)(2,1)S(1)}, u32[]{:S(2)}, u32[]{:S(2)}) collective-permute-start(bf16[272,128]{1,0:T(8,128)(2,1)S(1)} %get-tuple-element.44.refs_1_), channel_id=1, source_target_pairs={{0,4},{2,6},{4,0},{6,2},{8,12},{10,14},{12,8},{14,10},{1,5},{3,7},... | collective-permute-start | bytes 208904 | tf_op jit(solution)/shard_map/ppermute | solution.py:441
  28.5 9.3 %copy-start.3 = (bf16[512,512]{1,0:T(8,128)(2,1)S(1)}, bf16[512,512]{1,0:T(8,128)(2,1)}, u32[]{:S(2)}) copy-start(bf16[512,512]{1,0:T(8,128)(2,1)} %query_w.1) | copy-start | bytes 1572868
  35.3 7.3 %copy-start.2 = (bf16[512,1024]{1,0:T(8,128)(2,1)S(1)}, bf16[512,1024]{1,0:T(8,128)(2,1)}, u32[]{:S(2)}) copy-start(bf16[512,1024]{1,0:T(8,128)(2,1)} %refs_12_.1) | copy-start | bytes 3145732
  35.3 7.3 %copy-start.4 = (bf16[512,512]{1,0:T(8,128)(2,1)S(1)}, bf16[512,512]{1,0:T(8,128)(2,1)}, u32[]{:S(2)}) copy-start(bf16[512,512]{1,0:T(8,128)(2,1)} %refs_11_.1) | copy-start | bytes 1572868
  35.4 7.3 %copy-start.8 = (f32[8]{0:T(128)S(1)}, f32[8]{0:T(128)}, u32[]{:S(2)}) copy-start(f32[8]{0:T(128)} %scale.1) | copy-start | bytes 100
  35.4 7.3 %collective-permute-start.3 = (bf16[272,128]{1,0:T(8,128)(2,1)S(1)}, bf16[272,128]{1,0:T(8,128)(2,1)S(1)}, u32[]{:S(2)}, u32[]{:S(2)}) collective-permute-start(bf16[272,128]{1,0:T(8,128)(2,1)S(1)} %get-tuple-element.47), channel_id=1, source_target_pairs={{0,8},{2,10},{4,12},{6,14},{8,0},{10,2},{12,4},{14,6},{1,9},{3,11}... | collective-permute-start | bytes 208904 | tf_op jit(solution)/shard_map/ppermute | solution.py:441
  55.0 7.1 %collective-permute-start.7 = (bf16[256,640]{1,0:T(8,128)(2,1)S(1)}, bf16[256,640]{1,0:T(8,128)(2,1)S(1)}, u32[]{:S(2)}, u32[]{:S(2)}) collective-permute-start(bf16[256,640]{1,0:T(8,128)(2,1)S(1)} %get-tuple-element.55), channel_id=1, source_target_pairs={{0,2},{2,0},{4,6},{6,4},{8,10},{10,8},{12,14},{14,12},{1,3},{3,1},... | collective-permute-start | bytes 983048 | tf_op jit(solution)/shard_map/ppermute | solution.py:441
  62.0 12.7 %copy-start = (bf16[512,512]{1,0:T(8,128)(2,1)S(1)}, bf16[512,512]{1,0:T(8,128)(2,1)}, u32[]{:S(2)}) copy-start(bf16[512,512]{1,0:T(8,128)(2,1)} %out_w.1) | copy-start | bytes 1572868
  62.6 6.3 %collective-permute-start.8 = (bf16[128,640]{1,0:T(8,128)(2,1)S(1)}, bf16[128,640]{1,0:T(8,128)(2,1)S(1)}, u32[]{:S(2)}, u32[]{:S(2)}) collective-permute-start(bf16[128,640]{1,0:T(8,128)(2,1)S(1)} %get-tuple-element.58), channel_id=1, source_target_pairs={{0,4},{2,6},{4,0},{6,2},{8,12},{10,14},{12,8},{14,10},{1,5},{3,7},... | collective-permute-start | bytes 491528 | tf_op jit(solution)/shard_map/ppermute | solution.py:441
  69.2 5.4 %collective-permute-start.9 = (bf16[64,640]{1,0:T(8,128)(2,1)S(1)}, bf16[64,640]{1,0:T(8,128)(2,1)S(1)}, u32[]{:S(2)}, u32[]{:S(2)}) collective-permute-start(bf16[64,640]{1,0:T(8,128)(2,1)S(1)} %get-tuple-element.61), channel_id=1, source_target_pairs={{0,8},{2,10},{4,12},{6,14},{8,0},{10,2},{12,4},{14,6},{1,9},{3,11}... | collective-permute-start | bytes 245768 | tf_op jit(solution)/shard_map/ppermute | solution.py:441

commit v2 on v0

v2 whole, which is shorter than its diff:
```python
import math

import jax
import jax.numpy as jnp
from jax import lax
from jax.experimental import pallas as pl
from jax.experimental.pallas import tpu as pltpu
from jax.sharding import PartitionSpec as P

f32, bf16, i32 = jnp.float32, jnp.bfloat16, jnp.int32
CHUNK = 256
KEYS = 512
LANES = 128
LOG2E = math.log2(math.e)
DEAD = -1e30
VMEM_LIMIT = 40 << 20


def dot(a, b):
    return jnp.dot(a, b, preferred_element_type=f32)


def contract(a, b, left, right):
    return lax.dot_general(a, b, (((left,), (right,)), ((), ())), preferred_element_type=f32)


def iota(shape, axis):
    return lax.broadcasted_iota(i32, shape, axis)


def thirds(value):
    high = value.astype(bf16).astype(f32)
    rest = value - high
    mid = rest.astype(bf16).astype(f32)
    return high, mid, rest - mid


def first_half(shape):
    return iota(shape, len(shape) - 1) % LANES < LANES // 2


def half_masks():
    low = first_half((1, LANES))
    return jnp.where(low, 1.0, 0.0).astype(bf16), jnp.where(low, 0.0, 1.0).astype(bf16)


def same_head():
    dims = (2 * LANES, 2 * LANES)
    return jnp.where(iota(dims, 0) // 64 == iota(dims, 1) // 64, 1.0, 0.0).astype(bf16)


def head_means(value, ones):
    square = (value * value).astype(bf16)
    step = ones.shape[0]
    parts = [dot(square[:, c : c + step], ones) for c in range(0, value.shape[1], step)]
    return jnp.concatenate(parts, axis=1) * (1.0 / 64.0)


def head_spread(heads, first, count):
    dims = (2 * heads, 64 * count)
    return jnp.where(iota(dims, 1) // 64 + first == iota(dims, 0) % heads, 1.0, 0.0).astype(bf16)


def spread(value, matrix):
    heads = value.shape[1] // 2
    high = value.astype(bf16).astype(f32)
    both = jnp.where(iota(value.shape, 1) < heads, high, value - high)
    return dot(both.astype(bf16), matrix)


def stored_slots(ids, stored):
    groups = stored.shape[0]
    n = ids.shape[1]
    pick = jnp.where(iota((groups, n), 0) == ids // LANES, 1.0, 0.0).astype(bf16)
    high = contract((stored // 64).astype(f32).astype(bf16), pick, 0, 0)
    low = contract((stored % 64).astype(f32).astype(bf16), pick, 0, 0)
    rows = jnp.where(iota((LANES, n), 0) == ids % LANES, high * 64.0 + low, 0.0)
    return jnp.sum(rows, axis=0, keepdims=True)


def picked_rows(slots, first, table):
    count = table.shape[0]
    hot = jnp.where(iota((count, slots.shape[1]), 0) == slots.astype(i32) - first, 1.0, 0.0)
    return contract(hot.astype(bf16), table[...], 0, 0)


def chunk(i):
    return slice(i * CHUNK, (i + 1) * CHUNK)


def pair_cut(p):
    return slice(p * LANES, (p + 1) * LANES)


def own_rows_kernel(sc, ids, stored, decay, own, part_o, slot_o, crow_o, ccol_o, ctl_o):
    n, half, heads = ids.shape[1], own.shape[0], decay.shape[0]
    slots = stored_slots(ids[...], stored[...])
    slot_o[...] = slots
    upto = jnp.where(
        iota((CHUNK, CHUNK), 0) <= iota((CHUNK, CHUNK), 1), 1.0, 0.0
    ).astype(bf16)
    low = first_half((1, LANES))
    for i in range(n // CHUNK):
        part_o[chunk(i), :] = picked_rows(slots[:, chunk(i)], sc[3] * half, own).astype(bf16)
        pieces = jnp.concatenate(thirds(decay[:, chunk(i)]), axis=0)
        sums = dot(pieces.astype(bf16), upto)
        cum = sums[:heads] + sums[heads : 2 * heads] + sums[2 * heads :]
        crow_o[i] = cum
        ccol_o[chunk(i), :] = jnp.transpose(jnp.concatenate([cum, cum], axis=0))
        for p in range(heads // 2):
            r = i * (heads // 2) + p
            ctl_o[r : r + 1, :] = jnp.where(
                low, cum[2 * p : 2 * p + 1, CHUNK - 1 :], cum[2 * p + 1 : 2 * p + 2, CHUNK - 1 :]
            )


def summary_kernel(
    sc, part, peer, slot, ccol, ctl, id_rows, weight, emb_o, key_o, val_o, enter_o, pay_o
):
    n, width = part.shape
    half, heads = peer.shape[0], ccol.shape[1] // 2
    pairs = heads // 2
    block = LANES // 2
    ones, lanes = same_head(), head_spread(heads, 0, heads)
    low = first_half((1, LANES))
    chunks = n // CHUNK

    def project(i):
        other = picked_rows(slot[:, chunk(i)], (1 - sc[3]) * half, peer)
        emb = (part[chunk(i), :].astype(f32) + other).astype(bf16)
        emb_o[chunk(i), :] = emb
        return dot(emb, weight[:, width : 2 * width]), dot(emb, weight[:, 2 * width :])

    total = [jnp.zeros((block, LANES), f32)] * pairs
    ready = project(0)
    for i in range(chunks):
        key, val = ready
        if i + 1 < chunks:
            ready = project(i + 1)
        alive = sc[1] + i * CHUNK + iota((CHUNK, 1), 0) < sc[2]
        val = jnp.where(alive, val, 0.0).astype(bf16)
        val_o[chunk(i), :] = val
        unit = lax.rsqrt(head_means(key, ones) + 1e-06) * 0.125
        normed = jnp.where(alive, key * unit, 0.0)
        key_o[chunk(i), :] = normed.astype(bf16)
        cum = ccol[chunk(i), :]
        keyed = (normed * spread(jnp.exp(cum[CHUNK - 1 :, :] - cum), lanes)).astype(bf16)
        for p in range(pairs):
            both = contract(keyed[:, pair_cut(p)], val[:, pair_cut(p)], 0, 0)
            fresh = jnp.where(low, both[:block], both[block:])
            enter_o[i, p * block : (p + 1) * block, :] = total[p]
            total[p] = total[p] * jnp.exp(ctl[i * pairs + p : i * pairs + p + 1, :]) + fresh
    logs = ctl[0:pairs, :]
    for i in range(1, chunks):
        logs = logs + ctl[i * pairs : (i + 1) * pairs, :]
    pay_o[...] = pack_state(jnp.concatenate(total, axis=0), logs, id_rows[...])


def state_rows(pairs, ids):
    return pairs * 64 + -(-(3 * pairs + ids) // 16) * 16


def pack_state(state, logs, id_rows):
    pairs, ids = logs.shape[0], id_rows.shape[0]
    pad = state_rows(pairs, ids) - state.shape[0] - 3 * pairs - ids
    parts = [state, *thirds(logs), id_rows] + [jnp.zeros((pad, LANES), f32)] * (pad > 0)
    return jnp.concatenate(parts, axis=0).astype(bf16)


def unpack_state(packed, pairs):
    whole = packed.astype(f32)
    rows = pairs * 64
    logs = whole[rows : rows + pairs]
    for k in (1, 2):
        logs = logs + whole[rows + k * pairs : rows + (k + 1) * pairs]
    return whole[:rows], logs, whole[rows + 3 * pairs :]


def row_factors(logs):
    factors = jnp.exp(logs)
    return jnp.concatenate(
        [jnp.broadcast_to(factors[p : p + 1], (64, LANES)) for p in range(logs.shape[0])], axis=0
    )


def join_kernel(bit, ids, pairs, sc, mine, got, *refs):
    pay_o, prefix_o, logs_o, ids_o = refs[-4:]
    upper = (sc[0] >> bit) & 1 == 1
    state, logs, rows = unpack_state(mine[...], pairs)
    other, other_logs, other_rows = unpack_state(got[...], pairs)
    early = jnp.where(upper, other, state)
    late = jnp.where(upper, state, other)
    factor = row_factors(jnp.where(upper, logs, other_logs))
    id_rows = jnp.concatenate([rows[:ids], other_rows[:ids]], axis=0)
    ids_o[...] = id_rows
    sent = id_rows if pay_o.shape[0] >= state_rows(pairs, 2 * ids) else id_rows[:1]
    pay_o[...] = pack_state(early * factor + late, logs + other_logs, sent)
    if bit == 0:
        prefix_o[...] = jnp.where(upper, other, 0.0)
        logs_o[...] = jnp.where(upper, other_logs, 0.0)
    else:
        prefix, prefix_logs = refs[0][...], refs[1][...]
        prefix_o[...] = jnp.where(upper, prefix + row_factors(prefix_logs) * other, prefix)
        logs_o[...] = jnp.where(upper, prefix_logs + other_logs, prefix_logs)


def local_kernel(first, emb, key, val, crow, ccol, weight, query_o, intra_o):
    n, width = query_o.shape
    heads = ccol.shape[1] // 2
    ones, lanes = same_head(), head_spread(heads, first // 64, width // 64)
    mask_a, mask_b = half_masks()
    causal = iota((CHUNK, CHUNK), 0) >= iota((CHUNK, CHUNK), 1)

    def queries(i):
        query = dot(emb[chunk(i), :], weight[:, first : first + width])
        unit = lax.rsqrt(head_means(query, ones) + 1e-06) * 0.125
        query = query * unit
        decayed = query * spread(jnp.exp(ccol[chunk(i), :]), lanes)
        query_o[chunk(i), :] = decayed.astype(bf16)
        return query.astype(bf16)

    def scores(i, p, b, query):
        cut = pair_cut(p)
        wide = slice(first + p * LANES, first + (p + 1) * LANES)
        return contract(query[:, cut] * (mask_b if b else mask_a), key[chunk(i), wide], 1, 1)

    units = [(i, p, b) for i in range(n // CHUNK) for p in range(width // LANES) for b in (0, 1)]
    query = {0: queries(0)}
    ready = scores(*units[0], query[0])
    held = None
    for u, (i, p, b) in enumerate(units):
        current = ready
        if u + 1 < len(units):
            j = units[u + 1][0]
            if j not in query:
                query[j] = queries(j)
            ready = scores(*units[u + 1], query[j])
        h = first // 64 + 2 * p + b
        gap = ccol[chunk(i), h : h + 1] - crow[i, h : h + 1, :]
        weights = jnp.where(causal, current * jnp.exp(gap), 0.0).astype(bf16)
        wide = slice(first + p * LANES, first + (p + 1) * LANES)
        part = dot(weights, val[chunk(i), wide] * (mask_b if b else mask_a))
        if b == 0:
            held = part
        else:
            intra_o[chunk(i), pair_cut(p)] = held + part


def candidate_kernel(order, owned, sc, id_rows, stored, own, peer, query_w, pair_w, query_o, val_w_o):
    half, width = own.shape
    ids = id_rows[...]
    ids = (ids * float(LANES) + pltpu.roll(ids, LANES // 2, 1)).astype(i32)
    slots = [stored_slots(ids[j : j + 1], stored[...]) for j in order]
    step = max(1, LANES // owned)
    tiles = []
    for start in range(0, len(order), step):
        tile = slots[start]
        for k in range(1, min(step, len(order) - start)):
            moved = pltpu.roll(slots[start + k], k * owned, 1)
            tile = jnp.where(iota((1, LANES), 1) >= k * owned, moved, tile)
        tiles.append(tile)
    slots = jnp.concatenate(tiles, axis=1)
    for c in range(0, slots.shape[1], CHUNK):
        some = slots[:, c : c + CHUNK]
        rows = picked_rows(some, sc[3] * half, own) + picked_rows(some, (1 - sc[3]) * half, peer)
        query = dot(rows.astype(bf16), query_w[...])
        query_o[:, c : c + CHUNK] = jnp.transpose(query).astype(bf16)
    val_w_o[...] = jnp.transpose(pair_w[:, width:].astype(f32)).astype(bf16)


def attend(sc, scale, query, first, cols, key, val, emit):
    n, width = key.shape
    blocks = range(0, n, KEYS)

    def padded(h):
        rows = query[h * 64 : (h + 1) * 64, first : first + cols]
        zero = jnp.zeros_like(rows)
        return jnp.concatenate([zero, rows] if h % 2 else [rows, zero], axis=0)

    def scores(h, block, weights):
        rows = slice(block, block + KEYS)
        values = dot(key[rows, pair_cut(h // 2)], weights)
        alive = sc[1] + block + iota((KEYS, 1), 0) < sc[2]
        return jnp.where(alive, values, DEAD)

    def store(h, block, weights, buffer, peak):
        values = scores(h, block, weights)
        buffer[block : block + KEYS, :] = values
        top = jnp.max(values.reshape(KEYS // 8, 8, cols), axis=0)
        return top if peak is None else jnp.maximum(peak, top)

    def run(buffers):
        ones = jnp.ones((16, KEYS), bf16)
        peak, weights = None, padded(0)
        for block in blocks:
            peak = store(0, block, weights, buffers[0], peak)
        for h in range(width // 64):
            factor = scale[h] * LOG2E
            peak = jnp.max(peak, axis=0, keepdims=True)
            following = None
            more = h + 1 < width // 64
            weights = padded(h + 1) if more else None
            sums = None
            for block in blocks:
                if more:
                    following = store(h + 1, block, weights, buffers[(h + 1) % 2], following)
                gap = buffers[h % 2][block : block + KEYS, :] - peak
                probs = jnp.exp2(gap * factor).astype(bf16)
                side = jnp.concatenate(
                    [val[h * 64 : (h + 1) * 64, block : block + KEYS], ones], axis=0
                )
                part = dot(side, probs)
                sums = part if sums is None else sums + part
            total = sums[64:65]
            emit(h, sums[:64] / total, peak * factor + jnp.log2(total))
            peak = following

    return run


def finish_kernel(
    bit, sc, scale, emb, query_a, query_b, intra_a, intra_b, enter, ctl, got, prefix, prefix_logs,
    out_w, pair_w, val_w, cand_q, hist_o, key_o, val_o, pay_o, *buffers,
):
    n, width = emb.shape
    pairs = width // LANES
    ones = same_head()
    upper = (sc[0] >> bit) & 1 == 1
    state = unpack_state(got[...], pairs)[0]
    before, before_logs = prefix[...], prefix_logs[...]
    entering = jnp.where(upper, before + row_factors(before_logs) * state, before)
    lane = iota((1, 2 * LANES), 1) // 64
    chunks = n // CHUNK
    gone = [jnp.zeros((pairs, LANES), f32)]
    for i in range(chunks - 1):
        gone.append(gone[-1] + ctl[i * pairs : (i + 1) * pairs, :])

    def normed(i):
        states = enter[i] + row_factors(gone[i]) * entering
        parts = []
        for p in range(0, pairs, 2):
            wide = jnp.concatenate(
                [states[p * 64 : (p + 1) * 64], states[(p + 1) * 64 : (p + 2) * 64]], axis=1
            )
            matrix = jnp.concatenate([jnp.where(lane == k, wide, 0.0) for k in range(4)], axis=0)
            query, intra = (query_a, intra_a) if p < pairs // 2 else (query_b, intra_b)
            c = (p % (pairs // 2)) * LANES
            cut = slice(c, c + 2 * LANES)
            parts.append(dot(query[chunk(i), cut], matrix.astype(bf16)) + intra[chunk(i), cut])
        mixed = jnp.concatenate(parts, axis=1)
        return (mixed * lax.rsqrt(head_means(mixed, ones) + 1e-05)).astype(bf16)

    ready = normed(0)
    for i in range(chunks):
        current = ready
        if i + 1 < chunks:
            ready = normed(i + 1)
        hidden_sum = emb[chunk(i), :].astype(f32) + dot(current, out_w[...])
        alive = sc[1] + i * CHUNK + iota((CHUNK, 1), 0) < sc[2]
        hist_o[chunk(i), :] = jnp.where(alive, hidden_sum, 0.0)
        hidden = hidden_sum.astype(bf16)
        key_o[chunk(i), :] = dot(hidden, pair_w[:, :width]).astype(bf16)
        val_o[:, chunk(i)] = contract(val_w[...], hidden, 1, 1).astype(bf16)
    count = pay_o.shape[1]
    heads = width // 64
    any_alive = sc[1] < sc[2]
    log_rows = []

    def emit(h, attended, logs):
        pay_o[h * 64 : (h + 1) * 64, :] = attended.astype(bf16)
        log_rows.append(jnp.where(any_alive, logs, DEAD))

    attend(sc, scale, cand_q, count, count, key_o, val_o, emit)(buffers)
    pay_o[width:, :] = pack_logs(jnp.concatenate(log_rows, axis=0))


def pack_logs(logs):
    heads, cols = logs.shape
    return jnp.concatenate(
        [*thirds(logs), jnp.zeros((log_pad(heads) - 3 * heads, cols), f32)], axis=0
    ).astype(bf16)


def log_pad(heads):
    return -(-3 * heads // 16) * 16


def unpack_logs(rows, heads):
    rows = rows.astype(f32)
    return rows[:heads] + rows[heads : 2 * heads] + rows[2 * heads : 3 * heads]


def keep_kernel(sc, scale, cand_q, key, val, mean_o, logs_o, *buffers):
    any_alive = sc[1] < sc[2]

    def emit(h, attended, logs):
        mean_o[h * 64 : (h + 1) * 64, :] = attended
        logs_o[h : h + 1, :] = jnp.where(any_alive, logs, DEAD)

    attend(sc, scale, cand_q, 0, mean_o.shape[1], key, val, emit)(buffers)


def over_heads(rows):
    return jnp.concatenate(
        [jnp.broadcast_to(rows[h : h + 1], (64, rows.shape[1])) for h in range(rows.shape[0])],
        axis=0,
    )


def merge(parts):
    peak = parts[0][1]
    for _, logs in parts[1:]:
        peak = jnp.maximum(peak, logs)
    shares = [jnp.exp2(logs - peak) for _, logs in parts]
    total = sum(shares[1:], shares[0])
    mean = None
    for (value, _), share in zip(parts, shares):
        term = value * over_heads(share / total)
        mean = term if mean is None else mean + term
    return mean, peak + jnp.log2(total)


def received(got, heads):
    width = heads * 64
    return got[:width, :].astype(f32), unpack_logs(got[width:, :], heads)


def fold_kernel(mean, logs, got, mean_o, logs_o, pay_o):
    heads, keep = logs_o.shape
    width = heads * 64
    new_mean, new_logs = merge([(mean[...], logs[...]), received(got, heads)])
    mean_o[...] = new_mean[:, :keep]
    logs_o[...] = new_logs[:, :keep]
    pay_o[:width, :] = new_mean[:, keep:].astype(bf16)
    pay_o[width:, :] = pack_logs(new_logs[:, keep:])


def deal_kernel(mean, logs, got, mean_o, logs_o, *sends):
    heads, cols = logs_o.shape
    new_mean, new_logs = merge([(mean[...], logs[...]), received(got, heads)])
    mean_o[...] = new_mean[:, :cols]
    logs_o[...] = new_logs[:, :cols]
    whole = jnp.concatenate([new_mean, pack_logs(new_logs).astype(f32)], axis=0)
    owned = whole.shape[1] // 4
    half = whole.shape[0] // 2
    low = first_half((1, LANES))
    for k, send in enumerate(sends):
        start = (k + 1) * owned
        if 2 * owned == LANES:
            tile = whole[:, start // LANES * LANES : start // LANES * LANES + LANES]
            top, bottom = tile[:half], tile[half:]
            if start % LANES:
                top = pltpu.roll(top, owned, 1)
            else:
                bottom = pltpu.roll(bottom, owned, 1)
            send[...] = jnp.where(low, top, bottom).astype(bf16)
        else:
            send[...] = whole[:, start : start + owned].astype(bf16)


def last_kernel(owned, mean, logs, got_a, got_b, got_c, out_w, cand_o):
    heads = logs.shape[0]
    parts = [(mean[...], logs[...])]
    for got in (got_a, got_b, got_c):
        if 2 * owned == LANES:
            value = got[...].astype(f32)
            value = jnp.concatenate([value, pltpu.roll(value, owned, 1)], axis=0)
        else:
            value = got[...].astype(f32)
        parts.append((value[: heads * 64], unpack_logs(value[heads * 64 :], heads)))
    attended = merge(parts)[0].astype(bf16)
    cand_o[...] = contract(attended, out_w[...], 0, 0)[: cand_o.shape[0]]


def shape(dims, dtype):
    return jax.ShapeDtypeStruct(dims, dtype)


VMEM = pl.BlockSpec(memory_space=pltpu.VMEM)
SMEM = pl.BlockSpec(memory_space=pltpu.SMEM)
ANY = pl.BlockSpec(memory_space=pl.ANY)


def call(kernel, name, scalars, operands, outs, scratch=(), after=(), flops=0):
    count = len(scalars) + len(operands)

    def body(*refs):
        kernel(*refs[:count], *refs[count + len(after) :])

    return pl.pallas_call(
        body,
        name=name,
        in_specs=[SMEM] * len(scalars) + [VMEM] * len(operands) + [ANY] * len(after),
        out_specs=[VMEM] * len(outs),
        out_shape=outs,
        scratch_shapes=list(scratch),
        compiler_params=pltpu.CompilerParams(vmem_limit_bytes=VMEM_LIMIT),
        cost_estimate=pl.CostEstimate(flops=flops, transcendentals=0, bytes_accessed=0),
    )(*scalars, *operands, *after)


def reversed_bits(value, bits):
    return sum(((value >> b) & 1) << (bits - 1 - b) for b in range(bits))


def shards(
    history_item_index,
    log_head_retention,
    user_history_length,
    candidate_item_index,
    item_stored_row,
    item_embedding_table,
    head_score_scale,
    history_query_key_value_weight,
    history_output_weight,
    candidate_key_value_weight,
    candidate_query_weight,
    candidate_output_weight,
):
    users, n = history_item_index.shape
    heads = log_head_retention.shape[1]
    half, width = item_embedding_table.shape
    owned = candidate_item_index.shape[1]
    seq = lax.axis_size("seq")
    bits = seq.bit_length() - 1
    assert users == 1 and lax.axis_size("dp") == 2 and seq == 1 << bits and bits > 2
    assert width == heads * 64 and heads % 4 == 0 and owned <= 64
    pairs = heads // 2
    rows = pairs * 64
    cands = owned * seq
    rank = lax.axis_index("seq")

    def swap(value, mask):
        return lax.ppermute(value, "seq", [(j, j ^ mask) for j in range(seq)])

    peer = lax.ppermute(item_embedding_table, "dp", [(0, 1), (1, 0)])
    far_ids = swap(candidate_item_index, seq // 2)
    sc = jnp.stack(
        [rank, rank * n, user_history_length[0], lax.axis_index("dp")]
    ).astype(i32)
    stored = item_stored_row.reshape(-1, LANES)
    decay = log_head_retention.reshape(heads, n)
    ids = jnp.concatenate([candidate_item_index, far_ids], axis=0)
    ids = jnp.pad(ids, ((0, 0), (0, 64 - owned)))
    id_rows = jnp.concatenate([ids // LANES, ids % LANES], axis=1).astype(f32)

    part, slot, crow, ccol, ctl = call(
        own_rows_kernel, "own_rows", [sc],
        [history_item_index, stored, decay, item_embedding_table],
        [
            shape((n, width), bf16), shape((1, n), f32), shape((n // CHUNK, heads, CHUNK), f32),
            shape((n, 2 * heads), f32), shape((n // CHUNK * pairs, LANES), f32),
        ],
        flops=2 * n * half * width,
    )
    emb, key, val, enter, pay = call(
        summary_kernel, "summary", [sc],
        [part, peer, slot, ccol, ctl, id_rows, history_query_key_value_weight],
        [
            shape((n, width), bf16), shape((n, width), bf16), shape((n, width), bf16),
            shape((n // CHUNK, rows, LANES), f32), shape((state_rows(pairs, 2), LANES), bf16),
        ],
        flops=2 * n * half * width,
    )

    def local(first, name, after):
        return call(
            lambda *refs: local_kernel(first, *refs), name, [],
            [emb, key, val, crow, ccol, history_query_key_value_weight],
            [shape((n, width // 2), bf16), shape((n, width // 2), f32)],
            after=after, flops=2 * n * half * width // 2,
        )

    early = [local(0, "local_a", [])]
    prefix = logs = None
    for bit in range(bits - 1):
        got = swap(pay, 1 << bit)
        if bit == 1:
            early.append(local(width // 2, "local_b", [prefix]))
        count = 2 << bit
        sent = 2 * count if bit < bits - 2 else 1
        pay, prefix, logs, id_rows = call(
            lambda *refs, bit=bit, count=count: join_kernel(bit, count, pairs, *refs), "join", [sc],
            [pay, got] + ([prefix, logs] if bit else []),
            [
                shape((state_rows(pairs, sent), LANES), bf16), shape((rows, LANES), f32),
                shape((pairs, LANES), f32), shape((2 * count, LANES), f32),
            ],
            after=[early[-1][1]],
        )
    got = swap(pay, 1 << (bits - 1))
    half_seq = seq // 2
    places = {}
    for j in range(seq):
        places[(j & 1) * half_seq + (j >> 1)] = j
    order = [places[reversed_bits(j, bits)] for j in range(seq)]
    cand_q, val_w = call(
        lambda *refs: candidate_kernel(order, owned, *refs), "candidates", [sc],
        [
            id_rows, stored, item_embedding_table, peer, candidate_query_weight,
            candidate_key_value_weight,
        ],
        [shape((width, cands), bf16), shape((width, width), bf16)],
        flops=2 * cands * 2 * half * width,
    )
    (query_a, intra_a), (query_b, intra_b) = early
    send = cands // 2
    buffers = [pltpu.VMEM((n, send), f32)] * 2
    message = width + log_pad(heads)
    hist, key_two, val_two, pay = call(
        lambda *refs: finish_kernel(bits - 1, *refs), "finish", [sc, head_score_scale],
        [
            emb, query_a, query_b, intra_a, intra_b, enter, ctl, got, prefix, logs,
            history_output_weight, candidate_key_value_weight, val_w, cand_q,
        ],
        [
            shape((n, width), f32), shape((n, width), bf16), shape((width, n), bf16),
            shape((message, send), bf16),
        ],
        buffers,
        flops=2 * n * half * width,
    )
    mean, logs = call(
        keep_kernel, "keep", [sc, head_score_scale], [cand_q, key_two, val_two],
        [shape((width, send), f32), shape((heads, send), f32)],
        buffers,
        flops=2 * n * half * width,
    )
    for bit in range(bits - 3):
        got = swap(pay, 1 << bit)
        send //= 2
        mean, logs, pay = call(
            fold_kernel, "fold", [], [mean, logs, got],
            [shape((width, send), f32), shape((heads, send), f32), shape((message, send), bf16)],
        )
    got = swap(pay, 1 << (bits - 3))
    packed = 2 * owned == LANES
    cols = LANES if packed else owned
    mean, logs, *sends = call(
        deal_kernel, "deal", [], [mean, logs, got],
        [shape((width, cols), f32), shape((heads, cols), f32)]
        + [shape((message // 2, LANES) if packed else (message, owned), bf16)] * 3,
    )
    masks = [seq // 2, seq // 4, seq // 2 + seq // 4]
    gots = [swap(value, mask) for value, mask in zip(sends, masks)]
    (cand_out,) = call(
        lambda *refs: last_kernel(owned, *refs), "last", [],
        [mean, logs, *gots, candidate_output_weight],
        [shape((owned, width), f32)],
    )
    return hist[None], cand_out[None]


def solution(mesh):
    in_specs = (
        P(("groups", "dp"), "seq"),
        P(("groups", "dp"), None, "seq"),
        P(("groups", "dp")),
        P(("groups", "dp"), "seq"),
        P(),
        P("dp", None),
        P(),
        P(),
        P(),
        P(),
        P(),
        P(),
    )
    out_specs = (P(("groups", "dp"), "seq", None), P(("groups", "dp"), "seq", None))
    return jax.shard_map(shards, mesh=mesh, in_specs=in_specs, out_specs=out_specs, check_vma=False)
```

time: 235 us -> 59.1 us (0.25)
  blocking collectives: 56.2 us -> 0 us
  matrix products: 44.3 us -> 0 us
  other arithmetic: 34.1 us -> 0.17 us
  Pallas kernels: 0 us -> 32.1 us
  local copies, waits for them, and re-layouts: 34.7 us -> 3.79 us
  waiting for transfers between devices: 27.9 us -> 7.66 us
  between operations: 15.8 us -> 1.39 us
  starting transfers between devices: 20.8 us -> 13.7 us
    dot_general x10 -> x0, matrix products: 44.3 us -> none  [the longest x1 16.9 us: block_terms(): jnp.einsum('hst,thd->shd', weights, val_rows, preferred_element_type=jnp....]
    all_gather x1 -> x0, blocking collectives: 33 us -> none  [shards(): candidate_query_rows = lax.all_gather(own_query, 'seq', axis=1, tiled=True)]
    pallas_call x0 -> x11, Pallas kernels: none -> 32.1 us  [call(): pl.pallas_call(body, name=name, in_specs=[SMEM] * len(scalars) + [VMEM] *...]
    all_to_all x5 -> x0, waiting for transfers between devices: 27.9 us -> none  [the longest x1 20.8 us: shards(): lax.all_to_all(weighted[None], 'seq', split_axis=2, concat_axis=0, tiled=...]
    unnamed x1 -> x0, blocking collectives: 23.2 us -> none
    all_to_all x5 -> x0, starting transfers between devices: 20.8 us -> none  [the longest x1 5.65 us: shards(): lax.all_to_all(weighted[None], 'seq', split_axis=2, concat_axis=0, tiled=...]
    ppermute x0 -> x9, starting transfers between devices: none -> 13.7 us  [the longest x8 13.1 us: swap(): return lax.ppermute(value, 'seq', [(j, j ^ mask) for j in range(seq)])]
    gather x2 -> x0, local copies, waits for them, and re-layouts: 13.6 us -> none  [the longest x1 7.45 us: fetch_rows(): item_embedding_table[local_rows]]
  transfers between devices with their start and end apart: 6 -> 9, of which waited for: 4 -> 6; matrix products, arithmetic and copies ran while one was open for 8% -> 0% of each run, Pallas kernels for 0% -> 28%
where the time goes in v2:
time: 59.1 us; the launch traced here: 58.8 us
  Pallas kernels  32.1 us (54%)
  starting transfers between devices  13.7 us (23%)
  waiting for transfers between devices  7.66 us (13%)
  local copies, waits for them, and re-layouts  3.79 us (6%)
  between operations  1.39 us (2%)
    pallas_call x11, Pallas kernels, call(): pl.pallas_call(body, name=name, in_specs=[SMEM] * len(scalars) + [VMEM] *...  32.1 us
    ppermute x8, starting transfers between devices, swap(): return lax.ppermute(value, 'seq', [(j, j ^ mask) for j in range(seq)])  13.1 us
    ppermute x8, waiting for transfers between devices, swap(): return lax.ppermute(value, 'seq', [(j, j ^ mask) for j in range(seq)])  7.66 us
    unnamed x26, local copies, waits for them, and re-layouts  3.79 us
  transfers between devices with their start and end apart: 9, of which 6 were waited for; matrix products, arithmetic and copies ran while one was open for 0% of the time, Pallas kernels for 28%

profile of v2, /device:TPU:0, one launch (start us, length us, event | category | flops | bytes accessed | tf_op | source)
XLA Modules:
  0.0 58.8 jit_solution(8727957933965379480)
XLA Ops:
  0.6 0.5 collective-permute-start
  1.1 3.7 %collective-permute-start.1 = (s32[1,64]{1,0:T(1,128)}, s32[1,64]{1,0:T(1,128)S(1)}, u32[]{:S(2)}, u32[]{:S(2)}) collective-permute-start(s32[1,64]{1,0:T(1,128)} %param.15), channel_id=1, source_target_pairs={{0,8},{2,10},{4,12},{6,14},{8,0},{10,2},{12,4},{14,6},{1,9},{3,11}... | collective-permute-start | bytes 776 | tf_op jit(solution)/shard_map/ppermute | solution.py:534
  5.5 0.1 pad_add_fusion.1.refs_0_
  5.5 0.0 copy-start.2
  5.5 1.6 %copy-done.2 = bf16[2048,512]{1,0:T(8,128)(2,1)S(1)} copy-done((bf16[2048,512]{1,0:T(8,128)(2,1)S(1)}, bf16[2048,512]{1,0:T(8,128)(2,1)}, u32[]{:S(2)}) %copy-start.2) | copy-done | bytes 2097176
  7.1 0.8 %copy-done.7 = f32[1,8,1024]{2,1,0:T(8,128)S(1)} copy-done((f32[1,8,1024]{2,1,0:T(8,128)S(1)}, f32[1,8,1024]{2,1,0:T(8,128)}, u32[]{:S(2)}) %copy-start.7) | copy-done | bytes 32792
  7.9 0.0 copy-start.8
  7.9 0.7 %copy-done.8 = s32[4096]{0:T(1024)S(1)} copy-done((s32[4096]{0:T(1024)S(1)}, s32[4096]{0:T(1024)}, u32[]{:S(2)}) %copy-start.8) | copy-done | bytes 16408
  8.6 0.7 %copy-done.10 = s32[1,1024]{1,0:T(1,128)S(1)} copy-done((s32[1,1024]{1,0:T(1,128)S(1)}, s32[1,1024]{1,0:T(1,128)}, u32[]{:S(2)}) %copy-start.10) | copy-done | bytes 4120
  9.3 3.4 %own_rows.1 = (bf16[1024,512]{1,0:T(8,128)(2,1)S(1)}, f32[1,1024]{1,0:T(1,128)S(1)}, f32[4,8,256]{2,1,0:T(8,128)S(1)}, f32[1024,16]{1,0:T(8,128)S(1)}, f32[16,128]{1,0:T(8,128)S(1)}) custom-call(s32[4]{0:T(128)S(1)} %pad_add_fusion.1.refs_0_, s32[1,1024]{1,0:T(1,128)S(1)} %copy-done.10, s32[32,128]{1,0:T(8,128)S(1)} %bitcast.8, f32[8,1024]{1,0:T(8,128)S(1)} %bitcast.7, ...), custom_call_target="tpu_custom_call" | custom-call | flops 2147483648 | tf_op jit(solution)/shard_map/own_rows/pallas_call | solution.py:490
  12.7 0.0 collective-permute-done.1
  12.7 0.0 copy-done.12
  12.8 0.1 add_convert_fusion.refs_6_
  12.8 0.0 collective-permute-done.refs_2_.refs_4_
  12.8 0.0 copy-done
  12.8 6.0 %summary.1 = (bf16[1024,512]{1,0:T(8,128)(2,1)S(1)}, bf16[1024,512]{1,0:T(8,128)(2,1)S(1)}, bf16[1024,512]{1,0:T(8,128)(2,1)S(1)}, f32[4,256,128]{2,1,0:T(8,128)S(1)}, bf16[272,128]{1,0:T(8,128)(2,1)S(1)}) custom-call(s32[4]{0:T(128)S(1)} %pad_add_fusion.1.refs_0_, bf16[1024,512]{1,0:T(8,128)(2,1)S(1)} %get-tuple-element.36.refs_1_, ...), custom_call_target="tpu_custom_call" | custom-call | flops 2147483648 | tf_op jit(solution)/shard_map/summary/pallas_call | solution.py:490
  18.8 1.6 %collective-permute-start.2 = (bf16[272,128]{1,0:T(8,128)(2,1)S(1)}, bf16[272,128]{1,0:T(8,128)(2,1)S(1)}, u32[]{:S(2)}, u32[]{:S(2)}) collective-permute-start(bf16[272,128]{1,0:T(8,128)(2,1)S(1)} %get-tuple-element.45.refs_1_), channel_id=1, source_target_pairs={{0,2},{2,0},{4,6},{6,4},{8,10},{10,8},{12,14},{14,12},{1,3},{3,1},... | collective-permute-start | bytes 208904 | tf_op jit(solution)/shard_map/ppermute | solution.py:534
  20.4 2.7 %local_a.1 = (bf16[1024,256]{1,0:T(8,128)(2,1)S(1)}, f32[1024,256]{1,0:T(8,128)S(1)}) custom-call(bf16[1024,512]{1,0:T(8,128)(2,1)S(1)} %get-tuple-element.40.refs_0_.refs_2_, bf16[1024,512]{1,0:T(8,128)(2,1)S(1)} %get-tuple-element.41.refs_1_, bf16[1024,512]{1,0:T(8,128)(2,1)S(1)} %get-tuple-element.42.refs_2_, f32[4,8,256]{2,1,0:T(8,128)S(1)} %get-tuple-element.43.refs_3_, ...), custom_call_target="tpu_custom_call" | custom-call | flops 1073741824 | tf_op jit(solution)/shard_map/local_a/pallas_call | solution.py:490
  23.0 0.2 collective-permute-done.2.refs_2_
  23.2 1.1 %join.2 = (bf16[272,128]{1,0:T(8,128)(2,1)S(1)}, f32[256,128]{1,0:T(8,128)S(1)}, f32[4,128]{1,0:T(4,128)S(1)}, f32[4,128]{1,0:T(4,128)}) custom-call(s32[4]{0:T(128)S(1)} %pad_add_fusion.1.refs_0_, bf16[272,128]{1,0:T(8,128)(2,1)S(1)} %get-tuple-element.45.refs_1_, bf16[272,128]{1,0:T(8,128)(2,1)S(1)} %collective-permute-done.2.refs_2_, ...), custom_call_target="tpu_custom_call" | custom-call | tf_op jit(solution)/shard_map/join/pallas_call | solution.py:490
  24.3 1.6 %collective-permute-start.3 = (bf16[272,128]{1,0:T(8,128)(2,1)S(1)}, bf16[272,128]{1,0:T(8,128)(2,1)S(1)}, u32[]{:S(2)}, u32[]{:S(2)}) collective-permute-start(bf16[272,128]{1,0:T(8,128)(2,1)S(1)} %get-tuple-element.51.refs_1_), channel_id=1, source_target_pairs={{0,4},{2,6},{4,0},{6,2},{8,12},{10,14},{12,8},{14,10},{1,5},{3,7},... | collective-permute-start | bytes 208904 | tf_op jit(solution)/shard_map/ppermute | solution.py:534
  25.9 2.8 %local_b.1 = (bf16[1024,256]{1,0:T(8,128)(2,1)S(1)}, f32[1024,256]{1,0:T(8,128)S(1)}) custom-call(bf16[1024,512]{1,0:T(8,128)(2,1)S(1)} %get-tuple-element.40.refs_0_.refs_2_, bf16[1024,512]{1,0:T(8,128)(2,1)S(1)} %get-tuple-element.41.refs_1_, bf16[1024,512]{1,0:T(8,128)(2,1)S(1)} %get-tuple-element.42.refs_2_, f32[4,8,256]{2,1,0:T(8,128)S(1)} %get-tuple-element.43.refs_3_, ...), custom_call_target="tpu_custom_call" | custom-call | flops 1073741824 | tf_op jit(solution)/shard_map/local_b/pallas_call | solution.py:490
  28.7 0.0 collective-permute-done.3.refs_2_
  28.8 0.6 %join.3 = (bf16[272,128]{1,0:T(8,128)(2,1)S(1)}, f32[256,128]{1,0:T(8,128)S(1)}, f32[4,128]{1,0:T(4,128)S(1)}, f32[8,128]{1,0:T(8,128)S(1)}) custom-call(s32[4]{0:T(128)S(1)} %pad_add_fusion.1.refs_0_, bf16[272,128]{1,0:T(8,128)(2,1)S(1)} %get-tuple-element.51.refs_1_, bf16[272,128]{1,0:T(8,128)(2,1)S(1)} %collective-permute-done.3.refs_2_, ...), custom_call_target="tpu_custom_call" | custom-call | tf_op jit(solution)/shard_map/join/pallas_call | solution.py:490
  29.4 0.4 collective-permute-start.4
  29.8 0.0 copy-done.3
  29.8 0.0 copy-done.4
  29.8 0.0 copy-done.5
  29.8 0.0 copy-done.9
  29.8 0.0 copy-start.6
  29.8 0.0 copy-start.11
  29.8 3.8 %candidates.1 = (bf16[512,512]{1,0:T(8,128)(2,1)S(1)}, bf16[512,512]{1,0:T(8,128)(2,1)S(1)}) custom-call(s32[4]{0:T(128)S(1)} %pad_add_fusion.1.refs_0_, f32[8,128]{1,0:T(8,128)S(1)} %get-tuple-element.56.refs_1_, s32[32,128]{1,0:T(8,128)S(1)} %bitcast.9, bf16[2048,512]{1,0:T(8,128)(2,1)S(1)} %copy-done.3, ...), custom_call_target="tpu_custom_call" | custom-call | flops 2147483648 | tf_op jit(solution)/shard_map/candidates/pallas_call | solution.py:490
  33.6 1.0 %collective-permute-done.4.refs_9_ = bf16[272,128]{1,0:T(8,128)(2,1)S(1)} collective-permute-done((bf16[272,128]{1,0:T(8,128)(2,1)S(1)}, bf16[272,128]{1,0:T(8,128)(2,1)S(1)}, u32[]{:S(2)}, u32[]{:S(2)}) %collective-permute-start.4) | collective-permute-done | bytes 69664 | tf_op jit(solution)/shard_map/ppermute | solution.py:534
  34.6 0.0 copy-done.6
  34.6 0.0 copy-done.11
  34.6 6.8 %finish.1 = (f32[1024,512]{1,0:T(8,128)}, bf16[1024,512]{1,0:T(8,128)(2,1)S(1)}, bf16[512,1024]{1,0:T(8,128)(2,1)S(1)}, bf16[544,256]{1,0:T(8,128)(2,1)S(1)}) custom-call(s32[4]{0:T(128)S(1)} %pad_add_fusion.1.refs_0_, f32[8]{0:T(128)S(1)} %copy-done.11, bf16[1024,512]{1,0:T(8,128)(2,1)S(1)} %get-tuple-element.40.refs_0_.refs_2_, ...), custom_call_target="tpu_custom_call" | custom-call | flops 2147483648 | tf_op jit(solution)/shard_map/finish/pallas_call | solution.py:490
  41.5 1.5 %collective-permute-start.5 = (bf16[544,256]{1,0:T(8,128)(2,1)S(1)}, bf16[544,256]{1,0:T(8,128)(2,1)S(1)}, u32[]{:S(2)}, u32[]{:S(2)}) collective-permute-start(bf16[544,256]{1,0:T(8,128)(2,1)S(1)} %get-tuple-element.64), channel_id=1, source_target_pairs={{0,2},{2,0},{4,6},{6,4},{8,10},{10,8},{12,14},{14,12},{1,3},{3,1},... | collective-permute-start | bytes 835592 | tf_op jit(solution)/shard_map/ppermute | solution.py:534
  43.0 3.7 %keep.1 = (f32[512,256]{1,0:T(8,128)S(1)}, f32[8,256]{1,0:T(8,128)S(1)}) custom-call(s32[4]{0:T(128)S(1)} %pad_add_fusion.1.refs_0_, f32[8]{0:T(128)S(1)} %copy-done.11, bf16[512,512]{1,0:T(8,128)(2,1)S(1)} %get-tuple-element.58.refs_15_.refs_2_, bf16[1024,512]{1,0:T(8,128)(2,1)S(1)} %get-tuple-element.60.refs_3_, ...), custom_call_target="tpu_custom_call" | custom-call | flops 2147483648 | tf_op jit(solution)/shard_map/keep/pallas_call | solution.py:490
  46.6 2.5 %collective-permute-done.5.refs_2_ = bf16[544,256]{1,0:T(8,128)(2,1)S(1)} collective-permute-done((bf16[544,256]{1,0:T(8,128)(2,1)S(1)}, bf16[544,256]{1,0:T(8,128)(2,1)S(1)}, u32[]{:S(2)}, u32[]{:S(2)}) %collective-permute-start.5) | collective-permute-done | bytes 278560 | tf_op jit(solution)/shard_map/ppermute | solution.py:534
  49.1 0.2 deal.1
  49.3 1.8 %collective-permute-start.6 = (bf16[272,128]{1,0:T(8,128)(2,1)S(1)}, bf16[272,128]{1,0:T(8,128)(2,1)S(1)}, u32[]{:S(2)}, u32[]{:S(2)}) collective-permute-start(bf16[272,128]{1,0:T(8,128)(2,1)S(1)} %get-tuple-element.67), channel_id=1, source_target_pairs={{0,8},{2,10},{4,12},{6,14},{8,0},{10,2},{12,4},{14,6},{1,9},{3,11}... | collective-permute-start | bytes 208904 | tf_op jit(solution)/shard_map/ppermute | solution.py:534
  51.1 0.6 collective-permute-start.7
  51.6 2.1 %collective-permute-start.8 = (bf16[272,128]{1,0:T(8,128)(2,1)S(1)}, bf16[272,128]{1,0:T(8,128)(2,1)S(1)}, u32[]{:S(2)}, u32[]{:S(2)}) collective-permute-start(bf16[272,128]{1,0:T(8,128)(2,1)S(1)} %get-tuple-element.69), channel_id=1, source_target_pairs={{0,12},{2,14},{4,8},{6,10},{8,4},{10,6},{12,0},{14,2},{1,13},{3,15... | collective-permute-start | bytes 208904 | tf_op jit(solution)/shard_map/ppermute | solution.py:534
  53.7 2.2 %collective-permute-done.6.refs_2_ = bf16[272,128]{1,0:T(8,128)(2,1)S(1)} collective-permute-done((bf16[272,128]{1,0:T(8,128)(2,1)S(1)}, bf16[272,128]{1,0:T(8,128)(2,1)S(1)}, u32[]{:S(2)}, u32[]{:S(2)}) %collective-permute-start.6) | collective-permute-done | bytes 69664 | tf_op jit(solution)/shard_map/ppermute | solution.py:534
  55.9 0.4 collective-permute-done.7.refs_3_
  56.3 1.5 %collective-permute-done.8.refs_4_ = bf16[272,128]{1,0:T(8,128)(2,1)S(1)} collective-permute-done((bf16[272,128]{1,0:T(8,128)(2,1)S(1)}, bf16[272,128]{1,0:T(8,128)(2,1)S(1)}, u32[]{:S(2)}, u32[]{:S(2)}) %collective-permute-start.8) | collective-permute-done | bytes 69664 | tf_op jit(solution)/shard_map/ppermute | solution.py:534
  57.7 0.0 copy-done.1
  57.7 1.0 %last.1 = f32[64,512]{1,0:T(8,128)} custom-call(f32[512,128]{1,0:T(8,128)S(1)} %get-tuple-element.65.refs_0_, f32[8,128]{1,0:T(8,128)S(1)} %get-tuple-element.66.refs_1_, bf16[272,128]{1,0:T(8,128)(2,1)S(1)} %collective-permute-done.6.refs_2_, bf16[272,128]{1,0:T(8,128)(2,1)S(1)} %collective-permute-done.7.refs_3_, ...), custom_call_target="tpu_custom_call" | custom-call | tf_op jit(solution)/shard_map/last/pallas_call | solution.py:490
  (10 shorter events, 0.0 us)
Async XLA Ops:
  0.6 12.2 %collective-permute-start = (bf16[2048,512]{1,0:T(8,128)(2,1)}, bf16[2048,512]{1,0:T(8,128)(2,1)S(1)}, u32[]{:S(2)}, u32[]{:S(2)}) collective-permute-start(bf16[2048,512]{1,0:T(8,128)(2,1)} %refs_3_.1), channel_id=1, source_target_pairs={{0,1},{1,0},{2,3},{3,2},{4,5},{5,4},{6,7},{7,6},{8,9},{9,8},{10,11... | collective-permute-start | bytes 6291464 | tf_op jit(solution)/shard_map/ppermute | solution.py:536
  1.1 11.6 %collective-permute-start.1 = (s32[1,64]{1,0:T(1,128)}, s32[1,64]{1,0:T(1,128)S(1)}, u32[]{:S(2)}, u32[]{:S(2)}) collective-permute-start(s32[1,64]{1,0:T(1,128)} %param.15), channel_id=1, source_target_pairs={{0,8},{2,10},{4,12},{6,14},{8,0},{10,2},{12,4},{14,6},{1,9},{3,11}... | collective-permute-start | bytes 776 | tf_op jit(solution)/shard_map/ppermute | solution.py:534
  5.5 1.6 %copy-start.2 = (bf16[2048,512]{1,0:T(8,128)(2,1)S(1)}, bf16[2048,512]{1,0:T(8,128)(2,1)}, u32[]{:S(2)}) copy-start(bf16[2048,512]{1,0:T(8,128)(2,1)} %refs_3_.1) | copy-start | bytes 6291460
  7.1 0.8 %copy-start.7 = (f32[1,8,1024]{2,1,0:T(8,128)S(1)}, f32[1,8,1024]{2,1,0:T(8,128)}, u32[]{:S(2)}) copy-start(f32[1,8,1024]{2,1,0:T(8,128)} %param.13) | copy-start | bytes 98308
  7.9 0.7 %copy-start.8 = (s32[4096]{0:T(1024)S(1)}, s32[4096]{0:T(1024)}, u32[]{:S(2)}) copy-start(s32[4096]{0:T(1024)} %param.16) | copy-start | bytes 49156
  8.6 0.7 %copy-start.10 = (s32[1,1024]{1,0:T(1,128)S(1)}, s32[1,1024]{1,0:T(1,128)}, u32[]{:S(2)}) copy-start(s32[1,1024]{1,0:T(1,128)} %refs_1_.3) | copy-start | bytes 12292
  9.3 3.4 %copy-start.12 = (s32[1,64]{1,0:T(1,128)S(1)}, s32[1,64]{1,0:T(1,128)}, u32[]{:S(2)}) copy-start(s32[1,64]{1,0:T(1,128)} %param.15) | copy-start | bytes 772
  9.3 3.5 %copy-start = (bf16[512,1536]{1,0:T(8,128)(2,1)S(1)}, bf16[512,1536]{1,0:T(8,128)(2,1)}, u32[]{:S(2)}) copy-start(bf16[512,1536]{1,0:T(8,128)(2,1)} %refs_5_.5) | copy-start | bytes 4718596
  18.8 4.4 %collective-permute-start.2 = (bf16[272,128]{1,0:T(8,128)(2,1)S(1)}, bf16[272,128]{1,0:T(8,128)(2,1)S(1)}, u32[]{:S(2)}, u32[]{:S(2)}) collective-permute-start(bf16[272,128]{1,0:T(8,128)(2,1)S(1)} %get-tuple-element.45.refs_1_), channel_id=1, source_target_pairs={{0,2},{2,0},{4,6},{6,4},{8,10},{10,8},{12,14},{14,12},{1,3},{3,1},... | collective-permute-start | bytes 208904 | tf_op jit(solution)/shard_map/ppermute | solution.py:534
  24.3 4.4 %collective-permute-start.3 = (bf16[272,128]{1,0:T(8,128)(2,1)S(1)}, bf16[272,128]{1,0:T(8,128)(2,1)S(1)}, u32[]{:S(2)}, u32[]{:S(2)}) collective-permute-start(bf16[272,128]{1,0:T(8,128)(2,1)S(1)} %get-tuple-element.51.refs_1_), channel_id=1, source_target_pairs={{0,4},{2,6},{4,0},{6,2},{8,12},{10,14},{12,8},{14,10},{1,5},{3,7},... | collective-permute-start | bytes 208904 | tf_op jit(solution)/shard_map/ppermute | solution.py:534
  25.9 3.9 %copy-start.3 = (bf16[2048,512]{1,0:T(8,128)(2,1)S(1)}, bf16[2048,512]{1,0:T(8,128)(2,1)}, u32[]{:S(2)}) copy-start(bf16[2048,512]{1,0:T(8,128)(2,1)} %refs_3_.1) | copy-start | bytes 6291460
  25.9 3.9 %copy-start.4 = (bf16[512,1024]{1,0:T(8,128)(2,1)S(1)}, bf16[512,1024]{1,0:T(8,128)(2,1)}, u32[]{:S(2)}) copy-start(bf16[512,1024]{1,0:T(8,128)(2,1)} %refs_13_.1) | copy-start | bytes 3145732
  25.9 3.9 %copy-start.5 = (bf16[512,512]{1,0:T(8,128)(2,1)S(1)}, bf16[512,512]{1,0:T(8,128)(2,1)}, u32[]{:S(2)}) copy-start(bf16[512,512]{1,0:T(8,128)(2,1)} %refs_5_.6) | copy-start | bytes 1572868
  25.9 3.9 %copy-start.9 = (s32[4096]{0:T(1024)S(1)}, s32[4096]{0:T(1024)}, u32[]{:S(2)}) copy-start(s32[4096]{0:T(1024)} %param.16) | copy-start | bytes 49156
  29.4 5.3 %collective-permute-start.4 = (bf16[272,128]{1,0:T(8,128)(2,1)S(1)}, bf16[272,128]{1,0:T(8,128)(2,1)S(1)}, u32[]{:S(2)}, u32[]{:S(2)}) collective-permute-start(bf16[272,128]{1,0:T(8,128)(2,1)S(1)} %get-tuple-element.53), channel_id=1, source_target_pairs={{0,8},{2,10},{4,12},{6,14},{8,0},{10,2},{12,4},{14,6},{1,9},{3,11}... | collective-permute-start | bytes 208904 | tf_op jit(solution)/shard_map/ppermute | solution.py:534
  29.8 4.9 %copy-start.6 = (bf16[512,512]{1,0:T(8,128)(2,1)S(1)}, bf16[512,512]{1,0:T(8,128)(2,1)}, u32[]{:S(2)}) copy-start(bf16[512,512]{1,0:T(8,128)(2,1)} %refs_12_.1) | copy-start | bytes 1572868
  29.8 4.9 %copy-start.11 = (f32[8]{0:T(128)S(1)}, f32[8]{0:T(128)}, u32[]{:S(2)}) copy-start(f32[8]{0:T(128)} %refs_1_.5) | copy-start | bytes 100
  41.5 7.6 %collective-permute-start.5 = (bf16[544,256]{1,0:T(8,128)(2,1)S(1)}, bf16[544,256]{1,0:T(8,128)(2,1)S(1)}, u32[]{:S(2)}, u32[]{:S(2)}) collective-permute-start(bf16[544,256]{1,0:T(8,128)(2,1)S(1)} %get-tuple-element.64), channel_id=1, source_target_pairs={{0,2},{2,0},{4,6},{6,4},{8,10},{10,8},{12,14},{14,12},{1,3},{3,1},... | collective-permute-start | bytes 835592 | tf_op jit(solution)/shard_map/ppermute | solution.py:534
  43.0 14.8 %copy-start.1 = (bf16[512,512]{1,0:T(8,128)(2,1)S(1)}, bf16[512,512]{1,0:T(8,128)(2,1)}, u32[]{:S(2)}) copy-start(bf16[512,512]{1,0:T(8,128)(2,1)} %refs_5_.7) | copy-start | bytes 1572868
  49.3 6.6 %collective-permute-start.6 = (bf16[272,128]{1,0:T(8,128)(2,1)S(1)}, bf16[272,128]{1,0:T(8,128)(2,1)S(1)}, u32[]{:S(2)}, u32[]{:S(2)}) collective-permute-start(bf16[272,128]{1,0:T(8,128)(2,1)S(1)} %get-tuple-element.67), channel_id=1, source_target_pairs={{0,8},{2,10},{4,12},{6,14},{8,0},{10,2},{12,4},{14,6},{1,9},{3,11}... | collective-permute-start | bytes 208904 | tf_op jit(solution)/shard_map/ppermute | solution.py:534
  51.1 5.2 %collective-permute-start.7 = (bf16[272,128]{1,0:T(8,128)(2,1)S(1)}, bf16[272,128]{1,0:T(8,128)(2,1)S(1)}, u32[]{:S(2)}, u32[]{:S(2)}) collective-permute-start(bf16[272,128]{1,0:T(8,128)(2,1)S(1)} %get-tuple-element.68), channel_id=1, source_target_pairs={{0,4},{2,6},{4,0},{6,2},{8,12},{10,14},{12,8},{14,10},{1,5},{3,7},... | collective-permute-start | bytes 208904 | tf_op jit(solution)/shard_map/ppermute | solution.py:534
  51.6 6.1 %collective-permute-start.8 = (bf16[272,128]{1,0:T(8,128)(2,1)S(1)}, bf16[272,128]{1,0:T(8,128)(2,1)S(1)}, u32[]{:S(2)}, u32[]{:S(2)}) collective-permute-start(bf16[272,128]{1,0:T(8,128)(2,1)S(1)} %get-tuple-element.69), channel_id=1, source_target_pairs={{0,12},{2,14},{4,8},{6,10},{8,4},{10,6},{12,0},{14,2},{1,13},{3,15... | collective-permute-start | bytes 208904 | tf_op jit(solution)/shard_map/ppermute | solution.py:534

commit v3 on v2

--- a/solution.py
+++ b/solution.py
@@ -92,16 +92,29 @@
     return slice(p * LANES, (p + 1) * LANES)
 
 
-def own_rows_kernel(sc, ids, stored, decay, own, part_o, slot_o, crow_o, ccol_o, ctl_o):
+def own_rows_kernel(
+    ids_in, stored_in, decay_in, own_in, part_o, slot_o, crow_o, ccol_o, ctl_o,
+    ids, stored, decay, own, sem,
+):
     n, half, heads = ids.shape[1], own.shape[0], decay.shape[0]
+    copies = [
+        pltpu.make_async_copy(source, target, sem.at[k])
+        for k, (source, target) in enumerate(
+            ((ids_in, ids), (stored_in, stored), (decay_in, decay), (own_in, own))
+        )
+    ]
+    for copy in copies:
+        copy.start()
+    copies[0].wait()
+    copies[1].wait()
     slots = stored_slots(ids[...], stored[...])
     slot_o[...] = slots
+    copies[2].wait()
     upto = jnp.where(
         iota((CHUNK, CHUNK), 0) <= iota((CHUNK, CHUNK), 1), 1.0, 0.0
     ).astype(bf16)
     low = first_half((1, LANES))
     for i in range(n // CHUNK):
-        part_o[chunk(i), :] = picked_rows(slots[:, chunk(i)], sc[3] * half, own).astype(bf16)
         pieces = jnp.concatenate(thirds(decay[:, chunk(i)]), axis=0)
         sums = dot(pieces.astype(bf16), upto)
         cum = sums[:heads] + sums[heads : 2 * heads] + sums[2 * heads :]
@@ -112,10 +125,14 @@
             ctl_o[r : r + 1, :] = jnp.where(
                 low, cum[2 * p : 2 * p + 1, CHUNK - 1 :], cum[2 * p + 1 : 2 * p + 2, CHUNK - 1 :]
             )
+    copies[3].wait()
+    first = lax.axis_index("dp") * half
+    for i in range(n // CHUNK):
+        part_o[chunk(i), :] = picked_rows(slots[:, chunk(i)], first, own).astype(bf16)
 
 
 def summary_kernel(
-    sc, part, peer, slot, ccol, ctl, id_rows, weight, emb_o, key_o, val_o, enter_o, pay_o
+    length, part, peer, slot, ccol, ctl, id_rows, weight, emb_o, key_o, val_o, enter_o, pay_o
 ):
     n, width = part.shape
     half, heads = peer.shape[0], ccol.shape[1] // 2
@@ -126,7 +143,7 @@
     chunks = n // CHUNK
 
     def project(i):
-        other = picked_rows(slot[:, chunk(i)], (1 - sc[3]) * half, peer)
+        other = picked_rows(slot[:, chunk(i)], (1 - lax.axis_index("dp")) * half, peer)
         emb = (part[chunk(i), :].astype(f32) + other).astype(bf16)
         emb_o[chunk(i), :] = emb
         return dot(emb, weight[:, width : 2 * width]), dot(emb, weight[:, 2 * width :])
@@ -137,7 +154,7 @@
         key, val = ready
         if i + 1 < chunks:
             ready = project(i + 1)
-        alive = sc[1] + i * CHUNK + iota((CHUNK, 1), 0) < sc[2]
+        alive = iota((CHUNK, 1), 0) < length[0] - lax.axis_index("seq") * n - i * CHUNK
         val = jnp.where(alive, val, 0.0).astype(bf16)
         val_o[chunk(i), :] = val
         unit = lax.rsqrt(head_means(key, ones) + 1e-06) * 0.125
@@ -183,23 +200,26 @@
     )
 
 
-def join_kernel(bit, ids, pairs, sc, mine, got, *refs):
-    pay_o, prefix_o, logs_o, ids_o = refs[-4:]
-    upper = (sc[0] >> bit) & 1 == 1
+def join_kernel(bit, ids, pairs, mine, got, *refs):
+    before = refs[: 2 if bit else 0]
+    pay_o, prefix_o, logs_o, *ids_o = refs[len(before) :]
+    upper = (lax.axis_index("seq") >> bit) & 1 == 1
     state, logs, rows = unpack_state(mine[...], pairs)
     other, other_logs, other_rows = unpack_state(got[...], pairs)
     early = jnp.where(upper, other, state)
     late = jnp.where(upper, state, other)
     factor = row_factors(jnp.where(upper, logs, other_logs))
     id_rows = jnp.concatenate([rows[:ids], other_rows[:ids]], axis=0)
-    ids_o[...] = id_rows
-    sent = id_rows if pay_o.shape[0] >= state_rows(pairs, 2 * ids) else id_rows[:1]
-    pay_o[...] = pack_state(early * factor + late, logs + other_logs, sent)
+    if ids_o:
+        ids_o[0][...] = id_rows
+    pay_o[...] = pack_state(
+        early * factor + late, logs + other_logs, id_rows[:1] if ids_o else id_rows
+    )
     if bit == 0:
         prefix_o[...] = jnp.where(upper, other, 0.0)
         logs_o[...] = jnp.where(upper, other_logs, 0.0)
     else:
-        prefix, prefix_logs = refs[0][...], refs[1][...]
+        prefix, prefix_logs = before[0][...], before[1][...]
         prefix_o[...] = jnp.where(upper, prefix + row_factors(prefix_logs) * other, prefix)
         logs_o[...] = jnp.where(upper, prefix_logs + other_logs, prefix_logs)
 
@@ -246,7 +266,7 @@
             intra_o[chunk(i), pair_cut(p)] = held + part
 
 
-def candidate_kernel(order, owned, sc, id_rows, stored, own, peer, query_w, pair_w, query_o, val_w_o):
+def candidate_kernel(order, owned, id_rows, stored, own, peer, query_w, pair_w, query_o, val_w_o):
     half, width = own.shape
     ids = id_rows[...]
     ids = (ids * float(LANES) + pltpu.roll(ids, LANES // 2, 1)).astype(i32)
@@ -262,13 +282,14 @@
     slots = jnp.concatenate(tiles, axis=1)
     for c in range(0, slots.shape[1], CHUNK):
         some = slots[:, c : c + CHUNK]
-        rows = picked_rows(some, sc[3] * half, own) + picked_rows(some, (1 - sc[3]) * half, peer)
+        dp = lax.axis_index("dp")
+        rows = picked_rows(some, dp * half, own) + picked_rows(some, (1 - dp) * half, peer)
         query = dot(rows.astype(bf16), query_w[...])
         query_o[:, c : c + CHUNK] = jnp.transpose(query).astype(bf16)
     val_w_o[...] = jnp.transpose(pair_w[:, width:].astype(f32)).astype(bf16)
 
 
-def attend(sc, scale, query, first, cols, key, val, emit):
+def attend(alive_count, scale, query, first, cols, key, val, emit):
     n, width = key.shape
     blocks = range(0, n, KEYS)
 
@@ -280,7 +301,7 @@
     def scores(h, block, weights):
         rows = slice(block, block + KEYS)
         values = dot(key[rows, pair_cut(h // 2)], weights)
-        alive = sc[1] + block + iota((KEYS, 1), 0) < sc[2]
+        alive = iota((KEYS, 1), 0) < alive_count - block
         return jnp.where(alive, values, DEAD)
 
     def store(h, block, weights, buffer, peak):
@@ -319,13 +340,13 @@
 
 
 def finish_kernel(
-    bit, sc, scale, emb, query_a, query_b, intra_a, intra_b, enter, ctl, got, prefix, prefix_logs,
+    bit, length, scale, emb, query_a, query_b, intra_a, intra_b, enter, ctl, got, prefix, prefix_logs,
     out_w, pair_w, val_w, cand_q, hist_o, key_o, val_o, pay_o, *buffers,
 ):
     n, width = emb.shape
     pairs = width // LANES
     ones = same_head()
-    upper = (sc[0] >> bit) & 1 == 1
+    upper = (lax.axis_index("seq") >> bit) & 1 == 1
     state = unpack_state(got[...], pairs)[0]
     before, before_logs = prefix[...], prefix_logs[...]
     entering = jnp.where(upper, before + row_factors(before_logs) * state, before)
@@ -356,21 +377,21 @@
         if i + 1 < chunks:
             ready = normed(i + 1)
         hidden_sum = emb[chunk(i), :].astype(f32) + dot(current, out_w[...])
-        alive = sc[1] + i * CHUNK + iota((CHUNK, 1), 0) < sc[2]
+        alive = iota((CHUNK, 1), 0) < length[0] - lax.axis_index("seq") * n - i * CHUNK
         hist_o[chunk(i), :] = jnp.where(alive, hidden_sum, 0.0)
         hidden = hidden_sum.astype(bf16)
         key_o[chunk(i), :] = dot(hidden, pair_w[:, :width]).astype(bf16)
         val_o[:, chunk(i)] = contract(val_w[...], hidden, 1, 1).astype(bf16)
     count = pay_o.shape[1]
     heads = width // 64
-    any_alive = sc[1] < sc[2]
+    alive_count = length[0] - lax.axis_index("seq") * n
     log_rows = []
 
     def emit(h, attended, logs):
         pay_o[h * 64 : (h + 1) * 64, :] = attended.astype(bf16)
-        log_rows.append(jnp.where(any_alive, logs, DEAD))
-
-    attend(sc, scale, cand_q, count, count, key_o, val_o, emit)(buffers)
+        log_rows.append(jnp.where(alive_count > 0, logs, DEAD))
+
+    attend(alive_count, scale, cand_q, count, count, key_o, val_o, emit)(buffers)
     pay_o[width:, :] = pack_logs(jnp.concatenate(log_rows, axis=0))
 
 
@@ -390,14 +411,14 @@
     return rows[:heads] + rows[heads : 2 * heads] + rows[2 * heads : 3 * heads]
 
 
-def keep_kernel(sc, scale, cand_q, key, val, mean_o, logs_o, *buffers):
-    any_alive = sc[1] < sc[2]
+def keep_kernel(length, scale, cand_q, key, val, mean_o, logs_o, *buffers):
+    alive_count = length[0] - lax.axis_index("seq") * key.shape[0]
 
     def emit(h, attended, logs):
         mean_o[h * 64 : (h + 1) * 64, :] = attended
-        logs_o[h : h + 1, :] = jnp.where(any_alive, logs, DEAD)
-
-    attend(sc, scale, cand_q, 0, mean_o.shape[1], key, val, emit)(buffers)
+        logs_o[h : h + 1, :] = jnp.where(alive_count > 0, logs, DEAD)
+
+    attend(alive_count, scale, cand_q, 0, mean_o.shape[1], key, val, emit)(buffers)
 
 
 def over_heads(rows):
@@ -481,7 +502,7 @@
 ANY = pl.BlockSpec(memory_space=pl.ANY)
 
 
-def call(kernel, name, scalars, operands, outs, scratch=(), after=(), flops=0):
+def call(kernel, name, scalars, operands, outs, scratch=(), after=(), flops=0, space=VMEM):
     count = len(scalars) + len(operands)
 
     def body(*refs):
@@ -490,7 +511,7 @@
     return pl.pallas_call(
         body,
         name=name,
-        in_specs=[SMEM] * len(scalars) + [VMEM] * len(operands) + [ANY] * len(after),
+        in_specs=[SMEM] * len(scalars) + [space] * len(operands) + [ANY] * len(after),
         out_specs=[VMEM] * len(outs),
         out_shape=outs,
         scratch_shapes=list(scratch),
@@ -528,16 +549,12 @@
     pairs = heads // 2
     rows = pairs * 64
     cands = owned * seq
-    rank = lax.axis_index("seq")
 
     def swap(value, mask):
         return lax.ppermute(value, "seq", [(j, j ^ mask) for j in range(seq)])
 
     peer = lax.ppermute(item_embedding_table, "dp", [(0, 1), (1, 0)])
     far_ids = swap(candidate_item_index, seq // 2)
-    sc = jnp.stack(
-        [rank, rank * n, user_history_length[0], lax.axis_index("dp")]
-    ).astype(i32)
     stored = item_stored_row.reshape(-1, LANES)
     decay = log_head_retention.reshape(heads, n)
     ids = jnp.concatenate([candidate_item_index, far_ids], axis=0)
@@ -545,16 +562,21 @@
     id_rows = jnp.concatenate([ids // LANES, ids % LANES], axis=1).astype(f32)
 
     part, slot, crow, ccol, ctl = call(
-        own_rows_kernel, "own_rows", [sc],
+        own_rows_kernel, "own_rows", [],
         [history_item_index, stored, decay, item_embedding_table],
         [
             shape((n, width), bf16), shape((1, n), f32), shape((n // CHUNK, heads, CHUNK), f32),
             shape((n, 2 * heads), f32), shape((n // CHUNK * pairs, LANES), f32),
         ],
+        [
+            pltpu.VMEM((1, n), i32), pltpu.VMEM(stored.shape, i32), pltpu.VMEM((heads, n), f32),
+            pltpu.VMEM((half, width), bf16), pltpu.SemaphoreType.DMA((4,)),
+        ],
+        space=ANY,
         flops=2 * n * half * width,
     )
     emb, key, val, enter, pay = call(
-        summary_kernel, "summary", [sc],
+        summary_kernel, "summary", [user_history_length],
         [part, peer, slot, ccol, ctl, id_rows, history_query_key_value_weight],
         [
             shape((n, width), bf16), shape((n, width), bf16), shape((n, width), bf16),
@@ -578,14 +600,15 @@
         if bit == 1:
             early.append(local(width // 2, "local_b", [prefix]))
         count = 2 << bit
-        sent = 2 * count if bit < bits - 2 else 1
-        pay, prefix, logs, id_rows = call(
-            lambda *refs, bit=bit, count=count: join_kernel(bit, count, pairs, *refs), "join", [sc],
+        final = bit == bits - 2
+        sent = 1 if final else 2 * count
+        pay, prefix, logs, *id_rows = call(
+            lambda *refs, bit=bit, count=count: join_kernel(bit, count, pairs, *refs), "join", [],
             [pay, got] + ([prefix, logs] if bit else []),
             [
                 shape((state_rows(pairs, sent), LANES), bf16), shape((rows, LANES), f32),
-                shape((pairs, LANES), f32), shape((2 * count, LANES), f32),
-            ],
+                shape((pairs, LANES), f32),
+            ] + [shape((2 * count, LANES), f32)] * final,
             after=[early[-1][1]],
         )
     got = swap(pay, 1 << (bits - 1))
@@ -595,9 +618,9 @@
         places[(j & 1) * half_seq + (j >> 1)] = j
     order = [places[reversed_bits(j, bits)] for j in range(seq)]
     cand_q, val_w = call(
-        lambda *refs: candidate_kernel(order, owned, *refs), "candidates", [sc],
+        lambda *refs: candidate_kernel(order, owned, *refs), "candidates", [],
         [
-            id_rows, stored, item_embedding_table, peer, candidate_query_weight,
+            id_rows[0], stored, item_embedding_table, peer, candidate_query_weight,
             candidate_key_value_weight,
         ],
         [shape((width, cands), bf16), shape((width, width), bf16)],
@@ -608,7 +631,7 @@
     buffers = [pltpu.VMEM((n, send), f32)] * 2
     message = width + log_pad(heads)
     hist, key_two, val_two, pay = call(
-        lambda *refs: finish_kernel(bits - 1, *refs), "finish", [sc, head_score_scale],
+        lambda *refs: finish_kernel(bits - 1, *refs), "finish", [user_history_length, head_score_scale],
         [
             emb, query_a, query_b, intra_a, intra_b, enter, ctl, got, prefix, logs,
             history_output_weight, candidate_key_value_weight, val_w, cand_q,
@@ -621,7 +644,7 @@
         flops=2 * n * half * width,
     )
     mean, logs = call(
-        keep_kernel, "keep", [sc, head_score_scale], [cand_q, key_two, val_two],
+        keep_kernel, "keep", [user_history_length, head_score_scale], [cand_q, key_two, val_two],
         [shape((width, send), f32), shape((heads, send), f32)],
         buffers,
         flops=2 * n * half * width,

time: 59.1 us -> 56.1 us (0.949)
  Pallas kernels: 32.1 us -> 29 us
    pallas_call x11, Pallas kernels: 32.1 us -> 29 us  [call(): pl.pallas_call(body, name=name, in_specs=[SMEM] * len(scalars) + [space]...]
where the time goes in v3:
time: 56.1 us; the launch traced here: 55.8 us
  Pallas kernels  29 us (52%)
  starting transfers between devices  13.8 us (25%)
  waiting for transfers between devices  7.65 us (14%)
  local copies, waits for them, and re-layouts  3.79 us (7%)
  between operations  1.41 us (3%)
    pallas_call x11, Pallas kernels, call(): pl.pallas_call(body, name=name, in_specs=[SMEM] * len(scalars) + [space]...  29 us
    ppermute x8, starting transfers between devices, swap(): return lax.ppermute(value, 'seq', [(j, j ^ mask) for j in range(seq)])  13.3 us
    ppermute x8, waiting for transfers between devices, swap(): return lax.ppermute(value, 'seq', [(j, j ^ mask) for j in range(seq)])  7.64 us
    unnamed x26, local copies, waits for them, and re-layouts  3.79 us
  transfers between devices with their start and end apart: 9, of which 6 were waited for; matrix products, arithmetic and copies ran while one was open for 0% of the time, Pallas kernels for 28%

profile of v3, /device:TPU:0, one launch (start us, length us, event | category | flops | bytes accessed | tf_op | source)
XLA Modules:
  0.0 55.8 jit_solution(14027095598127320089)
XLA Ops:
  0.6 0.5 collective-permute-start
  1.1 3.7 %collective-permute-start.1 = (s32[1,64]{1,0:T(1,128)}, s32[1,64]{1,0:T(1,128)S(1)}, u32[]{:S(2)}, u32[]{:S(2)}) collective-permute-start(s32[1,64]{1,0:T(1,128)} %param.15), channel_id=1, source_target_pairs={{0,8},{2,10},{4,12},{6,14},{8,0},{10,2},{12,4},{14,6},{1,9},{3,11}... | collective-permute-start | bytes 776 | tf_op jit(solution)/shard_map/ppermute | solution.py:554
  4.8 0.0 copy-start.2
  4.8 1.6 %copy-done.2 = bf16[2048,512]{1,0:T(8,128)(2,1)S(1)} copy-done((bf16[2048,512]{1,0:T(8,128)(2,1)S(1)}, bf16[2048,512]{1,0:T(8,128)(2,1)}, u32[]{:S(2)}) %copy-start.2) | copy-done | bytes 2097176
  6.4 0.0 copy-start.7
  6.4 0.8 %copy-done.7 = f32[1,8,1024]{2,1,0:T(8,128)S(1)} copy-done((f32[1,8,1024]{2,1,0:T(8,128)S(1)}, f32[1,8,1024]{2,1,0:T(8,128)}, u32[]{:S(2)}) %copy-start.7) | copy-done | bytes 32792
  7.2 0.0 copy-start.8
  7.2 0.7 %copy-done.8 = s32[4096]{0:T(1024)S(1)} copy-done((s32[4096]{0:T(1024)S(1)}, s32[4096]{0:T(1024)}, u32[]{:S(2)}) %copy-start.8) | copy-done | bytes 16408
  7.9 0.7 %copy-done.10 = s32[1,1024]{1,0:T(1,128)S(1)} copy-done((s32[1,1024]{1,0:T(1,128)S(1)}, s32[1,1024]{1,0:T(1,128)}, u32[]{:S(2)}) %copy-start.10) | copy-done | bytes 4120
  8.6 3.4 %own_rows.1 = (bf16[1024,512]{1,0:T(8,128)(2,1)S(1)}, f32[1,1024]{1,0:T(1,128)S(1)}, f32[4,8,256]{2,1,0:T(8,128)S(1)}, f32[1024,16]{1,0:T(8,128)S(1)}, f32[16,128]{1,0:T(8,128)S(1)}) custom-call(s32[1,1024]{1,0:T(1,128)S(1)} %copy-done.10, s32[32,128]{1,0:T(8,128)S(1)} %bitcast.5, f32[8,1024]{1,0:T(8,128)S(1)} %bitcast.4, bf16[2048,512]{1,0:T(8,128)(2,1)S(1)} %copy-done.2), custom_call_target="tpu_custom_call" | custom-call | flops 2147483648 | tf_op jit(solution)/shard_map/own_rows/pallas_call | solution.py:511
  12.7 0.0 collective-permute-done.1
  12.7 0.0 copy-done.12
  12.7 0.1 add_convert_fusion.refs_6_
  12.8 0.0 collective-permute-done.refs_2_.refs_3_
  12.8 0.0 copy-done
  12.8 5.4 %summary.1 = (bf16[1024,512]{1,0:T(8,128)(2,1)S(1)}, bf16[1024,512]{1,0:T(8,128)(2,1)S(1)}, bf16[1024,512]{1,0:T(8,128)(2,1)S(1)}, f32[4,256,128]{2,1,0:T(8,128)S(1)}, bf16[272,128]{1,0:T(8,128)(2,1)S(1)}) custom-call(s32[1]{0:T(128)S(6)} %copy.14.refs_0_, bf16[1024,512]{1,0:T(8,128)(2,1)S(1)} %get-tuple-element.36.refs_1_, ...), custom_call_target="tpu_custom_call" | custom-call | flops 2147483648 | tf_op jit(solution)/shard_map/summary/pallas_call | solution.py:511
  18.2 1.6 %collective-permute-start.2 = (bf16[272,128]{1,0:T(8,128)(2,1)S(1)}, bf16[272,128]{1,0:T(8,128)(2,1)S(1)}, u32[]{:S(2)}, u32[]{:S(2)}) collective-permute-start(bf16[272,128]{1,0:T(8,128)(2,1)S(1)} %get-tuple-element.45.refs_0_), channel_id=1, source_target_pairs={{0,2},{2,0},{4,6},{6,4},{8,10},{10,8},{12,14},{14,12},{1,3},{3,1},... | collective-permute-start | bytes 208904 | tf_op jit(solution)/shard_map/ppermute | solution.py:554
  19.8 2.7 %local_a.1 = (bf16[1024,256]{1,0:T(8,128)(2,1)S(1)}, f32[1024,256]{1,0:T(8,128)S(1)}) custom-call(bf16[1024,512]{1,0:T(8,128)(2,1)S(1)} %get-tuple-element.40.refs_0_.refs_2_, bf16[1024,512]{1,0:T(8,128)(2,1)S(1)} %get-tuple-element.41.refs_1_, bf16[1024,512]{1,0:T(8,128)(2,1)S(1)} %get-tuple-element.42.refs_2_, f32[4,8,256]{2,1,0:T(8,128)S(1)} %get-tuple-element.43.refs_3_, ...), custom_call_target="tpu_custom_call" | custom-call | flops 1073741824 | tf_op jit(solution)/shard_map/local_a/pallas_call | solution.py:511
  22.4 0.1 collective-permute-done.2.refs_1_
  22.6 0.1 join.2
  22.6 1.6 %collective-permute-start.3 = (bf16[272,128]{1,0:T(8,128)(2,1)S(1)}, bf16[272,128]{1,0:T(8,128)(2,1)S(1)}, u32[]{:S(2)}, u32[]{:S(2)}) collective-permute-start(bf16[272,128]{1,0:T(8,128)(2,1)S(1)} %get-tuple-element.51.refs_0_), channel_id=1, source_target_pairs={{0,4},{2,6},{4,0},{6,2},{8,12},{10,14},{12,8},{14,10},{1,5},{3,7},... | collective-permute-start | bytes 208904 | tf_op jit(solution)/shard_map/ppermute | solution.py:554
  24.3 2.9 %local_b.1 = (bf16[1024,256]{1,0:T(8,128)(2,1)S(1)}, f32[1024,256]{1,0:T(8,128)S(1)}) custom-call(bf16[1024,512]{1,0:T(8,128)(2,1)S(1)} %get-tuple-element.40.refs_0_.refs_2_, bf16[1024,512]{1,0:T(8,128)(2,1)S(1)} %get-tuple-element.41.refs_1_, bf16[1024,512]{1,0:T(8,128)(2,1)S(1)} %get-tuple-element.42.refs_2_, f32[4,8,256]{2,1,0:T(8,128)S(1)} %get-tuple-element.43.refs_3_, ...), custom_call_target="tpu_custom_call" | custom-call | flops 1073741824 | tf_op jit(solution)/shard_map/local_b/pallas_call | solution.py:511
  27.2 0.0 collective-permute-done.3.refs_1_
  27.2 0.1 join.3
  27.2 0.4 collective-permute-start.4
  27.7 0.0 copy-done.3
  27.7 0.0 copy-done.4
  27.7 0.0 copy-done.5
  27.7 0.0 copy-done.9
  27.7 0.0 copy-start.6
  27.7 0.0 copy-start.11
  27.7 3.3 %candidates.1 = (bf16[512,512]{1,0:T(8,128)(2,1)S(1)}, bf16[512,512]{1,0:T(8,128)(2,1)S(1)}) custom-call(f32[8,128]{1,0:T(8,128)S(1)} %get-tuple-element.56.refs_0_, s32[32,128]{1,0:T(8,128)S(1)} %bitcast.6, bf16[2048,512]{1,0:T(8,128)(2,1)S(1)} %copy-done.3, bf16[2048,512]{1,0:T(8,128)(2,1)S(1)} %collective-permute-done.refs_2_.refs_3_, ...), custom_call_target="tpu_custom_call" | custom-call | flops 2147483648 | tf_op jit(solution)/shard_map/candidates/pallas_call | solution.py:511
  31.0 1.5 %collective-permute-done.4.refs_9_ = bf16[272,128]{1,0:T(8,128)(2,1)S(1)} collective-permute-done((bf16[272,128]{1,0:T(8,128)(2,1)S(1)}, bf16[272,128]{1,0:T(8,128)(2,1)S(1)}, u32[]{:S(2)}, u32[]{:S(2)}) %collective-permute-start.4) | collective-permute-done | bytes 69664 | tf_op jit(solution)/shard_map/ppermute | solution.py:554
  32.5 0.0 copy-done.6
  32.5 0.0 copy-done.11
  32.5 6.4 %finish.1 = (f32[1024,512]{1,0:T(8,128)}, bf16[1024,512]{1,0:T(8,128)(2,1)S(1)}, bf16[512,1024]{1,0:T(8,128)(2,1)S(1)}, bf16[544,256]{1,0:T(8,128)(2,1)S(1)}) custom-call(s32[1]{0:T(128)S(6)} %copy.14.refs_0_, f32[8]{0:T(128)S(1)} %copy-done.11, bf16[1024,512]{1,0:T(8,128)(2,1)S(1)} %get-tuple-element.40.refs_0_.refs_2_, ...), custom_call_target="tpu_custom_call" | custom-call | flops 2147483648 | tf_op jit(solution)/shard_map/finish/pallas_call | solution.py:511
  38.9 1.6 %collective-permute-start.5 = (bf16[544,256]{1,0:T(8,128)(2,1)S(1)}, bf16[544,256]{1,0:T(8,128)(2,1)S(1)}, u32[]{:S(2)}, u32[]{:S(2)}) collective-permute-start(bf16[544,256]{1,0:T(8,128)(2,1)S(1)} %get-tuple-element.64), channel_id=1, source_target_pairs={{0,2},{2,0},{4,6},{6,4},{8,10},{10,8},{12,14},{14,12},{1,3},{3,1},... | collective-permute-start | bytes 835592 | tf_op jit(solution)/shard_map/ppermute | solution.py:554
  40.5 3.6 %keep.1 = (f32[512,256]{1,0:T(8,128)S(1)}, f32[8,256]{1,0:T(8,128)S(1)}) custom-call(s32[1]{0:T(128)S(6)} %copy.14.refs_0_, f32[8]{0:T(128)S(1)} %copy-done.11, bf16[512,512]{1,0:T(8,128)(2,1)S(1)} %get-tuple-element.58.refs_15_.refs_2_, bf16[1024,512]{1,0:T(8,128)(2,1)S(1)} %get-tuple-element.60.refs_3_, bf16[512,1024]{1,0:T(8,128)(2,1)S(1)} %get-tuple-element.61.refs_4_), custom_call_target="tpu_custom_call" | custom-call | flops 2147483648 | tf_op jit(solution)/shard_map/keep/pallas_call | solution.py:511
  44.1 2.5 %collective-permute-done.5.refs_2_ = bf16[544,256]{1,0:T(8,128)(2,1)S(1)} collective-permute-done((bf16[544,256]{1,0:T(8,128)(2,1)S(1)}, bf16[544,256]{1,0:T(8,128)(2,1)S(1)}, u32[]{:S(2)}, u32[]{:S(2)}) %collective-permute-start.5) | collective-permute-done | bytes 278560 | tf_op jit(solution)/shard_map/ppermute | solution.py:554
  46.6 0.2 deal.1
  46.8 1.3 %collective-permute-start.6 = (bf16[272,128]{1,0:T(8,128)(2,1)S(1)}, bf16[272,128]{1,0:T(8,128)(2,1)S(1)}, u32[]{:S(2)}, u32[]{:S(2)}) collective-permute-start(bf16[272,128]{1,0:T(8,128)(2,1)S(1)} %get-tuple-element.67), channel_id=1, source_target_pairs={{0,8},{2,10},{4,12},{6,14},{8,0},{10,2},{12,4},{14,6},{1,9},{3,11}... | collective-permute-start | bytes 208904 | tf_op jit(solution)/shard_map/ppermute | solution.py:554
  48.1 0.5 collective-permute-start.7
  48.6 2.6 %collective-permute-start.8 = (bf16[272,128]{1,0:T(8,128)(2,1)S(1)}, bf16[272,128]{1,0:T(8,128)(2,1)S(1)}, u32[]{:S(2)}, u32[]{:S(2)}) collective-permute-start(bf16[272,128]{1,0:T(8,128)(2,1)S(1)} %get-tuple-element.69), channel_id=1, source_target_pairs={{0,12},{2,14},{4,8},{6,10},{8,4},{10,6},{12,0},{14,2},{1,13},{3,15... | collective-permute-start | bytes 208904 | tf_op jit(solution)/shard_map/ppermute | solution.py:554
  51.2 1.7 %collective-permute-done.6.refs_2_ = bf16[272,128]{1,0:T(8,128)(2,1)S(1)} collective-permute-done((bf16[272,128]{1,0:T(8,128)(2,1)S(1)}, bf16[272,128]{1,0:T(8,128)(2,1)S(1)}, u32[]{:S(2)}, u32[]{:S(2)}) %collective-permute-start.6) | collective-permute-done | bytes 69664 | tf_op jit(solution)/shard_map/ppermute | solution.py:554
  52.9 0.2 collective-permute-done.7.refs_3_
  53.1 1.6 %collective-permute-done.8.refs_4_ = bf16[272,128]{1,0:T(8,128)(2,1)S(1)} collective-permute-done((bf16[272,128]{1,0:T(8,128)(2,1)S(1)}, bf16[272,128]{1,0:T(8,128)(2,1)S(1)}, u32[]{:S(2)}, u32[]{:S(2)}) %collective-permute-start.8) | collective-permute-done | bytes 69664 | tf_op jit(solution)/shard_map/ppermute | solution.py:554
  54.7 0.0 copy-done.1
  54.7 1.1 %last.1 = f32[64,512]{1,0:T(8,128)} custom-call(f32[512,128]{1,0:T(8,128)S(1)} %get-tuple-element.65.refs_0_, f32[8,128]{1,0:T(8,128)S(1)} %get-tuple-element.66.refs_1_, bf16[272,128]{1,0:T(8,128)(2,1)S(1)} %collective-permute-done.6.refs_2_, bf16[272,128]{1,0:T(8,128)(2,1)S(1)} %collective-permute-done.7.refs_3_, ...), custom_call_target="tpu_custom_call" | custom-call | tf_op jit(solution)/shard_map/last/pallas_call | solution.py:511
  (9 shorter events, 0.0 us)
Async XLA Ops:
  0.6 12.2 %collective-permute-start = (bf16[2048,512]{1,0:T(8,128)(2,1)}, bf16[2048,512]{1,0:T(8,128)(2,1)S(1)}, u32[]{:S(2)}, u32[]{:S(2)}) collective-permute-start(bf16[2048,512]{1,0:T(8,128)(2,1)} %refs_2_.1), channel_id=1, source_target_pairs={{0,1},{1,0},{2,3},{3,2},{4,5},{5,4},{6,7},{7,6},{8,9},{9,8},{10,11... | collective-permute-start | bytes 6291464 | tf_op jit(solution)/shard_map/ppermute | solution.py:556
  1.1 11.5 %collective-permute-start.1 = (s32[1,64]{1,0:T(1,128)}, s32[1,64]{1,0:T(1,128)S(1)}, u32[]{:S(2)}, u32[]{:S(2)}) collective-permute-start(s32[1,64]{1,0:T(1,128)} %param.15), channel_id=1, source_target_pairs={{0,8},{2,10},{4,12},{6,14},{8,0},{10,2},{12,4},{14,6},{1,9},{3,11}... | collective-permute-start | bytes 776 | tf_op jit(solution)/shard_map/ppermute | solution.py:554
  4.8 1.6 %copy-start.2 = (bf16[2048,512]{1,0:T(8,128)(2,1)S(1)}, bf16[2048,512]{1,0:T(8,128)(2,1)}, u32[]{:S(2)}) copy-start(bf16[2048,512]{1,0:T(8,128)(2,1)} %refs_2_.1) | copy-start | bytes 6291460
  6.4 0.8 %copy-start.7 = (f32[1,8,1024]{2,1,0:T(8,128)S(1)}, f32[1,8,1024]{2,1,0:T(8,128)}, u32[]{:S(2)}) copy-start(f32[1,8,1024]{2,1,0:T(8,128)} %param.13) | copy-start | bytes 98308
  7.2 0.7 %copy-start.8 = (s32[4096]{0:T(1024)S(1)}, s32[4096]{0:T(1024)}, u32[]{:S(2)}) copy-start(s32[4096]{0:T(1024)} %param.16) | copy-start | bytes 49156
  7.9 0.7 %copy-start.10 = (s32[1,1024]{1,0:T(1,128)S(1)}, s32[1,1024]{1,0:T(1,128)}, u32[]{:S(2)}) copy-start(s32[1,1024]{1,0:T(1,128)} %refs_0_.4) | copy-start | bytes 12292
  8.6 4.1 %copy-start.12 = (s32[1,64]{1,0:T(1,128)S(1)}, s32[1,64]{1,0:T(1,128)}, u32[]{:S(2)}) copy-start(s32[1,64]{1,0:T(1,128)} %param.15) | copy-start | bytes 772
  8.6 4.2 %copy-start = (bf16[512,1536]{1,0:T(8,128)(2,1)S(1)}, bf16[512,1536]{1,0:T(8,128)(2,1)}, u32[]{:S(2)}) copy-start(bf16[512,1536]{1,0:T(8,128)(2,1)} %refs_5_.5) | copy-start | bytes 4718596
  18.2 4.4 %collective-permute-start.2 = (bf16[272,128]{1,0:T(8,128)(2,1)S(1)}, bf16[272,128]{1,0:T(8,128)(2,1)S(1)}, u32[]{:S(2)}, u32[]{:S(2)}) collective-permute-start(bf16[272,128]{1,0:T(8,128)(2,1)S(1)} %get-tuple-element.45.refs_0_), channel_id=1, source_target_pairs={{0,2},{2,0},{4,6},{6,4},{8,10},{10,8},{12,14},{14,12},{1,3},{3,1},... | collective-permute-start | bytes 208904 | tf_op jit(solution)/shard_map/ppermute | solution.py:554
  22.6 4.5 %collective-permute-start.3 = (bf16[272,128]{1,0:T(8,128)(2,1)S(1)}, bf16[272,128]{1,0:T(8,128)(2,1)S(1)}, u32[]{:S(2)}, u32[]{:S(2)}) collective-permute-start(bf16[272,128]{1,0:T(8,128)(2,1)S(1)} %get-tuple-element.51.refs_0_), channel_id=1, source_target_pairs={{0,4},{2,6},{4,0},{6,2},{8,12},{10,14},{12,8},{14,10},{1,5},{3,7},... | collective-permute-start | bytes 208904 | tf_op jit(solution)/shard_map/ppermute | solution.py:554
  24.3 3.4 %copy-start.3 = (bf16[2048,512]{1,0:T(8,128)(2,1)S(1)}, bf16[2048,512]{1,0:T(8,128)(2,1)}, u32[]{:S(2)}) copy-start(bf16[2048,512]{1,0:T(8,128)(2,1)} %refs_2_.1) | copy-start | bytes 6291460
  24.3 3.4 %copy-start.4 = (bf16[512,1024]{1,0:T(8,128)(2,1)S(1)}, bf16[512,1024]{1,0:T(8,128)(2,1)}, u32[]{:S(2)}) copy-start(bf16[512,1024]{1,0:T(8,128)(2,1)} %refs_13_.1) | copy-start | bytes 3145732
  24.3 3.4 %copy-start.5 = (bf16[512,512]{1,0:T(8,128)(2,1)S(1)}, bf16[512,512]{1,0:T(8,128)(2,1)}, u32[]{:S(2)}) copy-start(bf16[512,512]{1,0:T(8,128)(2,1)} %refs_4_.1) | copy-start | bytes 1572868
  24.3 3.4 %copy-start.9 = (s32[4096]{0:T(1024)S(1)}, s32[4096]{0:T(1024)}, u32[]{:S(2)}) copy-start(s32[4096]{0:T(1024)} %param.16) | copy-start | bytes 49156
  27.2 5.3 %collective-permute-start.4 = (bf16[272,128]{1,0:T(8,128)(2,1)S(1)}, bf16[272,128]{1,0:T(8,128)(2,1)S(1)}, u32[]{:S(2)}, u32[]{:S(2)}) collective-permute-start(bf16[272,128]{1,0:T(8,128)(2,1)S(1)} %get-tuple-element.53), channel_id=1, source_target_pairs={{0,8},{2,10},{4,12},{6,14},{8,0},{10,2},{12,4},{14,6},{1,9},{3,11}... | collective-permute-start | bytes 208904 | tf_op jit(solution)/shard_map/ppermute | solution.py:554
  27.7 4.9 %copy-start.6 = (bf16[512,512]{1,0:T(8,128)(2,1)S(1)}, bf16[512,512]{1,0:T(8,128)(2,1)}, u32[]{:S(2)}) copy-start(bf16[512,512]{1,0:T(8,128)(2,1)} %refs_12_.1) | copy-start | bytes 1572868
  27.7 4.8 %copy-start.11 = (f32[8]{0:T(128)S(1)}, f32[8]{0:T(128)}, u32[]{:S(2)}) copy-start(f32[8]{0:T(128)} %refs_1_.3) | copy-start | bytes 100
  38.9 7.7 %collective-permute-start.5 = (bf16[544,256]{1,0:T(8,128)(2,1)S(1)}, bf16[544,256]{1,0:T(8,128)(2,1)S(1)}, u32[]{:S(2)}, u32[]{:S(2)}) collective-permute-start(bf16[544,256]{1,0:T(8,128)(2,1)S(1)} %get-tuple-element.64), channel_id=1, source_target_pairs={{0,2},{2,0},{4,6},{6,4},{8,10},{10,8},{12,14},{14,12},{1,3},{3,1},... | collective-permute-start | bytes 835592 | tf_op jit(solution)/shard_map/ppermute | solution.py:554
  40.5 14.2 %copy-start.1 = (bf16[512,512]{1,0:T(8,128)(2,1)S(1)}, bf16[512,512]{1,0:T(8,128)(2,1)}, u32[]{:S(2)}) copy-start(bf16[512,512]{1,0:T(8,128)(2,1)} %refs_5_.7) | copy-start | bytes 1572868
  46.8 6.1 %collective-permute-start.6 = (bf16[272,128]{1,0:T(8,128)(2,1)S(1)}, bf16[272,128]{1,0:T(8,128)(2,1)S(1)}, u32[]{:S(2)}, u32[]{:S(2)}) collective-permute-start(bf16[272,128]{1,0:T(8,128)(2,1)S(1)} %get-tuple-element.67), channel_id=1, source_target_pairs={{0,8},{2,10},{4,12},{6,14},{8,0},{10,2},{12,4},{14,6},{1,9},{3,11}... | collective-permute-start | bytes 208904 | tf_op jit(solution)/shard_map/ppermute | solution.py:554
  48.1 5.1 %collective-permute-start.7 = (bf16[272,128]{1,0:T(8,128)(2,1)S(1)}, bf16[272,128]{1,0:T(8,128)(2,1)S(1)}, u32[]{:S(2)}, u32[]{:S(2)}) collective-permute-start(bf16[272,128]{1,0:T(8,128)(2,1)S(1)} %get-tuple-element.68), channel_id=1, source_target_pairs={{0,4},{2,6},{4,0},{6,2},{8,12},{10,14},{12,8},{14,10},{1,5},{3,7},... | collective-permute-start | bytes 208904 | tf_op jit(solution)/shard_map/ppermute | solution.py:554
  48.6 6.1 %collective-permute-start.8 = (bf16[272,128]{1,0:T(8,128)(2,1)S(1)}, bf16[272,128]{1,0:T(8,128)(2,1)S(1)}, u32[]{:S(2)}, u32[]{:S(2)}) collective-permute-start(bf16[272,128]{1,0:T(8,128)(2,1)S(1)} %get-tuple-element.69), channel_id=1, source_target_pairs={{0,12},{2,14},{4,8},{6,10},{8,4},{10,6},{12,0},{14,2},{1,13},{3,15... | collective-permute-start | bytes 208904 | tf_op jit(solution)/shard_map/ppermute | solution.py:554

commit v4 on v3

--- a/solution.py
+++ b/solution.py
@@ -500,10 +500,14 @@
 VMEM = pl.BlockSpec(memory_space=pltpu.VMEM)
 SMEM = pl.BlockSpec(memory_space=pltpu.SMEM)
 ANY = pl.BlockSpec(memory_space=pl.ANY)
+HBM = pl.BlockSpec(memory_space=pltpu.HBM)
 
 
 def call(kernel, name, scalars, operands, outs, scratch=(), after=(), flops=0, space=VMEM):
     count = len(scalars) + len(operands)
+
+    if space is HBM:
+        operands = [pltpu.with_memory_space_constraint(value, pltpu.HBM) for value in operands]
 
     def body(*refs):
         kernel(*refs[:count], *refs[count + len(after) :])
@@ -572,7 +576,7 @@
             pltpu.VMEM((1, n), i32), pltpu.VMEM(stored.shape, i32), pltpu.VMEM((heads, n), f32),
             pltpu.VMEM((half, width), bf16), pltpu.SemaphoreType.DMA((4,)),
         ],
-        space=ANY,
+        space=HBM,
         flops=2 * n * half * width,
     )
     emb, key, val, enter, pay = call(

time: 56.1 us -> 52.9 us (0.943)
  local copies, waits for them, and re-layouts: 3.79 us -> 0.04 us
  Pallas kernels: 29 us -> 29.7 us
    unnamed x26 -> x18, local copies, waits for them, and re-layouts: 3.79 us -> 0.04 us
    pallas_call x11, Pallas kernels: 29 us -> 29.7 us  [call(): pl.pallas_call(body, name=name, in_specs=[SMEM] * len(scalars) + [space]...]
  transfers between devices with their start and end apart: 9 -> 9, of which waited for: 6 -> 6; matrix products, arithmetic and copies ran while one was open for 0% -> 0% of each run, Pallas kernels for 28% -> 31%
where the time goes in v4:
time: 52.9 us; the launch traced here: 52.7 us
  Pallas kernels  29.7 us (56%)
  starting transfers between devices  13.8 us (26%)
  waiting for transfers between devices  7.69 us (15%)
  between operations  1.41 us (3%)
    pallas_call x11, Pallas kernels, call(): pl.pallas_call(body, name=name, in_specs=[SMEM] * len(scalars) + [space]...  29.7 us
    ppermute x8, starting transfers between devices, swap(): return lax.ppermute(value, 'seq', [(j, j ^ mask) for j in range(seq)])  13.3 us
    ppermute x8, waiting for transfers between devices, swap(): return lax.ppermute(value, 'seq', [(j, j ^ mask) for j in range(seq)])  7.69 us
  transfers between devices with their start and end apart: 9, of which 6 were waited for; matrix products, arithmetic and copies ran while one was open for 0% of the time, Pallas kernels for 31%

profile of v4, /device:TPU:0, one launch (start us, length us, event | category | flops | bytes accessed | tf_op | source)
XLA Modules:
  0.0 52.7 jit_solution(17194705739042068002)
XLA Ops:
  0.6 0.5 collective-permute-start
  1.1 3.7 %collective-permute-start.1 = (s32[1,64]{1,0:T(1,128)}, s32[1,64]{1,0:T(1,128)S(1)}, u32[]{:S(2)}, u32[]{:S(2)}) collective-permute-start(s32[1,64]{1,0:T(1,128)} %param.15), channel_id=1, source_target_pairs={{0,8},{2,10},{4,12},{6,14},{8,0},{10,2},{12,4},{14,6},{1,9},{3,11}... | collective-permute-start | bytes 776 | tf_op jit(solution)/shard_map/ppermute | solution.py:558
  4.8 0.0 copy-start.8
  4.8 0.0 copy-start
  4.8 4.2 %own_rows.1 = (bf16[1024,512]{1,0:T(8,128)(2,1)S(1)}, f32[1,1024]{1,0:T(1,128)S(1)}, f32[4,8,256]{2,1,0:T(8,128)S(1)}, f32[1024,16]{1,0:T(8,128)S(1)}, f32[16,128]{1,0:T(8,128)S(1)}) custom-call(s32[1,1024]{1,0:T(1,128)} %refs_0_.4, s32[32,128]{1,0:T(8,128)} %bitcast.4, f32[8,1024]{1,0:T(8,128)} %bitcast.7, bf16[2048,512]{1,0:T(8,128)(2,1)} %refs_2_.1), custom_call_target="tpu_custom_call" | custom-call | flops 2147483648 | tf_op jit(solution)/shard_map/own_rows/pallas_call | solution.py:515
  9.6 0.0 collective-permute-done.1
  9.6 0.0 copy-done.8
  9.7 0.1 add_convert_fusion.refs_6_
  9.8 0.0 collective-permute-done.refs_2_.refs_3_
  9.8 0.0 copy-done
  9.8 5.4 %summary.1 = (bf16[1024,512]{1,0:T(8,128)(2,1)S(1)}, bf16[1024,512]{1,0:T(8,128)(2,1)S(1)}, bf16[1024,512]{1,0:T(8,128)(2,1)S(1)}, f32[4,256,128]{2,1,0:T(8,128)S(1)}, bf16[272,128]{1,0:T(8,128)(2,1)S(1)}) custom-call(s32[1]{0:T(128)S(6)} %copy.14.refs_0_, bf16[1024,512]{1,0:T(8,128)(2,1)S(1)} %get-tuple-element.36.refs_1_, ...), custom_call_target="tpu_custom_call" | custom-call | flops 2147483648 | tf_op jit(solution)/shard_map/summary/pallas_call | solution.py:515
  15.2 1.6 %collective-permute-start.2 = (bf16[272,128]{1,0:T(8,128)(2,1)S(1)}, bf16[272,128]{1,0:T(8,128)(2,1)S(1)}, u32[]{:S(2)}, u32[]{:S(2)}) collective-permute-start(bf16[272,128]{1,0:T(8,128)(2,1)S(1)} %get-tuple-element.45.refs_0_), channel_id=1, source_target_pairs={{0,2},{2,0},{4,6},{6,4},{8,10},{10,8},{12,14},{14,12},{1,3},{3,1},... | collective-permute-start | bytes 208904 | tf_op jit(solution)/shard_map/ppermute | solution.py:558
  16.8 2.7 %local_a.1 = (bf16[1024,256]{1,0:T(8,128)(2,1)S(1)}, f32[1024,256]{1,0:T(8,128)S(1)}) custom-call(bf16[1024,512]{1,0:T(8,128)(2,1)S(1)} %get-tuple-element.40.refs_0_.refs_2_, bf16[1024,512]{1,0:T(8,128)(2,1)S(1)} %get-tuple-element.41.refs_1_, bf16[1024,512]{1,0:T(8,128)(2,1)S(1)} %get-tuple-element.42.refs_2_, f32[4,8,256]{2,1,0:T(8,128)S(1)} %get-tuple-element.43.refs_3_, ...), custom_call_target="tpu_custom_call" | custom-call | flops 1073741824 | tf_op jit(solution)/shard_map/local_a/pallas_call | solution.py:515
  19.4 0.1 collective-permute-done.2.refs_1_
  19.6 0.1 join.2
  19.6 1.7 %collective-permute-start.3 = (bf16[272,128]{1,0:T(8,128)(2,1)S(1)}, bf16[272,128]{1,0:T(8,128)(2,1)S(1)}, u32[]{:S(2)}, u32[]{:S(2)}) collective-permute-start(bf16[272,128]{1,0:T(8,128)(2,1)S(1)} %get-tuple-element.51.refs_0_), channel_id=1, source_target_pairs={{0,4},{2,6},{4,0},{6,2},{8,12},{10,14},{12,8},{14,10},{1,5},{3,7},... | collective-permute-start | bytes 208904 | tf_op jit(solution)/shard_map/ppermute | solution.py:558
  21.3 0.0 copy-start.2
  21.3 0.0 copy-start.3
  21.3 0.0 copy-start.4
  21.3 0.0 copy-start.6
  21.3 2.9 %local_b.1 = (bf16[1024,256]{1,0:T(8,128)(2,1)S(1)}, f32[1024,256]{1,0:T(8,128)S(1)}) custom-call(bf16[1024,512]{1,0:T(8,128)(2,1)S(1)} %get-tuple-element.40.refs_0_.refs_2_, bf16[1024,512]{1,0:T(8,128)(2,1)S(1)} %get-tuple-element.41.refs_1_, bf16[1024,512]{1,0:T(8,128)(2,1)S(1)} %get-tuple-element.42.refs_2_, f32[4,8,256]{2,1,0:T(8,128)S(1)} %get-tuple-element.43.refs_3_, ...), custom_call_target="tpu_custom_call" | custom-call | flops 1073741824 | tf_op jit(solution)/shard_map/local_b/pallas_call | solution.py:515
  24.1 0.0 collective-permute-done.3.refs_1_
  24.1 0.1 join.3
  24.2 0.4 collective-permute-start.4
  24.6 0.0 copy-done.2
  24.6 0.0 copy-done.3
  24.6 0.0 copy-done.4
  24.6 0.0 copy-done.6
  24.6 0.0 copy-start.5
  24.6 0.0 copy-start.7
  24.7 3.3 %candidates.1 = (bf16[512,512]{1,0:T(8,128)(2,1)S(1)}, bf16[512,512]{1,0:T(8,128)(2,1)S(1)}) custom-call(f32[8,128]{1,0:T(8,128)S(1)} %get-tuple-element.56.refs_0_, s32[32,128]{1,0:T(8,128)S(1)} %bitcast.5, bf16[2048,512]{1,0:T(8,128)(2,1)S(1)} %copy-done.2, bf16[2048,512]{1,0:T(8,128)(2,1)S(1)} %collective-permute-done.refs_2_.refs_3_, ...), custom_call_target="tpu_custom_call" | custom-call | flops 2147483648 | tf_op jit(solution)/shard_map/candidates/pallas_call | solution.py:515
  28.0 1.5 %collective-permute-done.4.refs_9_ = bf16[272,128]{1,0:T(8,128)(2,1)S(1)} collective-permute-done((bf16[272,128]{1,0:T(8,128)(2,1)S(1)}, bf16[272,128]{1,0:T(8,128)(2,1)S(1)}, u32[]{:S(2)}, u32[]{:S(2)}) %collective-permute-start.4) | collective-permute-done | bytes 69664 | tf_op jit(solution)/shard_map/ppermute | solution.py:558
  29.5 0.0 copy-done.5
  29.5 0.0 copy-done.7
  29.5 6.4 %finish.1 = (f32[1024,512]{1,0:T(8,128)}, bf16[1024,512]{1,0:T(8,128)(2,1)S(1)}, bf16[512,1024]{1,0:T(8,128)(2,1)S(1)}, bf16[544,256]{1,0:T(8,128)(2,1)S(1)}) custom-call(s32[1]{0:T(128)S(6)} %copy.14.refs_0_, f32[8]{0:T(128)S(1)} %copy-done.7, bf16[1024,512]{1,0:T(8,128)(2,1)S(1)} %get-tuple-element.40.refs_0_.refs_2_, ...), custom_call_target="tpu_custom_call" | custom-call | flops 2147483648 | tf_op jit(solution)/shard_map/finish/pallas_call | solution.py:515
  35.9 1.6 %collective-permute-start.5 = (bf16[544,256]{1,0:T(8,128)(2,1)S(1)}, bf16[544,256]{1,0:T(8,128)(2,1)S(1)}, u32[]{:S(2)}, u32[]{:S(2)}) collective-permute-start(bf16[544,256]{1,0:T(8,128)(2,1)S(1)} %get-tuple-element.64), channel_id=1, source_target_pairs={{0,2},{2,0},{4,6},{6,4},{8,10},{10,8},{12,14},{14,12},{1,3},{3,1},... | collective-permute-start | bytes 835592 | tf_op jit(solution)/shard_map/ppermute | solution.py:558
  37.4 0.0 copy-start.1
  37.4 3.6 %keep.1 = (f32[512,256]{1,0:T(8,128)S(1)}, f32[8,256]{1,0:T(8,128)S(1)}) custom-call(s32[1]{0:T(128)S(6)} %copy.14.refs_0_, f32[8]{0:T(128)S(1)} %copy-done.7, bf16[512,512]{1,0:T(8,128)(2,1)S(1)} %get-tuple-element.58.refs_15_.refs_2_, bf16[1024,512]{1,0:T(8,128)(2,1)S(1)} %get-tuple-element.60.refs_3_, bf16[512,1024]{1,0:T(8,128)(2,1)S(1)} %get-tuple-element.61.refs_4_), custom_call_target="tpu_custom_call" | custom-call | flops 2147483648 | tf_op jit(solution)/shard_map/keep/pallas_call | solution.py:515
  41.0 2.5 %collective-permute-done.5.refs_2_ = bf16[544,256]{1,0:T(8,128)(2,1)S(1)} collective-permute-done((bf16[544,256]{1,0:T(8,128)(2,1)S(1)}, bf16[544,256]{1,0:T(8,128)(2,1)S(1)}, u32[]{:S(2)}, u32[]{:S(2)}) %collective-permute-start.5) | collective-permute-done | bytes 278560 | tf_op jit(solution)/shard_map/ppermute | solution.py:558
  43.5 0.2 deal.1
  43.7 1.3 %collective-permute-start.6 = (bf16[272,128]{1,0:T(8,128)(2,1)S(1)}, bf16[272,128]{1,0:T(8,128)(2,1)S(1)}, u32[]{:S(2)}, u32[]{:S(2)}) collective-permute-start(bf16[272,128]{1,0:T(8,128)(2,1)S(1)} %get-tuple-element.67), channel_id=1, source_target_pairs={{0,8},{2,10},{4,12},{6,14},{8,0},{10,2},{12,4},{14,6},{1,9},{3,11}... | collective-permute-start | bytes 208904 | tf_op jit(solution)/shard_map/ppermute | solution.py:558
  45.0 0.6 %collective-permute-start.7 = (bf16[272,128]{1,0:T(8,128)(2,1)S(1)}, bf16[272,128]{1,0:T(8,128)(2,1)S(1)}, u32[]{:S(2)}, u32[]{:S(2)}) collective-permute-start(bf16[272,128]{1,0:T(8,128)(2,1)S(1)} %get-tuple-element.68), channel_id=1, source_target_pairs={{0,4},{2,6},{4,0},{6,2},{8,12},{10,14},{12,8},{14,10},{1,5},{3,7},... | collective-permute-start | bytes 208904 | tf_op jit(solution)/shard_map/ppermute | solution.py:558
  45.6 2.6 %collective-permute-start.8 = (bf16[272,128]{1,0:T(8,128)(2,1)S(1)}, bf16[272,128]{1,0:T(8,128)(2,1)S(1)}, u32[]{:S(2)}, u32[]{:S(2)}) collective-permute-start(bf16[272,128]{1,0:T(8,128)(2,1)S(1)} %get-tuple-element.69), channel_id=1, source_target_pairs={{0,12},{2,14},{4,8},{6,10},{8,4},{10,6},{12,0},{14,2},{1,13},{3,15... | collective-permute-start | bytes 208904 | tf_op jit(solution)/shard_map/ppermute | solution.py:558
  48.2 1.7 %collective-permute-done.6.refs_2_ = bf16[272,128]{1,0:T(8,128)(2,1)S(1)} collective-permute-done((bf16[272,128]{1,0:T(8,128)(2,1)S(1)}, bf16[272,128]{1,0:T(8,128)(2,1)S(1)}, u32[]{:S(2)}, u32[]{:S(2)}) %collective-permute-start.6) | collective-permute-done | bytes 69664 | tf_op jit(solution)/shard_map/ppermute | solution.py:558
  49.9 0.2 collective-permute-done.7.refs_3_
  50.1 1.6 %collective-permute-done.8.refs_4_ = bf16[272,128]{1,0:T(8,128)(2,1)S(1)} collective-permute-done((bf16[272,128]{1,0:T(8,128)(2,1)S(1)}, bf16[272,128]{1,0:T(8,128)(2,1)S(1)}, u32[]{:S(2)}, u32[]{:S(2)}) %collective-permute-start.8) | collective-permute-done | bytes 69664 | tf_op jit(solution)/shard_map/ppermute | solution.py:558
  51.7 0.0 copy-done.1
  51.7 1.1 %last.1 = f32[64,512]{1,0:T(8,128)} custom-call(f32[512,128]{1,0:T(8,128)S(1)} %get-tuple-element.65.refs_0_, f32[8,128]{1,0:T(8,128)S(1)} %get-tuple-element.66.refs_1_, bf16[272,128]{1,0:T(8,128)(2,1)S(1)} %collective-permute-done.6.refs_2_, bf16[272,128]{1,0:T(8,128)(2,1)S(1)} %collective-permute-done.7.refs_3_, ...), custom_call_target="tpu_custom_call" | custom-call | tf_op jit(solution)/shard_map/last/pallas_call | solution.py:515
  (1 shorter events, 0.0 us)
Async XLA Ops:
  0.6 9.1 %collective-permute-start = (bf16[2048,512]{1,0:T(8,128)(2,1)}, bf16[2048,512]{1,0:T(8,128)(2,1)S(1)}, u32[]{:S(2)}, u32[]{:S(2)}) collective-permute-start(bf16[2048,512]{1,0:T(8,128)(2,1)} %refs_2_.1), channel_id=1, source_target_pairs={{0,1},{1,0},{2,3},{3,2},{4,5},{5,4},{6,7},{7,6},{8,9},{9,8},{10,11... | collective-permute-start | bytes 6291464 | tf_op jit(solution)/shard_map/ppermute | solution.py:560
  1.1 8.5 %collective-permute-start.1 = (s32[1,64]{1,0:T(1,128)}, s32[1,64]{1,0:T(1,128)S(1)}, u32[]{:S(2)}, u32[]{:S(2)}) collective-permute-start(s32[1,64]{1,0:T(1,128)} %param.15), channel_id=1, source_target_pairs={{0,8},{2,10},{4,12},{6,14},{8,0},{10,2},{12,4},{14,6},{1,9},{3,11}... | collective-permute-start | bytes 776 | tf_op jit(solution)/shard_map/ppermute | solution.py:558
  4.8 4.8 %copy-start.8 = (s32[1,64]{1,0:T(1,128)S(1)}, s32[1,64]{1,0:T(1,128)}, u32[]{:S(2)}) copy-start(s32[1,64]{1,0:T(1,128)} %param.15) | copy-start | bytes 772
  4.8 4.9 %copy-start = (bf16[512,1536]{1,0:T(8,128)(2,1)S(1)}, bf16[512,1536]{1,0:T(8,128)(2,1)}, u32[]{:S(2)}) copy-start(bf16[512,1536]{1,0:T(8,128)(2,1)} %refs_5_.5) | copy-start | bytes 4718596
  15.2 4.4 %collective-permute-start.2 = (bf16[272,128]{1,0:T(8,128)(2,1)S(1)}, bf16[272,128]{1,0:T(8,128)(2,1)S(1)}, u32[]{:S(2)}, u32[]{:S(2)}) collective-permute-start(bf16[272,128]{1,0:T(8,128)(2,1)S(1)} %get-tuple-element.45.refs_0_), channel_id=1, source_target_pairs={{0,2},{2,0},{4,6},{6,4},{8,10},{10,8},{12,14},{14,12},{1,3},{3,1},... | collective-permute-start | bytes 208904 | tf_op jit(solution)/shard_map/ppermute | solution.py:558
  19.6 4.5 %collective-permute-start.3 = (bf16[272,128]{1,0:T(8,128)(2,1)S(1)}, bf16[272,128]{1,0:T(8,128)(2,1)S(1)}, u32[]{:S(2)}, u32[]{:S(2)}) collective-permute-start(bf16[272,128]{1,0:T(8,128)(2,1)S(1)} %get-tuple-element.51.refs_0_), channel_id=1, source_target_pairs={{0,4},{2,6},{4,0},{6,2},{8,12},{10,14},{12,8},{14,10},{1,5},{3,7},... | collective-permute-start | bytes 208904 | tf_op jit(solution)/shard_map/ppermute | solution.py:558
  21.3 3.4 %copy-start.2 = (bf16[2048,512]{1,0:T(8,128)(2,1)S(1)}, bf16[2048,512]{1,0:T(8,128)(2,1)}, u32[]{:S(2)}) copy-start(bf16[2048,512]{1,0:T(8,128)(2,1)} %refs_2_.1) | copy-start | bytes 6291460
  21.3 3.4 %copy-start.3 = (bf16[512,1024]{1,0:T(8,128)(2,1)S(1)}, bf16[512,1024]{1,0:T(8,128)(2,1)}, u32[]{:S(2)}) copy-start(bf16[512,1024]{1,0:T(8,128)(2,1)} %refs_13_.1) | copy-start | bytes 3145732
  21.3 3.4 %copy-start.4 = (bf16[512,512]{1,0:T(8,128)(2,1)S(1)}, bf16[512,512]{1,0:T(8,128)(2,1)}, u32[]{:S(2)}) copy-start(bf16[512,512]{1,0:T(8,128)(2,1)} %refs_4_.1) | copy-start | bytes 1572868
  21.3 3.4 %copy-start.6 = (s32[4096]{0:T(1024)S(1)}, s32[4096]{0:T(1024)}, u32[]{:S(2)}) copy-start(s32[4096]{0:T(1024)} %param.16) | copy-start | bytes 49156
  24.2 5.3 %collective-permute-start.4 = (bf16[272,128]{1,0:T(8,128)(2,1)S(1)}, bf16[272,128]{1,0:T(8,128)(2,1)S(1)}, u32[]{:S(2)}, u32[]{:S(2)}) collective-permute-start(bf16[272,128]{1,0:T(8,128)(2,1)S(1)} %get-tuple-element.53), channel_id=1, source_target_pairs={{0,8},{2,10},{4,12},{6,14},{8,0},{10,2},{12,4},{14,6},{1,9},{3,11}... | collective-permute-start | bytes 208904 | tf_op jit(solution)/shard_map/ppermute | solution.py:558
  24.6 4.9 %copy-start.5 = (bf16[512,512]{1,0:T(8,128)(2,1)S(1)}, bf16[512,512]{1,0:T(8,128)(2,1)}, u32[]{:S(2)}) copy-start(bf16[512,512]{1,0:T(8,128)(2,1)} %refs_12_.1) | copy-start | bytes 1572868
  24.6 4.9 %copy-start.7 = (f32[8]{0:T(128)S(1)}, f32[8]{0:T(128)}, u32[]{:S(2)}) copy-start(f32[8]{0:T(128)} %refs_1_.3) | copy-start | bytes 100
  35.9 7.7 %collective-permute-start.5 = (bf16[544,256]{1,0:T(8,128)(2,1)S(1)}, bf16[544,256]{1,0:T(8,128)(2,1)S(1)}, u32[]{:S(2)}, u32[]{:S(2)}) collective-permute-start(bf16[544,256]{1,0:T(8,128)(2,1)S(1)} %get-tuple-element.64), channel_id=1, source_target_pairs={{0,2},{2,0},{4,6},{6,4},{8,10},{10,8},{12,14},{14,12},{1,3},{3,1},... | collective-permute-start | bytes 835592 | tf_op jit(solution)/shard_map/ppermute | solution.py:558
  37.4 14.3 %copy-start.1 = (bf16[512,512]{1,0:T(8,128)(2,1)S(1)}, bf16[512,512]{1,0:T(8,128)(2,1)}, u32[]{:S(2)}) copy-start(bf16[512,512]{1,0:T(8,128)(2,1)} %refs_5_.7) | copy-start | bytes 1572868
  43.7 6.1 %collective-permute-start.6 = (bf16[272,128]{1,0:T(8,128)(2,1)S(1)}, bf16[272,128]{1,0:T(8,128)(2,1)S(1)}, u32[]{:S(2)}, u32[]{:S(2)}) collective-permute-start(bf16[272,128]{1,0:T(8,128)(2,1)S(1)} %get-tuple-element.67), channel_id=1, source_target_pairs={{0,8},{2,10},{4,12},{6,14},{8,0},{10,2},{12,4},{14,6},{1,9},{3,11}... | collective-permute-start | bytes 208904 | tf_op jit(solution)/shard_map/ppermute | solution.py:558
  45.0 5.1 %collective-permute-start.7 = (bf16[272,128]{1,0:T(8,128)(2,1)S(1)}, bf16[272,128]{1,0:T(8,128)(2,1)S(1)}, u32[]{:S(2)}, u32[]{:S(2)}) collective-permute-start(bf16[272,128]{1,0:T(8,128)(2,1)S(1)} %get-tuple-element.68), channel_id=1, source_target_pairs={{0,4},{2,6},{4,0},{6,2},{8,12},{10,14},{12,8},{14,10},{1,5},{3,7},... | collective-permute-start | bytes 208904 | tf_op jit(solution)/shard_map/ppermute | solution.py:558
  45.6 6.1 %collective-permute-start.8 = (bf16[272,128]{1,0:T(8,128)(2,1)S(1)}, bf16[272,128]{1,0:T(8,128)(2,1)S(1)}, u32[]{:S(2)}, u32[]{:S(2)}) collective-permute-start(bf16[272,128]{1,0:T(8,128)(2,1)S(1)} %get-tuple-element.69), channel_id=1, source_target_pairs={{0,12},{2,14},{4,8},{6,10},{8,4},{10,6},{12,0},{14,2},{1,13},{3,15... | collective-permute-start | bytes 208904 | tf_op jit(solution)/shard_map/ppermute | solution.py:558

commit v5 on v4

--- a/solution.py
+++ b/solution.py
@@ -93,14 +93,16 @@
 
 
 def own_rows_kernel(
-    ids_in, stored_in, decay_in, own_in, part_o, slot_o, crow_o, ccol_o, ctl_o,
-    ids, stored, decay, own, sem,
+    ids_in, stored_in, decay_in, own_in, weight_in, part_o, slot_o, crow_o, ccol_o, ctl_o, key_w_o,
+    ids, stored, decay, own, key_w, sem,
 ):
     n, half, heads = ids.shape[1], own.shape[0], decay.shape[0]
+    width = own.shape[1]
+    middle = weight_in.at[:, width : 2 * width]
     copies = [
         pltpu.make_async_copy(source, target, sem.at[k])
         for k, (source, target) in enumerate(
-            ((ids_in, ids), (stored_in, stored), (decay_in, decay), (own_in, own))
+            ((ids_in, ids), (stored_in, stored), (decay_in, decay), (middle, key_w), (own_in, own))
         )
     ]
     for copy in copies:
@@ -126,27 +128,29 @@
                 low, cum[2 * p : 2 * p + 1, CHUNK - 1 :], cum[2 * p + 1 : 2 * p + 2, CHUNK - 1 :]
             )
     copies[3].wait()
+    key_w_o[...] = jnp.transpose(key_w[...].astype(f32)).astype(bf16)
+    copies[4].wait()
     first = lax.axis_index("dp") * half
     for i in range(n // CHUNK):
         part_o[chunk(i), :] = picked_rows(slots[:, chunk(i)], first, own).astype(bf16)
 
 
 def summary_kernel(
-    length, part, peer, slot, ccol, ctl, id_rows, weight, emb_o, key_o, val_o, enter_o, pay_o
+    length, part, peer, slot, crow, ctl, id_rows, key_w, weight, emb_o, key_o, val_o, enter_o, pay_o
 ):
     n, width = part.shape
-    half, heads = peer.shape[0], ccol.shape[1] // 2
+    half, heads = peer.shape[0], crow.shape[1]
     pairs = heads // 2
     block = LANES // 2
-    ones, lanes = same_head(), head_spread(heads, 0, heads)
     low = first_half((1, LANES))
     chunks = n // CHUNK
+    here = length[...] - lax.axis_index("seq") * n
 
     def project(i):
         other = picked_rows(slot[:, chunk(i)], (1 - lax.axis_index("dp")) * half, peer)
         emb = (part[chunk(i), :].astype(f32) + other).astype(bf16)
         emb_o[chunk(i), :] = emb
-        return dot(emb, weight[:, width : 2 * width]), dot(emb, weight[:, 2 * width :])
+        return contract(key_w[...], emb, 1, 1), dot(emb, weight[:, 2 * width :])
 
     total = [jnp.zeros((block, LANES), f32)] * pairs
     ready = project(0)
@@ -154,16 +158,22 @@
         key, val = ready
         if i + 1 < chunks:
             ready = project(i + 1)
-        alive = iota((CHUNK, 1), 0) < length[0] - lax.axis_index("seq") * n - i * CHUNK
-        val = jnp.where(alive, val, 0.0).astype(bf16)
+        val = jnp.where(iota((CHUNK, 1), 0) < here - i * CHUNK, val, 0.0).astype(bf16)
         val_o[chunk(i), :] = val
-        unit = lax.rsqrt(head_means(key, ones) + 1e-06) * 0.125
-        normed = jnp.where(alive, key * unit, 0.0)
-        key_o[chunk(i), :] = normed.astype(bf16)
-        cum = ccol[chunk(i), :]
-        keyed = (normed * spread(jnp.exp(cum[CHUNK - 1 :, :] - cum), lanes)).astype(bf16)
+        alive = iota((1, CHUNK), 1) < here - i * CHUNK
+        cum = crow[i]
+        tail = jnp.exp(cum[:, CHUNK - 1 :] - cum)
         for p in range(pairs):
-            both = contract(keyed[:, pair_cut(p)], val[:, pair_cut(p)], 0, 0)
+            keyed = []
+            for h in (2 * p, 2 * p + 1):
+                rows = key[h * 64 : (h + 1) * 64]
+                mean = jnp.sum(rows * rows, axis=0, keepdims=True) * (1.0 / 64.0)
+                unit = jnp.where(alive, lax.rsqrt(mean + 1e-06) * 0.125, 0.0)
+                normed = rows * unit
+                key_o[h * 64 : (h + 1) * 64, chunk(i)] = normed.astype(bf16)
+                keyed.append(normed * tail[h : h + 1])
+            keyed = jnp.concatenate(keyed, axis=0).astype(bf16)
+            both = dot(keyed, val[:, pair_cut(p)])
             fresh = jnp.where(low, both[:block], both[block:])
             enter_o[i, p * block : (p + 1) * block, :] = total[p]
             total[p] = total[p] * jnp.exp(ctl[i * pairs + p : i * pairs + p + 1, :]) + fresh
@@ -242,7 +252,7 @@
     def scores(i, p, b, query):
         cut = pair_cut(p)
         wide = slice(first + p * LANES, first + (p + 1) * LANES)
-        return contract(query[:, cut] * (mask_b if b else mask_a), key[chunk(i), wide], 1, 1)
+        return dot(query[:, cut] * (mask_b if b else mask_a), key[wide, chunk(i)])
 
     units = [(i, p, b) for i in range(n // CHUNK) for p in range(width // LANES) for b in (0, 1)]
     query = {0: queries(0)}
@@ -316,7 +326,7 @@
         for block in blocks:
             peak = store(0, block, weights, buffers[0], peak)
         for h in range(width // 64):
-            factor = scale[h] * LOG2E
+            factor = scale[0:1, h : h + 1] * LOG2E
             peak = jnp.max(peak, axis=0, keepdims=True)
             following = None
             more = h + 1 < width // 64
@@ -341,7 +351,8 @@
 
 def finish_kernel(
     bit, length, scale, emb, query_a, query_b, intra_a, intra_b, enter, ctl, got, prefix, prefix_logs,
-    out_w, pair_w, val_w, cand_q, hist_o, key_o, val_o, pay_o, *buffers,
+    out_w, pair_w, val_w, cand_q, hist_o, key_o, val_o, pay_o,
+    shown, sem, *buffers,
 ):
     n, width = emb.shape
     pairs = width // LANES
@@ -371,28 +382,39 @@
         mixed = jnp.concatenate(parts, axis=1)
         return (mixed * lax.rsqrt(head_means(mixed, ones) + 1e-05)).astype(bf16)
 
+    alive_count = length[...] - lax.axis_index("seq") * n
+    copies = [
+        pltpu.make_async_copy(shown.at[chunk(i), :], hist_o.at[chunk(i), :], sem.at[i])
+        for i in range(chunks)
+    ]
     ready = normed(0)
     for i in range(chunks):
         current = ready
         if i + 1 < chunks:
             ready = normed(i + 1)
         hidden_sum = emb[chunk(i), :].astype(f32) + dot(current, out_w[...])
-        alive = iota((CHUNK, 1), 0) < length[0] - lax.axis_index("seq") * n - i * CHUNK
-        hist_o[chunk(i), :] = jnp.where(alive, hidden_sum, 0.0)
+        alive = iota((CHUNK, 1), 0) < alive_count - i * CHUNK
+        shown[chunk(i), :] = jnp.where(alive, hidden_sum, 0.0)
+        copies[i].start()
         hidden = hidden_sum.astype(bf16)
         key_o[chunk(i), :] = dot(hidden, pair_w[:, :width]).astype(bf16)
         val_o[:, chunk(i)] = contract(val_w[...], hidden, 1, 1).astype(bf16)
     count = pay_o.shape[1]
     heads = width // 64
-    alive_count = length[0] - lax.axis_index("seq") * n
     log_rows = []
 
     def emit(h, attended, logs):
         pay_o[h * 64 : (h + 1) * 64, :] = attended.astype(bf16)
-        log_rows.append(jnp.where(alive_count > 0, logs, DEAD))
+        log_rows.append(live(alive_count, logs))
 
     attend(alive_count, scale, cand_q, count, count, key_o, val_o, emit)(buffers)
     pay_o[width:, :] = pack_logs(jnp.concatenate(log_rows, axis=0))
+    for copy in copies:
+        copy.wait()
+
+
+def live(alive_count, logs):
+    return jnp.where(jnp.broadcast_to(alive_count, logs.shape) > 0, logs, DEAD)
 
 
 def pack_logs(logs):
@@ -412,11 +434,11 @@
 
 
 def keep_kernel(length, scale, cand_q, key, val, mean_o, logs_o, *buffers):
-    alive_count = length[0] - lax.axis_index("seq") * key.shape[0]
+    alive_count = length[...] - lax.axis_index("seq") * key.shape[0]
 
     def emit(h, attended, logs):
         mean_o[h * 64 : (h + 1) * 64, :] = attended
-        logs_o[h : h + 1, :] = jnp.where(alive_count > 0, logs, DEAD)
+        logs_o[h : h + 1, :] = live(alive_count, logs)
 
     attend(alive_count, scale, cand_q, 0, mean_o.shape[1], key, val, emit)(buffers)
 
@@ -498,14 +520,12 @@
 
 
 VMEM = pl.BlockSpec(memory_space=pltpu.VMEM)
-SMEM = pl.BlockSpec(memory_space=pltpu.SMEM)
 ANY = pl.BlockSpec(memory_space=pl.ANY)
 HBM = pl.BlockSpec(memory_space=pltpu.HBM)
 
 
-def call(kernel, name, scalars, operands, outs, scratch=(), after=(), flops=0, space=VMEM):
-    count = len(scalars) + len(operands)
-
+def call(kernel, name, operands, outs, scratch=(), after=(), flops=0, space=VMEM, spaces=None):
+    count = len(operands)
     if space is HBM:
         operands = [pltpu.with_memory_space_constraint(value, pltpu.HBM) for value in operands]
 
@@ -515,13 +535,13 @@
     return pl.pallas_call(
         body,
         name=name,
-        in_specs=[SMEM] * len(scalars) + [space] * len(operands) + [ANY] * len(after),
-        out_specs=[VMEM] * len(outs),
+        in_specs=[space] * count + [ANY] * len(after),
+        out_specs=spaces or [VMEM] * len(outs),
         out_shape=outs,
         scratch_shapes=list(scratch),
         compiler_params=pltpu.CompilerParams(vmem_limit_bytes=VMEM_LIMIT),
         cost_estimate=pl.CostEstimate(flops=flops, transcendentals=0, bytes_accessed=0),
-    )(*scalars, *operands, *after)
+    )(*operands, *after)
 
 
 def reversed_bits(value, bits):
@@ -559,31 +579,38 @@
 
     peer = lax.ppermute(item_embedding_table, "dp", [(0, 1), (1, 0)])
     far_ids = swap(candidate_item_index, seq // 2)
+    length = user_history_length.reshape(1, 1)
+    scale = head_score_scale.reshape(1, heads)
     stored = item_stored_row.reshape(-1, LANES)
     decay = log_head_retention.reshape(heads, n)
     ids = jnp.concatenate([candidate_item_index, far_ids], axis=0)
     ids = jnp.pad(ids, ((0, 0), (0, 64 - owned)))
     id_rows = jnp.concatenate([ids // LANES, ids % LANES], axis=1).astype(f32)
 
-    part, slot, crow, ccol, ctl = call(
-        own_rows_kernel, "own_rows", [],
-        [history_item_index, stored, decay, item_embedding_table],
+    part, slot, crow, ccol, ctl, key_w = call(
+        own_rows_kernel, "own_rows",
+        [
+            history_item_index, stored, decay, item_embedding_table,
+            history_query_key_value_weight,
+        ],
         [
             shape((n, width), bf16), shape((1, n), f32), shape((n // CHUNK, heads, CHUNK), f32),
             shape((n, 2 * heads), f32), shape((n // CHUNK * pairs, LANES), f32),
+            shape((width, width), bf16),
         ],
         [
             pltpu.VMEM((1, n), i32), pltpu.VMEM(stored.shape, i32), pltpu.VMEM((heads, n), f32),
-            pltpu.VMEM((half, width), bf16), pltpu.SemaphoreType.DMA((4,)),
+            pltpu.VMEM((half, width), bf16), pltpu.VMEM((width, width), bf16),
+            pltpu.SemaphoreType.DMA((5,)),
         ],
         space=HBM,
         flops=2 * n * half * width,
     )
     emb, key, val, enter, pay = call(
-        summary_kernel, "summary", [user_history_length],
-        [part, peer, slot, ccol, ctl, id_rows, history_query_key_value_weight],
+        summary_kernel, "summary",
+        [length, part, peer, slot, crow, ctl, id_rows, key_w, history_query_key_value_weight],
         [
-            shape((n, width), bf16), shape((n, width), bf16), shape((n, width), bf16),
+            shape((n, width), bf16), shape((width, n), bf16), shape((n, width), bf16),
             shape((n // CHUNK, rows, LANES), f32), shape((state_rows(pairs, 2), LANES), bf16),
         ],
         flops=2 * n * half * width,
@@ -591,7 +618,7 @@
 
     def local(first, name, after):
         return call(
-            lambda *refs: local_kernel(first, *refs), name, [],
+            lambda *refs: local_kernel(first, *refs), name,
             [emb, key, val, crow, ccol, history_query_key_value_weight],
             [shape((n, width // 2), bf16), shape((n, width // 2), f32)],
             after=after, flops=2 * n * half * width // 2,
@@ -607,7 +634,7 @@
         final = bit == bits - 2
         sent = 1 if final else 2 * count
         pay, prefix, logs, *id_rows = call(
-            lambda *refs, bit=bit, count=count: join_kernel(bit, count, pairs, *refs), "join", [],
+            lambda *refs, bit=bit, count=count: join_kernel(bit, count, pairs, *refs), "join",
             [pay, got] + ([prefix, logs] if bit else []),
             [
                 shape((state_rows(pairs, sent), LANES), bf16), shape((rows, LANES), f32),
@@ -622,7 +649,7 @@
         places[(j & 1) * half_seq + (j >> 1)] = j
     order = [places[reversed_bits(j, bits)] for j in range(seq)]
     cand_q, val_w = call(
-        lambda *refs: candidate_kernel(order, owned, *refs), "candidates", [],
+        lambda *refs: candidate_kernel(order, owned, *refs), "candidates",
         [
             id_rows[0], stored, item_embedding_table, peer, candidate_query_weight,
             candidate_key_value_weight,
@@ -635,20 +662,21 @@
     buffers = [pltpu.VMEM((n, send), f32)] * 2
     message = width + log_pad(heads)
     hist, key_two, val_two, pay = call(
-        lambda *refs: finish_kernel(bits - 1, *refs), "finish", [user_history_length, head_score_scale],
+        lambda *refs: finish_kernel(bits - 1, *refs), "finish",
         [
-            emb, query_a, query_b, intra_a, intra_b, enter, ctl, got, prefix, logs,
+            length, scale, emb, query_a, query_b, intra_a, intra_b, enter, ctl, got, prefix, logs,
             history_output_weight, candidate_key_value_weight, val_w, cand_q,
         ],
         [
             shape((n, width), f32), shape((n, width), bf16), shape((width, n), bf16),
             shape((message, send), bf16),
         ],
-        buffers,
+        [pltpu.VMEM((n, width), f32), pltpu.SemaphoreType.DMA((n // CHUNK,))] + buffers,
+        spaces=[ANY, VMEM, VMEM, VMEM],
         flops=2 * n * half * width,
     )
     mean, logs = call(
-        keep_kernel, "keep", [user_history_length, head_score_scale], [cand_q, key_two, val_two],
+        keep_kernel, "keep", [length, scale, cand_q, key_two, val_two],
         [shape((width, send), f32), shape((heads, send), f32)],
         buffers,
         flops=2 * n * half * width,
@@ -657,21 +685,23 @@
         got = swap(pay, 1 << bit)
         send //= 2
         mean, logs, pay = call(
-            fold_kernel, "fold", [], [mean, logs, got],
+            fold_kernel, "fold", [mean, logs, got],
             [shape((width, send), f32), shape((heads, send), f32), shape((message, send), bf16)],
         )
     got = swap(pay, 1 << (bits - 3))
     packed = 2 * owned == LANES
     cols = LANES if packed else owned
     mean, logs, *sends = call(
-        deal_kernel, "deal", [], [mean, logs, got],
+        deal_kernel, "deal", [mean, logs, got],
         [shape((width, cols), f32), shape((heads, cols), f32)]
         + [shape((message // 2, LANES) if packed else (message, owned), bf16)] * 3,
     )
     masks = [seq // 2, seq // 4, seq // 2 + seq // 4]
-    gots = [swap(value, mask) for value, mask in zip(sends, masks)]
+    gots = [None] * 3
+    for k in (0, 2, 1):
+        gots[k] = swap(sends[k], masks[k])
     (cand_out,) = call(
-        lambda *refs: last_kernel(owned, *refs), "last", [],
+        lambda *refs: last_kernel(owned, *refs), "last",
         [mean, logs, *gots, candidate_output_weight],
         [shape((owned, width), f32)],
     )

time: 52.9 us -> 51.9 us (0.981)
  Pallas kernels: 29.7 us -> 28 us
  waiting for transfers between devices: 7.69 us -> 8.41 us
    pallas_call x11, Pallas kernels: 29.7 us -> 28 us  [call(): pl.pallas_call(body, name=name, in_specs=[space] * count + [ANY] * len(af...]
    ppermute x8, waiting for transfers between devices: 7.69 us -> 8.41 us  [swap(): return lax.ppermute(value, 'seq', [(j, j ^ mask) for j in range(seq)])]
where the time goes in v5:
time: 51.9 us; the launch traced here: 51.7 us
  Pallas kernels  28 us (54%)
  starting transfers between devices  13.8 us (27%)
  waiting for transfers between devices  8.41 us (16%)
  between operations  1.41 us (3%)
    pallas_call x11, Pallas kernels, call(): pl.pallas_call(body, name=name, in_specs=[space] * count + [ANY] * len(af...  28 us
    ppermute x8, starting transfers between devices, swap(): return lax.ppermute(value, 'seq', [(j, j ^ mask) for j in range(seq)])  13.3 us
    ppermute x8, waiting for transfers between devices, swap(): return lax.ppermute(value, 'seq', [(j, j ^ mask) for j in range(seq)])  8.41 us
  transfers between devices with their start and end apart: 9, of which 6 were waited for; matrix products, arithmetic and copies ran while one was open for 0% of the time, Pallas kernels for 31%

profile of v5, /device:TPU:0, one launch (start us, length us, event | category | flops | bytes accessed | tf_op | source)
XLA Modules:
  0.0 51.7 jit_solution(1097231287644975679)
XLA Ops:
  0.6 0.5 %collective-permute-start = (bf16[2048,512]{1,0:T(8,128)(2,1)}, bf16[2048,512]{1,0:T(8,128)(2,1)S(1)}, u32[]{:S(2)}, u32[]{:S(2)}) collective-permute-start(bf16[2048,512]{1,0:T(8,128)(2,1)} %refs_2_.1), channel_id=1, source_target_pairs={{0,1},{1,0},{2,3},{3,2},{4,5},{5,4},{6,7},{7,6},{8,9},{9,8},{10,11... | collective-permute-start | bytes 6291464 | tf_op jit(solution)/shard_map/ppermute | solution.py:580
  1.1 3.7 %collective-permute-start.1 = (s32[1,64]{1,0:T(1,128)}, s32[1,64]{1,0:T(1,128)S(1)}, u32[]{:S(2)}, u32[]{:S(2)}) collective-permute-start(s32[1,64]{1,0:T(1,128)} %param.15), channel_id=1, source_target_pairs={{0,8},{2,10},{4,12},{6,14},{8,0},{10,2},{12,4},{14,6},{1,9},{3,11}... | collective-permute-start | bytes 776 | tf_op jit(solution)/shard_map/ppermute | solution.py:578
  4.8 0.0 copy-start.8
  4.8 0.0 copy-start
  4.8 4.3 %own_rows.1 = (bf16[1024,512]{1,0:T(8,128)(2,1)S(1)}, f32[1,1024]{1,0:T(1,128)S(1)}, f32[4,8,256]{2,1,0:T(8,128)S(1)}, f32[1024,16]{1,0:T(8,128)S(1)}, f32[16,12...) custom-call(s32[1,1024]{1,0:T(1,128)} %refs_0_.1, s32[32,128]{1,0:T(8,128)} %bitcast.9, f32[8,1024]{1,0:T(8,128)} %bitcast.14, ...), custom_call_target="tpu_custom_call" | custom-call | flops 2147483648 | tf_op jit(solution)/shard_map/own_rows/pallas_call | solution.py:535
  9.8 0.0 collective-permute-done.1
  9.8 0.0 copy-done.8
  9.9 0.1 add_convert_fusion.refs_6_
  9.9 0.0 collective-permute-done.refs_2_.refs_3_
  9.9 0.0 copy-done
  9.9 4.5 %summary.1 = (bf16[1024,512]{1,0:T(8,128)(2,1)S(1)}, bf16[512,1024]{1,0:T(8,128)(2,1)S(1)}, bf16[1024,512]{1,0:T(8,128)(2,1)S(1)}, f32[4,256,128]{2,1,0:T(8,128)S(1)}, bf16[272,128]{1,0:T(8,128)(2,1)S(1)}) custom-call(s32[1,1]{1,0:T(1,128)} %bitcast.6.refs_0_, bf16[1024,512]{1,0:T(8,128)(2,1)S(1)} %get-tuple-element.37.refs_1_, ...), custom_call_target="tpu_custom_call" | custom-call | flops 2147483648 | tf_op jit(solution)/shard_map/summary/pallas_call | solution.py:535
  14.5 1.6 %collective-permute-start.2 = (bf16[272,128]{1,0:T(8,128)(2,1)S(1)}, bf16[272,128]{1,0:T(8,128)(2,1)S(1)}, u32[]{:S(2)}, u32[]{:S(2)}) collective-permute-start(bf16[272,128]{1,0:T(8,128)(2,1)S(1)} %get-tuple-element.47.refs_0_), channel_id=1, source_target_pairs={{0,2},{2,0},{4,6},{6,4},{8,10},{10,8},{12,14},{14,12},{1,3},{3,1},... | collective-permute-start | bytes 208904 | tf_op jit(solution)/shard_map/ppermute | solution.py:578
  16.1 2.7 %local_a.1 = (bf16[1024,256]{1,0:T(8,128)(2,1)S(1)}, f32[1024,256]{1,0:T(8,128)S(1)}) custom-call(bf16[1024,512]{1,0:T(8,128)(2,1)S(1)} %get-tuple-element.42.refs_0_.refs_2_, bf16[512,1024]{1,0:T(8,128)(2,1)S(1)} %get-tuple-element.43.refs_1_, bf16[1024,512]{1,0:T(8,128)(2,1)S(1)} %get-tuple-element.44.refs_2_, ...), custom_call_target="tpu_custom_call" | custom-call | flops 1073741824 | tf_op jit(solution)/shard_map/local_a/pallas_call | solution.py:535
  18.7 0.1 collective-permute-done.2.refs_1_
  18.9 0.1 join.2
  18.9 1.6 %collective-permute-start.3 = (bf16[272,128]{1,0:T(8,128)(2,1)S(1)}, bf16[272,128]{1,0:T(8,128)(2,1)S(1)}, u32[]{:S(2)}, u32[]{:S(2)}) collective-permute-start(bf16[272,128]{1,0:T(8,128)(2,1)S(1)} %get-tuple-element.53.refs_0_), channel_id=1, source_target_pairs={{0,4},{2,6},{4,0},{6,2},{8,12},{10,14},{12,8},{14,10},{1,5},{3,7},... | collective-permute-start | bytes 208904 | tf_op jit(solution)/shard_map/ppermute | solution.py:578
  20.6 0.0 copy-start.2
  20.6 0.0 copy-start.3
  20.6 0.0 copy-start.4
  20.6 0.0 copy-start.6
  20.6 2.9 %local_b.1 = (bf16[1024,256]{1,0:T(8,128)(2,1)S(1)}, f32[1024,256]{1,0:T(8,128)S(1)}) custom-call(bf16[1024,512]{1,0:T(8,128)(2,1)S(1)} %get-tuple-element.42.refs_0_.refs_2_, bf16[512,1024]{1,0:T(8,128)(2,1)S(1)} %get-tuple-element.43.refs_1_, bf16[1024,512]{1,0:T(8,128)(2,1)S(1)} %get-tuple-element.44.refs_2_, ...), custom_call_target="tpu_custom_call" | custom-call | flops 1073741824 | tf_op jit(solution)/shard_map/local_b/pallas_call | solution.py:535
  23.4 0.0 collective-permute-done.3.refs_1_
  23.5 0.1 join.3
  23.5 0.4 collective-permute-start.4
  23.9 0.0 copy-done.2
  23.9 0.0 copy-done.3
  23.9 0.0 copy-done.4
  23.9 0.0 copy-done.6
  23.9 0.0 copy-start.5
  23.9 0.0 copy-start.7
  24.0 3.3 %candidates.1 = (bf16[512,512]{1,0:T(8,128)(2,1)S(1)}, bf16[512,512]{1,0:T(8,128)(2,1)S(1)}) custom-call(f32[8,128]{1,0:T(8,128)S(1)} %get-tuple-element.58.refs_0_, s32[32,128]{1,0:T(8,128)S(1)} %bitcast.10, bf16[2048,512]{1,0:T(8,128)(2,1)S(1)} %copy-done.2, bf16[2048,512]{1,0:T(8,128)(2,1)S(1)} %collective-permute-done.refs_2_.refs_3_, ...), custom_call_target="tpu_custom_call" | custom-call | flops 2147483648 | tf_op jit(solution)/shard_map/candidates/pallas_call | solution.py:535
  27.3 1.5 %collective-permute-done.4.refs_9_ = bf16[272,128]{1,0:T(8,128)(2,1)S(1)} collective-permute-done((bf16[272,128]{1,0:T(8,128)(2,1)S(1)}, bf16[272,128]{1,0:T(8,128)(2,1)S(1)}, u32[]{:S(2)}, u32[]{:S(2)}) %collective-permute-start.4) | collective-permute-done | bytes 69664 | tf_op jit(solution)/shard_map/ppermute | solution.py:578
  28.8 0.0 copy-done.5
  28.8 0.0 copy-done.7
  28.8 6.0 %finish.1 = (f32[1024,512]{1,0:T(8,128)}, bf16[1024,512]{1,0:T(8,128)(2,1)S(1)}, bf16[512,1024]{1,0:T(8,128)(2,1)S(1)}, bf16[544,256]{1,0:T(8,128)(2,1)S(1)}) custom-call(s32[1,1]{1,0:T(1,128)} %bitcast.7.refs_0_, f32[1,8]{1,0:T(1,128)S(1)} %bitcast.11, bf16[1024,512]{1,0:T(8,128)(2,1)S(1)} %get-tuple-element.42.refs_0_.refs_2_, ...), custom_call_target="tpu_custom_call" | custom-call | flops 2147483648 | tf_op jit(solution)/shard_map/finish/pallas_call | solution.py:535
  34.9 1.6 %collective-permute-start.5 = (bf16[544,256]{1,0:T(8,128)(2,1)S(1)}, bf16[544,256]{1,0:T(8,128)(2,1)S(1)}, u32[]{:S(2)}, u32[]{:S(2)}) collective-permute-start(bf16[544,256]{1,0:T(8,128)(2,1)S(1)} %get-tuple-element.66), channel_id=1, source_target_pairs={{0,2},{2,0},{4,6},{6,4},{8,10},{10,8},{12,14},{14,12},{1,3},{3,1},... | collective-permute-start | bytes 835592 | tf_op jit(solution)/shard_map/ppermute | solution.py:578
  36.4 0.0 copy-start.1
  36.4 2.9 %keep.1 = (f32[512,256]{1,0:T(8,128)S(1)}, f32[8,256]{1,0:T(8,128)S(1)}) custom-call(s32[1,1]{1,0:T(1,128)} %bitcast.8.refs_0_, f32[1,8]{1,0:T(1,128)S(1)} %bitcast.12, bf16[512,512]{1,0:T(8,128)(2,1)S(1)} %get-tuple-element.60.refs_15_.refs_2_, bf16[1024,512]{1,0:T(8,128)(2,1)S(1)} %get-tuple-element.62.refs_3_, bf16[512,1024]{1,0:T(8,128)(2,1)S(1)} %get-tuple-element.63.refs_4_), custom_call_target="tpu_custom_call" | custom-call | flops 2147483648 | tf_op jit(solution)/shard_map/keep/pallas_call | solution.py:535
  39.3 3.3 %collective-permute-done.5.refs_2_ = bf16[544,256]{1,0:T(8,128)(2,1)S(1)} collective-permute-done((bf16[544,256]{1,0:T(8,128)(2,1)S(1)}, bf16[544,256]{1,0:T(8,128)(2,1)S(1)}, u32[]{:S(2)}, u32[]{:S(2)}) %collective-permute-start.5) | collective-permute-done | bytes 278560 | tf_op jit(solution)/shard_map/ppermute | solution.py:578
  42.6 0.2 deal.1
  42.7 1.3 %collective-permute-start.6 = (bf16[272,128]{1,0:T(8,128)(2,1)S(1)}, bf16[272,128]{1,0:T(8,128)(2,1)S(1)}, u32[]{:S(2)}, u32[]{:S(2)}) collective-permute-start(bf16[272,128]{1,0:T(8,128)(2,1)S(1)} %get-tuple-element.69), channel_id=1, source_target_pairs={{0,8},{2,10},{4,12},{6,14},{8,0},{10,2},{12,4},{14,6},{1,9},{3,11}... | collective-permute-start | bytes 208904 | tf_op jit(solution)/shard_map/ppermute | solution.py:578
  44.0 0.5 collective-permute-start.7
  44.5 2.6 %collective-permute-start.8 = (bf16[272,128]{1,0:T(8,128)(2,1)S(1)}, bf16[272,128]{1,0:T(8,128)(2,1)S(1)}, u32[]{:S(2)}, u32[]{:S(2)}) collective-permute-start(bf16[272,128]{1,0:T(8,128)(2,1)S(1)} %get-tuple-element.71), channel_id=1, source_target_pairs={{0,12},{2,14},{4,8},{6,10},{8,4},{10,6},{12,0},{14,2},{1,13},{3,15... | collective-permute-start | bytes 208904 | tf_op jit(solution)/shard_map/ppermute | solution.py:578
  47.2 1.7 %collective-permute-done.6.refs_2_ = bf16[272,128]{1,0:T(8,128)(2,1)S(1)} collective-permute-done((bf16[272,128]{1,0:T(8,128)(2,1)S(1)}, bf16[272,128]{1,0:T(8,128)(2,1)S(1)}, u32[]{:S(2)}, u32[]{:S(2)}) %collective-permute-start.6) | collective-permute-done | bytes 69664 | tf_op jit(solution)/shard_map/ppermute | solution.py:578
  48.9 0.2 collective-permute-done.7.refs_3_
  49.1 1.6 %collective-permute-done.8.refs_4_ = bf16[272,128]{1,0:T(8,128)(2,1)S(1)} collective-permute-done((bf16[272,128]{1,0:T(8,128)(2,1)S(1)}, bf16[272,128]{1,0:T(8,128)(2,1)S(1)}, u32[]{:S(2)}, u32[]{:S(2)}) %collective-permute-start.8) | collective-permute-done | bytes 69664 | tf_op jit(solution)/shard_map/ppermute | solution.py:578
  50.6 0.0 copy-done.1
  50.7 1.1 %last.1 = f32[64,512]{1,0:T(8,128)} custom-call(f32[512,128]{1,0:T(8,128)S(1)} %get-tuple-element.67.refs_0_, f32[8,128]{1,0:T(8,128)S(1)} %get-tuple-element.68.refs_1_, bf16[272,128]{1,0:T(8,128)(2,1)S(1)} %collective-permute-done.6.refs_2_, bf16[272,128]{1,0:T(8,128)(2,1)S(1)} %collective-permute-done.7.refs_3_, ...), custom_call_target="tpu_custom_call" | custom-call | tf_op jit(solution)/shard_map/last/pallas_call | solution.py:535
  (1 shorter events, 0.0 us)
Async XLA Ops:
  0.6 9.3 %collective-permute-start = (bf16[2048,512]{1,0:T(8,128)(2,1)}, bf16[2048,512]{1,0:T(8,128)(2,1)S(1)}, u32[]{:S(2)}, u32[]{:S(2)}) collective-permute-start(bf16[2048,512]{1,0:T(8,128)(2,1)} %refs_2_.1), channel_id=1, source_target_pairs={{0,1},{1,0},{2,3},{3,2},{4,5},{5,4},{6,7},{7,6},{8,9},{9,8},{10,11... | collective-permute-start | bytes 6291464 | tf_op jit(solution)/shard_map/ppermute | solution.py:580
  1.1 8.7 %collective-permute-start.1 = (s32[1,64]{1,0:T(1,128)}, s32[1,64]{1,0:T(1,128)S(1)}, u32[]{:S(2)}, u32[]{:S(2)}) collective-permute-start(s32[1,64]{1,0:T(1,128)} %param.15), channel_id=1, source_target_pairs={{0,8},{2,10},{4,12},{6,14},{8,0},{10,2},{12,4},{14,6},{1,9},{3,11}... | collective-permute-start | bytes 776 | tf_op jit(solution)/shard_map/ppermute | solution.py:578
  4.8 5.0 %copy-start.8 = (s32[1,64]{1,0:T(1,128)S(1)}, s32[1,64]{1,0:T(1,128)}, u32[]{:S(2)}) copy-start(s32[1,64]{1,0:T(1,128)} %param.15) | copy-start | bytes 772
  4.8 5.1 %copy-start = (bf16[512,1536]{1,0:T(8,128)(2,1)S(1)}, bf16[512,1536]{1,0:T(8,128)(2,1)}, u32[]{:S(2)}) copy-start(bf16[512,1536]{1,0:T(8,128)(2,1)} %refs_5_.5) | copy-start | bytes 4718596
  14.5 4.4 %collective-permute-start.2 = (bf16[272,128]{1,0:T(8,128)(2,1)S(1)}, bf16[272,128]{1,0:T(8,128)(2,1)S(1)}, u32[]{:S(2)}, u32[]{:S(2)}) collective-permute-start(bf16[272,128]{1,0:T(8,128)(2,1)S(1)} %get-tuple-element.47.refs_0_), channel_id=1, source_target_pairs={{0,2},{2,0},{4,6},{6,4},{8,10},{10,8},{12,14},{14,12},{1,3},{3,1},... | collective-permute-start | bytes 208904 | tf_op jit(solution)/shard_map/ppermute | solution.py:578
  18.9 4.5 %collective-permute-start.3 = (bf16[272,128]{1,0:T(8,128)(2,1)S(1)}, bf16[272,128]{1,0:T(8,128)(2,1)S(1)}, u32[]{:S(2)}, u32[]{:S(2)}) collective-permute-start(bf16[272,128]{1,0:T(8,128)(2,1)S(1)} %get-tuple-element.53.refs_0_), channel_id=1, source_target_pairs={{0,4},{2,6},{4,0},{6,2},{8,12},{10,14},{12,8},{14,10},{1,5},{3,7},... | collective-permute-start | bytes 208904 | tf_op jit(solution)/shard_map/ppermute | solution.py:578
  20.6 3.4 %copy-start.2 = (bf16[2048,512]{1,0:T(8,128)(2,1)S(1)}, bf16[2048,512]{1,0:T(8,128)(2,1)}, u32[]{:S(2)}) copy-start(bf16[2048,512]{1,0:T(8,128)(2,1)} %refs_2_.1) | copy-start | bytes 6291460
  20.6 3.4 %copy-start.3 = (bf16[512,1024]{1,0:T(8,128)(2,1)S(1)}, bf16[512,1024]{1,0:T(8,128)(2,1)}, u32[]{:S(2)}) copy-start(bf16[512,1024]{1,0:T(8,128)(2,1)} %refs_13_.1) | copy-start | bytes 3145732
  20.6 3.4 %copy-start.4 = (bf16[512,512]{1,0:T(8,128)(2,1)S(1)}, bf16[512,512]{1,0:T(8,128)(2,1)}, u32[]{:S(2)}) copy-start(bf16[512,512]{1,0:T(8,128)(2,1)} %refs_4_.3) | copy-start | bytes 1572868
  20.6 3.4 %copy-start.6 = (s32[4096]{0:T(1024)S(1)}, s32[4096]{0:T(1024)}, u32[]{:S(2)}) copy-start(s32[4096]{0:T(1024)} %param.16) | copy-start | bytes 49156
  23.5 5.3 %collective-permute-start.4 = (bf16[272,128]{1,0:T(8,128)(2,1)S(1)}, bf16[272,128]{1,0:T(8,128)(2,1)S(1)}, u32[]{:S(2)}, u32[]{:S(2)}) collective-permute-start(bf16[272,128]{1,0:T(8,128)(2,1)S(1)} %get-tuple-element.55), channel_id=1, source_target_pairs={{0,8},{2,10},{4,12},{6,14},{8,0},{10,2},{12,4},{14,6},{1,9},{3,11}... | collective-permute-start | bytes 208904 | tf_op jit(solution)/shard_map/ppermute | solution.py:578
  23.9 4.9 %copy-start.5 = (bf16[512,512]{1,0:T(8,128)(2,1)S(1)}, bf16[512,512]{1,0:T(8,128)(2,1)}, u32[]{:S(2)}) copy-start(bf16[512,512]{1,0:T(8,128)(2,1)} %refs_12_.1) | copy-start | bytes 1572868
  23.9 4.9 %copy-start.7 = (f32[8]{0:T(128)S(1)}, f32[8]{0:T(128)}, u32[]{:S(2)}) copy-start(f32[8]{0:T(128)} %param.18) | copy-start | bytes 100
  34.9 7.7 %collective-permute-start.5 = (bf16[544,256]{1,0:T(8,128)(2,1)S(1)}, bf16[544,256]{1,0:T(8,128)(2,1)S(1)}, u32[]{:S(2)}, u32[]{:S(2)}) collective-permute-start(bf16[544,256]{1,0:T(8,128)(2,1)S(1)} %get-tuple-element.66), channel_id=1, source_target_pairs={{0,2},{2,0},{4,6},{6,4},{8,10},{10,8},{12,14},{14,12},{1,3},{3,1},... | collective-permute-start | bytes 835592 | tf_op jit(solution)/shard_map/ppermute | solution.py:578
  36.4 14.2 %copy-start.1 = (bf16[512,512]{1,0:T(8,128)(2,1)S(1)}, bf16[512,512]{1,0:T(8,128)(2,1)}, u32[]{:S(2)}) copy-start(bf16[512,512]{1,0:T(8,128)(2,1)} %refs_5_.7) | copy-start | bytes 1572868
  42.7 6.2 %collective-permute-start.6 = (bf16[272,128]{1,0:T(8,128)(2,1)S(1)}, bf16[272,128]{1,0:T(8,128)(2,1)S(1)}, u32[]{:S(2)}, u32[]{:S(2)}) collective-permute-start(bf16[272,128]{1,0:T(8,128)(2,1)S(1)} %get-tuple-element.69), channel_id=1, source_target_pairs={{0,8},{2,10},{4,12},{6,14},{8,0},{10,2},{12,4},{14,6},{1,9},{3,11}... | collective-permute-start | bytes 208904 | tf_op jit(solution)/shard_map/ppermute | solution.py:578
  44.0 5.1 %collective-permute-start.7 = (bf16[272,128]{1,0:T(8,128)(2,1)S(1)}, bf16[272,128]{1,0:T(8,128)(2,1)S(1)}, u32[]{:S(2)}, u32[]{:S(2)}) collective-permute-start(bf16[272,128]{1,0:T(8,128)(2,1)S(1)} %get-tuple-element.70), channel_id=1, source_target_pairs={{0,4},{2,6},{4,0},{6,2},{8,12},{10,14},{12,8},{14,10},{1,5},{3,7},... | collective-permute-start | bytes 208904 | tf_op jit(solution)/shard_map/ppermute | solution.py:578
  44.5 6.1 %collective-permute-start.8 = (bf16[272,128]{1,0:T(8,128)(2,1)S(1)}, bf16[272,128]{1,0:T(8,128)(2,1)S(1)}, u32[]{:S(2)}, u32[]{:S(2)}) collective-permute-start(bf16[272,128]{1,0:T(8,128)(2,1)S(1)} %get-tuple-element.71), channel_id=1, source_target_pairs={{0,12},{2,14},{4,8},{6,10},{8,4},{10,6},{12,0},{14,2},{1,13},{3,15... | collective-permute-start | bytes 208904 | tf_op jit(solution)/shard_map/ppermute | solution.py:578

commit v6 on v5

--- a/solution.py
+++ b/solution.py
@@ -102,7 +102,11 @@
     copies = [
         pltpu.make_async_copy(source, target, sem.at[k])
         for k, (source, target) in enumerate(
-            ((ids_in, ids), (stored_in, stored), (decay_in, decay), (middle, key_w), (own_in, own))
+            (
+                (ids_in, ids), (stored_in, stored), (decay_in, decay), (middle, key_w),
+                (own_in.at[: half // 2], own.at[: half // 2]),
+                (own_in.at[half // 2 :], own.at[half // 2 :]),
+            )
         )
     ]
     for copy in copies:
@@ -129,14 +133,20 @@
             )
     copies[3].wait()
     key_w_o[...] = jnp.transpose(key_w[...].astype(f32)).astype(bf16)
-    copies[4].wait()
     first = lax.axis_index("dp") * half
-    for i in range(n // CHUNK):
-        part_o[chunk(i), :] = picked_rows(slots[:, chunk(i)], first, own).astype(bf16)
+    for k in range(2):
+        copies[4 + k].wait()
+        piece = own.at[k * half // 2 : (k + 1) * half // 2]
+        for i in range(n // CHUNK):
+            rows = picked_rows(slots[:, chunk(i)], first + k * half // 2, piece)
+            if k:
+                rows += part_o[chunk(i), :].astype(f32)
+            part_o[chunk(i), :] = rows.astype(bf16)
 
 
 def summary_kernel(
-    length, part, peer, slot, crow, ctl, id_rows, key_w, weight, emb_o, key_o, val_o, enter_o, pay_o
+    length, part, peer, slot, crow, ctl, id_rows, key_w, weight,
+    emb_o, key_o, val_o, enter_o, pay_o, here_o,
 ):
     n, width = part.shape
     half, heads = peer.shape[0], crow.shape[1]
@@ -144,7 +154,8 @@
     block = LANES // 2
     low = first_half((1, LANES))
     chunks = n // CHUNK
-    here = length[...] - lax.axis_index("seq") * n
+    here = length[0] - lax.axis_index("seq") * n
+    here_o[...] = jnp.full(here_o.shape, here, i32)
 
     def project(i):
         other = picked_rows(slot[:, chunk(i)], (1 - lax.axis_index("dp")) * half, peer)
@@ -212,7 +223,7 @@
 
 def join_kernel(bit, ids, pairs, mine, got, *refs):
     before = refs[: 2 if bit else 0]
-    pay_o, prefix_o, logs_o, *ids_o = refs[len(before) :]
+    pay_o, prefix_o, logs_o = refs[len(before) :]
     upper = (lax.axis_index("seq") >> bit) & 1 == 1
     state, logs, rows = unpack_state(mine[...], pairs)
     other, other_logs, other_rows = unpack_state(got[...], pairs)
@@ -220,11 +231,7 @@
     late = jnp.where(upper, state, other)
     factor = row_factors(jnp.where(upper, logs, other_logs))
     id_rows = jnp.concatenate([rows[:ids], other_rows[:ids]], axis=0)
-    if ids_o:
-        ids_o[0][...] = id_rows
-    pay_o[...] = pack_state(
-        early * factor + late, logs + other_logs, id_rows[:1] if ids_o else id_rows
-    )
+    pay_o[...] = pack_state(early * factor + late, logs + other_logs, id_rows)
     if bit == 0:
         prefix_o[...] = jnp.where(upper, other, 0.0)
         logs_o[...] = jnp.where(upper, other_logs, 0.0)
@@ -276,35 +283,40 @@
             intra_o[chunk(i), pair_cut(p)] = held + part
 
 
-def candidate_kernel(order, owned, id_rows, stored, own, peer, query_w, pair_w, query_o, val_w_o):
+def candidate_kernel(order, owned, message, stored, own, peer, query_w, *refs):
     half, width = own.shape
-    ids = id_rows[...]
+    pairs = width // LANES
+    ids = message[pairs * 64 :, :].astype(f32)
     ids = (ids * float(LANES) + pltpu.roll(ids, LANES // 2, 1)).astype(i32)
-    slots = [stored_slots(ids[j : j + 1], stored[...]) for j in order]
-    step = max(1, LANES // owned)
+    slots = [stored_slots(ids[3 * pairs + j : 3 * pairs + j + 1], stored[...]) for j in order]
+    step = LANES // owned
     tiles = []
     for start in range(0, len(order), step):
         tile = slots[start]
-        for k in range(1, min(step, len(order) - start)):
+        for k in range(1, step):
             moved = pltpu.roll(slots[start + k], k * owned, 1)
             tile = jnp.where(iota((1, LANES), 1) >= k * owned, moved, tile)
         tiles.append(tile)
     slots = jnp.concatenate(tiles, axis=1)
-    for c in range(0, slots.shape[1], CHUNK):
-        some = slots[:, c : c + CHUNK]
-        dp = lax.axis_index("dp")
-        rows = picked_rows(some, dp * half, own) + picked_rows(some, (1 - dp) * half, peer)
-        query = dot(rows.astype(bf16), query_w[...])
-        query_o[:, c : c + CHUNK] = jnp.transpose(query).astype(bf16)
-    val_w_o[...] = jnp.transpose(pair_w[:, width:].astype(f32)).astype(bf16)
-
-
-def attend(alive_count, scale, query, first, cols, key, val, emit):
-    n, width = key.shape
+    dp = lax.axis_index("dp")
+    rows = picked_rows(slots, dp * half, own) + picked_rows(slots, (1 - dp) * half, peer)
+    query = jnp.transpose(dot(rows.astype(bf16), query_w[...])).astype(bf16)
+    if len(refs) > 2:
+        pair_w, *refs, val_w_o = refs
+        val_w_o[...] = jnp.transpose(pair_w[:, width:].astype(f32)).astype(bf16)
+    part = query.shape[1] // 2
+    refs[0][...] = query[:, :part]
+    refs[1][...] = query[:, part:]
+
+
+def attend(alive_count, scale, heads, queries, key, val, emit):
+    n = key.shape[0]
+    cols = sum(query.shape[1] for query in queries)
     blocks = range(0, n, KEYS)
 
     def padded(h):
-        rows = query[h * 64 : (h + 1) * 64, first : first + cols]
+        cut = slice(h * 64, (h + 1) * 64)
+        rows = jnp.concatenate([query[cut, :] for query in queries], axis=1)
         zero = jnp.zeros_like(rows)
         return jnp.concatenate([zero, rows] if h % 2 else [rows, zero], axis=0)
 
@@ -322,14 +334,14 @@
 
     def run(buffers):
         ones = jnp.ones((16, KEYS), bf16)
-        peak, weights = None, padded(0)
+        peak, weights = None, padded(heads[0])
         for block in blocks:
-            peak = store(0, block, weights, buffers[0], peak)
-        for h in range(width // 64):
+            peak = store(heads[0], block, weights, buffers[heads[0] % 2], peak)
+        for h in heads:
             factor = scale[0:1, h : h + 1] * LOG2E
             peak = jnp.max(peak, axis=0, keepdims=True)
             following = None
-            more = h + 1 < width // 64
+            more = h + 1 in heads
             weights = padded(h + 1) if more else None
             sums = None
             for block in blocks:
@@ -350,8 +362,8 @@
 
 
 def finish_kernel(
-    bit, length, scale, emb, query_a, query_b, intra_a, intra_b, enter, ctl, got, prefix, prefix_logs,
-    out_w, pair_w, val_w, cand_q, hist_o, key_o, val_o, pay_o,
+    bit, here, scale, emb, query_a, query_b, intra_a, intra_b, enter, ctl, got, prefix, prefix_logs,
+    out_w, pair_w, val_w, cand_a, cand_b, hist_o, key_o, val_o, pay_o,
     shown, sem, *buffers,
 ):
     n, width = emb.shape
@@ -382,7 +394,7 @@
         mixed = jnp.concatenate(parts, axis=1)
         return (mixed * lax.rsqrt(head_means(mixed, ones) + 1e-05)).astype(bf16)
 
-    alive_count = length[...] - lax.axis_index("seq") * n
+    alive_count = here[0:1, 0:1]
     copies = [
         pltpu.make_async_copy(shown.at[chunk(i), :], hist_o.at[chunk(i), :], sem.at[i])
         for i in range(chunks)
@@ -399,18 +411,28 @@
         hidden = hidden_sum.astype(bf16)
         key_o[chunk(i), :] = dot(hidden, pair_w[:, :width]).astype(bf16)
         val_o[:, chunk(i)] = contract(val_w[...], hidden, 1, 1).astype(bf16)
-    count = pay_o.shape[1]
-    heads = width // 64
+    send_part(alive_count, scale, 0, (cand_a, cand_b), key_o, val_o, pay_o, buffers)
+    for copy in copies:
+        copy.wait()
+
+
+def send_part(alive_count, scale, first, queries, key, val, pay_o, buffers):
+    heads = range(first, first + val.shape[0] // 128)
+    count = len(heads) * 64
     log_rows = []
 
     def emit(h, attended, logs):
+        h -= first
         pay_o[h * 64 : (h + 1) * 64, :] = attended.astype(bf16)
         log_rows.append(live(alive_count, logs))
 
-    attend(alive_count, scale, cand_q, count, count, key_o, val_o, emit)(buffers)
-    pay_o[width:, :] = pack_logs(jnp.concatenate(log_rows, axis=0))
-    for copy in copies:
-        copy.wait()
+    attend(alive_count, scale, heads, queries, key, val, emit)(buffers)
+    pay_o[count:, :] = pack_logs(jnp.concatenate(log_rows, axis=0))
+
+
+def send_kernel(here, scale, cand_a, cand_b, key, val, pay_o, *buffers):
+    first = val.shape[0] // 128
+    send_part(here[0:1, 0:1], scale, first, (cand_a, cand_b), key, val, pay_o, buffers)
 
 
 def live(alive_count, logs):
@@ -433,14 +455,15 @@
     return rows[:heads] + rows[heads : 2 * heads] + rows[2 * heads : 3 * heads]
 
 
-def keep_kernel(length, scale, cand_q, key, val, mean_o, logs_o, *buffers):
-    alive_count = length[...] - lax.axis_index("seq") * key.shape[0]
+def keep_kernel(here, scale, cand_a, cand_b, key, val, mean_o, logs_o, *buffers):
+    alive_count = here[0:1, 0:1]
 
     def emit(h, attended, logs):
         mean_o[h * 64 : (h + 1) * 64, :] = attended
         logs_o[h : h + 1, :] = live(alive_count, logs)
 
-    attend(alive_count, scale, cand_q, 0, mean_o.shape[1], key, val, emit)(buffers)
+    heads = range(val.shape[0] // 64)
+    attend(alive_count, scale, heads, (cand_a, cand_b), key, val, emit)(buffers)
 
 
 def over_heads(rows):
@@ -463,32 +486,36 @@
     return mean, peak + jnp.log2(total)
 
 
-def received(got, heads):
-    width = heads * 64
-    return got[:width, :].astype(f32), unpack_logs(got[width:, :], heads)
-
-
-def fold_kernel(mean, logs, got, mean_o, logs_o, pay_o):
+def received(gots, heads):
+    share = heads // len(gots)
+    means = [got[: share * 64, :].astype(f32) for got in gots]
+    logs = [unpack_logs(got[share * 64 :, :], share) for got in gots]
+    return jnp.concatenate(means, axis=0), jnp.concatenate(logs, axis=0)
+
+
+def fold_kernel(mean, logs, *refs):
+    gots, (mean_o, logs_o, pay_o) = refs[:-3], refs[-3:]
     heads, keep = logs_o.shape
     width = heads * 64
-    new_mean, new_logs = merge([(mean[...], logs[...]), received(got, heads)])
+    new_mean, new_logs = merge([(mean[...], logs[...]), received(gots, heads)])
     mean_o[...] = new_mean[:, :keep]
     logs_o[...] = new_logs[:, :keep]
     pay_o[:width, :] = new_mean[:, keep:].astype(bf16)
     pay_o[width:, :] = pack_logs(new_logs[:, keep:])
 
 
-def deal_kernel(mean, logs, got, mean_o, logs_o, *sends):
+def deal_kernel(blocks, mean, logs, *refs):
+    gots, mean_o, logs_o, sends = refs[:-5], refs[-5], refs[-4], refs[-3:]
     heads, cols = logs_o.shape
-    new_mean, new_logs = merge([(mean[...], logs[...]), received(got, heads)])
+    new_mean, new_logs = merge([(mean[...], logs[...]), received(gots, heads)])
     mean_o[...] = new_mean[:, :cols]
     logs_o[...] = new_logs[:, :cols]
     whole = jnp.concatenate([new_mean, pack_logs(new_logs).astype(f32)], axis=0)
     owned = whole.shape[1] // 4
     half = whole.shape[0] // 2
     low = first_half((1, LANES))
-    for k, send in enumerate(sends):
-        start = (k + 1) * owned
+    for block, send in zip(blocks, sends):
+        start = block * owned
         if 2 * owned == LANES:
             tile = whole[:, start // LANES * LANES : start // LANES * LANES + LANES]
             top, bottom = tile[:half], tile[half:]
@@ -520,12 +547,13 @@
 
 
 VMEM = pl.BlockSpec(memory_space=pltpu.VMEM)
+SMEM = pl.BlockSpec(memory_space=pltpu.SMEM)
 ANY = pl.BlockSpec(memory_space=pl.ANY)
 HBM = pl.BlockSpec(memory_space=pltpu.HBM)
 
 
-def call(kernel, name, operands, outs, scratch=(), after=(), flops=0, space=VMEM, spaces=None):
-    count = len(operands)
+def call(kernel, name, operands, outs, scratch=(), after=(), flops=0, space=VMEM, spaces=None, scalars=()):
+    count = len(scalars) + len(operands)
     if space is HBM:
         operands = [pltpu.with_memory_space_constraint(value, pltpu.HBM) for value in operands]
 
@@ -535,13 +563,13 @@
     return pl.pallas_call(
         body,
         name=name,
-        in_specs=[space] * count + [ANY] * len(after),
+        in_specs=[SMEM] * len(scalars) + [space] * len(operands) + [ANY] * len(after),
         out_specs=spaces or [VMEM] * len(outs),
         out_shape=outs,
         scratch_shapes=list(scratch),
         compiler_params=pltpu.CompilerParams(vmem_limit_bytes=VMEM_LIMIT),
         cost_estimate=pl.CostEstimate(flops=flops, transcendentals=0, bytes_accessed=0),
-    )(*operands, *after)
+    )(*scalars, *operands, *after)
 
 
 def reversed_bits(value, bits):
@@ -569,7 +597,7 @@
     seq = lax.axis_size("seq")
     bits = seq.bit_length() - 1
     assert users == 1 and lax.axis_size("dp") == 2 and seq == 1 << bits and bits > 2
-    assert width == heads * 64 and heads % 4 == 0 and owned <= 64
+    assert width == heads * 64 and heads % 4 == 0 and LANES % owned == 0 and owned <= 64
     pairs = heads // 2
     rows = pairs * 64
     cands = owned * seq
@@ -578,13 +606,10 @@
         return lax.ppermute(value, "seq", [(j, j ^ mask) for j in range(seq)])
 
     peer = lax.ppermute(item_embedding_table, "dp", [(0, 1), (1, 0)])
-    far_ids = swap(candidate_item_index, seq // 2)
-    length = user_history_length.reshape(1, 1)
     scale = head_score_scale.reshape(1, heads)
     stored = item_stored_row.reshape(-1, LANES)
     decay = log_head_retention.reshape(heads, n)
-    ids = jnp.concatenate([candidate_item_index, far_ids], axis=0)
-    ids = jnp.pad(ids, ((0, 0), (0, 64 - owned)))
+    ids = jnp.pad(candidate_item_index, ((0, 0), (0, 64 - owned)))
     id_rows = jnp.concatenate([ids // LANES, ids % LANES], axis=1).astype(f32)
 
     part, slot, crow, ccol, ctl, key_w = call(
@@ -601,18 +626,20 @@
         [
             pltpu.VMEM((1, n), i32), pltpu.VMEM(stored.shape, i32), pltpu.VMEM((heads, n), f32),
             pltpu.VMEM((half, width), bf16), pltpu.VMEM((width, width), bf16),
-            pltpu.SemaphoreType.DMA((5,)),
+            pltpu.SemaphoreType.DMA((6,)),
         ],
         space=HBM,
         flops=2 * n * half * width,
     )
-    emb, key, val, enter, pay = call(
+    emb, key, val, enter, pay, here = call(
         summary_kernel, "summary",
-        [length, part, peer, slot, crow, ctl, id_rows, key_w, history_query_key_value_weight],
+        [part, peer, slot, crow, ctl, id_rows, key_w, history_query_key_value_weight],
         [
             shape((n, width), bf16), shape((width, n), bf16), shape((n, width), bf16),
-            shape((n // CHUNK, rows, LANES), f32), shape((state_rows(pairs, 2), LANES), bf16),
+            shape((n // CHUNK, rows, LANES), f32), shape((state_rows(pairs, 1), LANES), bf16),
+            shape((8, LANES), i32),
         ],
+        scalars=[user_history_length],
         flops=2 * n * half * width,
     )
 
@@ -630,76 +657,85 @@
         got = swap(pay, 1 << bit)
         if bit == 1:
             early.append(local(width // 2, "local_b", [prefix]))
-        count = 2 << bit
-        final = bit == bits - 2
-        sent = 1 if final else 2 * count
-        pay, prefix, logs, *id_rows = call(
+        count = 1 << bit
+        pay, prefix, logs = call(
             lambda *refs, bit=bit, count=count: join_kernel(bit, count, pairs, *refs), "join",
             [pay, got] + ([prefix, logs] if bit else []),
             [
-                shape((state_rows(pairs, sent), LANES), bf16), shape((rows, LANES), f32),
+                shape((state_rows(pairs, 2 * count), LANES), bf16), shape((rows, LANES), f32),
                 shape((pairs, LANES), f32),
-            ] + [shape((2 * count, LANES), f32)] * final,
+            ],
             after=[early[-1][1]],
         )
     got = swap(pay, 1 << (bits - 1))
-    half_seq = seq // 2
-    places = {}
-    for j in range(seq):
-        places[(j & 1) * half_seq + (j >> 1)] = j
-    order = [places[reversed_bits(j, bits)] for j in range(seq)]
-    cand_q, val_w = call(
-        lambda *refs: candidate_kernel(order, owned, *refs), "candidates",
-        [
-            id_rows[0], stored, item_embedding_table, peer, candidate_query_weight,
-            candidate_key_value_weight,
-        ],
-        [shape((width, cands), bf16), shape((width, width), bf16)],
-        flops=2 * cands * 2 * half * width,
-    )
+    order = [reversed_bits(j, bits) for j in range(seq)]
+    half_order = list(range(seq // 2))
+    if seq == 8:
+        half_order = [0, 2, 1, 3]
+        order = [0, 2, 4, 6, 1, 3, 5, 7]
+    quarter = cands // 4
+
+    def candidates(message, name, pair_w):
+        return call(
+            lambda *refs: candidate_kernel(half_order, owned, *refs), name,
+            [message, stored, item_embedding_table, peer, candidate_query_weight, *pair_w],
+            [shape((width, quarter), bf16)] * 2 + [shape((width, width), bf16)] * len(pair_w),
+            flops=cands * 2 * half * width,
+        )
+
+    keep_a, send_a, val_w = candidates(pay, "near", [candidate_key_value_weight])
+    keep_b, send_b = candidates(got, "far", [])
+    if seq != 8:
+        every = jnp.concatenate([keep_a, send_a, keep_b, send_b], axis=1)
+        every = every.reshape(width, seq, owned)[:, jnp.array(order)].reshape(width, cands)
+        keep_a, keep_b, send_a, send_b = (
+            every[:, k * quarter : (k + 1) * quarter] for k in range(4)
+        )
     (query_a, intra_a), (query_b, intra_b) = early
     send = cands // 2
     buffers = [pltpu.VMEM((n, send), f32)] * 2
     message = width + log_pad(heads)
-    hist, key_two, val_two, pay = call(
+    share = width // 2 + log_pad(heads // 2)
+    hist, key_two, val_two, pay_a = call(
         lambda *refs: finish_kernel(bits - 1, *refs), "finish",
         [
-            length, scale, emb, query_a, query_b, intra_a, intra_b, enter, ctl, got, prefix, logs,
-            history_output_weight, candidate_key_value_weight, val_w, cand_q,
+            here, scale, emb, query_a, query_b, intra_a, intra_b, enter, ctl, got, prefix, logs,
+            history_output_weight, candidate_key_value_weight, val_w, send_a, send_b,
         ],
         [
             shape((n, width), f32), shape((n, width), bf16), shape((width, n), bf16),
-            shape((message, send), bf16),
+            shape((share, send), bf16),
         ],
         [pltpu.VMEM((n, width), f32), pltpu.SemaphoreType.DMA((n // CHUNK,))] + buffers,
         spaces=[ANY, VMEM, VMEM, VMEM],
         flops=2 * n * half * width,
     )
+    (pay_b,) = call(
+        send_kernel, "send", [here, scale, send_a, send_b, key_two, val_two],
+        [shape((share, send), bf16)], buffers, flops=n * half * width,
+    )
+    gots = [swap(pay_a, 1), swap(pay_b, 1)]
     mean, logs = call(
-        keep_kernel, "keep", [length, scale, cand_q, key_two, val_two],
-        [shape((width, send), f32), shape((heads, send), f32)],
-        buffers,
+        keep_kernel, "keep", [here, scale, keep_a, keep_b, key_two, val_two],
+        [shape((width, send), f32), shape((heads, send), f32)], buffers, after=[pay_b],
         flops=2 * n * half * width,
     )
-    for bit in range(bits - 3):
-        got = swap(pay, 1 << bit)
+    for bit in range(1, bits - 2):
         send //= 2
         mean, logs, pay = call(
-            fold_kernel, "fold", [mean, logs, got],
+            fold_kernel, "fold", [mean, logs, *gots],
             [shape((width, send), f32), shape((heads, send), f32), shape((message, send), bf16)],
         )
-    got = swap(pay, 1 << (bits - 3))
+        gots = [swap(pay, 1 << bit)]
     packed = 2 * owned == LANES
     cols = LANES if packed else owned
+    blocks = [2, 3, 1] if seq == 8 else [1, 3, 2]
     mean, logs, *sends = call(
-        deal_kernel, "deal", [mean, logs, got],
+        lambda *refs: deal_kernel(blocks, *refs), "deal", [mean, logs, *gots],
         [shape((width, cols), f32), shape((heads, cols), f32)]
         + [shape((message // 2, LANES) if packed else (message, owned), bf16)] * 3,
     )
-    masks = [seq // 2, seq // 4, seq // 2 + seq // 4]
-    gots = [None] * 3
-    for k in (0, 2, 1):
-        gots[k] = swap(sends[k], masks[k])
+    gots = [swap(value, order[block]) for value, block in zip(sends, blocks)]
     (cand_out,) = call(
         lambda *refs: last_kernel(owned, *refs), "last",
         [mean, logs, *gots, candidate_output_weight],

time: 51.9 us -> 52.6 us (1.013)
  waiting for transfers between devices: 8.41 us -> 7.11 us
  starting transfers between devices: 13.8 us -> 14.6 us
  other arithmetic: 0.09 us -> 0.74 us
    ppermute x8, waiting for transfers between devices: 8.41 us -> 7.1 us  [swap(): return lax.ppermute(value, 'seq', [(j, j ^ mask) for j in range(seq)])]
    ppermute x8, starting transfers between devices: 13.3 us -> 14.1 us  [swap(): return lax.ppermute(value, 'seq', [(j, j ^ mask) for j in range(seq)])]
    select_n x1, other arithmetic: 0.02 us -> 0.67 us  [shards(): id_rows = jnp.concatenate([ids // LANES, ids % LANES], axis=1).astype(f32)]
    pallas_call x11 -> x13, Pallas kernels: 28 us -> 28.5 us  [call(): pl.pallas_call(body, name=name, in_specs=[SMEM] * len(scalars) + [space]...]
  transfers between devices with their start and end apart: 9 -> 9, of which waited for: 6 -> 6; matrix products, arithmetic and copies ran while one was open for 0% -> 1% of each run, Pallas kernels for 31% -> 28%
where the time goes in v6:
time: 52.6 us; the launch traced here: 52.4 us
  Pallas kernels  28.5 us (54%)
  starting transfers between devices  14.6 us (28%)
  waiting for transfers between devices  7.11 us (14%)
  between operations  1.44 us (3%)
  other arithmetic  0.74 us (1%)
    pallas_call x13, Pallas kernels, call(): pl.pallas_call(body, name=name, in_specs=[SMEM] * len(scalars) + [space]...  28.5 us
    ppermute x8, starting transfers between devices, swap(): return lax.ppermute(value, 'seq', [(j, j ^ mask) for j in range(seq)])  14.1 us
    ppermute x8, waiting for transfers between devices, swap(): return lax.ppermute(value, 'seq', [(j, j ^ mask) for j in range(seq)])  7.1 us
  transfers between devices with their start and end apart: 9, of which 6 were waited for; matrix products, arithmetic and copies ran while one was open for 1% of the time, Pallas kernels for 28%

profile of v6, /device:TPU:0, one launch (start us, length us, event | category | flops | bytes accessed | tf_op | source)
XLA Modules:
  0.0 52.4 jit_solution(8603544295882746027)
XLA Ops:
  0.6 0.5 collective-permute-start
  1.8 0.7 %and_select_fusion.1 = (s32[1,64]{1,0:T(1,128)S(1)}, s32[1,64]{1,0:T(1,128)S(1)}) fusion(s32[1,64]{1,0:T(1,128)} %param.15), kind=kLoop, calls=%fused_computation.1 | loop fusion | flops 1216 | bytes 768 | tf_op jit(solution)/shard_map/jit(floor_divide)/jit(_where)/select_n | solution.py:613
  2.5 0.1 add_convert_fusion.refs_6_
  2.5 4.5 %own_rows.1 = (bf16[1024,512]{1,0:T(8,128)(2,1)S(1)}, f32[1,1024]{1,0:T(1,128)S(1)}, f32[4,8,256]{2,1,0:T(8,128)S(1)}, f32[1024,16]{1,0:T(8,128)S(1)}, f32[16,12...) custom-call(s32[1,1024]{1,0:T(1,128)} %refs_0_.2, s32[32,128]{1,0:T(8,128)} %bitcast.5, f32[8,1024]{1,0:T(8,128)} %bitcast.12, ...), custom_call_target="tpu_custom_call" | custom-call | flops 2147483648 | tf_op jit(solution)/shard_map/own_rows/pallas_call | solution.py:563
  7.1 0.0 collective-permute-done.refs_2_.refs_3_
  7.1 0.0 copy-done.1
  7.1 4.4 %summary.1 = (bf16[1024,512]{1,0:T(8,128)(2,1)S(1)}, bf16[512,1024]{1,0:T(8,128)(2,1)S(1)}, bf16[1024,512]{1,0:T(8,128)(2,1)S(1)}, f32[4,256,128]{2,1,0:T(8,128)...) custom-call(s32[1]{0:T(128)S(6)} %copy.14.refs_0_, bf16[1024,512]{1,0:T(8,128)(2,1)S(1)} %get-tuple-element.40.refs_1_, ...), custom_call_target="tpu_custom_call" | custom-call | flops 2147483648 | tf_op jit(solution)/shard_map/summary/pallas_call | solution.py:563
  11.5 2.6 %collective-permute-start.1 = (bf16[272,128]{1,0:T(8,128)(2,1)S(1)}, bf16[272,128]{1,0:T(8,128)(2,1)S(1)}, u32[]{:S(2)}, u32[]{:S(2)}) collective-permute-start(bf16[272,128]{1,0:T(8,128)(2,1)S(1)} %get-tuple-element.51.refs_0_), channel_id=1, source_target_pairs={{0,2},{2,0},{4,6},{6,4},{8,10},{10,8},{12,14},{14,12},{1,3},{3,1},... | collective-permute-start | bytes 208904 | tf_op jit(solution)/shard_map/ppermute | solution.py:606
  14.1 2.7 %local_a.1 = (bf16[1024,256]{1,0:T(8,128)(2,1)S(1)}, f32[1024,256]{1,0:T(8,128)S(1)}) custom-call(bf16[1024,512]{1,0:T(8,128)(2,1)S(1)} %get-tuple-element.46.refs_0_.refs_2_, bf16[512,1024]{1,0:T(8,128)(2,1)S(1)} %get-tuple-element.47.refs_1_, bf16[1024,512]{1,0:T(8,128)(2,1)S(1)} %get-tuple-element.48.refs_2_, ...), custom_call_target="tpu_custom_call" | custom-call | flops 1073741824 | tf_op jit(solution)/shard_map/local_a/pallas_call | solution.py:563
  16.8 0.2 collective-permute-done.1.refs_1_
  16.9 0.1 join.2
  17.0 1.9 %collective-permute-start.2 = (bf16[272,128]{1,0:T(8,128)(2,1)S(1)}, bf16[272,128]{1,0:T(8,128)(2,1)S(1)}, u32[]{:S(2)}, u32[]{:S(2)}) collective-permute-start(bf16[272,128]{1,0:T(8,128)(2,1)S(1)} %get-tuple-element.57.refs_0_), channel_id=1, source_target_pairs={{0,4},{2,6},{4,0},{6,2},{8,12},{10,14},{12,8},{14,10},{1,5},{3,7},... | collective-permute-start | bytes 208904 | tf_op jit(solution)/shard_map/ppermute | solution.py:606
  18.9 0.0 copy-start
  18.9 0.0 copy-start.2
  18.9 0.0 copy-start.3
  18.9 0.0 copy-start.5
  18.9 2.8 %local_b.1 = (bf16[1024,256]{1,0:T(8,128)(2,1)S(1)}, f32[1024,256]{1,0:T(8,128)S(1)}) custom-call(bf16[1024,512]{1,0:T(8,128)(2,1)S(1)} %get-tuple-element.46.refs_0_.refs_2_, bf16[512,1024]{1,0:T(8,128)(2,1)S(1)} %get-tuple-element.47.refs_1_, bf16[1024,512]{1,0:T(8,128)(2,1)S(1)} %get-tuple-element.48.refs_2_, ...), custom_call_target="tpu_custom_call" | custom-call | flops 1073741824 | tf_op jit(solution)/shard_map/local_b/pallas_call | solution.py:563
  21.7 0.0 collective-permute-done.2.refs_1_
  21.7 0.1 join.3
  21.8 2.7 %collective-permute-start.3 = (bf16[272,128]{1,0:T(8,128)(2,1)S(1)}, bf16[272,128]{1,0:T(8,128)(2,1)S(1)}, u32[]{:S(2)}, u32[]{:S(2)}) collective-permute-start(bf16[272,128]{1,0:T(8,128)(2,1)S(1)} %get-tuple-element.59.refs_0_), channel_id=1, source_target_pairs={{0,8},{2,10},{4,12},{6,14},{8,0},{10,2},{12,4},{14,6},{1,9},{3,11}... | collective-permute-start | bytes 208904 | tf_op jit(solution)/shard_map/ppermute | solution.py:606
  24.5 0.0 copy-done
  24.5 0.0 copy-done.2
  24.5 0.0 copy-done.3
  24.5 0.0 copy-done.5
  24.5 1.9 %near.1 = (bf16[512,128]{1,0:T(8,128)(2,1)S(1)}, bf16[512,128]{1,0:T(8,128)(2,1)S(1)}, bf16[512,512]{1,0:T(8,128)(2,1)S(1)}) custom-call(bf16[272,128]{1,0:T(8,128)(2,1)S(1)} %get-tuple-element.59.refs_0_, s32[32,128]{1,0:T(8,128)S(1)} %bitcast.6, bf16[2048,512]{1,0:T(8,128)(2,1)S(1)} %copy-done, bf16[2048,512]{1,0:T(8,128)(2,1)S(1)} %collective-permute-done.refs_2_.refs_3_, ...), custom_call_target="tpu_custom_call" | custom-call | flops 1073741824 | tf_op jit(solution)/shard_map/near/pallas_call | solution.py:563
  26.4 0.0 copy-start.6
  26.4 0.0 copy-start.7
  26.4 0.7 %collective-permute-done.3.refs_0_.refs_9_ = bf16[272,128]{1,0:T(8,128)(2,1)S(1)} collective-permute-done((bf16[272,128]{1,0:T(8,128)(2,1)S(1)}, bf16[272,128]{1,0:T(8,128)(2,1)S(1)}, u32[]{:S(2)}, u32[]{:S(2)}) %collective-permute-start.3) | collective-permute-done | bytes 69664 | tf_op jit(solution)/shard_map/ppermute | solution.py:606
  27.1 1.9 %far.1 = (bf16[512,128]{1,0:T(8,128)(2,1)S(1)}, bf16[512,128]{1,0:T(8,128)(2,1)S(1)}) custom-call(bf16[272,128]{1,0:T(8,128)(2,1)S(1)} %collective-permute-done.3.refs_0_.refs_9_, s32[32,128]{1,0:T(8,128)S(1)} %bitcast.7, bf16[2048,512]{1,0:T(8,128)(2,1)S(1)} %copy-done, bf16[2048,512]{1,0:T(8,128)(2,1)S(1)} %collective-permute-done.refs_2_.refs_3_, ...), custom_call_target="tpu_custom_call" | custom-call | flops 1073741824 | tf_op jit(solution)/shard_map/far/pallas_call | solution.py:563
  29.0 0.0 copy-done.6
  29.0 0.0 copy-done.7
  29.1 4.6 %finish.1 = (f32[1024,512]{1,0:T(8,128)}, bf16[1024,512]{1,0:T(8,128)(2,1)S(1)}, bf16[512,1024]{1,0:T(8,128)(2,1)S(1)}, bf16[272,256]{1,0:T(8,128)(2,1)S(1)}) custom-call(s32[8,128]{1,0:T(8,128)S(1)} %get-tuple-element.45.refs_0_, f32[1,8]{1,0:T(1,128)S(1)} %bitcast.8, bf16[1024,512]{1,0:T(8,128)(2,1)S(1)} %get-tuple-element.46.refs_0_.refs_2_, ...), custom_call_target="tpu_custom_call" | custom-call | flops 2147483648 | tf_op jit(solution)/shard_map/finish/pallas_call | solution.py:563
  33.6 1.5 %collective-permute-start.4 = (bf16[272,256]{1,0:T(8,128)(2,1)S(1)}, bf16[272,256]{1,0:T(8,128)(2,1)S(1)}, u32[]{:S(2)}, u32[]{:S(2)}) collective-permute-start(bf16[272,256]{1,0:T(8,128)(2,1)S(1)} %get-tuple-element.72), channel_id=1, source_target_pairs={{0,2},{2,0},{4,6},{6,4},{8,10},{10,8},{12,14},{14,12},{1,3},{3,1},... | collective-permute-start | bytes 417800 | tf_op jit(solution)/shard_map/ppermute | solution.py:606
  35.2 1.5 %send.1.refs_6_ = bf16[272,256]{1,0:T(8,128)(2,1)S(1)} custom-call(s32[8,128]{1,0:T(8,128)S(1)} %get-tuple-element.45.refs_0_, f32[1,8]{1,0:T(1,128)S(1)} %bitcast.9, bf16[512,128]{1,0:T(8,128)(2,1)S(1)} %get-tuple-element.63.refs_15_.refs_2_, bf16[512,128]{1,0:T(8,128)(2,1)S(1)} %get-tuple-element.64.refs_16_.refs_3_, ...), custom_call_target="tpu_custom_call" | custom-call | flops 1073741824 | tf_op jit(solution)/shard_map/send/pallas_call | solution.py:563
  36.7 0.6 %collective-permute-start.5 = (bf16[272,256]{1,0:T(8,128)(2,1)S(1)}, bf16[272,256]{1,0:T(8,128)(2,1)S(1)}, u32[]{:S(2)}, u32[]{:S(2)}) collective-permute-start(bf16[272,256]{1,0:T(8,128)(2,1)S(1)} %send.1.refs_6_), channel_id=1, source_target_pairs={{0,2},{2,0},{4,6},{6,4},{8,10},{10,8},{12,14},{14,12},{1,3},{3,1},... | collective-permute-start | bytes 417800 | tf_op jit(solution)/shard_map/ppermute | solution.py:606
  37.3 0.0 copy-start.4
  37.3 2.8 %keep.1 = (f32[512,256]{1,0:T(8,128)S(1)}, f32[8,256]{1,0:T(8,128)S(1)}) custom-call(s32[8,128]{1,0:T(8,128)S(1)} %get-tuple-element.45.refs_0_, f32[1,8]{1,0:T(1,128)S(1)} %bitcast.10, bf16[512,128]{1,0:T(8,128)(2,1)S(1)} %get-tuple-element.66.refs_2_, bf16[512,128]{1,0:T(8,128)(2,1)S(1)} %get-tuple-element.67.refs_3_, ...), custom_call_target="tpu_custom_call" | custom-call | flops 2147483648 | tf_op jit(solution)/shard_map/keep/pallas_call | solution.py:563
  40.1 0.0 collective-permute-done.4.refs_2_
  40.1 1.7 %collective-permute-done.5.refs_3_ = bf16[272,256]{1,0:T(8,128)(2,1)S(1)} collective-permute-done((bf16[272,256]{1,0:T(8,128)(2,1)S(1)}, bf16[272,256]{1,0:T(8,128)(2,1)S(1)}, u32[]{:S(2)}, u32[]{:S(2)}) %collective-permute-start.5) | collective-permute-done | bytes 139296 | tf_op jit(solution)/shard_map/ppermute | solution.py:606
  41.8 0.2 deal.1
  42.0 2.7 %collective-permute-start.6 = (bf16[272,128]{1,0:T(8,128)(2,1)S(1)}, bf16[272,128]{1,0:T(8,128)(2,1)S(1)}, u32[]{:S(2)}, u32[]{:S(2)}) collective-permute-start(bf16[272,128]{1,0:T(8,128)(2,1)S(1)} %get-tuple-element.75), channel_id=1, source_target_pairs={{0,8},{2,10},{4,12},{6,14},{8,0},{10,2},{12,4},{14,6},{1,9},{3,11}... | collective-permute-start | bytes 208904 | tf_op jit(solution)/shard_map/ppermute | solution.py:606
  44.7 1.6 %collective-permute-start.7 = (bf16[272,128]{1,0:T(8,128)(2,1)S(1)}, bf16[272,128]{1,0:T(8,128)(2,1)S(1)}, u32[]{:S(2)}, u32[]{:S(2)}) collective-permute-start(bf16[272,128]{1,0:T(8,128)(2,1)S(1)} %get-tuple-element.76), channel_id=1, source_target_pairs={{0,12},{2,14},{4,8},{6,10},{8,4},{10,6},{12,0},{14,2},{1,13},{3,15... | collective-permute-start | bytes 208904 | tf_op jit(solution)/shard_map/ppermute | solution.py:606
  46.3 0.5 collective-permute-start.8
  46.8 0.4 collective-permute-done.6.refs_2_
  47.2 3.7 %collective-permute-done.7.refs_3_ = bf16[272,128]{1,0:T(8,128)(2,1)S(1)} collective-permute-done((bf16[272,128]{1,0:T(8,128)(2,1)S(1)}, bf16[272,128]{1,0:T(8,128)(2,1)S(1)}, u32[]{:S(2)}, u32[]{:S(2)}) %collective-permute-start.7) | collective-permute-done | bytes 69664 | tf_op jit(solution)/shard_map/ppermute | solution.py:606
  51.0 0.4 collective-permute-done.8.refs_4_
  51.4 0.0 copy-done.4
  51.4 1.0 %last.1 = f32[64,512]{1,0:T(8,128)} custom-call(f32[512,128]{1,0:T(8,128)S(1)} %get-tuple-element.73.refs_0_, f32[8,128]{1,0:T(8,128)S(1)} %get-tuple-element.74.refs_1_, bf16[272,128]{1,0:T(8,128)(2,1)S(1)} %collective-permute-done.6.refs_2_, bf16[272,128]{1,0:T(8,128)(2,1)S(1)} %collective-permute-done.7.refs_3_, ...), custom_call_target="tpu_custom_call" | custom-call | tf_op jit(solution)/shard_map/last/pallas_call | solution.py:563
  (1 shorter events, 0.0 us)
Async XLA Ops:
  0.6 6.4 %collective-permute-start = (bf16[2048,512]{1,0:T(8,128)(2,1)}, bf16[2048,512]{1,0:T(8,128)(2,1)S(1)}, u32[]{:S(2)}, u32[]{:S(2)}) collective-permute-start(bf16[2048,512]{1,0:T(8,128)(2,1)} %refs_2_.3), channel_id=1, source_target_pairs={{0,1},{1,0},{2,3},{3,2},{4,5},{5,4},{6,7},{7,6},{8,9},{9,8},{10,11... | collective-permute-start | bytes 6291464 | tf_op jit(solution)/shard_map/ppermute | solution.py:608
  2.5 4.5 %copy-start.1 = (bf16[512,1536]{1,0:T(8,128)(2,1)S(1)}, bf16[512,1536]{1,0:T(8,128)(2,1)}, u32[]{:S(2)}) copy-start(bf16[512,1536]{1,0:T(8,128)(2,1)} %refs_5_.5) | copy-start | bytes 4718596
  11.5 5.4 %collective-permute-start.1 = (bf16[272,128]{1,0:T(8,128)(2,1)S(1)}, bf16[272,128]{1,0:T(8,128)(2,1)S(1)}, u32[]{:S(2)}, u32[]{:S(2)}) collective-permute-start(bf16[272,128]{1,0:T(8,128)(2,1)S(1)} %get-tuple-element.51.refs_0_), channel_id=1, source_target_pairs={{0,2},{2,0},{4,6},{6,4},{8,10},{10,8},{12,14},{14,12},{1,3},{3,1},... | collective-permute-start | bytes 208904 | tf_op jit(solution)/shard_map/ppermute | solution.py:606
  17.0 4.7 %collective-permute-start.2 = (bf16[272,128]{1,0:T(8,128)(2,1)S(1)}, bf16[272,128]{1,0:T(8,128)(2,1)S(1)}, u32[]{:S(2)}, u32[]{:S(2)}) collective-permute-start(bf16[272,128]{1,0:T(8,128)(2,1)S(1)} %get-tuple-element.57.refs_0_), channel_id=1, source_target_pairs={{0,4},{2,6},{4,0},{6,2},{8,12},{10,14},{12,8},{14,10},{1,5},{3,7},... | collective-permute-start | bytes 208904 | tf_op jit(solution)/shard_map/ppermute | solution.py:606
  18.9 5.6 %copy-start = (bf16[2048,512]{1,0:T(8,128)(2,1)S(1)}, bf16[2048,512]{1,0:T(8,128)(2,1)}, u32[]{:S(2)}) copy-start(bf16[2048,512]{1,0:T(8,128)(2,1)} %refs_2_.3) | copy-start | bytes 6291460
  18.9 5.6 %copy-start.2 = (bf16[512,512]{1,0:T(8,128)(2,1)S(1)}, bf16[512,512]{1,0:T(8,128)(2,1)}, u32[]{:S(2)}) copy-start(bf16[512,512]{1,0:T(8,128)(2,1)} %refs_4_.5) | copy-start | bytes 1572868
  18.9 5.6 %copy-start.3 = (bf16[512,1024]{1,0:T(8,128)(2,1)S(1)}, bf16[512,1024]{1,0:T(8,128)(2,1)}, u32[]{:S(2)}) copy-start(bf16[512,1024]{1,0:T(8,128)(2,1)} %refs_13_.1) | copy-start | bytes 3145732
  18.9 5.6 %copy-start.5 = (s32[4096]{0:T(1024)S(1)}, s32[4096]{0:T(1024)}, u32[]{:S(2)}) copy-start(s32[4096]{0:T(1024)} %param.16) | copy-start | bytes 49156
  21.8 5.3 %collective-permute-start.3 = (bf16[272,128]{1,0:T(8,128)(2,1)S(1)}, bf16[272,128]{1,0:T(8,128)(2,1)S(1)}, u32[]{:S(2)}, u32[]{:S(2)}) collective-permute-start(bf16[272,128]{1,0:T(8,128)(2,1)S(1)} %get-tuple-element.59.refs_0_), channel_id=1, source_target_pairs={{0,8},{2,10},{4,12},{6,14},{8,0},{10,2},{12,4},{14,6},{1,9},{3,11}... | collective-permute-start | bytes 208904 | tf_op jit(solution)/shard_map/ppermute | solution.py:606
  26.4 2.6 %copy-start.6 = (bf16[512,512]{1,0:T(8,128)(2,1)S(1)}, bf16[512,512]{1,0:T(8,128)(2,1)}, u32[]{:S(2)}) copy-start(bf16[512,512]{1,0:T(8,128)(2,1)} %refs_12_.1) | copy-start | bytes 1572868
  26.4 2.6 %copy-start.7 = (f32[8]{0:T(128)S(1)}, f32[8]{0:T(128)}, u32[]{:S(2)}) copy-start(f32[8]{0:T(128)} %param.18) | copy-start | bytes 100
  33.6 6.5 %collective-permute-start.4 = (bf16[272,256]{1,0:T(8,128)(2,1)S(1)}, bf16[272,256]{1,0:T(8,128)(2,1)S(1)}, u32[]{:S(2)}, u32[]{:S(2)}) collective-permute-start(bf16[272,256]{1,0:T(8,128)(2,1)S(1)} %get-tuple-element.72), channel_id=1, source_target_pairs={{0,2},{2,0},{4,6},{6,4},{8,10},{10,8},{12,14},{14,12},{1,3},{3,1},... | collective-permute-start | bytes 417800 | tf_op jit(solution)/shard_map/ppermute | solution.py:606
  36.7 5.1 %collective-permute-start.5 = (bf16[272,256]{1,0:T(8,128)(2,1)S(1)}, bf16[272,256]{1,0:T(8,128)(2,1)S(1)}, u32[]{:S(2)}, u32[]{:S(2)}) collective-permute-start(bf16[272,256]{1,0:T(8,128)(2,1)S(1)} %send.1.refs_6_), channel_id=1, source_target_pairs={{0,2},{2,0},{4,6},{6,4},{8,10},{10,8},{12,14},{14,12},{1,3},{3,1},... | collective-permute-start | bytes 417800 | tf_op jit(solution)/shard_map/ppermute | solution.py:606
  37.3 14.1 %copy-start.4 = (bf16[512,512]{1,0:T(8,128)(2,1)S(1)}, bf16[512,512]{1,0:T(8,128)(2,1)}, u32[]{:S(2)}) copy-start(bf16[512,512]{1,0:T(8,128)(2,1)} %refs_5_.7) | copy-start | bytes 1572868
  42.0 5.3 %collective-permute-start.6 = (bf16[272,128]{1,0:T(8,128)(2,1)S(1)}, bf16[272,128]{1,0:T(8,128)(2,1)S(1)}, u32[]{:S(2)}, u32[]{:S(2)}) collective-permute-start(bf16[272,128]{1,0:T(8,128)(2,1)S(1)} %get-tuple-element.75), channel_id=1, source_target_pairs={{0,8},{2,10},{4,12},{6,14},{8,0},{10,2},{12,4},{14,6},{1,9},{3,11}... | collective-permute-start | bytes 208904 | tf_op jit(solution)/shard_map/ppermute | solution.py:606
  44.7 6.3 %collective-permute-start.7 = (bf16[272,128]{1,0:T(8,128)(2,1)S(1)}, bf16[272,128]{1,0:T(8,128)(2,1)S(1)}, u32[]{:S(2)}, u32[]{:S(2)}) collective-permute-start(bf16[272,128]{1,0:T(8,128)(2,1)S(1)} %get-tuple-element.76), channel_id=1, source_target_pairs={{0,12},{2,14},{4,8},{6,10},{8,4},{10,6},{12,0},{14,2},{1,13},{3,15... | collective-permute-start | bytes 208904 | tf_op jit(solution)/shard_map/ppermute | solution.py:606
  46.3 5.1 %collective-permute-start.8 = (bf16[272,128]{1,0:T(8,128)(2,1)S(1)}, bf16[272,128]{1,0:T(8,128)(2,1)S(1)}, u32[]{:S(2)}, u32[]{:S(2)}) collective-permute-start(bf16[272,128]{1,0:T(8,128)(2,1)S(1)} %get-tuple-element.77), channel_id=1, source_target_pairs={{0,4},{2,6},{4,0},{6,2},{8,12},{10,14},{12,8},{14,10},{1,5},{3,7},... | collective-permute-start | bytes 208904 | tf_op jit(solution)/shard_map/ppermute | solution.py:606

commit v7 on v6

--- a/solution.py
+++ b/solution.py
@@ -93,8 +93,9 @@
 
 
 def own_rows_kernel(
-    ids_in, stored_in, decay_in, own_in, weight_in, part_o, slot_o, crow_o, ccol_o, ctl_o, key_w_o,
-    ids, stored, decay, own, key_w, sem,
+    ids_in, stored_in, decay_in, own_in, weight_in, cand_in,
+    part_o, slot_o, crow_o, ccol_o, ctl_o, key_w_o, id_rows_o,
+    ids, stored, decay, own, key_w, cand, sem,
 ):
     n, half, heads = ids.shape[1], own.shape[0], decay.shape[0]
     width = own.shape[1]
@@ -105,7 +106,7 @@
             (
                 (ids_in, ids), (stored_in, stored), (decay_in, decay), (middle, key_w),
                 (own_in.at[: half // 2], own.at[: half // 2]),
-                (own_in.at[half // 2 :], own.at[half // 2 :]),
+                (own_in.at[half // 2 :], own.at[half // 2 :]), (cand_in, cand),
             )
         )
     ]
@@ -115,6 +116,11 @@
     copies[1].wait()
     slots = stored_slots(ids[...], stored[...])
     slot_o[...] = slots
+    copies[6].wait()
+    wide = jnp.concatenate([cand[...], jnp.zeros((1, LANES - cand.shape[1]), i32)], axis=1).astype(f32)
+    high = jnp.floor(wide * (1.0 / LANES))
+    low = pltpu.roll(jnp.broadcast_to(wide - high * LANES, (8, LANES)), LANES // 2, 1)[:1]
+    id_rows_o[...] = jnp.where(first_half((1, LANES)), high, low)
     copies[2].wait()
     upto = jnp.where(
         iota((CHUNK, CHUNK), 0) <= iota((CHUNK, CHUNK), 1), 1.0, 0.0
@@ -283,15 +289,15 @@
             intra_o[chunk(i), pair_cut(p)] = held + part
 
 
-def candidate_kernel(order, owned, message, stored, own, peer, query_w, *refs):
+def candidate_queries(ids, owned, message, stored, own, peer, query_w):
     half, width = own.shape
     pairs = width // LANES
-    ids = message[pairs * 64 :, :].astype(f32)
-    ids = (ids * float(LANES) + pltpu.roll(ids, LANES // 2, 1)).astype(i32)
-    slots = [stored_slots(ids[3 * pairs + j : 3 * pairs + j + 1], stored[...]) for j in order]
+    rows = message[pairs * 64 :, :].astype(f32)
+    rows = (rows * float(LANES) + pltpu.roll(rows, LANES // 2, 1)).astype(i32)[3 * pairs :]
+    slots = [stored_slots(rows[j : j + 1], stored[...]) for j in range(ids)]
     step = LANES // owned
     tiles = []
-    for start in range(0, len(order), step):
+    for start in range(0, ids, step):
         tile = slots[start]
         for k in range(1, step):
             moved = pltpu.roll(slots[start + k], k * owned, 1)
@@ -299,71 +305,85 @@
         tiles.append(tile)
     slots = jnp.concatenate(tiles, axis=1)
     dp = lax.axis_index("dp")
-    rows = picked_rows(slots, dp * half, own) + picked_rows(slots, (1 - dp) * half, peer)
-    query = jnp.transpose(dot(rows.astype(bf16), query_w[...])).astype(bf16)
-    if len(refs) > 2:
-        pair_w, *refs, val_w_o = refs
-        val_w_o[...] = jnp.transpose(pair_w[:, width:].astype(f32)).astype(bf16)
-    part = query.shape[1] // 2
-    refs[0][...] = query[:, :part]
-    refs[1][...] = query[:, part:]
-
-
-def attend(alive_count, scale, heads, queries, key, val, emit):
-    n = key.shape[0]
-    cols = sum(query.shape[1] for query in queries)
+    found = picked_rows(slots, dp * half, own) + picked_rows(slots, (1 - dp) * half, peer)
+    return jnp.transpose(dot(found.astype(bf16), query_w[...]))
+
+
+def near_kernel(ids, owned, message, stored, own, peer, query_w, pair_w, query_o, val_w_o):
+    query = candidate_queries(ids, owned, message, stored, own, peer, query_w)
+    query_o[...] = query.astype(bf16)
+    val_w_o[...] = jnp.transpose(pair_w[:, own.shape[1] :].astype(f32)).astype(bf16)
+
+
+def far_kernel(ids, owned, message, stored, own, peer, query_w, *refs):
+    far = candidate_queries(ids, owned, message, stored, own, peer, query_w)
+    if len(refs) == 1:
+        refs[0][...] = far.astype(bf16)
+        return
+    near, outs = refs[0][...].astype(f32), refs[1:]
+    low = first_half((1, LANES))
+    for k, out in enumerate(outs):
+        cut = pair_cut(k // 2)
+        left, right = near[:, cut], far[:, cut]
+        if k % 2:
+            left = pltpu.roll(left, LANES // 2, 1)
+        else:
+            right = pltpu.roll(right, LANES // 2, 1)
+        out[...] = jnp.where(low, left, right).astype(bf16)
+
+
+def attend(alive_count, scale, query, key, val, buffers, emit):
+    n, width = key.shape
     blocks = range(0, n, KEYS)
-
-    def padded(h):
-        cut = slice(h * 64, (h + 1) * 64)
-        rows = jnp.concatenate([query[cut, :] for query in queries], axis=1)
-        zero = jnp.zeros_like(rows)
-        return jnp.concatenate([zero, rows] if h % 2 else [rows, zero], axis=0)
-
-    def scores(h, block, weights):
-        rows = slice(block, block + KEYS)
-        values = dot(key[rows, pair_cut(h // 2)], weights)
-        alive = iota((KEYS, 1), 0) < alive_count - block
-        return jnp.where(alive, values, DEAD)
-
-    def store(h, block, weights, buffer, peak):
-        values = scores(h, block, weights)
-        buffer[block : block + KEYS, :] = values
-        top = jnp.max(values.reshape(KEYS // 8, 8, cols), axis=0)
+    pairs = width // LANES
+    ones = jnp.ones((16, KEYS), bf16)
+
+    def weights_of(p):
+        rows = query[pair_cut(p), :]
+        zero = jnp.zeros((64, LANES), bf16)
+        top = jnp.concatenate([rows[:64], zero], axis=1)
+        return jnp.concatenate([top, jnp.concatenate([zero, rows[64:]], axis=1)], axis=0)
+
+    def store(p, block, weights, peak):
+        values = dot(key[block : block + KEYS, pair_cut(p)], weights)
+        values = jnp.where(iota((KEYS, 1), 0) < alive_count - block, values, DEAD)
+        buffers[p % 2][block : block + KEYS, :] = values
+        top = jnp.max(values.reshape(KEYS // 8, 8, 2 * LANES), axis=0)
         return top if peak is None else jnp.maximum(peak, top)
 
-    def run(buffers):
-        ones = jnp.ones((16, KEYS), bf16)
-        peak, weights = None, padded(heads[0])
+    peak, weights = None, weights_of(0)
+    for block in blocks:
+        peak = store(0, block, weights, peak)
+    for p in range(pairs):
+        factor = [
+            jnp.broadcast_to(scale[0:1, h : h + 1], (1, LANES)) for h in (2 * p, 2 * p + 1)
+        ]
+        factor = jnp.concatenate(factor, axis=1) * LOG2E
+        peak = jnp.max(peak, axis=0, keepdims=True)
+        following = sums = None
+        more = p + 1 < pairs
+        if more:
+            weights = weights_of(p + 1)
         for block in blocks:
-            peak = store(heads[0], block, weights, buffers[heads[0] % 2], peak)
-        for h in heads:
-            factor = scale[0:1, h : h + 1] * LOG2E
-            peak = jnp.max(peak, axis=0, keepdims=True)
-            following = None
-            more = h + 1 in heads
-            weights = padded(h + 1) if more else None
-            sums = None
-            for block in blocks:
-                if more:
-                    following = store(h + 1, block, weights, buffers[(h + 1) % 2], following)
-                gap = buffers[h % 2][block : block + KEYS, :] - peak
-                probs = jnp.exp2(gap * factor).astype(bf16)
-                side = jnp.concatenate(
-                    [val[h * 64 : (h + 1) * 64, block : block + KEYS], ones], axis=0
-                )
-                part = dot(side, probs)
-                sums = part if sums is None else sums + part
-            total = sums[64:65]
-            emit(h, sums[:64] / total, peak * factor + jnp.log2(total))
-            peak = following
-
-    return run
+            if more:
+                following = store(p + 1, block, weights, following)
+            gap = buffers[p % 2][block : block + KEYS, :] - peak
+            probs = jnp.exp2(gap * factor).astype(bf16)
+            side = jnp.concatenate([val[pair_cut(p), block : block + KEYS], ones], axis=0)
+            part = dot(side, probs)
+            sums = part if sums is None else sums + part
+        total = sums[LANES : LANES + 1]
+        logs = live(alive_count, peak * factor + jnp.log2(total))
+        for b in (0, 1):
+            cut = pair_cut(b)
+            mean = sums[b * 64 : (b + 1) * 64, cut] / total[:, cut]
+            emit(2 * p + b, mean, logs[:, cut])
+        peak = following
 
 
 def finish_kernel(
     bit, here, scale, emb, query_a, query_b, intra_a, intra_b, enter, ctl, got, prefix, prefix_logs,
-    out_w, pair_w, val_w, cand_a, cand_b, hist_o, key_o, val_o, pay_o,
+    out_w, pair_w, val_w, cand_q, hist_o, key_o, val_o, pay_o,
     shown, sem, *buffers,
 ):
     n, width = emb.shape
@@ -411,28 +431,24 @@
         hidden = hidden_sum.astype(bf16)
         key_o[chunk(i), :] = dot(hidden, pair_w[:, :width]).astype(bf16)
         val_o[:, chunk(i)] = contract(val_w[...], hidden, 1, 1).astype(bf16)
-    send_part(alive_count, scale, 0, (cand_a, cand_b), key_o, val_o, pay_o, buffers)
+    send_part(alive_count, scale, cand_q, key_o, val_o, pay_o, buffers)
     for copy in copies:
         copy.wait()
 
 
-def send_part(alive_count, scale, first, queries, key, val, pay_o, buffers):
-    heads = range(first, first + val.shape[0] // 128)
-    count = len(heads) * 64
+def send_part(alive_count, scale, query, key, val, pay_o, buffers):
     log_rows = []
 
-    def emit(h, attended, logs):
-        h -= first
-        pay_o[h * 64 : (h + 1) * 64, :] = attended.astype(bf16)
-        log_rows.append(live(alive_count, logs))
-
-    attend(alive_count, scale, heads, queries, key, val, emit)(buffers)
-    pay_o[count:, :] = pack_logs(jnp.concatenate(log_rows, axis=0))
-
-
-def send_kernel(here, scale, cand_a, cand_b, key, val, pay_o, *buffers):
-    first = val.shape[0] // 128
-    send_part(here[0:1, 0:1], scale, first, (cand_a, cand_b), key, val, pay_o, buffers)
+    def emit(h, mean, logs):
+        pay_o[h * 64 : (h + 1) * 64, :] = mean.astype(bf16)
+        log_rows.append(logs)
+
+    attend(alive_count, scale, query, key, val, buffers, emit)
+    pay_o[val.shape[0] :, :] = pack_logs(jnp.concatenate(log_rows, axis=0))
+
+
+def send_kernel(here, scale, query, key, val, pay_o, *buffers):
+    send_part(here[0:1, 0:1], scale, query, key, val, pay_o, buffers)
 
 
 def live(alive_count, logs):
@@ -455,15 +471,12 @@
     return rows[:heads] + rows[heads : 2 * heads] + rows[2 * heads : 3 * heads]
 
 
-def keep_kernel(here, scale, cand_a, cand_b, key, val, mean_o, logs_o, *buffers):
-    alive_count = here[0:1, 0:1]
-
-    def emit(h, attended, logs):
-        mean_o[h * 64 : (h + 1) * 64, :] = attended
-        logs_o[h : h + 1, :] = live(alive_count, logs)
-
-    heads = range(val.shape[0] // 64)
-    attend(alive_count, scale, heads, (cand_a, cand_b), key, val, emit)(buffers)
+def keep_kernel(here, scale, query, key, val, mean_o, logs_o, *buffers):
+    def emit(h, mean, logs):
+        mean_o[h * 64 : (h + 1) * 64, :] = mean
+        logs_o[h : h + 1, :] = logs
+
+    attend(here[0:1, 0:1], scale, query, key, val, buffers, emit)
 
 
 def over_heads(rows):
@@ -486,60 +499,35 @@
     return mean, peak + jnp.log2(total)
 
 
-def received(gots, heads):
-    share = heads // len(gots)
-    means = [got[: share * 64, :].astype(f32) for got in gots]
-    logs = [unpack_logs(got[share * 64 :, :], share) for got in gots]
-    return jnp.concatenate(means, axis=0), jnp.concatenate(logs, axis=0)
+def received(got, heads):
+    value = got[...].astype(f32)
+    if value.shape[0] < heads * 64:
+        value = jnp.concatenate([value, pltpu.roll(value, LANES // 2, 1)], axis=0)
+    return value[: heads * 64], unpack_logs(value[heads * 64 :], heads)
 
 
 def fold_kernel(mean, logs, *refs):
     gots, (mean_o, logs_o, pay_o) = refs[:-3], refs[-3:]
     heads, keep = logs_o.shape
-    width = heads * 64
-    new_mean, new_logs = merge([(mean[...], logs[...]), received(gots, heads)])
+    parts = [(mean[...], logs[...])] + [received(got, heads) for got in gots]
+    new_mean, new_logs = merge(parts)
     mean_o[...] = new_mean[:, :keep]
     logs_o[...] = new_logs[:, :keep]
-    pay_o[:width, :] = new_mean[:, keep:].astype(bf16)
-    pay_o[width:, :] = pack_logs(new_logs[:, keep:])
-
-
-def deal_kernel(blocks, mean, logs, *refs):
-    gots, mean_o, logs_o, sends = refs[:-5], refs[-5], refs[-4], refs[-3:]
-    heads, cols = logs_o.shape
-    new_mean, new_logs = merge([(mean[...], logs[...]), received(gots, heads)])
-    mean_o[...] = new_mean[:, :cols]
-    logs_o[...] = new_logs[:, :cols]
     whole = jnp.concatenate([new_mean, pack_logs(new_logs).astype(f32)], axis=0)
-    owned = whole.shape[1] // 4
-    half = whole.shape[0] // 2
-    low = first_half((1, LANES))
-    for block, send in zip(blocks, sends):
-        start = block * owned
-        if 2 * owned == LANES:
-            tile = whole[:, start // LANES * LANES : start // LANES * LANES + LANES]
-            top, bottom = tile[:half], tile[half:]
-            if start % LANES:
-                top = pltpu.roll(top, owned, 1)
-            else:
-                bottom = pltpu.roll(bottom, owned, 1)
-            send[...] = jnp.where(low, top, bottom).astype(bf16)
-        else:
-            send[...] = whole[:, start : start + owned].astype(bf16)
-
-
-def last_kernel(owned, mean, logs, got_a, got_b, got_c, out_w, cand_o):
-    heads = logs.shape[0]
-    parts = [(mean[...], logs[...])]
-    for got in (got_a, got_b, got_c):
-        if 2 * owned == LANES:
-            value = got[...].astype(f32)
-            value = jnp.concatenate([value, pltpu.roll(value, owned, 1)], axis=0)
-        else:
-            value = got[...].astype(f32)
-        parts.append((value[: heads * 64], unpack_logs(value[heads * 64 :], heads)))
+    if 2 * keep == LANES:
+        half = whole.shape[0] // 2
+        top = pltpu.roll(whole[:half], keep, 1)
+        pay_o[...] = jnp.where(first_half((1, LANES)), top, whole[half:]).astype(bf16)
+    else:
+        pay_o[...] = whole[:, keep:].astype(bf16)
+
+
+def last_kernel(mean, logs, got, out_w, cand_o):
+    heads, cols = logs.shape
+    other_mean, other_logs = received(got, heads)
+    parts = [(mean[...], logs[...]), (other_mean[:, :cols], other_logs[:, :cols])]
     attended = merge(parts)[0].astype(bf16)
-    cand_o[...] = contract(attended, out_w[...], 0, 0)[: cand_o.shape[0]]
+    cand_o[...] = contract(attended, out_w[...], 0, 0)
 
 
 def shape(dims, dtype):
@@ -596,11 +584,12 @@
     owned = candidate_item_index.shape[1]
     seq = lax.axis_size("seq")
     bits = seq.bit_length() - 1
+    cands = owned * seq
     assert users == 1 and lax.axis_size("dp") == 2 and seq == 1 << bits and bits > 2
     assert width == heads * 64 and heads % 4 == 0 and LANES % owned == 0 and owned <= 64
+    assert cands == 4 * LANES
     pairs = heads // 2
     rows = pairs * 64
-    cands = owned * seq
 
     def swap(value, mask):
         return lax.ppermute(value, "seq", [(j, j ^ mask) for j in range(seq)])
@@ -609,24 +598,22 @@
     scale = head_score_scale.reshape(1, heads)
     stored = item_stored_row.reshape(-1, LANES)
     decay = log_head_retention.reshape(heads, n)
-    ids = jnp.pad(candidate_item_index, ((0, 0), (0, 64 - owned)))
-    id_rows = jnp.concatenate([ids // LANES, ids % LANES], axis=1).astype(f32)
-
-    part, slot, crow, ccol, ctl, key_w = call(
+
+    part, slot, crow, ccol, ctl, key_w, id_rows = call(
         own_rows_kernel, "own_rows",
         [
             history_item_index, stored, decay, item_embedding_table,
-            history_query_key_value_weight,
+            history_query_key_value_weight, candidate_item_index,
         ],
         [
             shape((n, width), bf16), shape((1, n), f32), shape((n // CHUNK, heads, CHUNK), f32),
             shape((n, 2 * heads), f32), shape((n // CHUNK * pairs, LANES), f32),
-            shape((width, width), bf16),
+            shape((width, width), bf16), shape((1, LANES), f32),
         ],
         [
             pltpu.VMEM((1, n), i32), pltpu.VMEM(stored.shape, i32), pltpu.VMEM((heads, n), f32),
             pltpu.VMEM((half, width), bf16), pltpu.VMEM((width, width), bf16),
-            pltpu.SemaphoreType.DMA((6,)),
+            pltpu.VMEM((1, owned), i32), pltpu.SemaphoreType.DMA((7,)),
         ],
         space=HBM,
         flops=2 * n * half * width,
@@ -668,77 +655,72 @@
             after=[early[-1][1]],
         )
     got = swap(pay, 1 << (bits - 1))
-    order = [reversed_bits(j, bits) for j in range(seq)]
-    half_order = list(range(seq // 2))
-    if seq == 8:
-        half_order = [0, 2, 1, 3]
-        order = [0, 2, 4, 6, 1, 3, 5, 7]
-    quarter = cands // 4
-
-    def candidates(message, name, pair_w):
-        return call(
-            lambda *refs: candidate_kernel(half_order, owned, *refs), name,
-            [message, stored, item_embedding_table, peer, candidate_query_weight, *pair_w],
-            [shape((width, quarter), bf16)] * 2 + [shape((width, width), bf16)] * len(pair_w),
-            flops=cands * 2 * half * width,
+    half_seq = seq // 2
+    tables = [stored, item_embedding_table, peer, candidate_query_weight]
+    work = cands * 2 * half * width
+    near, val_w = call(
+        lambda *refs: near_kernel(half_seq, owned, *refs), "near",
+        [pay, *tables, candidate_key_value_weight],
+        [shape((width, cands // 2), bf16), shape((width, width), bf16)], flops=work,
+    )
+    if 2 * owned == LANES:
+        quarters = call(
+            lambda *refs: far_kernel(half_seq, owned, *refs), "far", [got, *tables, near],
+            [shape((width, LANES), bf16)] * 4, flops=work,
         )
-
-    keep_a, send_a, val_w = candidates(pay, "near", [candidate_key_value_weight])
-    keep_b, send_b = candidates(got, "far", [])
-    if seq != 8:
-        every = jnp.concatenate([keep_a, send_a, keep_b, send_b], axis=1)
-        every = every.reshape(width, seq, owned)[:, jnp.array(order)].reshape(width, cands)
-        keep_a, keep_b, send_a, send_b = (
-            every[:, k * quarter : (k + 1) * quarter] for k in range(4)
+    else:
+        (far,) = call(
+            lambda *refs: far_kernel(half_seq, owned, *refs), "far", [got, *tables],
+            [shape((width, cands // 2), bf16)], flops=work,
         )
+        order = [t + 4 * reversed_bits(k, bits - 2) for t in range(4) for k in range(seq // 4)]
+        every = jnp.concatenate([near, far], axis=1).reshape(width, seq, owned)
+        every = every[:, jnp.array(order)].reshape(width, cands)
+        quarters = [every[:, t * LANES : (t + 1) * LANES] for t in range(4)]
     (query_a, intra_a), (query_b, intra_b) = early
-    send = cands // 2
-    buffers = [pltpu.VMEM((n, send), f32)] * 2
+    buffers = [pltpu.VMEM((n, 2 * LANES), f32)] * 2
     message = width + log_pad(heads)
-    share = width // 2 + log_pad(heads // 2)
-    hist, key_two, val_two, pay_a = call(
+    hist, key_two, val_two, pay = call(
         lambda *refs: finish_kernel(bits - 1, *refs), "finish",
         [
             here, scale, emb, query_a, query_b, intra_a, intra_b, enter, ctl, got, prefix, logs,
-            history_output_weight, candidate_key_value_weight, val_w, send_a, send_b,
+            history_output_weight, candidate_key_value_weight, val_w, quarters[3],
         ],
         [
             shape((n, width), f32), shape((n, width), bf16), shape((width, n), bf16),
-            shape((share, send), bf16),
+            shape((message, LANES), bf16),
         ],
         [pltpu.VMEM((n, width), f32), pltpu.SemaphoreType.DMA((n // CHUNK,))] + buffers,
         spaces=[ANY, VMEM, VMEM, VMEM],
         flops=2 * n * half * width,
     )
-    (pay_b,) = call(
-        send_kernel, "send", [here, scale, send_a, send_b, key_two, val_two],
-        [shape((share, send), bf16)], buffers, flops=n * half * width,
-    )
-    gots = [swap(pay_a, 1), swap(pay_b, 1)]
+    gots = [swap(pay, 3)]
+    for t in (2, 1):
+        (pay,) = call(
+            send_kernel, "send", [here, scale, quarters[t], key_two, val_two],
+            [shape((message, LANES), bf16)], buffers, after=[pay], flops=work,
+        )
+        gots.append(swap(pay, t))
     mean, logs = call(
-        keep_kernel, "keep", [here, scale, keep_a, keep_b, key_two, val_two],
-        [shape((width, send), f32), shape((heads, send), f32)], buffers, after=[pay_b],
-        flops=2 * n * half * width,
-    )
-    for bit in range(1, bits - 2):
-        send //= 2
+        keep_kernel, "keep", [here, scale, quarters[0], key_two, val_two],
+        [shape((width, LANES), f32), shape((heads, LANES), f32)], buffers, after=[pay], flops=work,
+    )
+    cols = LANES
+    for bit in range(2, bits):
+        cols //= 2
+        packed = 2 * cols == LANES
         mean, logs, pay = call(
             fold_kernel, "fold", [mean, logs, *gots],
-            [shape((width, send), f32), shape((heads, send), f32), shape((message, send), bf16)],
+            [
+                shape((width, cols), f32), shape((heads, cols), f32),
+                shape((message // 2, LANES) if packed else (message, cols), bf16),
+            ],
         )
+        if packed and bit < bits - 1:
+            pay = jnp.concatenate([pay[:, :cols], pay[:, cols:]], axis=0)
         gots = [swap(pay, 1 << bit)]
-    packed = 2 * owned == LANES
-    cols = LANES if packed else owned
-    blocks = [2, 3, 1] if seq == 8 else [1, 3, 2]
-    mean, logs, *sends = call(
-        lambda *refs: deal_kernel(blocks, *refs), "deal", [mean, logs, *gots],
-        [shape((width, cols), f32), shape((heads, cols), f32)]
-        + [shape((message // 2, LANES) if packed else (message, owned), bf16)] * 3,
-    )
-    gots = [swap(value, order[block]) for value, block in zip(sends, blocks)]
     (cand_out,) = call(
-        lambda *refs: last_kernel(owned, *refs), "last",
-        [mean, logs, *gots, candidate_output_weight],
+        last_kernel, "last", [mean, logs, *gots, candidate_output_weight],
         [shape((owned, width), f32)],
     )
     return hist[None], cand_out[None]

time: 52.6 us -> 53.8 us (1.023)
  Pallas kernels: 28.5 us -> 29.9 us
  other arithmetic: 0.74 us -> 0 us
  starting transfers between devices: 14.6 us -> 15.2 us
    pallas_call x13 -> x14, Pallas kernels: 28.5 us -> 29.9 us  [call(): pl.pallas_call(body, name=name, in_specs=[SMEM] * len(scalars) + [space]...]
    select_n x1 -> x0, other arithmetic: 0.67 us -> none  [shards(): id_rows = jnp.concatenate([ids // LANES, ids % LANES], axis=1).astype(f32)]
    ppermute x8 -> x7, starting transfers between devices: 14.1 us -> 14.7 us  [swap(): return lax.ppermute(value, 'seq', [(j, j ^ mask) for j in range(seq)])]
    ppermute x8 -> x7, waiting for transfers between devices: 7.1 us -> 7.02 us  [swap(): return lax.ppermute(value, 'seq', [(j, j ^ mask) for j in range(seq)])]
  transfers between devices with their start and end apart: 9 -> 8, of which waited for: 6 -> 6; matrix products, arithmetic and copies ran while one was open for 1% -> 0% of each run, Pallas kernels for 28% -> 26%
where the time goes in v7:
time: 53.8 us; the launch traced here: 53.6 us
  Pallas kernels  29.9 us (56%)
  starting transfers between devices  15.2 us (28%)
  waiting for transfers between devices  7.02 us (13%)
  between operations  1.43 us (3%)
    pallas_call x14, Pallas kernels, call(): pl.pallas_call(body, name=name, in_specs=[SMEM] * len(scalars) + [space]...  29.9 us
    ppermute x7, starting transfers between devices, swap(): return lax.ppermute(value, 'seq', [(j, j ^ mask) for j in range(seq)])  14.7 us
    ppermute x7, waiting for transfers between devices, swap(): return lax.ppermute(value, 'seq', [(j, j ^ mask) for j in range(seq)])  7.02 us
  transfers between devices with their start and end apart: 8, of which 6 were waited for; matrix products, arithmetic and copies ran while one was open for 0% of the time, Pallas kernels for 26%

profile of v7, /device:TPU:0, one launch (start us, length us, event | category | flops | bytes accessed | tf_op | source)
XLA Modules:
  0.0 53.6 jit_solution(8676688374677749558)
XLA Ops:
  0.6 0.5 collective-permute-start
  1.8 0.0 copy-start.1
  1.8 5.0 %own_rows.1 = (bf16[1024,512]{1,0:T(8,128)(2,1)S(1)}, f32[1,1024]{1,0:T(1,128)S(1)}, f32[4,8,256]{2,1,0:T(8,128)S(1)}, f32[1024,16]{1,0:T(8,128)S(1)}, f32[16,12...) custom-call(s32[1,1024]{1,0:T(1,128)} %refs_0_.2, s32[32,128]{1,0:T(8,128)} %bitcast.5, ...), custom_call_target="tpu_custom_call" | custom-call | flops 2147483648 | tf_op jit(solution)/shard_map/own_rows/pallas_call | solution.py:551
  6.8 0.0 collective-permute-done.refs_2_.refs_3_
  6.8 0.0 copy-done.1
  6.8 4.4 %summary.1 = (bf16[1024,512]{1,0:T(8,128)(2,1)S(1)}, bf16[512,1024]{1,0:T(8,128)(2,1)S(1)}, bf16[1024,512]{1,0:T(8,128)(2,1)S(1)}, f32[4,256,128]{2,1,0:T(8,128)...) custom-call(s32[1]{0:T(128)S(6)} %copy.14.refs_0_, bf16[1024,512]{1,0:T(8,128)(2,1)S(1)} %get-tuple-element.40.refs_1_, ...), custom_call_target="tpu_custom_call" | custom-call | flops 2147483648 | tf_op jit(solution)/shard_map/summary/pallas_call | solution.py:551
  11.2 2.6 %collective-permute-start.1 = (bf16[272,128]{1,0:T(8,128)(2,1)S(1)}, bf16[272,128]{1,0:T(8,128)(2,1)S(1)}, u32[]{:S(2)}, u32[]{:S(2)}) collective-permute-start(bf16[272,128]{1,0:T(8,128)(2,1)S(1)} %get-tuple-element.52.refs_0_), channel_id=1, source_target_pairs={{0,2},{2,0},{4,6},{6,4},{8,10},{10,8},{12,14},{14,12},{1,3},{3,1},... | collective-permute-start | bytes 208904 | tf_op jit(solution)/shard_map/ppermute | solution.py:595
  13.8 2.6 %local_a.1 = (bf16[1024,256]{1,0:T(8,128)(2,1)S(1)}, f32[1024,256]{1,0:T(8,128)S(1)}) custom-call(bf16[1024,512]{1,0:T(8,128)(2,1)S(1)} %get-tuple-element.47.refs_0_.refs_2_, bf16[512,1024]{1,0:T(8,128)(2,1)S(1)} %get-tuple-element.48.refs_1_, bf16[1024,512]{1,0:T(8,128)(2,1)S(1)} %get-tuple-element.49.refs_2_, ...), custom_call_target="tpu_custom_call" | custom-call | flops 1073741824 | tf_op jit(solution)/shard_map/local_a/pallas_call | solution.py:551
  16.4 0.2 collective-permute-done.1.refs_1_
  16.7 0.1 join.2
  16.7 1.9 %collective-permute-start.2 = (bf16[272,128]{1,0:T(8,128)(2,1)S(1)}, bf16[272,128]{1,0:T(8,128)(2,1)S(1)}, u32[]{:S(2)}, u32[]{:S(2)}) collective-permute-start(bf16[272,128]{1,0:T(8,128)(2,1)S(1)} %get-tuple-element.58.refs_0_), channel_id=1, source_target_pairs={{0,4},{2,6},{4,0},{6,2},{8,12},{10,14},{12,8},{14,10},{1,5},{3,7},... | collective-permute-start | bytes 208904 | tf_op jit(solution)/shard_map/ppermute | solution.py:595
  18.6 0.0 copy-start
  18.6 0.0 copy-start.2
  18.6 0.0 copy-start.3
  18.6 0.0 copy-start.5
  18.6 2.8 %local_b.1 = (bf16[1024,256]{1,0:T(8,128)(2,1)S(1)}, f32[1024,256]{1,0:T(8,128)S(1)}) custom-call(bf16[1024,512]{1,0:T(8,128)(2,1)S(1)} %get-tuple-element.47.refs_0_.refs_2_, bf16[512,1024]{1,0:T(8,128)(2,1)S(1)} %get-tuple-element.48.refs_1_, bf16[1024,512]{1,0:T(8,128)(2,1)S(1)} %get-tuple-element.49.refs_2_, ...), custom_call_target="tpu_custom_call" | custom-call | flops 1073741824 | tf_op jit(solution)/shard_map/local_b/pallas_call | solution.py:551
  21.4 0.0 collective-permute-done.2.refs_1_
  21.4 0.1 join.3
  21.5 2.6 %collective-permute-start.3 = (bf16[272,128]{1,0:T(8,128)(2,1)S(1)}, bf16[272,128]{1,0:T(8,128)(2,1)S(1)}, u32[]{:S(2)}, u32[]{:S(2)}) collective-permute-start(bf16[272,128]{1,0:T(8,128)(2,1)S(1)} %get-tuple-element.60.refs_0_), channel_id=1, source_target_pairs={{0,8},{2,10},{4,12},{6,14},{8,0},{10,2},{12,4},{14,6},{1,9},{3,11}... | collective-permute-start | bytes 208904 | tf_op jit(solution)/shard_map/ppermute | solution.py:595
  24.1 0.0 copy-done
  24.1 0.0 copy-done.2
  24.2 0.0 copy-done.3
  24.2 0.0 copy-done.5
  24.2 1.9 %near.1 = (bf16[512,256]{1,0:T(8,128)(2,1)S(1)}, bf16[512,512]{1,0:T(8,128)(2,1)S(1)}) custom-call(bf16[272,128]{1,0:T(8,128)(2,1)S(1)} %get-tuple-element.60.refs_0_, s32[32,128]{1,0:T(8,128)S(1)} %bitcast.6, bf16[2048,512]{1,0:T(8,128)(2,1)S(1)} %copy-done, bf16[2048,512]{1,0:T(8,128)(2,1)S(1)} %collective-permute-done.refs_2_.refs_3_, ...), custom_call_target="tpu_custom_call" | custom-call | flops 1073741824 | tf_op jit(solution)/shard_map/near/pallas_call | solution.py:551
  26.1 0.7 %collective-permute-done.3.refs_0_.refs_9_ = bf16[272,128]{1,0:T(8,128)(2,1)S(1)} collective-permute-done((bf16[272,128]{1,0:T(8,128)(2,1)S(1)}, bf16[272,128]{1,0:T(8,128)(2,1)S(1)}, u32[]{:S(2)}, u32[]{:S(2)}) %collective-permute-start.3) | collective-permute-done | bytes 69664 | tf_op jit(solution)/shard_map/ppermute | solution.py:595
  26.8 0.0 copy-start.6
  26.8 0.0 copy-start.7
  26.8 2.0 %far.1 = (bf16[512,128]{1,0:T(8,128)(2,1)S(1)}, bf16[512,128]{1,0:T(8,128)(2,1)S(1)}, bf16[512,128]{1,0:T(8,128)(2,1)S(1)}, bf16[512,128]{1,0:T(8,128)(2,1)S(1)}) custom-call(bf16[272,128]{1,0:T(8,128)(2,1)S(1)} %collective-permute-done.3.refs_0_.refs_9_, s32[32,128]{1,0:T(8,128)S(1)} %bitcast.7, bf16[2048,512]{1,0:T(8,128)(2,1)S(1)} %copy-done, ...), custom_call_target="tpu_custom_call" | custom-call | flops 1073741824 | tf_op jit(solution)/shard_map/far/pallas_call | solution.py:551
  28.8 0.0 copy-done.6
  28.8 0.0 copy-done.7
  28.8 4.6 %finish.1 = (f32[1024,512]{1,0:T(8,128)}, bf16[1024,512]{1,0:T(8,128)(2,1)S(1)}, bf16[512,1024]{1,0:T(8,128)(2,1)S(1)}, bf16[544,128]{1,0:T(8,128)(2,1)S(1)}) custom-call(s32[8,128]{1,0:T(8,128)S(1)} %get-tuple-element.46.refs_0_, f32[1,8]{1,0:T(1,128)S(1)} %bitcast.8, bf16[1024,512]{1,0:T(8,128)(2,1)S(1)} %get-tuple-element.47.refs_0_.refs_2_, ...), custom_call_target="tpu_custom_call" | custom-call | flops 2147483648 | tf_op jit(solution)/shard_map/finish/pallas_call | solution.py:551
  33.4 1.8 %send.2.refs_5_ = bf16[544,128]{1,0:T(8,128)(2,1)S(1)} custom-call(s32[8,128]{1,0:T(8,128)S(1)} %get-tuple-element.46.refs_0_, f32[1,8]{1,0:T(1,128)S(1)} %bitcast.9, bf16[512,128]{1,0:T(8,128)(2,1)S(1)} %get-tuple-element.71.refs_2_, bf16[1024,512]{1,0:T(8,128)(2,1)S(1)} %get-tuple-element.68.refs_3_, bf16[512,1024]{1,0:T(8,128)(2,1)S(1)} %get-tuple-element.69.refs_4_, ...), custom_call_target="tpu_custom_call" | custom-call | flops 1073741824 | tf_op jit(solution)/shard_map/send/pallas_call | solution.py:551
  35.2 1.8 %send.3.refs_5_ = bf16[544,128]{1,0:T(8,128)(2,1)S(1)} custom-call(s32[8,128]{1,0:T(8,128)S(1)} %get-tuple-element.46.refs_0_, f32[1,8]{1,0:T(1,128)S(1)} %bitcast.10, bf16[512,128]{1,0:T(8,128)(2,1)S(1)} %get-tuple-element.70.refs_2_, bf16[1024,512]{1,0:T(8,128)(2,1)S(1)} %get-tuple-element.68.refs_3_, bf16[512,1024]{1,0:T(8,128)(2,1)S(1)} %get-tuple-element.69.refs_4_, ...), custom_call_target="tpu_custom_call" | custom-call | flops 1073741824 | tf_op jit(solution)/shard_map/send/pallas_call | solution.py:551
  37.0 1.5 %collective-permute-start.6 = (bf16[544,128]{1,0:T(8,128)(2,1)S(1)}, bf16[544,128]{1,0:T(8,128)(2,1)S(1)}, u32[]{:S(2)}, u32[]{:S(2)}) collective-permute-start(bf16[544,128]{1,0:T(8,128)(2,1)S(1)} %send.3.refs_5_), channel_id=1, source_target_pairs={{0,2},{2,0},{4,6},{6,4},{8,10},{10,8},{12,14},{14,12},{1,3},{3,1},... | collective-permute-start | bytes 417800 | tf_op jit(solution)/shard_map/ppermute | solution.py:595
  38.5 1.5 %collective-permute-start.5 = (bf16[544,128]{1,0:T(8,128)(2,1)S(1)}, bf16[544,128]{1,0:T(8,128)(2,1)S(1)}, u32[]{:S(2)}, u32[]{:S(2)}) collective-permute-start(bf16[544,128]{1,0:T(8,128)(2,1)S(1)} %send.2.refs_5_), channel_id=1, source_target_pairs={{0,4},{2,6},{4,0},{6,2},{8,12},{10,14},{12,8},{14,10},{1,5},{3,7},... | collective-permute-start | bytes 417800 | tf_op jit(solution)/shard_map/ppermute | solution.py:595
  40.0 0.6 %collective-permute-start.4 = (bf16[544,128]{1,0:T(8,128)(2,1)S(1)}, bf16[544,128]{1,0:T(8,128)(2,1)S(1)}, u32[]{:S(2)}, u32[]{:S(2)}) collective-permute-start(bf16[544,128]{1,0:T(8,128)(2,1)S(1)} %get-tuple-element.72.refs_5_), channel_id=1, source_target_pairs={{0,6},{2,4},{4,2},{6,0},{8,14},{10,12},{12,10},{14,8},{1,7},{3,5},... | collective-permute-start | bytes 417800 | tf_op jit(solution)/shard_map/ppermute | solution.py:595
  40.5 0.0 copy-start.4
  40.5 1.8 %keep.1 = (f32[512,128]{1,0:T(8,128)S(1)}, f32[8,128]{1,0:T(8,128)S(1)}) custom-call(s32[8,128]{1,0:T(8,128)S(1)} %get-tuple-element.46.refs_0_, f32[1,8]{1,0:T(1,128)S(1)} %bitcast.11, bf16[512,128]{1,0:T(8,128)(2,1)S(1)} %get-tuple-element.67.refs_2_, bf16[1024,512]{1,0:T(8,128)(2,1)S(1)} %get-tuple-element.68.refs_3_, ...), custom_call_target="tpu_custom_call" | custom-call | flops 1073741824 | tf_op jit(solution)/shard_map/keep/pallas_call | solution.py:551
  42.3 1.2 %collective-permute-done.6.refs_4_ = bf16[544,128]{1,0:T(8,128)(2,1)S(1)} collective-permute-done((bf16[544,128]{1,0:T(8,128)(2,1)S(1)}, bf16[544,128]{1,0:T(8,128)(2,1)S(1)}, u32[]{:S(2)}, u32[]{:S(2)}) %collective-permute-start.6) | collective-permute-done | bytes 139296 | tf_op jit(solution)/shard_map/ppermute | solution.py:595
  43.6 0.7 %collective-permute-done.5.refs_3_ = bf16[544,128]{1,0:T(8,128)(2,1)S(1)} collective-permute-done((bf16[544,128]{1,0:T(8,128)(2,1)S(1)}, bf16[544,128]{1,0:T(8,128)(2,1)S(1)}, u32[]{:S(2)}, u32[]{:S(2)}) %collective-permute-start.5) | collective-permute-done | bytes 139296 | tf_op jit(solution)/shard_map/ppermute | solution.py:595
  44.3 1.6 %collective-permute-done.4.refs_2_ = bf16[544,128]{1,0:T(8,128)(2,1)S(1)} collective-permute-done((bf16[544,128]{1,0:T(8,128)(2,1)S(1)}, bf16[544,128]{1,0:T(8,128)(2,1)S(1)}, u32[]{:S(2)}, u32[]{:S(2)}) %collective-permute-start.4) | collective-permute-done | bytes 139296 | tf_op jit(solution)/shard_map/ppermute | solution.py:595
  45.9 0.1 fold.1
  46.1 4.0 %collective-permute-start.7 = (bf16[272,128]{1,0:T(8,128)(2,1)S(1)}, bf16[272,128]{1,0:T(8,128)(2,1)S(1)}, u32[]{:S(2)}, u32[]{:S(2)}) collective-permute-start(bf16[272,128]{1,0:T(8,128)(2,1)S(1)} %get-tuple-element.77), channel_id=1, source_target_pairs={{0,8},{2,10},{4,12},{6,14},{8,0},{10,2},{12,4},{14,6},{1,9},{3,11}... | collective-permute-start | bytes 208904 | tf_op jit(solution)/shard_map/ppermute | solution.py:595
  50.1 2.5 %collective-permute-done.7.refs_2_ = bf16[272,128]{1,0:T(8,128)(2,1)S(1)} collective-permute-done((bf16[272,128]{1,0:T(8,128)(2,1)S(1)}, bf16[272,128]{1,0:T(8,128)(2,1)S(1)}, u32[]{:S(2)}, u32[]{:S(2)}) %collective-permute-start.7) | collective-permute-done | bytes 69664 | tf_op jit(solution)/shard_map/ppermute | solution.py:595
  52.6 0.0 copy-done.4
  52.6 1.0 %last.1 = f32[64,512]{1,0:T(8,128)} custom-call(f32[512,64]{1,0:T(8,128)S(1)} %get-tuple-element.75.refs_0_, f32[8,64]{1,0:T(8,128)S(1)} %get-tuple-element.76.refs_1_, bf16[272,128]{1,0:T(8,128)(2,1)S(1)} %collective-permute-done.7.refs_2_, bf16[512,512]{1,0:T(8,128)(2,1)S(1)} %copy-done.4), custom_call_target="tpu_custom_call" | custom-call | tf_op jit(solution)/shard_map/last/pallas_call | solution.py:551
Async XLA Ops:
  0.6 6.2 %collective-permute-start = (bf16[2048,512]{1,0:T(8,128)(2,1)}, bf16[2048,512]{1,0:T(8,128)(2,1)S(1)}, u32[]{:S(2)}, u32[]{:S(2)}) collective-permute-start(bf16[2048,512]{1,0:T(8,128)(2,1)} %refs_2_.3), channel_id=1, source_target_pairs={{0,1},{1,0},{2,3},{3,2},{4,5},{5,4},{6,7},{7,6},{8,9},{9,8},{10,11... | collective-permute-start | bytes 6291464 | tf_op jit(solution)/shard_map/ppermute | solution.py:597
  1.8 5.0 %copy-start.1 = (bf16[512,1536]{1,0:T(8,128)(2,1)S(1)}, bf16[512,1536]{1,0:T(8,128)(2,1)}, u32[]{:S(2)}) copy-start(bf16[512,1536]{1,0:T(8,128)(2,1)} %refs_5_.6) | copy-start | bytes 4718596
  11.2 5.4 %collective-permute-start.1 = (bf16[272,128]{1,0:T(8,128)(2,1)S(1)}, bf16[272,128]{1,0:T(8,128)(2,1)S(1)}, u32[]{:S(2)}, u32[]{:S(2)}) collective-permute-start(bf16[272,128]{1,0:T(8,128)(2,1)S(1)} %get-tuple-element.52.refs_0_), channel_id=1, source_target_pairs={{0,2},{2,0},{4,6},{6,4},{8,10},{10,8},{12,14},{14,12},{1,3},{3,1},... | collective-permute-start | bytes 208904 | tf_op jit(solution)/shard_map/ppermute | solution.py:595
  16.7 4.7 %collective-permute-start.2 = (bf16[272,128]{1,0:T(8,128)(2,1)S(1)}, bf16[272,128]{1,0:T(8,128)(2,1)S(1)}, u32[]{:S(2)}, u32[]{:S(2)}) collective-permute-start(bf16[272,128]{1,0:T(8,128)(2,1)S(1)} %get-tuple-element.58.refs_0_), channel_id=1, source_target_pairs={{0,4},{2,6},{4,0},{6,2},{8,12},{10,14},{12,8},{14,10},{1,5},{3,7},... | collective-permute-start | bytes 208904 | tf_op jit(solution)/shard_map/ppermute | solution.py:595
  18.6 5.6 %copy-start = (bf16[2048,512]{1,0:T(8,128)(2,1)S(1)}, bf16[2048,512]{1,0:T(8,128)(2,1)}, u32[]{:S(2)}) copy-start(bf16[2048,512]{1,0:T(8,128)(2,1)} %refs_2_.3) | copy-start | bytes 6291460
  18.6 5.6 %copy-start.2 = (bf16[512,512]{1,0:T(8,128)(2,1)S(1)}, bf16[512,512]{1,0:T(8,128)(2,1)}, u32[]{:S(2)}) copy-start(bf16[512,512]{1,0:T(8,128)(2,1)} %refs_4_.5) | copy-start | bytes 1572868
  18.6 5.6 %copy-start.3 = (bf16[512,1024]{1,0:T(8,128)(2,1)S(1)}, bf16[512,1024]{1,0:T(8,128)(2,1)}, u32[]{:S(2)}) copy-start(bf16[512,1024]{1,0:T(8,128)(2,1)} %refs_13_.1) | copy-start | bytes 3145732
  18.6 5.6 %copy-start.5 = (s32[4096]{0:T(1024)S(1)}, s32[4096]{0:T(1024)}, u32[]{:S(2)}) copy-start(s32[4096]{0:T(1024)} %param.16) | copy-start | bytes 49156
  21.5 5.3 %collective-permute-start.3 = (bf16[272,128]{1,0:T(8,128)(2,1)S(1)}, bf16[272,128]{1,0:T(8,128)(2,1)S(1)}, u32[]{:S(2)}, u32[]{:S(2)}) collective-permute-start(bf16[272,128]{1,0:T(8,128)(2,1)S(1)} %get-tuple-element.60.refs_0_), channel_id=1, source_target_pairs={{0,8},{2,10},{4,12},{6,14},{8,0},{10,2},{12,4},{14,6},{1,9},{3,11}... | collective-permute-start | bytes 208904 | tf_op jit(solution)/shard_map/ppermute | solution.py:595
  26.8 2.0 %copy-start.6 = (bf16[512,512]{1,0:T(8,128)(2,1)S(1)}, bf16[512,512]{1,0:T(8,128)(2,1)}, u32[]{:S(2)}) copy-start(bf16[512,512]{1,0:T(8,128)(2,1)} %refs_12_.1) | copy-start | bytes 1572868
  26.8 2.0 %copy-start.7 = (f32[8]{0:T(128)S(1)}, f32[8]{0:T(128)}, u32[]{:S(2)}) copy-start(f32[8]{0:T(128)} %param.18) | copy-start | bytes 100
  37.0 6.6 %collective-permute-start.6 = (bf16[544,128]{1,0:T(8,128)(2,1)S(1)}, bf16[544,128]{1,0:T(8,128)(2,1)S(1)}, u32[]{:S(2)}, u32[]{:S(2)}) collective-permute-start(bf16[544,128]{1,0:T(8,128)(2,1)S(1)} %send.3.refs_5_), channel_id=1, source_target_pairs={{0,2},{2,0},{4,6},{6,4},{8,10},{10,8},{12,14},{14,12},{1,3},{3,1},... | collective-permute-start | bytes 417800 | tf_op jit(solution)/shard_map/ppermute | solution.py:595
  38.5 5.8 %collective-permute-start.5 = (bf16[544,128]{1,0:T(8,128)(2,1)S(1)}, bf16[544,128]{1,0:T(8,128)(2,1)S(1)}, u32[]{:S(2)}, u32[]{:S(2)}) collective-permute-start(bf16[544,128]{1,0:T(8,128)(2,1)S(1)} %send.2.refs_5_), channel_id=1, source_target_pairs={{0,4},{2,6},{4,0},{6,2},{8,12},{10,14},{12,8},{14,10},{1,5},{3,7},... | collective-permute-start | bytes 417800 | tf_op jit(solution)/shard_map/ppermute | solution.py:595
  40.0 6.0 %collective-permute-start.4 = (bf16[544,128]{1,0:T(8,128)(2,1)S(1)}, bf16[544,128]{1,0:T(8,128)(2,1)S(1)}, u32[]{:S(2)}, u32[]{:S(2)}) collective-permute-start(bf16[544,128]{1,0:T(8,128)(2,1)S(1)} %get-tuple-element.72.refs_5_), channel_id=1, source_target_pairs={{0,6},{2,4},{4,2},{6,0},{8,14},{10,12},{12,10},{14,8},{1,7},{3,5},... | collective-permute-start | bytes 417800 | tf_op jit(solution)/shard_map/ppermute | solution.py:595
  40.5 12.1 %copy-start.4 = (bf16[512,512]{1,0:T(8,128)(2,1)S(1)}, bf16[512,512]{1,0:T(8,128)(2,1)}, u32[]{:S(2)}) copy-start(bf16[512,512]{1,0:T(8,128)(2,1)} %refs_3_.3) | copy-start | bytes 1572868
  46.1 6.5 %collective-permute-start.7 = (bf16[272,128]{1,0:T(8,128)(2,1)S(1)}, bf16[272,128]{1,0:T(8,128)(2,1)S(1)}, u32[]{:S(2)}, u32[]{:S(2)}) collective-permute-start(bf16[272,128]{1,0:T(8,128)(2,1)S(1)} %get-tuple-element.77), channel_id=1, source_target_pairs={{0,8},{2,10},{4,12},{6,14},{8,0},{10,2},{12,4},{14,6},{1,9},{3,11}... | collective-permute-start | bytes 208904 | tf_op jit(solution)/shard_map/ppermute | solution.py:595

commit v8 on v7

--- a/solution.py
+++ b/solution.py
@@ -104,9 +104,9 @@
         pltpu.make_async_copy(source, target, sem.at[k])
         for k, (source, target) in enumerate(
             (
-                (ids_in, ids), (stored_in, stored), (decay_in, decay), (middle, key_w),
+                (ids_in, ids), (stored_in, stored), (cand_in, cand), (decay_in, decay),
                 (own_in.at[: half // 2], own.at[: half // 2]),
-                (own_in.at[half // 2 :], own.at[half // 2 :]), (cand_in, cand),
+                (own_in.at[half // 2 :], own.at[half // 2 :]), (middle, key_w),
             )
         )
     ]
@@ -116,12 +116,12 @@
     copies[1].wait()
     slots = stored_slots(ids[...], stored[...])
     slot_o[...] = slots
-    copies[6].wait()
+    copies[2].wait()
     wide = jnp.concatenate([cand[...], jnp.zeros((1, LANES - cand.shape[1]), i32)], axis=1).astype(f32)
     high = jnp.floor(wide * (1.0 / LANES))
     low = pltpu.roll(jnp.broadcast_to(wide - high * LANES, (8, LANES)), LANES // 2, 1)[:1]
     id_rows_o[...] = jnp.where(first_half((1, LANES)), high, low)
-    copies[2].wait()
+    copies[3].wait()
     upto = jnp.where(
         iota((CHUNK, CHUNK), 0) <= iota((CHUNK, CHUNK), 1), 1.0, 0.0
     ).astype(bf16)
@@ -137,8 +137,6 @@
             ctl_o[r : r + 1, :] = jnp.where(
                 low, cum[2 * p : 2 * p + 1, CHUNK - 1 :], cum[2 * p + 1 : 2 * p + 2, CHUNK - 1 :]
             )
-    copies[3].wait()
-    key_w_o[...] = jnp.transpose(key_w[...].astype(f32)).astype(bf16)
     first = lax.axis_index("dp") * half
     for k in range(2):
         copies[4 + k].wait()
@@ -148,6 +146,8 @@
             if k:
                 rows += part_o[chunk(i), :].astype(f32)
             part_o[chunk(i), :] = rows.astype(bf16)
+    copies[6].wait()
+    key_w_o[...] = jnp.transpose(key_w[...].astype(f32)).astype(bf16)
 
 
 def summary_kernel(
@@ -698,12 +698,12 @@
     for t in (2, 1):
         (pay,) = call(
             send_kernel, "send", [here, scale, quarters[t], key_two, val_two],
-            [shape((message, LANES), bf16)], buffers, after=[pay], flops=work,
+            [shape((message, LANES), bf16)], buffers, after=[pay], flops=8 * work,
         )
         gots.append(swap(pay, t))
     mean, logs = call(
         keep_kernel, "keep", [here, scale, quarters[0], key_two, val_two],
-        [shape((width, LANES), f32), shape((heads, LANES), f32)], buffers, after=[pay], flops=work,
+        [shape((width, LANES), f32), shape((heads, LANES), f32)], buffers, after=[pay], flops=8 * work,
     )
     cols = LANES
     for bit in range(2, bits):

time: 53.8 us -> 51.4 us (0.955)
  starting transfers between devices: 15.2 us -> 14.2 us
  waiting for transfers between devices: 7.02 us -> 6.04 us
    ppermute x7, starting transfers between devices: 14.7 us -> 13.7 us  [swap(): return lax.ppermute(value, 'seq', [(j, j ^ mask) for j in range(seq)])]
    ppermute x7, waiting for transfers between devices: 7.02 us -> 6.04 us  [swap(): return lax.ppermute(value, 'seq', [(j, j ^ mask) for j in range(seq)])]
  transfers between devices with their start and end apart: 8 -> 8, of which waited for: 6 -> 4; matrix products, arithmetic and copies ran while one was open for 0% -> 0% of each run, Pallas kernels for 26% -> 27%
where the time goes in v8:
time: 51.4 us; the launch traced here: 51.2 us
  Pallas kernels  29.5 us (57%)
  starting transfers between devices  14.2 us (28%)
  waiting for transfers between devices  6.04 us (12%)
  between operations  1.43 us (3%)
    pallas_call x14, Pallas kernels, call(): pl.pallas_call(body, name=name, in_specs=[SMEM] * len(scalars) + [space]...  29.5 us
    ppermute x7, starting transfers between devices, swap(): return lax.ppermute(value, 'seq', [(j, j ^ mask) for j in range(seq)])  13.7 us
    ppermute x7, waiting for transfers between devices, swap(): return lax.ppermute(value, 'seq', [(j, j ^ mask) for j in range(seq)])  6.04 us
  transfers between devices with their start and end apart: 8, of which 4 were waited for; matrix products, arithmetic and copies ran while one was open for 0% of the time, Pallas kernels for 27%

profile of v8, /device:TPU:0, one launch (start us, length us, event | category | flops | bytes accessed | tf_op | source)
XLA Modules:
  0.0 51.2 jit_solution(7248354683724171502)
XLA Ops:
  0.6 0.5 %collective-permute-start = (bf16[2048,512]{1,0:T(8,128)(2,1)}, bf16[2048,512]{1,0:T(8,128)(2,1)S(1)}, u32[]{:S(2)}, u32[]{:S(2)}) collective-permute-start(bf16[2048,512]{1,0:T(8,128)(2,1)} %refs_2_.3), channel_id=1, source_target_pairs={{0,1},{1,0},{2,3},{3,2},{4,5},{5,4},{6,7},{7,6},{8,9},{9,8},{10,11... | collective-permute-start | bytes 6291464 | tf_op jit(solution)/shard_map/ppermute | solution.py:597
  1.8 0.0 copy-start.1
  1.8 4.6 %own_rows.1 = (bf16[1024,512]{1,0:T(8,128)(2,1)S(1)}, f32[1,1024]{1,0:T(1,128)S(1)}, f32[4,8,256]{2,1,0:T(8,128)S(1)}, f32[1024,16]{1,0:T(8,128)S(1)}, f32[16,12...) custom-call(s32[1,1024]{1,0:T(1,128)} %refs_0_.2, s32[32,128]{1,0:T(8,128)} %bitcast.5, ...), custom_call_target="tpu_custom_call" | custom-call | flops 2147483648 | tf_op jit(solution)/shard_map/own_rows/pallas_call | solution.py:551
  6.4 0.0 collective-permute-done.refs_2_.refs_3_
  6.4 0.0 copy-done.1
  6.4 4.4 %summary.1 = (bf16[1024,512]{1,0:T(8,128)(2,1)S(1)}, bf16[512,1024]{1,0:T(8,128)(2,1)S(1)}, bf16[1024,512]{1,0:T(8,128)(2,1)S(1)}, f32[4,256,128]{2,1,0:T(8,128)...) custom-call(s32[1]{0:T(128)S(6)} %copy.14.refs_0_, bf16[1024,512]{1,0:T(8,128)(2,1)S(1)} %get-tuple-element.40.refs_1_, ...), custom_call_target="tpu_custom_call" | custom-call | flops 2147483648 | tf_op jit(solution)/shard_map/summary/pallas_call | solution.py:551
  10.9 2.6 %collective-permute-start.1 = (bf16[272,128]{1,0:T(8,128)(2,1)S(1)}, bf16[272,128]{1,0:T(8,128)(2,1)S(1)}, u32[]{:S(2)}, u32[]{:S(2)}) collective-permute-start(bf16[272,128]{1,0:T(8,128)(2,1)S(1)} %get-tuple-element.52.refs_0_), channel_id=1, source_target_pairs={{0,2},{2,0},{4,6},{6,4},{8,10},{10,8},{12,14},{14,12},{1,3},{3,1},... | collective-permute-start | bytes 208904 | tf_op jit(solution)/shard_map/ppermute | solution.py:595
  13.4 2.6 %local_a.1 = (bf16[1024,256]{1,0:T(8,128)(2,1)S(1)}, f32[1024,256]{1,0:T(8,128)S(1)}) custom-call(bf16[1024,512]{1,0:T(8,128)(2,1)S(1)} %get-tuple-element.47.refs_0_.refs_2_, bf16[512,1024]{1,0:T(8,128)(2,1)S(1)} %get-tuple-element.48.refs_1_, bf16[1024,512]{1,0:T(8,128)(2,1)S(1)} %get-tuple-element.49.refs_2_, ...), custom_call_target="tpu_custom_call" | custom-call | flops 1073741824 | tf_op jit(solution)/shard_map/local_a/pallas_call | solution.py:551
  16.1 0.2 collective-permute-done.1.refs_1_
  16.3 0.1 join.2
  16.3 1.9 %collective-permute-start.2 = (bf16[272,128]{1,0:T(8,128)(2,1)S(1)}, bf16[272,128]{1,0:T(8,128)(2,1)S(1)}, u32[]{:S(2)}, u32[]{:S(2)}) collective-permute-start(bf16[272,128]{1,0:T(8,128)(2,1)S(1)} %get-tuple-element.58.refs_0_), channel_id=1, source_target_pairs={{0,4},{2,6},{4,0},{6,2},{8,12},{10,14},{12,8},{14,10},{1,5},{3,7},... | collective-permute-start | bytes 208904 | tf_op jit(solution)/shard_map/ppermute | solution.py:595
  18.2 0.0 copy-start
  18.2 0.0 copy-start.2
  18.2 0.0 copy-start.3
  18.2 0.0 copy-start.5
  18.2 2.8 %local_b.1 = (bf16[1024,256]{1,0:T(8,128)(2,1)S(1)}, f32[1024,256]{1,0:T(8,128)S(1)}) custom-call(bf16[1024,512]{1,0:T(8,128)(2,1)S(1)} %get-tuple-element.47.refs_0_.refs_2_, bf16[512,1024]{1,0:T(8,128)(2,1)S(1)} %get-tuple-element.48.refs_1_, bf16[1024,512]{1,0:T(8,128)(2,1)S(1)} %get-tuple-element.49.refs_2_, ...), custom_call_target="tpu_custom_call" | custom-call | flops 1073741824 | tf_op jit(solution)/shard_map/local_b/pallas_call | solution.py:551
  21.0 0.0 collective-permute-done.2.refs_1_
  21.1 0.1 join.3
  21.1 2.7 %collective-permute-start.3 = (bf16[272,128]{1,0:T(8,128)(2,1)S(1)}, bf16[272,128]{1,0:T(8,128)(2,1)S(1)}, u32[]{:S(2)}, u32[]{:S(2)}) collective-permute-start(bf16[272,128]{1,0:T(8,128)(2,1)S(1)} %get-tuple-element.60.refs_0_), channel_id=1, source_target_pairs={{0,8},{2,10},{4,12},{6,14},{8,0},{10,2},{12,4},{14,6},{1,9},{3,11}... | collective-permute-start | bytes 208904 | tf_op jit(solution)/shard_map/ppermute | solution.py:595
  23.8 0.0 copy-done
  23.8 0.0 copy-done.2
  23.8 0.0 copy-done.3
  23.8 0.0 copy-done.5
  23.8 1.9 %near.1 = (bf16[512,256]{1,0:T(8,128)(2,1)S(1)}, bf16[512,512]{1,0:T(8,128)(2,1)S(1)}) custom-call(bf16[272,128]{1,0:T(8,128)(2,1)S(1)} %get-tuple-element.60.refs_0_, s32[32,128]{1,0:T(8,128)S(1)} %bitcast.6, bf16[2048,512]{1,0:T(8,128)(2,1)S(1)} %copy-done, bf16[2048,512]{1,0:T(8,128)(2,1)S(1)} %collective-permute-done.refs_2_.refs_3_, ...), custom_call_target="tpu_custom_call" | custom-call | flops 1073741824 | tf_op jit(solution)/shard_map/near/pallas_call | solution.py:551
  25.7 0.7 %collective-permute-done.3.refs_0_.refs_9_ = bf16[272,128]{1,0:T(8,128)(2,1)S(1)} collective-permute-done((bf16[272,128]{1,0:T(8,128)(2,1)S(1)}, bf16[272,128]{1,0:T(8,128)(2,1)S(1)}, u32[]{:S(2)}, u32[]{:S(2)}) %collective-permute-start.3) | collective-permute-done | bytes 69664 | tf_op jit(solution)/shard_map/ppermute | solution.py:595
  26.4 0.0 copy-start.6
  26.4 0.0 copy-start.7
  26.4 2.0 %far.1 = (bf16[512,128]{1,0:T(8,128)(2,1)S(1)}, bf16[512,128]{1,0:T(8,128)(2,1)S(1)}, bf16[512,128]{1,0:T(8,128)(2,1)S(1)}, bf16[512,128]{1,0:T(8,128)(2,1)S(1)}) custom-call(bf16[272,128]{1,0:T(8,128)(2,1)S(1)} %collective-permute-done.3.refs_0_.refs_9_, s32[32,128]{1,0:T(8,128)S(1)} %bitcast.7, bf16[2048,512]{1,0:T(8,128)(2,1)S(1)} %copy-done, ...), custom_call_target="tpu_custom_call" | custom-call | flops 1073741824 | tf_op jit(solution)/shard_map/far/pallas_call | solution.py:551
  28.4 0.0 copy-done.6
  28.5 0.0 copy-done.7
  28.5 4.5 %finish.1 = (f32[1024,512]{1,0:T(8,128)}, bf16[1024,512]{1,0:T(8,128)(2,1)S(1)}, bf16[512,1024]{1,0:T(8,128)(2,1)S(1)}, bf16[544,128]{1,0:T(8,128)(2,1)S(1)}) custom-call(s32[8,128]{1,0:T(8,128)S(1)} %get-tuple-element.46.refs_0_, f32[1,8]{1,0:T(1,128)S(1)} %bitcast.8, bf16[1024,512]{1,0:T(8,128)(2,1)S(1)} %get-tuple-element.47.refs_0_.refs_2_, ...), custom_call_target="tpu_custom_call" | custom-call | flops 2147483648 | tf_op jit(solution)/shard_map/finish/pallas_call | solution.py:551
  33.0 2.5 %collective-permute-start.4 = (bf16[544,128]{1,0:T(8,128)(2,1)S(1)}, bf16[544,128]{1,0:T(8,128)(2,1)S(1)}, u32[]{:S(2)}, u32[]{:S(2)}) collective-permute-start(bf16[544,128]{1,0:T(8,128)(2,1)S(1)} %get-tuple-element.72.refs_5_), channel_id=1, source_target_pairs={{0,6},{2,4},{4,2},{6,0},{8,14},{10,12},{12,10},{14,8},{1,7},{3,5},... | collective-permute-start | bytes 417800 | tf_op jit(solution)/shard_map/ppermute | solution.py:595
  35.4 1.8 %send.2.refs_5_ = bf16[544,128]{1,0:T(8,128)(2,1)S(1)} custom-call(s32[8,128]{1,0:T(8,128)S(1)} %get-tuple-element.46.refs_0_, f32[1,8]{1,0:T(1,128)S(1)} %bitcast.9, bf16[512,128]{1,0:T(8,128)(2,1)S(1)} %get-tuple-element.71.refs_2_, bf16[1024,512]{1,0:T(8,128)(2,1)S(1)} %get-tuple-element.68.refs_3_, bf16[512,1024]{1,0:T(8,128)(2,1)S(1)} %get-tuple-element.69.refs_4_, ...), custom_call_target="tpu_custom_call" | custom-call | flops 8589934592 | tf_op jit(solution)/shard_map/send/pallas_call | solution.py:551
  37.2 0.6 %collective-permute-start.5 = (bf16[544,128]{1,0:T(8,128)(2,1)S(1)}, bf16[544,128]{1,0:T(8,128)(2,1)S(1)}, u32[]{:S(2)}, u32[]{:S(2)}) collective-permute-start(bf16[544,128]{1,0:T(8,128)(2,1)S(1)} %send.2.refs_5_), channel_id=1, source_target_pairs={{0,4},{2,6},{4,0},{6,2},{8,12},{10,14},{12,8},{14,10},{1,5},{3,7},... | collective-permute-start | bytes 417800 | tf_op jit(solution)/shard_map/ppermute | solution.py:595
  37.9 1.8 %send.3.refs_5_ = bf16[544,128]{1,0:T(8,128)(2,1)S(1)} custom-call(s32[8,128]{1,0:T(8,128)S(1)} %get-tuple-element.46.refs_0_, f32[1,8]{1,0:T(1,128)S(1)} %bitcast.10, bf16[512,128]{1,0:T(8,128)(2,1)S(1)} %get-tuple-element.70.refs_2_, bf16[1024,512]{1,0:T(8,128)(2,1)S(1)} %get-tuple-element.68.refs_3_, bf16[512,1024]{1,0:T(8,128)(2,1)S(1)} %get-tuple-element.69.refs_4_, ...), custom_call_target="tpu_custom_call" | custom-call | flops 8589934592 | tf_op jit(solution)/shard_map/send/pallas_call | solution.py:551
  39.7 0.6 %collective-permute-start.6 = (bf16[544,128]{1,0:T(8,128)(2,1)S(1)}, bf16[544,128]{1,0:T(8,128)(2,1)S(1)}, u32[]{:S(2)}, u32[]{:S(2)}) collective-permute-start(bf16[544,128]{1,0:T(8,128)(2,1)S(1)} %send.3.refs_5_), channel_id=1, source_target_pairs={{0,2},{2,0},{4,6},{6,4},{8,10},{10,8},{12,14},{14,12},{1,3},{3,1},... | collective-permute-start | bytes 417800 | tf_op jit(solution)/shard_map/ppermute | solution.py:595
  40.3 0.0 copy-start.4
  40.3 1.8 %keep.1 = (f32[512,128]{1,0:T(8,128)S(1)}, f32[8,128]{1,0:T(8,128)S(1)}) custom-call(s32[8,128]{1,0:T(8,128)S(1)} %get-tuple-element.46.refs_0_, f32[1,8]{1,0:T(1,128)S(1)} %bitcast.11, bf16[512,128]{1,0:T(8,128)(2,1)S(1)} %get-tuple-element.67.refs_2_, bf16[1024,512]{1,0:T(8,128)(2,1)S(1)} %get-tuple-element.68.refs_3_, ...), custom_call_target="tpu_custom_call" | custom-call | flops 8589934592 | tf_op jit(solution)/shard_map/keep/pallas_call | solution.py:551
  42.1 2.7 %collective-permute-done.6.refs_4_ = bf16[544,128]{1,0:T(8,128)(2,1)S(1)} collective-permute-done((bf16[544,128]{1,0:T(8,128)(2,1)S(1)}, bf16[544,128]{1,0:T(8,128)(2,1)S(1)}, u32[]{:S(2)}, u32[]{:S(2)}) %collective-permute-start.6) | collective-permute-done | bytes 139296 | tf_op jit(solution)/shard_map/ppermute | solution.py:595
  44.8 0.0 collective-permute-done.5.refs_3_
  44.8 0.0 collective-permute-done.4.refs_2_
  44.8 0.1 fold.1
  45.0 2.9 %collective-permute-start.7 = (bf16[272,128]{1,0:T(8,128)(2,1)S(1)}, bf16[272,128]{1,0:T(8,128)(2,1)S(1)}, u32[]{:S(2)}, u32[]{:S(2)}) collective-permute-start(bf16[272,128]{1,0:T(8,128)(2,1)S(1)} %get-tuple-element.77), channel_id=1, source_target_pairs={{0,8},{2,10},{4,12},{6,14},{8,0},{10,2},{12,4},{14,6},{1,9},{3,11}... | collective-permute-start | bytes 208904 | tf_op jit(solution)/shard_map/ppermute | solution.py:595
  47.8 2.4 %collective-permute-done.7.refs_2_ = bf16[272,128]{1,0:T(8,128)(2,1)S(1)} collective-permute-done((bf16[272,128]{1,0:T(8,128)(2,1)S(1)}, bf16[272,128]{1,0:T(8,128)(2,1)S(1)}, u32[]{:S(2)}, u32[]{:S(2)}) %collective-permute-start.7) | collective-permute-done | bytes 69664 | tf_op jit(solution)/shard_map/ppermute | solution.py:595
  50.2 0.0 copy-done.4
  50.2 1.0 %last.1 = f32[64,512]{1,0:T(8,128)} custom-call(f32[512,64]{1,0:T(8,128)S(1)} %get-tuple-element.75.refs_0_, f32[8,64]{1,0:T(8,128)S(1)} %get-tuple-element.76.refs_1_, bf16[272,128]{1,0:T(8,128)(2,1)S(1)} %collective-permute-done.7.refs_2_, bf16[512,512]{1,0:T(8,128)(2,1)S(1)} %copy-done.4), custom_call_target="tpu_custom_call" | custom-call | tf_op jit(solution)/shard_map/last/pallas_call | solution.py:551
Async XLA Ops:
  0.6 5.8 %collective-permute-start = (bf16[2048,512]{1,0:T(8,128)(2,1)}, bf16[2048,512]{1,0:T(8,128)(2,1)S(1)}, u32[]{:S(2)}, u32[]{:S(2)}) collective-permute-start(bf16[2048,512]{1,0:T(8,128)(2,1)} %refs_2_.3), channel_id=1, source_target_pairs={{0,1},{1,0},{2,3},{3,2},{4,5},{5,4},{6,7},{7,6},{8,9},{9,8},{10,11... | collective-permute-start | bytes 6291464 | tf_op jit(solution)/shard_map/ppermute | solution.py:597
  1.8 4.6 %copy-start.1 = (bf16[512,1536]{1,0:T(8,128)(2,1)S(1)}, bf16[512,1536]{1,0:T(8,128)(2,1)}, u32[]{:S(2)}) copy-start(bf16[512,1536]{1,0:T(8,128)(2,1)} %refs_5_.6) | copy-start | bytes 4718596
  10.9 5.4 %collective-permute-start.1 = (bf16[272,128]{1,0:T(8,128)(2,1)S(1)}, bf16[272,128]{1,0:T(8,128)(2,1)S(1)}, u32[]{:S(2)}, u32[]{:S(2)}) collective-permute-start(bf16[272,128]{1,0:T(8,128)(2,1)S(1)} %get-tuple-element.52.refs_0_), channel_id=1, source_target_pairs={{0,2},{2,0},{4,6},{6,4},{8,10},{10,8},{12,14},{14,12},{1,3},{3,1},... | collective-permute-start | bytes 208904 | tf_op jit(solution)/shard_map/ppermute | solution.py:595
  16.3 4.7 %collective-permute-start.2 = (bf16[272,128]{1,0:T(8,128)(2,1)S(1)}, bf16[272,128]{1,0:T(8,128)(2,1)S(1)}, u32[]{:S(2)}, u32[]{:S(2)}) collective-permute-start(bf16[272,128]{1,0:T(8,128)(2,1)S(1)} %get-tuple-element.58.refs_0_), channel_id=1, source_target_pairs={{0,4},{2,6},{4,0},{6,2},{8,12},{10,14},{12,8},{14,10},{1,5},{3,7},... | collective-permute-start | bytes 208904 | tf_op jit(solution)/shard_map/ppermute | solution.py:595
  18.2 5.6 %copy-start = (bf16[2048,512]{1,0:T(8,128)(2,1)S(1)}, bf16[2048,512]{1,0:T(8,128)(2,1)}, u32[]{:S(2)}) copy-start(bf16[2048,512]{1,0:T(8,128)(2,1)} %refs_2_.3) | copy-start | bytes 6291460
  18.2 5.6 %copy-start.2 = (bf16[512,512]{1,0:T(8,128)(2,1)S(1)}, bf16[512,512]{1,0:T(8,128)(2,1)}, u32[]{:S(2)}) copy-start(bf16[512,512]{1,0:T(8,128)(2,1)} %refs_4_.5) | copy-start | bytes 1572868
  18.2 5.6 %copy-start.3 = (bf16[512,1024]{1,0:T(8,128)(2,1)S(1)}, bf16[512,1024]{1,0:T(8,128)(2,1)}, u32[]{:S(2)}) copy-start(bf16[512,1024]{1,0:T(8,128)(2,1)} %refs_13_.1) | copy-start | bytes 3145732
  18.2 5.6 %copy-start.5 = (s32[4096]{0:T(1024)S(1)}, s32[4096]{0:T(1024)}, u32[]{:S(2)}) copy-start(s32[4096]{0:T(1024)} %param.16) | copy-start | bytes 49156
  21.1 5.3 %collective-permute-start.3 = (bf16[272,128]{1,0:T(8,128)(2,1)S(1)}, bf16[272,128]{1,0:T(8,128)(2,1)S(1)}, u32[]{:S(2)}, u32[]{:S(2)}) collective-permute-start(bf16[272,128]{1,0:T(8,128)(2,1)S(1)} %get-tuple-element.60.refs_0_), channel_id=1, source_target_pairs={{0,8},{2,10},{4,12},{6,14},{8,0},{10,2},{12,4},{14,6},{1,9},{3,11}... | collective-permute-start | bytes 208904 | tf_op jit(solution)/shard_map/ppermute | solution.py:595
  26.4 2.0 %copy-start.6 = (bf16[512,512]{1,0:T(8,128)(2,1)S(1)}, bf16[512,512]{1,0:T(8,128)(2,1)}, u32[]{:S(2)}) copy-start(bf16[512,512]{1,0:T(8,128)(2,1)} %refs_12_.1) | copy-start | bytes 1572868
  26.4 2.0 %copy-start.7 = (f32[8]{0:T(128)S(1)}, f32[8]{0:T(128)}, u32[]{:S(2)}) copy-start(f32[8]{0:T(128)} %param.18) | copy-start | bytes 100
  33.0 11.8 %collective-permute-start.4 = (bf16[544,128]{1,0:T(8,128)(2,1)S(1)}, bf16[544,128]{1,0:T(8,128)(2,1)S(1)}, u32[]{:S(2)}, u32[]{:S(2)}) collective-permute-start(bf16[544,128]{1,0:T(8,128)(2,1)S(1)} %get-tuple-element.72.refs_5_), channel_id=1, source_target_pairs={{0,6},{2,4},{4,2},{6,0},{8,14},{10,12},{12,10},{14,8},{1,7},{3,5},... | collective-permute-start | bytes 417800 | tf_op jit(solution)/shard_map/ppermute | solution.py:595
  37.2 7.5 %collective-permute-start.5 = (bf16[544,128]{1,0:T(8,128)(2,1)S(1)}, bf16[544,128]{1,0:T(8,128)(2,1)S(1)}, u32[]{:S(2)}, u32[]{:S(2)}) collective-permute-start(bf16[544,128]{1,0:T(8,128)(2,1)S(1)} %send.2.refs_5_), channel_id=1, source_target_pairs={{0,4},{2,6},{4,0},{6,2},{8,12},{10,14},{12,8},{14,10},{1,5},{3,7},... | collective-permute-start | bytes 417800 | tf_op jit(solution)/shard_map/ppermute | solution.py:595
  39.7 5.1 %collective-permute-start.6 = (bf16[544,128]{1,0:T(8,128)(2,1)S(1)}, bf16[544,128]{1,0:T(8,128)(2,1)S(1)}, u32[]{:S(2)}, u32[]{:S(2)}) collective-permute-start(bf16[544,128]{1,0:T(8,128)(2,1)S(1)} %send.3.refs_5_), channel_id=1, source_target_pairs={{0,2},{2,0},{4,6},{6,4},{8,10},{10,8},{12,14},{14,12},{1,3},{3,1},... | collective-permute-start | bytes 417800 | tf_op jit(solution)/shard_map/ppermute | solution.py:595
  40.3 9.9 %copy-start.4 = (bf16[512,512]{1,0:T(8,128)(2,1)S(1)}, bf16[512,512]{1,0:T(8,128)(2,1)}, u32[]{:S(2)}) copy-start(bf16[512,512]{1,0:T(8,128)(2,1)} %refs_3_.3) | copy-start | bytes 1572868
  45.0 5.3 %collective-permute-start.7 = (bf16[272,128]{1,0:T(8,128)(2,1)S(1)}, bf16[272,128]{1,0:T(8,128)(2,1)S(1)}, u32[]{:S(2)}, u32[]{:S(2)}) collective-permute-start(bf16[272,128]{1,0:T(8,128)(2,1)S(1)} %get-tuple-element.77), channel_id=1, source_target_pairs={{0,8},{2,10},{4,12},{6,14},{8,0},{10,2},{12,4},{14,6},{1,9},{3,11}... | collective-permute-start | bytes 208904 | tf_op jit(solution)/shard_map/ppermute | solution.py:595

commit v9 on v8

--- a/solution.py
+++ b/solution.py
@@ -93,9 +93,8 @@
 
 
 def own_rows_kernel(
-    ids_in, stored_in, decay_in, own_in, weight_in, cand_in,
-    part_o, slot_o, crow_o, ccol_o, ctl_o, key_w_o, id_rows_o,
-    ids, stored, decay, own, key_w, cand, sem,
+    ids_in, stored_in, decay_in, own_in, weight_in, part_o, slot_o, crow_o, ccol_o, ctl_o, key_w_o,
+    ids, stored, decay, own, key_w, sem,
 ):
     n, half, heads = ids.shape[1], own.shape[0], decay.shape[0]
     width = own.shape[1]
@@ -104,7 +103,7 @@
         pltpu.make_async_copy(source, target, sem.at[k])
         for k, (source, target) in enumerate(
             (
-                (ids_in, ids), (stored_in, stored), (cand_in, cand), (decay_in, decay),
+                (ids_in, ids), (stored_in, stored), (decay_in, decay),
                 (own_in.at[: half // 2], own.at[: half // 2]),
                 (own_in.at[half // 2 :], own.at[half // 2 :]), (middle, key_w),
             )
@@ -117,11 +116,6 @@
     slots = stored_slots(ids[...], stored[...])
     slot_o[...] = slots
     copies[2].wait()
-    wide = jnp.concatenate([cand[...], jnp.zeros((1, LANES - cand.shape[1]), i32)], axis=1).astype(f32)
-    high = jnp.floor(wide * (1.0 / LANES))
-    low = pltpu.roll(jnp.broadcast_to(wide - high * LANES, (8, LANES)), LANES // 2, 1)[:1]
-    id_rows_o[...] = jnp.where(first_half((1, LANES)), high, low)
-    copies[3].wait()
     upto = jnp.where(
         iota((CHUNK, CHUNK), 0) <= iota((CHUNK, CHUNK), 1), 1.0, 0.0
     ).astype(bf16)
@@ -139,14 +133,14 @@
             )
     first = lax.axis_index("dp") * half
     for k in range(2):
-        copies[4 + k].wait()
+        copies[3 + k].wait()
         piece = own.at[k * half // 2 : (k + 1) * half // 2]
         for i in range(n // CHUNK):
             rows = picked_rows(slots[:, chunk(i)], first + k * half // 2, piece)
             if k:
                 rows += part_o[chunk(i), :].astype(f32)
             part_o[chunk(i), :] = rows.astype(bf16)
-    copies[6].wait()
+    copies[5].wait()
     key_w_o[...] = jnp.transpose(key_w[...].astype(f32)).astype(bf16)
 
 
@@ -229,7 +223,7 @@
 
 def join_kernel(bit, ids, pairs, mine, got, *refs):
     before = refs[: 2 if bit else 0]
-    pay_o, prefix_o, logs_o = refs[len(before) :]
+    pay_o, prefix_o, logs_o, *ids_o = refs[len(before) :]
     upper = (lax.axis_index("seq") >> bit) & 1 == 1
     state, logs, rows = unpack_state(mine[...], pairs)
     other, other_logs, other_rows = unpack_state(got[...], pairs)
@@ -237,7 +231,10 @@
     late = jnp.where(upper, state, other)
     factor = row_factors(jnp.where(upper, logs, other_logs))
     id_rows = jnp.concatenate([rows[:ids], other_rows[:ids]], axis=0)
-    pay_o[...] = pack_state(early * factor + late, logs + other_logs, id_rows)
+    if ids_o:
+        ids_o[0][...] = id_rows
+    sent = id_rows[:1] if ids_o else id_rows
+    pay_o[...] = pack_state(early * factor + late, logs + other_logs, sent)
     if bit == 0:
         prefix_o[...] = jnp.where(upper, other, 0.0)
         logs_o[...] = jnp.where(upper, other_logs, 0.0)
@@ -289,47 +286,32 @@
             intra_o[chunk(i), pair_cut(p)] = held + part
 
 
-def candidate_queries(ids, owned, message, stored, own, peer, query_w):
+def candidate_kernel(
+    order, owned, id_rows, stored, own, peer, query_w, pair_w, val_w_o, *quarters
+):
     half, width = own.shape
-    pairs = width // LANES
-    rows = message[pairs * 64 :, :].astype(f32)
-    rows = (rows * float(LANES) + pltpu.roll(rows, LANES // 2, 1)).astype(i32)[3 * pairs :]
-    slots = [stored_slots(rows[j : j + 1], stored[...]) for j in range(ids)]
+    ids = id_rows[...]
+    ids = (ids * float(LANES) + pltpu.roll(ids, LANES // 2, 1)).astype(i32)
     step = LANES // owned
-    tiles = []
-    for start in range(0, ids, step):
-        tile = slots[start]
-        for k in range(1, step):
-            moved = pltpu.roll(slots[start + k], k * owned, 1)
-            tile = jnp.where(iota((1, LANES), 1) >= k * owned, moved, tile)
-        tiles.append(tile)
-    slots = jnp.concatenate(tiles, axis=1)
     dp = lax.axis_index("dp")
-    found = picked_rows(slots, dp * half, own) + picked_rows(slots, (1 - dp) * half, peer)
-    return jnp.transpose(dot(found.astype(bf16), query_w[...]))
-
-
-def near_kernel(ids, owned, message, stored, own, peer, query_w, pair_w, query_o, val_w_o):
-    query = candidate_queries(ids, owned, message, stored, own, peer, query_w)
-    query_o[...] = query.astype(bf16)
-    val_w_o[...] = jnp.transpose(pair_w[:, own.shape[1] :].astype(f32)).astype(bf16)
-
-
-def far_kernel(ids, owned, message, stored, own, peer, query_w, *refs):
-    far = candidate_queries(ids, owned, message, stored, own, peer, query_w)
-    if len(refs) == 1:
-        refs[0][...] = far.astype(bf16)
-        return
-    near, outs = refs[0][...].astype(f32), refs[1:]
-    low = first_half((1, LANES))
-    for k, out in enumerate(outs):
-        cut = pair_cut(k // 2)
-        left, right = near[:, cut], far[:, cut]
-        if k % 2:
-            left = pltpu.roll(left, LANES // 2, 1)
-        else:
-            right = pltpu.roll(right, LANES // 2, 1)
-        out[...] = jnp.where(low, left, right).astype(bf16)
+    for start in range(0, len(order), 2 * step):
+        tiles = []
+        for first in (start, start + step):
+            tile = None
+            for k in range(step):
+                j = order[first + k]
+                slots = stored_slots(ids[j : j + 1], stored[...])
+                if k:
+                    moved = pltpu.roll(slots, k * owned, 1)
+                    slots = jnp.where(iota((1, LANES), 1) >= k * owned, moved, tile)
+                tile = slots
+            tiles.append(tile)
+        slots = jnp.concatenate(tiles, axis=1)
+        found = picked_rows(slots, dp * half, own) + picked_rows(slots, (1 - dp) * half, peer)
+        query = jnp.transpose(dot(found.astype(bf16), query_w[...])).astype(bf16)
+        for k in (0, 1):
+            quarters[start // step + k][...] = query[:, pair_cut(k)]
+    val_w_o[...] = jnp.transpose(pair_w[:, width:].astype(f32)).astype(bf16)
 
 
 def attend(alive_count, scale, query, key, val, buffers, emit):
@@ -595,25 +577,29 @@
         return lax.ppermute(value, "seq", [(j, j ^ mask) for j in range(seq)])
 
     peer = lax.ppermute(item_embedding_table, "dp", [(0, 1), (1, 0)])
+    far_ids = swap(candidate_item_index, seq // 2)
     scale = head_score_scale.reshape(1, heads)
     stored = item_stored_row.reshape(-1, LANES)
+    ids = jnp.concatenate([candidate_item_index, far_ids], axis=0)
+    ids = jnp.pad(ids, ((0, 0), (0, 64 - owned)))
+    id_rows = jnp.concatenate([ids // LANES, ids % LANES], axis=1).astype(f32)
     decay = log_head_retention.reshape(heads, n)
 
-    part, slot, crow, ccol, ctl, key_w, id_rows = call(
+    part, slot, crow, ccol, ctl, key_w = call(
         own_rows_kernel, "own_rows",
         [
             history_item_index, stored, decay, item_embedding_table,
-            history_query_key_value_weight, candidate_item_index,
+            history_query_key_value_weight,
         ],
         [
             shape((n, width), bf16), shape((1, n), f32), shape((n // CHUNK, heads, CHUNK), f32),
             shape((n, 2 * heads), f32), shape((n // CHUNK * pairs, LANES), f32),
-            shape((width, width), bf16), shape((1, LANES), f32),
+            shape((width, width), bf16),
         ],
         [
             pltpu.VMEM((1, n), i32), pltpu.VMEM(stored.shape, i32), pltpu.VMEM((heads, n), f32),
             pltpu.VMEM((half, width), bf16), pltpu.VMEM((width, width), bf16),
-            pltpu.VMEM((1, owned), i32), pltpu.SemaphoreType.DMA((7,)),
+            pltpu.SemaphoreType.DMA((6,)),
         ],
         space=HBM,
         flops=2 * n * half * width,
@@ -623,7 +609,7 @@
         [part, peer, slot, crow, ctl, id_rows, key_w, history_query_key_value_weight],
         [
             shape((n, width), bf16), shape((width, n), bf16), shape((n, width), bf16),
-            shape((n // CHUNK, rows, LANES), f32), shape((state_rows(pairs, 1), LANES), bf16),
+            shape((n // CHUNK, rows, LANES), f32), shape((state_rows(pairs, 2), LANES), bf16),
             shape((8, LANES), i32),
         ],
         scalars=[user_history_length],
@@ -644,39 +630,29 @@
         got = swap(pay, 1 << bit)
         if bit == 1:
             early.append(local(width // 2, "local_b", [prefix]))
-        count = 1 << bit
-        pay, prefix, logs = call(
+        count = 2 << bit
+        final = bit == bits - 2
+        pay, prefix, logs, *every = call(
             lambda *refs, bit=bit, count=count: join_kernel(bit, count, pairs, *refs), "join",
             [pay, got] + ([prefix, logs] if bit else []),
             [
-                shape((state_rows(pairs, 2 * count), LANES), bf16), shape((rows, LANES), f32),
-                shape((pairs, LANES), f32),
-            ],
+                shape((state_rows(pairs, 1 if final else 2 * count), LANES), bf16),
+                shape((rows, LANES), f32), shape((pairs, LANES), f32),
+            ] + [shape((2 * count, LANES), f32)] * final,
             after=[early[-1][1]],
         )
     got = swap(pay, 1 << (bits - 1))
-    half_seq = seq // 2
-    tables = [stored, item_embedding_table, peer, candidate_query_weight]
+    order = [t + 4 * reversed_bits(k, bits - 2) for t in range(4) for k in range(seq // 4)]
+    order = [2 * (j % (seq // 2)) + j // (seq // 2) for j in order]
     work = cands * 2 * half * width
-    near, val_w = call(
-        lambda *refs: near_kernel(half_seq, owned, *refs), "near",
-        [pay, *tables, candidate_key_value_weight],
-        [shape((width, cands // 2), bf16), shape((width, width), bf16)], flops=work,
-    )
-    if 2 * owned == LANES:
-        quarters = call(
-            lambda *refs: far_kernel(half_seq, owned, *refs), "far", [got, *tables, near],
-            [shape((width, LANES), bf16)] * 4, flops=work,
-        )
-    else:
-        (far,) = call(
-            lambda *refs: far_kernel(half_seq, owned, *refs), "far", [got, *tables],
-            [shape((width, cands // 2), bf16)], flops=work,
-        )
-        order = [t + 4 * reversed_bits(k, bits - 2) for t in range(4) for k in range(seq // 4)]
-        every = jnp.concatenate([near, far], axis=1).reshape(width, seq, owned)
-        every = every[:, jnp.array(order)].reshape(width, cands)
-        quarters = [every[:, t * LANES : (t + 1) * LANES] for t in range(4)]
+    val_w, *quarters = call(
+        lambda *refs: candidate_kernel(order, owned, *refs), "candidates",
+        [
+            every[0], stored, item_embedding_table, peer, candidate_query_weight,
+            candidate_key_value_weight,
+        ],
+        [shape((width, width), bf16)] + [shape((width, LANES), bf16)] * 4, flops=2 * work,
+    )
     (query_a, intra_a), (query_b, intra_b) = early
     buffers = [pltpu.VMEM((n, 2 * LANES), f32)] * 2
     message = width + log_pad(heads)

time: 51.4 us -> 51.8 us (level)
  waiting for transfers between devices: 6.04 us -> 8.01 us
  starting transfers between devices: 14.2 us -> 12.9 us
    ppermute x7 -> x8, waiting for transfers between devices: 6.04 us -> 8 us  [swap(): return lax.ppermute(value, 'seq', [(j, j ^ mask) for j in range(seq)])]
    ppermute x7 -> x8, starting transfers between devices: 13.7 us -> 12.3 us  [swap(): return lax.ppermute(value, 'seq', [(j, j ^ mask) for j in range(seq)])]
    pallas_call x14 -> x13, Pallas kernels: 29.5 us -> 29.2 us  [call(): pl.pallas_call(body, name=name, in_specs=[SMEM] * len(scalars) + [space]...]
  transfers between devices with their start and end apart: 8 -> 9, of which waited for: 4 -> 4; matrix products, arithmetic and copies ran while one was open for 0% -> 0% of each run, Pallas kernels for 27% -> 30%
where the time goes in v9:
time: 51.8 us; the launch traced here: 51.6 us
  Pallas kernels  29.2 us (56%)
  starting transfers between devices  12.9 us (25%)
  waiting for transfers between devices  8.01 us (15%)
  between operations  1.42 us (3%)
    pallas_call x13, Pallas kernels, call(): pl.pallas_call(body, name=name, in_specs=[SMEM] * len(scalars) + [space]...  29.2 us
    ppermute x8, starting transfers between devices, swap(): return lax.ppermute(value, 'seq', [(j, j ^ mask) for j in range(seq)])  12.3 us
    ppermute x8, waiting for transfers between devices, swap(): return lax.ppermute(value, 'seq', [(j, j ^ mask) for j in range(seq)])  8 us
  transfers between devices with their start and end apart: 9, of which 4 were waited for; matrix products, arithmetic and copies ran while one was open for 0% of the time, Pallas kernels for 30%

profile of v9, /device:TPU:0, one launch (start us, length us, event | category | flops | bytes accessed | tf_op | source)
XLA Modules:
  0.0 51.6 jit_solution(14959780741264494829)
XLA Ops:
  0.6 0.5 %collective-permute-start = (bf16[2048,512]{1,0:T(8,128)(2,1)}, bf16[2048,512]{1,0:T(8,128)(2,1)S(1)}, u32[]{:S(2)}, u32[]{:S(2)}) collective-permute-start(bf16[2048,512]{1,0:T(8,128)(2,1)} %refs_2_.1), channel_id=1, source_target_pairs={{0,1},{1,0},{2,3},{3,2},{4,5},{5,4},{6,7},{7,6},{8,9},{9,8},{10,11... | collective-permute-start | bytes 6291464 | tf_op jit(solution)/shard_map/ppermute | solution.py:579
  1.1 3.7 %collective-permute-start.1 = (s32[1,64]{1,0:T(1,128)}, s32[1,64]{1,0:T(1,128)S(1)}, u32[]{:S(2)}, u32[]{:S(2)}) collective-permute-start(s32[1,64]{1,0:T(1,128)} %param.15), channel_id=1, source_target_pairs={{0,8},{2,10},{4,12},{6,14},{8,0},{10,2},{12,4},{14,6},{1,9},{3,11}... | collective-permute-start | bytes 776 | tf_op jit(solution)/shard_map/ppermute | solution.py:577
  4.8 0.0 copy-start.8
  4.8 0.0 copy-start
  4.8 4.6 %own_rows.1 = (bf16[1024,512]{1,0:T(8,128)(2,1)S(1)}, f32[1,1024]{1,0:T(1,128)S(1)}, f32[4,8,256]{2,1,0:T(8,128)S(1)}, f32[1024,16]{1,0:T(8,128)S(1)}, f32[16,12...) custom-call(s32[1,1024]{1,0:T(1,128)} %refs_0_.2, s32[32,128]{1,0:T(8,128)} %bitcast.5, f32[8,1024]{1,0:T(8,128)} %bitcast.12, ...), custom_call_target="tpu_custom_call" | custom-call | flops 2147483648 | tf_op jit(solution)/shard_map/own_rows/pallas_call | solution.py:533
  10.0 0.0 collective-permute-done.1
  10.0 0.0 copy-done.8
  10.1 0.1 add_convert_fusion.refs_6_
  10.1 0.0 collective-permute-done.refs_2_.refs_3_
  10.1 0.0 copy-done
  10.2 4.4 %summary.1 = (bf16[1024,512]{1,0:T(8,128)(2,1)S(1)}, bf16[512,1024]{1,0:T(8,128)(2,1)S(1)}, bf16[1024,512]{1,0:T(8,128)(2,1)S(1)}, f32[4,256,128]{2,1,0:T(8,128)...) custom-call(s32[1]{0:T(128)S(6)} %copy.14.refs_0_, bf16[1024,512]{1,0:T(8,128)(2,1)S(1)} %get-tuple-element.39.refs_1_, ...), custom_call_target="tpu_custom_call" | custom-call | flops 2147483648 | tf_op jit(solution)/shard_map/summary/pallas_call | solution.py:533
  14.6 1.6 %collective-permute-start.2 = (bf16[272,128]{1,0:T(8,128)(2,1)S(1)}, bf16[272,128]{1,0:T(8,128)(2,1)S(1)}, u32[]{:S(2)}, u32[]{:S(2)}) collective-permute-start(bf16[272,128]{1,0:T(8,128)(2,1)S(1)} %get-tuple-element.50.refs_0_), channel_id=1, source_target_pairs={{0,2},{2,0},{4,6},{6,4},{8,10},{10,8},{12,14},{14,12},{1,3},{3,1},... | collective-permute-start | bytes 208904 | tf_op jit(solution)/shard_map/ppermute | solution.py:577
  16.1 2.7 %local_a.1 = (bf16[1024,256]{1,0:T(8,128)(2,1)S(1)}, f32[1024,256]{1,0:T(8,128)S(1)}) custom-call(bf16[1024,512]{1,0:T(8,128)(2,1)S(1)} %get-tuple-element.45.refs_0_.refs_2_, bf16[512,1024]{1,0:T(8,128)(2,1)S(1)} %get-tuple-element.46.refs_1_, bf16[1024,512]{1,0:T(8,128)(2,1)S(1)} %get-tuple-element.47.refs_2_, ...), custom_call_target="tpu_custom_call" | custom-call | flops 1073741824 | tf_op jit(solution)/shard_map/local_a/pallas_call | solution.py:533
  18.8 0.1 collective-permute-done.2.refs_1_
  19.0 0.1 join.2
  19.0 1.6 %collective-permute-start.3 = (bf16[272,128]{1,0:T(8,128)(2,1)S(1)}, bf16[272,128]{1,0:T(8,128)(2,1)S(1)}, u32[]{:S(2)}, u32[]{:S(2)}) collective-permute-start(bf16[272,128]{1,0:T(8,128)(2,1)S(1)} %get-tuple-element.56.refs_0_), channel_id=1, source_target_pairs={{0,4},{2,6},{4,0},{6,2},{8,12},{10,14},{12,8},{14,10},{1,5},{3,7},... | collective-permute-start | bytes 208904 | tf_op jit(solution)/shard_map/ppermute | solution.py:577
  20.6 0.0 copy-start.2
  20.6 0.0 copy-start.3
  20.7 0.0 copy-start.4
  20.7 2.9 %local_b.1 = (bf16[1024,256]{1,0:T(8,128)(2,1)S(1)}, f32[1024,256]{1,0:T(8,128)S(1)}) custom-call(bf16[1024,512]{1,0:T(8,128)(2,1)S(1)} %get-tuple-element.45.refs_0_.refs_2_, bf16[512,1024]{1,0:T(8,128)(2,1)S(1)} %get-tuple-element.46.refs_1_, bf16[1024,512]{1,0:T(8,128)(2,1)S(1)} %get-tuple-element.47.refs_2_, ...), custom_call_target="tpu_custom_call" | custom-call | flops 1073741824 | tf_op jit(solution)/shard_map/local_b/pallas_call | solution.py:533
  23.5 0.0 collective-permute-done.3.refs_1_
  23.5 0.1 join.3
  23.6 0.4 collective-permute-start.4
  24.0 0.0 copy-done.2
  24.0 0.0 copy-done.3
  24.0 0.0 copy-done.4
  24.0 0.0 copy-done.6
  24.0 0.0 copy-start.5
  24.0 0.0 copy-start.7
  24.0 3.6 %candidates.1 = (bf16[512,512]{1,0:T(8,128)(2,1)S(1)}, bf16[512,128]{1,0:T(8,128)(2,1)S(1)}, bf16[512,128]{1,0:T(8,128)(2,1)S(1)}, bf16[512,128]{1,0:T(8,128)(2,1)S(1)}, bf16[512,128]{1,0:T(8,128)(2,1)S(1)}) custom-call(f32[8,128]{1,0:T(8,128)S(1)} %get-tuple-element.61.refs_0_, s32[32,128]{1,0:T(8,128)S(1)} %bitcast.6, bf16[2048,512]{1,0:T(8,128)(2,1)S(1)} %copy-done.2, ...), custom_call_target="tpu_custom_call" | custom-call | flops 2147483648 | tf_op jit(solution)/shard_map/candidates/pallas_call | solution.py:533
  27.6 1.3 %collective-permute-done.4.refs_9_ = bf16[272,128]{1,0:T(8,128)(2,1)S(1)} collective-permute-done((bf16[272,128]{1,0:T(8,128)(2,1)S(1)}, bf16[272,128]{1,0:T(8,128)(2,1)S(1)}, u32[]{:S(2)}, u32[]{:S(2)}) %collective-permute-start.4) | collective-permute-done | bytes 69664 | tf_op jit(solution)/shard_map/ppermute | solution.py:577
  28.9 0.0 copy-done.5
  28.9 0.0 copy-done.7
  28.9 4.6 %finish.1 = (f32[1024,512]{1,0:T(8,128)}, bf16[1024,512]{1,0:T(8,128)(2,1)S(1)}, bf16[512,1024]{1,0:T(8,128)(2,1)S(1)}, bf16[544,128]{1,0:T(8,128)(2,1)S(1)}) custom-call(s32[8,128]{1,0:T(8,128)S(1)} %get-tuple-element.44.refs_0_, f32[1,8]{1,0:T(1,128)S(1)} %bitcast.7, bf16[1024,512]{1,0:T(8,128)(2,1)S(1)} %get-tuple-element.45.refs_0_.refs_2_, ...), custom_call_target="tpu_custom_call" | custom-call | flops 2147483648 | tf_op jit(solution)/shard_map/finish/pallas_call | solution.py:533
  33.5 2.4 %collective-permute-start.5 = (bf16[544,128]{1,0:T(8,128)(2,1)S(1)}, bf16[544,128]{1,0:T(8,128)(2,1)S(1)}, u32[]{:S(2)}, u32[]{:S(2)}) collective-permute-start(bf16[544,128]{1,0:T(8,128)(2,1)S(1)} %get-tuple-element.70.refs_5_), channel_id=1, source_target_pairs={{0,6},{2,4},{4,2},{6,0},{8,14},{10,12},{12,10},{14,8},{1,7},{3,5},... | collective-permute-start | bytes 417800 | tf_op jit(solution)/shard_map/ppermute | solution.py:577
  35.9 1.8 %send.2.refs_5_ = bf16[544,128]{1,0:T(8,128)(2,1)S(1)} custom-call(s32[8,128]{1,0:T(8,128)S(1)} %get-tuple-element.44.refs_0_, f32[1,8]{1,0:T(1,128)S(1)} %bitcast.8, bf16[512,128]{1,0:T(8,128)(2,1)S(1)} %get-tuple-element.69.refs_2_, bf16[1024,512]{1,0:T(8,128)(2,1)S(1)} %get-tuple-element.66.refs_3_, bf16[512,1024]{1,0:T(8,128)(2,1)S(1)} %get-tuple-element.67.refs_4_, ...), custom_call_target="tpu_custom_call" | custom-call | flops 8589934592 | tf_op jit(solution)/shard_map/send/pallas_call | solution.py:533
  37.6 0.7 %collective-permute-start.6 = (bf16[544,128]{1,0:T(8,128)(2,1)S(1)}, bf16[544,128]{1,0:T(8,128)(2,1)S(1)}, u32[]{:S(2)}, u32[]{:S(2)}) collective-permute-start(bf16[544,128]{1,0:T(8,128)(2,1)S(1)} %send.2.refs_5_), channel_id=1, source_target_pairs={{0,4},{2,6},{4,0},{6,2},{8,12},{10,14},{12,8},{14,10},{1,5},{3,7},... | collective-permute-start | bytes 417800 | tf_op jit(solution)/shard_map/ppermute | solution.py:577
  38.3 1.8 %send.3.refs_5_ = bf16[544,128]{1,0:T(8,128)(2,1)S(1)} custom-call(s32[8,128]{1,0:T(8,128)S(1)} %get-tuple-element.44.refs_0_, f32[1,8]{1,0:T(1,128)S(1)} %bitcast.9, bf16[512,128]{1,0:T(8,128)(2,1)S(1)} %get-tuple-element.68.refs_2_, bf16[1024,512]{1,0:T(8,128)(2,1)S(1)} %get-tuple-element.66.refs_3_, bf16[512,1024]{1,0:T(8,128)(2,1)S(1)} %get-tuple-element.67.refs_4_, ...), custom_call_target="tpu_custom_call" | custom-call | flops 8589934592 | tf_op jit(solution)/shard_map/send/pallas_call | solution.py:533
  40.1 0.6 %collective-permute-start.7 = (bf16[544,128]{1,0:T(8,128)(2,1)S(1)}, bf16[544,128]{1,0:T(8,128)(2,1)S(1)}, u32[]{:S(2)}, u32[]{:S(2)}) collective-permute-start(bf16[544,128]{1,0:T(8,128)(2,1)S(1)} %send.3.refs_5_), channel_id=1, source_target_pairs={{0,2},{2,0},{4,6},{6,4},{8,10},{10,8},{12,14},{14,12},{1,3},{3,1},... | collective-permute-start | bytes 417800 | tf_op jit(solution)/shard_map/ppermute | solution.py:577
  40.7 1.8 %keep.1 = (f32[512,128]{1,0:T(8,128)S(1)}, f32[8,128]{1,0:T(8,128)S(1)}) custom-call(s32[8,128]{1,0:T(8,128)S(1)} %get-tuple-element.44.refs_0_, f32[1,8]{1,0:T(1,128)S(1)} %bitcast.10, bf16[512,128]{1,0:T(8,128)(2,1)S(1)} %get-tuple-element.65.refs_2_, bf16[1024,512]{1,0:T(8,128)(2,1)S(1)} %get-tuple-element.66.refs_3_, ...), custom_call_target="tpu_custom_call" | custom-call | flops 8589934592 | tf_op jit(solution)/shard_map/keep/pallas_call | solution.py:533
  42.5 2.7 %collective-permute-done.7.refs_4_ = bf16[544,128]{1,0:T(8,128)(2,1)S(1)} collective-permute-done((bf16[544,128]{1,0:T(8,128)(2,1)S(1)}, bf16[544,128]{1,0:T(8,128)(2,1)S(1)}, u32[]{:S(2)}, u32[]{:S(2)}) %collective-permute-start.7) | collective-permute-done | bytes 139296 | tf_op jit(solution)/shard_map/ppermute | solution.py:577
  45.2 0.0 collective-permute-done.6.refs_3_
  45.2 0.0 collective-permute-done.5.refs_2_
  45.2 0.1 fold.1
  45.4 1.4 %collective-permute-start.8 = (bf16[272,128]{1,0:T(8,128)(2,1)S(1)}, bf16[272,128]{1,0:T(8,128)(2,1)S(1)}, u32[]{:S(2)}, u32[]{:S(2)}) collective-permute-start(bf16[272,128]{1,0:T(8,128)(2,1)S(1)} %get-tuple-element.75), channel_id=1, source_target_pairs={{0,8},{2,10},{4,12},{6,14},{8,0},{10,2},{12,4},{14,6},{1,9},{3,11}... | collective-permute-start | bytes 208904 | tf_op jit(solution)/shard_map/ppermute | solution.py:577
  46.8 3.9 %collective-permute-done.8.refs_2_ = bf16[272,128]{1,0:T(8,128)(2,1)S(1)} collective-permute-done((bf16[272,128]{1,0:T(8,128)(2,1)S(1)}, bf16[272,128]{1,0:T(8,128)(2,1)S(1)}, u32[]{:S(2)}, u32[]{:S(2)}) %collective-permute-start.8) | collective-permute-done | bytes 69664 | tf_op jit(solution)/shard_map/ppermute | solution.py:577
  50.7 0.0 copy-done.1
  50.7 1.0 %last.1 = f32[64,512]{1,0:T(8,128)} custom-call(f32[512,64]{1,0:T(8,128)S(1)} %get-tuple-element.73.refs_0_, f32[8,64]{1,0:T(8,128)S(1)} %get-tuple-element.74.refs_1_, bf16[272,128]{1,0:T(8,128)(2,1)S(1)} %collective-permute-done.8.refs_2_, bf16[512,512]{1,0:T(8,128)(2,1)S(1)} %copy-done.1), custom_call_target="tpu_custom_call" | custom-call | tf_op jit(solution)/shard_map/last/pallas_call | solution.py:533
  (3 shorter events, 0.0 us)
Async XLA Ops:
  0.6 9.5 %collective-permute-start = (bf16[2048,512]{1,0:T(8,128)(2,1)}, bf16[2048,512]{1,0:T(8,128)(2,1)S(1)}, u32[]{:S(2)}, u32[]{:S(2)}) collective-permute-start(bf16[2048,512]{1,0:T(8,128)(2,1)} %refs_2_.1), channel_id=1, source_target_pairs={{0,1},{1,0},{2,3},{3,2},{4,5},{5,4},{6,7},{7,6},{8,9},{9,8},{10,11... | collective-permute-start | bytes 6291464 | tf_op jit(solution)/shard_map/ppermute | solution.py:579
  1.1 8.9 %collective-permute-start.1 = (s32[1,64]{1,0:T(1,128)}, s32[1,64]{1,0:T(1,128)S(1)}, u32[]{:S(2)}, u32[]{:S(2)}) collective-permute-start(s32[1,64]{1,0:T(1,128)} %param.15), channel_id=1, source_target_pairs={{0,8},{2,10},{4,12},{6,14},{8,0},{10,2},{12,4},{14,6},{1,9},{3,11}... | collective-permute-start | bytes 776 | tf_op jit(solution)/shard_map/ppermute | solution.py:577
  4.8 5.2 %copy-start.8 = (s32[1,64]{1,0:T(1,128)S(1)}, s32[1,64]{1,0:T(1,128)}, u32[]{:S(2)}) copy-start(s32[1,64]{1,0:T(1,128)} %param.15) | copy-start | bytes 772
  4.8 5.3 %copy-start = (bf16[512,1536]{1,0:T(8,128)(2,1)S(1)}, bf16[512,1536]{1,0:T(8,128)(2,1)}, u32[]{:S(2)}) copy-start(bf16[512,1536]{1,0:T(8,128)(2,1)} %refs_5_.4) | copy-start | bytes 4718596
  14.6 4.4 %collective-permute-start.2 = (bf16[272,128]{1,0:T(8,128)(2,1)S(1)}, bf16[272,128]{1,0:T(8,128)(2,1)S(1)}, u32[]{:S(2)}, u32[]{:S(2)}) collective-permute-start(bf16[272,128]{1,0:T(8,128)(2,1)S(1)} %get-tuple-element.50.refs_0_), channel_id=1, source_target_pairs={{0,2},{2,0},{4,6},{6,4},{8,10},{10,8},{12,14},{14,12},{1,3},{3,1},... | collective-permute-start | bytes 208904 | tf_op jit(solution)/shard_map/ppermute | solution.py:577
  19.0 4.5 %collective-permute-start.3 = (bf16[272,128]{1,0:T(8,128)(2,1)S(1)}, bf16[272,128]{1,0:T(8,128)(2,1)S(1)}, u32[]{:S(2)}, u32[]{:S(2)}) collective-permute-start(bf16[272,128]{1,0:T(8,128)(2,1)S(1)} %get-tuple-element.56.refs_0_), channel_id=1, source_target_pairs={{0,4},{2,6},{4,0},{6,2},{8,12},{10,14},{12,8},{14,10},{1,5},{3,7},... | collective-permute-start | bytes 208904 | tf_op jit(solution)/shard_map/ppermute | solution.py:577
  20.6 3.3 %copy-start.2 = (bf16[2048,512]{1,0:T(8,128)(2,1)S(1)}, bf16[2048,512]{1,0:T(8,128)(2,1)}, u32[]{:S(2)}) copy-start(bf16[2048,512]{1,0:T(8,128)(2,1)} %refs_2_.1) | copy-start | bytes 6291460
  20.6 3.3 %copy-start.3 = (bf16[512,1024]{1,0:T(8,128)(2,1)S(1)}, bf16[512,1024]{1,0:T(8,128)(2,1)}, u32[]{:S(2)}) copy-start(bf16[512,1024]{1,0:T(8,128)(2,1)} %refs_13_.1) | copy-start | bytes 3145732
  20.7 3.3 %copy-start.4 = (bf16[512,512]{1,0:T(8,128)(2,1)S(1)}, bf16[512,512]{1,0:T(8,128)(2,1)}, u32[]{:S(2)}) copy-start(bf16[512,512]{1,0:T(8,128)(2,1)} %refs_4_.3) | copy-start | bytes 1572868
  20.7 3.3 %copy-start.6 = (s32[4096]{0:T(1024)S(1)}, s32[4096]{0:T(1024)}, u32[]{:S(2)}) copy-start(s32[4096]{0:T(1024)} %param.16) | copy-start | bytes 49156
  23.6 5.3 %collective-permute-start.4 = (bf16[272,128]{1,0:T(8,128)(2,1)S(1)}, bf16[272,128]{1,0:T(8,128)(2,1)S(1)}, u32[]{:S(2)}, u32[]{:S(2)}) collective-permute-start(bf16[272,128]{1,0:T(8,128)(2,1)S(1)} %get-tuple-element.58), channel_id=1, source_target_pairs={{0,8},{2,10},{4,12},{6,14},{8,0},{10,2},{12,4},{14,6},{1,9},{3,11}... | collective-permute-start | bytes 208904 | tf_op jit(solution)/shard_map/ppermute | solution.py:577
  24.0 4.9 %copy-start.5 = (bf16[512,512]{1,0:T(8,128)(2,1)S(1)}, bf16[512,512]{1,0:T(8,128)(2,1)}, u32[]{:S(2)}) copy-start(bf16[512,512]{1,0:T(8,128)(2,1)} %refs_12_.1) | copy-start | bytes 1572868
  24.0 4.9 %copy-start.7 = (f32[8]{0:T(128)S(1)}, f32[8]{0:T(128)}, u32[]{:S(2)}) copy-start(f32[8]{0:T(128)} %param.18) | copy-start | bytes 100
  33.5 11.8 %collective-permute-start.5 = (bf16[544,128]{1,0:T(8,128)(2,1)S(1)}, bf16[544,128]{1,0:T(8,128)(2,1)S(1)}, u32[]{:S(2)}, u32[]{:S(2)}) collective-permute-start(bf16[544,128]{1,0:T(8,128)(2,1)S(1)} %get-tuple-element.70.refs_5_), channel_id=1, source_target_pairs={{0,6},{2,4},{4,2},{6,0},{8,14},{10,12},{12,10},{14,8},{1,7},{3,5},... | collective-permute-start | bytes 417800 | tf_op jit(solution)/shard_map/ppermute | solution.py:577
  37.6 7.6 %collective-permute-start.6 = (bf16[544,128]{1,0:T(8,128)(2,1)S(1)}, bf16[544,128]{1,0:T(8,128)(2,1)S(1)}, u32[]{:S(2)}, u32[]{:S(2)}) collective-permute-start(bf16[544,128]{1,0:T(8,128)(2,1)S(1)} %send.2.refs_5_), channel_id=1, source_target_pairs={{0,4},{2,6},{4,0},{6,2},{8,12},{10,14},{12,8},{14,10},{1,5},{3,7},... | collective-permute-start | bytes 417800 | tf_op jit(solution)/shard_map/ppermute | solution.py:577
  40.1 5.1 %collective-permute-start.7 = (bf16[544,128]{1,0:T(8,128)(2,1)S(1)}, bf16[544,128]{1,0:T(8,128)(2,1)S(1)}, u32[]{:S(2)}, u32[]{:S(2)}) collective-permute-start(bf16[544,128]{1,0:T(8,128)(2,1)S(1)} %send.3.refs_5_), channel_id=1, source_target_pairs={{0,2},{2,0},{4,6},{6,4},{8,10},{10,8},{12,14},{14,12},{1,3},{3,1},... | collective-permute-start | bytes 417800 | tf_op jit(solution)/shard_map/ppermute | solution.py:577
  40.7 9.9 %copy-start.1 = (bf16[512,512]{1,0:T(8,128)(2,1)S(1)}, bf16[512,512]{1,0:T(8,128)(2,1)}, u32[]{:S(2)}) copy-start(bf16[512,512]{1,0:T(8,128)(2,1)} %refs_3_.3) | copy-start | bytes 1572868
  45.4 5.3 %collective-permute-start.8 = (bf16[272,128]{1,0:T(8,128)(2,1)S(1)}, bf16[272,128]{1,0:T(8,128)(2,1)S(1)}, u32[]{:S(2)}, u32[]{:S(2)}) collective-permute-start(bf16[272,128]{1,0:T(8,128)(2,1)S(1)} %get-tuple-element.75), channel_id=1, source_target_pairs={{0,8},{2,10},{4,12},{6,14},{8,0},{10,2},{12,4},{14,6},{1,9},{3,11}... | collective-permute-start | bytes 208904 | tf_op jit(solution)/shard_map/ppermute | solution.py:577

commit v10 on v9

--- a/solution.py
+++ b/solution.py
@@ -314,59 +314,65 @@
     val_w_o[...] = jnp.transpose(pair_w[:, width:].astype(f32)).astype(bf16)
 
 
-def attend(alive_count, scale, query, key, val, buffers, emit):
+def attend(alive_count, scale, queries, key, val, buffers, emit):
     n, width = key.shape
     blocks = range(0, n, KEYS)
-    pairs = width // LANES
     ones = jnp.ones((16, KEYS), bf16)
-
-    def weights_of(p):
-        rows = query[pair_cut(p), :]
-        zero = jnp.zeros((64, LANES), bf16)
-        top = jnp.concatenate([rows[:64], zero], axis=1)
-        return jnp.concatenate([top, jnp.concatenate([zero, rows[64:]], axis=1)], axis=0)
-
-    def store(p, block, weights, peak):
-        values = dot(key[block : block + KEYS, pair_cut(p)], weights)
+    heads = width // 64
+    if len(queries) == 1:
+        units = [[(h, 0), (h + 1, 0)] for h in range(0, heads, 2)]
+    else:
+        units = [[(h, 0), (h, 1)] for h in range(heads)]
+
+    def weights_of(unit):
+        parts = []
+        for h, k in unit:
+            rows = queries[k][h * 64 : (h + 1) * 64, :]
+            zero = jnp.zeros_like(rows)
+            parts.append(jnp.concatenate([zero, rows] if h % 2 else [rows, zero], axis=0))
+        return jnp.concatenate(parts, axis=1)
+
+    def store(u, block, weights, peak):
+        values = dot(key[block : block + KEYS, pair_cut(units[u][0][0] // 2)], weights)
         values = jnp.where(iota((KEYS, 1), 0) < alive_count - block, values, DEAD)
-        buffers[p % 2][block : block + KEYS, :] = values
+        buffers[u % 2][block : block + KEYS, :] = values
         top = jnp.max(values.reshape(KEYS // 8, 8, 2 * LANES), axis=0)
         return top if peak is None else jnp.maximum(peak, top)
 
-    peak, weights = None, weights_of(0)
+    peak, weights = None, weights_of(units[0])
     for block in blocks:
         peak = store(0, block, weights, peak)
-    for p in range(pairs):
-        factor = [
-            jnp.broadcast_to(scale[0:1, h : h + 1], (1, LANES)) for h in (2 * p, 2 * p + 1)
-        ]
+    for u, unit in enumerate(units):
+        factor = [jnp.broadcast_to(scale[0:1, h : h + 1], (1, LANES)) for h, _ in unit]
         factor = jnp.concatenate(factor, axis=1) * LOG2E
+        first = unit[0][0] * 64
+        rows = (unit[-1][0] + 1) * 64 - first
         peak = jnp.max(peak, axis=0, keepdims=True)
         following = sums = None
-        more = p + 1 < pairs
+        more = u + 1 < len(units)
         if more:
-            weights = weights_of(p + 1)
+            weights = weights_of(units[u + 1])
         for block in blocks:
             if more:
-                following = store(p + 1, block, weights, following)
-            gap = buffers[p % 2][block : block + KEYS, :] - peak
+                following = store(u + 1, block, weights, following)
+            gap = buffers[u % 2][block : block + KEYS, :] - peak
             probs = jnp.exp2(gap * factor).astype(bf16)
-            side = jnp.concatenate([val[pair_cut(p), block : block + KEYS], ones], axis=0)
-            part = dot(side, probs)
+            side = [val[first : first + rows, block : block + KEYS], ones]
+            part = dot(jnp.concatenate(side, axis=0), probs)
             sums = part if sums is None else sums + part
-        total = sums[LANES : LANES + 1]
+        total = sums[rows : rows + 1]
         logs = live(alive_count, peak * factor + jnp.log2(total))
-        for b in (0, 1):
-            cut = pair_cut(b)
-            mean = sums[b * 64 : (b + 1) * 64, cut] / total[:, cut]
-            emit(2 * p + b, mean, logs[:, cut])
+        for b, (h, k) in enumerate(unit):
+            top = h * 64 - first
+            mean = sums[top : top + 64, pair_cut(b)] / total[:, pair_cut(b)]
+            emit(h, k, mean, logs[:, pair_cut(b)])
         peak = following
 
 
 def finish_kernel(
     bit, here, scale, emb, query_a, query_b, intra_a, intra_b, enter, ctl, got, prefix, prefix_logs,
-    out_w, pair_w, val_w, cand_q, hist_o, key_o, val_o, pay_o,
-    shown, sem, *buffers,
+    out_w, pair_w, val_w, cand_a, cand_b,
+    hist_o, key_o, val_o, pay_a, pay_b, shown, sem, *buffers,
 ):
     n, width = emb.shape
     pairs = width // LANES
@@ -413,24 +419,25 @@
         hidden = hidden_sum.astype(bf16)
         key_o[chunk(i), :] = dot(hidden, pair_w[:, :width]).astype(bf16)
         val_o[:, chunk(i)] = contract(val_w[...], hidden, 1, 1).astype(bf16)
-    send_part(alive_count, scale, cand_q, key_o, val_o, pay_o, buffers)
+    send_part(alive_count, scale, (cand_a, cand_b), key_o, val_o, (pay_a, pay_b), buffers)
     for copy in copies:
         copy.wait()
 
 
-def send_part(alive_count, scale, query, key, val, pay_o, buffers):
-    log_rows = []
-
-    def emit(h, mean, logs):
-        pay_o[h * 64 : (h + 1) * 64, :] = mean.astype(bf16)
-        log_rows.append(logs)
-
-    attend(alive_count, scale, query, key, val, buffers, emit)
-    pay_o[val.shape[0] :, :] = pack_logs(jnp.concatenate(log_rows, axis=0))
+def send_part(alive_count, scale, queries, key, val, pays, buffers):
+    log_rows = [[] for _ in pays]
+
+    def emit(h, k, mean, logs):
+        pays[k][h * 64 : (h + 1) * 64, :] = mean.astype(bf16)
+        log_rows[k].append(logs)
+
+    attend(alive_count, scale, queries, key, val, buffers, emit)
+    for pay, rows in zip(pays, log_rows):
+        pay[val.shape[0] :, :] = pack_logs(jnp.concatenate(rows, axis=0))
 
 
 def send_kernel(here, scale, query, key, val, pay_o, *buffers):
-    send_part(here[0:1, 0:1], scale, query, key, val, pay_o, buffers)
+    send_part(here[0:1, 0:1], scale, (query,), key, val, (pay_o,), buffers)
 
 
 def live(alive_count, logs):
@@ -454,11 +461,11 @@
 
 
 def keep_kernel(here, scale, query, key, val, mean_o, logs_o, *buffers):
-    def emit(h, mean, logs):
+    def emit(h, k, mean, logs):
         mean_o[h * 64 : (h + 1) * 64, :] = mean
         logs_o[h : h + 1, :] = logs
 
-    attend(here[0:1, 0:1], scale, query, key, val, buffers, emit)
+    attend(here[0:1, 0:1], scale, (query,), key, val, buffers, emit)
 
 
 def over_heads(rows):
@@ -656,27 +663,26 @@
     (query_a, intra_a), (query_b, intra_b) = early
     buffers = [pltpu.VMEM((n, 2 * LANES), f32)] * 2
     message = width + log_pad(heads)
-    hist, key_two, val_two, pay = call(
+    hist, key_two, val_two, pay, pay_b = call(
         lambda *refs: finish_kernel(bits - 1, *refs), "finish",
         [
             here, scale, emb, query_a, query_b, intra_a, intra_b, enter, ctl, got, prefix, logs,
-            history_output_weight, candidate_key_value_weight, val_w, quarters[3],
+            history_output_weight, candidate_key_value_weight, val_w, quarters[3], quarters[2],
         ],
         [
             shape((n, width), f32), shape((n, width), bf16), shape((width, n), bf16),
-            shape((message, LANES), bf16),
+            shape((message, LANES), bf16), shape((message, LANES), bf16),
         ],
         [pltpu.VMEM((n, width), f32), pltpu.SemaphoreType.DMA((n // CHUNK,))] + buffers,
-        spaces=[ANY, VMEM, VMEM, VMEM],
+        spaces=[ANY, VMEM, VMEM, VMEM, VMEM],
         flops=2 * n * half * width,
     )
-    gots = [swap(pay, 3)]
-    for t in (2, 1):
-        (pay,) = call(
-            send_kernel, "send", [here, scale, quarters[t], key_two, val_two],
-            [shape((message, LANES), bf16)], buffers, after=[pay], flops=8 * work,
-        )
-        gots.append(swap(pay, t))
+    gots = [swap(pay, 3), swap(pay_b, 2)]
+    (pay,) = call(
+        send_kernel, "send", [here, scale, quarters[1], key_two, val_two],
+        [shape((message, LANES), bf16)], buffers, after=[pay, pay_b], flops=20 * work,
+    )
+    gots.append(swap(pay, 1))
     mean, logs = call(
         keep_kernel, "keep", [here, scale, quarters[0], key_two, val_two],
         [shape((width, LANES), f32), shape((heads, LANES), f32)], buffers, after=[pay], flops=8 * work,

time: 51.8 us -> 51.3 us (level)
    pallas_call x13 -> x12, Pallas kernels: 29.2 us -> 28.8 us  [call(): pl.pallas_call(body, name=name, in_specs=[SMEM] * len(scalars) + [space]...]
where the time goes in v10:
time: 51.3 us; the launch traced here: 51.1 us
  Pallas kernels  28.8 us (56%)
  starting transfers between devices  12.8 us (25%)
  waiting for transfers between devices  7.99 us (16%)
  between operations  1.42 us (3%)
    pallas_call x12, Pallas kernels, call(): pl.pallas_call(body, name=name, in_specs=[SMEM] * len(scalars) + [space]...  28.8 us
    ppermute x8, starting transfers between devices, swap(): return lax.ppermute(value, 'seq', [(j, j ^ mask) for j in range(seq)])  12.3 us
    ppermute x8, waiting for transfers between devices, swap(): return lax.ppermute(value, 'seq', [(j, j ^ mask) for j in range(seq)])  7.99 us
  transfers between devices with their start and end apart: 9, of which 4 were waited for; matrix products, arithmetic and copies ran while one was open for 0% of the time, Pallas kernels for 30%

profile of v10, /device:TPU:0, one launch (start us, length us, event | category | flops | bytes accessed | tf_op | source)
XLA Modules:
  0.0 51.1 jit_solution(14516246368647236698)
XLA Ops:
  0.6 0.5 %collective-permute-start = (bf16[2048,512]{1,0:T(8,128)(2,1)}, bf16[2048,512]{1,0:T(8,128)(2,1)S(1)}, u32[]{:S(2)}, u32[]{:S(2)}) collective-permute-start(bf16[2048,512]{1,0:T(8,128)(2,1)} %refs_2_.1), channel_id=1, source_target_pairs={{0,1},{1,0},{2,3},{3,2},{4,5},{5,4},{6,7},{7,6},{8,9},{9,8},{10,11... | collective-permute-start | bytes 6291464 | tf_op jit(solution)/shard_map/ppermute | solution.py:586
  1.1 3.7 %collective-permute-start.1 = (s32[1,64]{1,0:T(1,128)}, s32[1,64]{1,0:T(1,128)S(1)}, u32[]{:S(2)}, u32[]{:S(2)}) collective-permute-start(s32[1,64]{1,0:T(1,128)} %param.15), channel_id=1, source_target_pairs={{0,8},{2,10},{4,12},{6,14},{8,0},{10,2},{12,4},{14,6},{1,9},{3,11}... | collective-permute-start | bytes 776 | tf_op jit(solution)/shard_map/ppermute | solution.py:584
  4.8 0.0 copy-start.8
  4.8 0.0 copy-start
  4.8 4.6 %own_rows.1 = (bf16[1024,512]{1,0:T(8,128)(2,1)S(1)}, f32[1,1024]{1,0:T(1,128)S(1)}, f32[4,8,256]{2,1,0:T(8,128)S(1)}, f32[1024,16]{1,0:T(8,128)S(1)}, f32[16,12...) custom-call(s32[1,1024]{1,0:T(1,128)} %refs_0_.2, s32[32,128]{1,0:T(8,128)} %bitcast.5, f32[8,1024]{1,0:T(8,128)} %bitcast.11, ...), custom_call_target="tpu_custom_call" | custom-call | flops 2147483648 | tf_op jit(solution)/shard_map/own_rows/pallas_call | solution.py:540
  10.0 0.0 collective-permute-done.1
  10.0 0.0 copy-done.8
  10.1 0.1 add_convert_fusion.refs_6_
  10.1 0.0 collective-permute-done.refs_2_.refs_3_
  10.1 0.0 copy-done
  10.2 4.4 %summary.1 = (bf16[1024,512]{1,0:T(8,128)(2,1)S(1)}, bf16[512,1024]{1,0:T(8,128)(2,1)S(1)}, bf16[1024,512]{1,0:T(8,128)(2,1)S(1)}, f32[4,256,128]{2,1,0:T(8,128)...) custom-call(s32[1]{0:T(128)S(6)} %copy.14.refs_0_, bf16[1024,512]{1,0:T(8,128)(2,1)S(1)} %get-tuple-element.40.refs_1_, ...), custom_call_target="tpu_custom_call" | custom-call | flops 2147483648 | tf_op jit(solution)/shard_map/summary/pallas_call | solution.py:540
  14.6 1.6 %collective-permute-start.2 = (bf16[272,128]{1,0:T(8,128)(2,1)S(1)}, bf16[272,128]{1,0:T(8,128)(2,1)S(1)}, u32[]{:S(2)}, u32[]{:S(2)}) collective-permute-start(bf16[272,128]{1,0:T(8,128)(2,1)S(1)} %get-tuple-element.51.refs_0_), channel_id=1, source_target_pairs={{0,2},{2,0},{4,6},{6,4},{8,10},{10,8},{12,14},{14,12},{1,3},{3,1},... | collective-permute-start | bytes 208904 | tf_op jit(solution)/shard_map/ppermute | solution.py:584
  16.1 2.7 %local_a.1 = (bf16[1024,256]{1,0:T(8,128)(2,1)S(1)}, f32[1024,256]{1,0:T(8,128)S(1)}) custom-call(bf16[1024,512]{1,0:T(8,128)(2,1)S(1)} %get-tuple-element.46.refs_0_.refs_2_, bf16[512,1024]{1,0:T(8,128)(2,1)S(1)} %get-tuple-element.47.refs_1_, bf16[1024,512]{1,0:T(8,128)(2,1)S(1)} %get-tuple-element.48.refs_2_, ...), custom_call_target="tpu_custom_call" | custom-call | flops 1073741824 | tf_op jit(solution)/shard_map/local_a/pallas_call | solution.py:540
  18.8 0.1 collective-permute-done.2.refs_1_
  19.0 0.1 join.2
  19.0 1.6 %collective-permute-start.3 = (bf16[272,128]{1,0:T(8,128)(2,1)S(1)}, bf16[272,128]{1,0:T(8,128)(2,1)S(1)}, u32[]{:S(2)}, u32[]{:S(2)}) collective-permute-start(bf16[272,128]{1,0:T(8,128)(2,1)S(1)} %get-tuple-element.57.refs_0_), channel_id=1, source_target_pairs={{0,4},{2,6},{4,0},{6,2},{8,12},{10,14},{12,8},{14,10},{1,5},{3,7},... | collective-permute-start | bytes 208904 | tf_op jit(solution)/shard_map/ppermute | solution.py:584
  20.6 0.0 copy-start.2
  20.6 0.0 copy-start.3
  20.7 0.0 copy-start.4
  20.7 0.0 copy-start.6
  20.7 2.9 %local_b.1 = (bf16[1024,256]{1,0:T(8,128)(2,1)S(1)}, f32[1024,256]{1,0:T(8,128)S(1)}) custom-call(bf16[1024,512]{1,0:T(8,128)(2,1)S(1)} %get-tuple-element.46.refs_0_.refs_2_, bf16[512,1024]{1,0:T(8,128)(2,1)S(1)} %get-tuple-element.47.refs_1_, bf16[1024,512]{1,0:T(8,128)(2,1)S(1)} %get-tuple-element.48.refs_2_, ...), custom_call_target="tpu_custom_call" | custom-call | flops 1073741824 | tf_op jit(solution)/shard_map/local_b/pallas_call | solution.py:540
  23.5 0.0 collective-permute-done.3.refs_1_
  23.5 0.1 join.3
  23.6 0.4 collective-permute-start.4
  24.0 0.0 copy-done.2
  24.0 0.0 copy-done.3
  24.0 0.0 copy-done.4
  24.0 0.0 copy-done.6
  24.0 0.0 copy-start.5
  24.0 0.0 copy-start.7
  24.0 3.6 %candidates.1 = (bf16[512,512]{1,0:T(8,128)(2,1)S(1)}, bf16[512,128]{1,0:T(8,128)(2,1)S(1)}, bf16[512,128]{1,0:T(8,128)(2,1)S(1)}, bf16[512,128]{1,0:T(8,128)(2,1)S(1)}, bf16[512,128]{1,0:T(8,128)(2,1)S(1)}) custom-call(f32[8,128]{1,0:T(8,128)S(1)} %get-tuple-element.62.refs_0_, s32[32,128]{1,0:T(8,128)S(1)} %bitcast.6, bf16[2048,512]{1,0:T(8,128)(2,1)S(1)} %copy-done.2, ...), custom_call_target="tpu_custom_call" | custom-call | flops 2147483648 | tf_op jit(solution)/shard_map/candidates/pallas_call | solution.py:540
  27.6 1.3 %collective-permute-done.4.refs_9_ = bf16[272,128]{1,0:T(8,128)(2,1)S(1)} collective-permute-done((bf16[272,128]{1,0:T(8,128)(2,1)S(1)}, bf16[272,128]{1,0:T(8,128)(2,1)S(1)}, u32[]{:S(2)}, u32[]{:S(2)}) %collective-permute-start.4) | collective-permute-done | bytes 69664 | tf_op jit(solution)/shard_map/ppermute | solution.py:584
  28.9 0.0 copy-done.5
  28.9 0.0 copy-done.7
  28.9 5.9 %finish.1 = (f32[1024,512]{1,0:T(8,128)}, bf16[1024,512]{1,0:T(8,128)(2,1)S(1)}, bf16[512,1024]{1,0:T(8,128)(2,1)S(1)}, bf16[544,128]{1,0:T(8,128)(2,1)S(1)}, bf16[544,128]{1,0:T(8,128)(2,1)S(1)}) custom-call(s32[8,128]{1,0:T(8,128)S(1)} %get-tuple-element.45.refs_0_, f32[1,8]{1,0:T(1,128)S(1)} %bitcast.7, ...), custom_call_target="tpu_custom_call" | custom-call | flops 2147483648 | tf_op jit(solution)/shard_map/finish/pallas_call | solution.py:540
  34.8 2.4 %collective-permute-start.5 = (bf16[544,128]{1,0:T(8,128)(2,1)S(1)}, bf16[544,128]{1,0:T(8,128)(2,1)S(1)}, u32[]{:S(2)}, u32[]{:S(2)}) collective-permute-start(bf16[544,128]{1,0:T(8,128)(2,1)S(1)} %get-tuple-element.71.refs_5_), channel_id=1, source_target_pairs={{0,6},{2,4},{4,2},{6,0},{8,14},{10,12},{12,10},{14,8},{1,7},{3,5},... | collective-permute-start | bytes 417800 | tf_op jit(solution)/shard_map/ppermute | solution.py:584
  37.2 0.6 %collective-permute-start.6 = (bf16[544,128]{1,0:T(8,128)(2,1)S(1)}, bf16[544,128]{1,0:T(8,128)(2,1)S(1)}, u32[]{:S(2)}, u32[]{:S(2)}) collective-permute-start(bf16[544,128]{1,0:T(8,128)(2,1)S(1)} %get-tuple-element.72.refs_6_), channel_id=1, source_target_pairs={{0,4},{2,6},{4,0},{6,2},{8,12},{10,14},{12,8},{14,10},{1,5},{3,7},... | collective-permute-start | bytes 417800 | tf_op jit(solution)/shard_map/ppermute | solution.py:584
  37.8 1.8 %send.1.refs_5_ = bf16[544,128]{1,0:T(8,128)(2,1)S(1)} custom-call(s32[8,128]{1,0:T(8,128)S(1)} %get-tuple-element.45.refs_0_, f32[1,8]{1,0:T(1,128)S(1)} %bitcast.8, bf16[512,128]{1,0:T(8,128)(2,1)S(1)} %get-tuple-element.70.refs_2_, bf16[1024,512]{1,0:T(8,128)(2,1)S(1)} %get-tuple-element.68.refs_3_, bf16[512,1024]{1,0:T(8,128)(2,1)S(1)} %get-tuple-element.69.refs_4_, ...), custom_call_target="tpu_custom_call" | custom-call | flops 21474836480 | tf_op jit(solution)/shard_map/send/pallas_call | solution.py:540
  39.6 0.6 %collective-permute-start.7 = (bf16[544,128]{1,0:T(8,128)(2,1)S(1)}, bf16[544,128]{1,0:T(8,128)(2,1)S(1)}, u32[]{:S(2)}, u32[]{:S(2)}) collective-permute-start(bf16[544,128]{1,0:T(8,128)(2,1)S(1)} %send.1.refs_5_), channel_id=1, source_target_pairs={{0,2},{2,0},{4,6},{6,4},{8,10},{10,8},{12,14},{14,12},{1,3},{3,1},... | collective-permute-start | bytes 417800 | tf_op jit(solution)/shard_map/ppermute | solution.py:584
  40.2 1.8 %keep.1 = (f32[512,128]{1,0:T(8,128)S(1)}, f32[8,128]{1,0:T(8,128)S(1)}) custom-call(s32[8,128]{1,0:T(8,128)S(1)} %get-tuple-element.45.refs_0_, f32[1,8]{1,0:T(1,128)S(1)} %bitcast.9, bf16[512,128]{1,0:T(8,128)(2,1)S(1)} %get-tuple-element.67.refs_2_, bf16[1024,512]{1,0:T(8,128)(2,1)S(1)} %get-tuple-element.68.refs_3_, ...), custom_call_target="tpu_custom_call" | custom-call | flops 8589934592 | tf_op jit(solution)/shard_map/keep/pallas_call | solution.py:540
  42.0 2.7 %collective-permute-done.7.refs_4_ = bf16[544,128]{1,0:T(8,128)(2,1)S(1)} collective-permute-done((bf16[544,128]{1,0:T(8,128)(2,1)S(1)}, bf16[544,128]{1,0:T(8,128)(2,1)S(1)}, u32[]{:S(2)}, u32[]{:S(2)}) %collective-permute-start.7) | collective-permute-done | bytes 139296 | tf_op jit(solution)/shard_map/ppermute | solution.py:584
  44.7 0.0 collective-permute-done.5.refs_2_
  44.7 0.0 collective-permute-done.6.refs_3_
  44.7 0.1 fold.1
  44.9 1.4 %collective-permute-start.8 = (bf16[272,128]{1,0:T(8,128)(2,1)S(1)}, bf16[272,128]{1,0:T(8,128)(2,1)S(1)}, u32[]{:S(2)}, u32[]{:S(2)}) collective-permute-start(bf16[272,128]{1,0:T(8,128)(2,1)S(1)} %get-tuple-element.77), channel_id=1, source_target_pairs={{0,8},{2,10},{4,12},{6,14},{8,0},{10,2},{12,4},{14,6},{1,9},{3,11}... | collective-permute-start | bytes 208904 | tf_op jit(solution)/shard_map/ppermute | solution.py:584
  46.3 3.8 %collective-permute-done.8.refs_2_ = bf16[272,128]{1,0:T(8,128)(2,1)S(1)} collective-permute-done((bf16[272,128]{1,0:T(8,128)(2,1)S(1)}, bf16[272,128]{1,0:T(8,128)(2,1)S(1)}, u32[]{:S(2)}, u32[]{:S(2)}) %collective-permute-start.8) | collective-permute-done | bytes 69664 | tf_op jit(solution)/shard_map/ppermute | solution.py:584
  50.1 0.0 copy-done.1
  50.1 1.0 %last.1 = f32[64,512]{1,0:T(8,128)} custom-call(f32[512,64]{1,0:T(8,128)S(1)} %get-tuple-element.75.refs_0_, f32[8,64]{1,0:T(8,128)S(1)} %get-tuple-element.76.refs_1_, bf16[272,128]{1,0:T(8,128)(2,1)S(1)} %collective-permute-done.8.refs_2_, bf16[512,512]{1,0:T(8,128)(2,1)S(1)} %copy-done.1), custom_call_target="tpu_custom_call" | custom-call | tf_op jit(solution)/shard_map/last/pallas_call | solution.py:540
  (2 shorter events, 0.0 us)
Async XLA Ops:
  0.6 9.5 %collective-permute-start = (bf16[2048,512]{1,0:T(8,128)(2,1)}, bf16[2048,512]{1,0:T(8,128)(2,1)S(1)}, u32[]{:S(2)}, u32[]{:S(2)}) collective-permute-start(bf16[2048,512]{1,0:T(8,128)(2,1)} %refs_2_.1), channel_id=1, source_target_pairs={{0,1},{1,0},{2,3},{3,2},{4,5},{5,4},{6,7},{7,6},{8,9},{9,8},{10,11... | collective-permute-start | bytes 6291464 | tf_op jit(solution)/shard_map/ppermute | solution.py:586
  1.1 8.9 %collective-permute-start.1 = (s32[1,64]{1,0:T(1,128)}, s32[1,64]{1,0:T(1,128)S(1)}, u32[]{:S(2)}, u32[]{:S(2)}) collective-permute-start(s32[1,64]{1,0:T(1,128)} %param.15), channel_id=1, source_target_pairs={{0,8},{2,10},{4,12},{6,14},{8,0},{10,2},{12,4},{14,6},{1,9},{3,11}... | collective-permute-start | bytes 776 | tf_op jit(solution)/shard_map/ppermute | solution.py:584
  4.8 5.2 %copy-start.8 = (s32[1,64]{1,0:T(1,128)S(1)}, s32[1,64]{1,0:T(1,128)}, u32[]{:S(2)}) copy-start(s32[1,64]{1,0:T(1,128)} %param.15) | copy-start | bytes 772
  4.8 5.3 %copy-start = (bf16[512,1536]{1,0:T(8,128)(2,1)S(1)}, bf16[512,1536]{1,0:T(8,128)(2,1)}, u32[]{:S(2)}) copy-start(bf16[512,1536]{1,0:T(8,128)(2,1)} %refs_5_.4) | copy-start | bytes 4718596
  14.6 4.4 %collective-permute-start.2 = (bf16[272,128]{1,0:T(8,128)(2,1)S(1)}, bf16[272,128]{1,0:T(8,128)(2,1)S(1)}, u32[]{:S(2)}, u32[]{:S(2)}) collective-permute-start(bf16[272,128]{1,0:T(8,128)(2,1)S(1)} %get-tuple-element.51.refs_0_), channel_id=1, source_target_pairs={{0,2},{2,0},{4,6},{6,4},{8,10},{10,8},{12,14},{14,12},{1,3},{3,1},... | collective-permute-start | bytes 208904 | tf_op jit(solution)/shard_map/ppermute | solution.py:584
  19.0 4.5 %collective-permute-start.3 = (bf16[272,128]{1,0:T(8,128)(2,1)S(1)}, bf16[272,128]{1,0:T(8,128)(2,1)S(1)}, u32[]{:S(2)}, u32[]{:S(2)}) collective-permute-start(bf16[272,128]{1,0:T(8,128)(2,1)S(1)} %get-tuple-element.57.refs_0_), channel_id=1, source_target_pairs={{0,4},{2,6},{4,0},{6,2},{8,12},{10,14},{12,8},{14,10},{1,5},{3,7},... | collective-permute-start | bytes 208904 | tf_op jit(solution)/shard_map/ppermute | solution.py:584
  20.6 3.3 %copy-start.2 = (bf16[2048,512]{1,0:T(8,128)(2,1)S(1)}, bf16[2048,512]{1,0:T(8,128)(2,1)}, u32[]{:S(2)}) copy-start(bf16[2048,512]{1,0:T(8,128)(2,1)} %refs_2_.1) | copy-start | bytes 6291460
  20.6 3.3 %copy-start.3 = (bf16[512,1024]{1,0:T(8,128)(2,1)S(1)}, bf16[512,1024]{1,0:T(8,128)(2,1)}, u32[]{:S(2)}) copy-start(bf16[512,1024]{1,0:T(8,128)(2,1)} %refs_13_.1) | copy-start | bytes 3145732
  20.7 3.3 %copy-start.4 = (bf16[512,512]{1,0:T(8,128)(2,1)S(1)}, bf16[512,512]{1,0:T(8,128)(2,1)}, u32[]{:S(2)}) copy-start(bf16[512,512]{1,0:T(8,128)(2,1)} %refs_4_.3) | copy-start | bytes 1572868
  20.7 3.3 %copy-start.6 = (s32[4096]{0:T(1024)S(1)}, s32[4096]{0:T(1024)}, u32[]{:S(2)}) copy-start(s32[4096]{0:T(1024)} %param.16) | copy-start | bytes 49156
  23.6 5.3 %collective-permute-start.4 = (bf16[272,128]{1,0:T(8,128)(2,1)S(1)}, bf16[272,128]{1,0:T(8,128)(2,1)S(1)}, u32[]{:S(2)}, u32[]{:S(2)}) collective-permute-start(bf16[272,128]{1,0:T(8,128)(2,1)S(1)} %get-tuple-element.59), channel_id=1, source_target_pairs={{0,8},{2,10},{4,12},{6,14},{8,0},{10,2},{12,4},{14,6},{1,9},{3,11}... | collective-permute-start | bytes 208904 | tf_op jit(solution)/shard_map/ppermute | solution.py:584
  24.0 4.9 %copy-start.5 = (bf16[512,512]{1,0:T(8,128)(2,1)S(1)}, bf16[512,512]{1,0:T(8,128)(2,1)}, u32[]{:S(2)}) copy-start(bf16[512,512]{1,0:T(8,128)(2,1)} %refs_12_.1) | copy-start | bytes 1572868
  24.0 4.9 %copy-start.7 = (f32[8]{0:T(128)S(1)}, f32[8]{0:T(128)}, u32[]{:S(2)}) copy-start(f32[8]{0:T(128)} %param.18) | copy-start | bytes 100
  34.8 9.9 %collective-permute-start.5 = (bf16[544,128]{1,0:T(8,128)(2,1)S(1)}, bf16[544,128]{1,0:T(8,128)(2,1)S(1)}, u32[]{:S(2)}, u32[]{:S(2)}) collective-permute-start(bf16[544,128]{1,0:T(8,128)(2,1)S(1)} %get-tuple-element.71.refs_5_), channel_id=1, source_target_pairs={{0,6},{2,4},{4,2},{6,0},{8,14},{10,12},{12,10},{14,8},{1,7},{3,5},... | collective-permute-start | bytes 417800 | tf_op jit(solution)/shard_map/ppermute | solution.py:584
  37.2 7.5 %collective-permute-start.6 = (bf16[544,128]{1,0:T(8,128)(2,1)S(1)}, bf16[544,128]{1,0:T(8,128)(2,1)S(1)}, u32[]{:S(2)}, u32[]{:S(2)}) collective-permute-start(bf16[544,128]{1,0:T(8,128)(2,1)S(1)} %get-tuple-element.72.refs_6_), channel_id=1, source_target_pairs={{0,4},{2,6},{4,0},{6,2},{8,12},{10,14},{12,8},{14,10},{1,5},{3,7},... | collective-permute-start | bytes 417800 | tf_op jit(solution)/shard_map/ppermute | solution.py:584
  39.6 5.1 %collective-permute-start.7 = (bf16[544,128]{1,0:T(8,128)(2,1)S(1)}, bf16[544,128]{1,0:T(8,128)(2,1)S(1)}, u32[]{:S(2)}, u32[]{:S(2)}) collective-permute-start(bf16[544,128]{1,0:T(8,128)(2,1)S(1)} %send.1.refs_5_), channel_id=1, source_target_pairs={{0,2},{2,0},{4,6},{6,4},{8,10},{10,8},{12,14},{14,12},{1,3},{3,1},... | collective-permute-start | bytes 417800 | tf_op jit(solution)/shard_map/ppermute | solution.py:584
  40.2 9.9 %copy-start.1 = (bf16[512,512]{1,0:T(8,128)(2,1)S(1)}, bf16[512,512]{1,0:T(8,128)(2,1)}, u32[]{:S(2)}) copy-start(bf16[512,512]{1,0:T(8,128)(2,1)} %refs_3_.3) | copy-start | bytes 1572868
  44.9 5.3 %collective-permute-start.8 = (bf16[272,128]{1,0:T(8,128)(2,1)S(1)}, bf16[272,128]{1,0:T(8,128)(2,1)S(1)}, u32[]{:S(2)}, u32[]{:S(2)}) collective-permute-start(bf16[272,128]{1,0:T(8,128)(2,1)S(1)} %get-tuple-element.77), channel_id=1, source_target_pairs={{0,8},{2,10},{4,12},{6,14},{8,0},{10,2},{12,4},{14,6},{1,9},{3,11}... | collective-permute-start | bytes 208904 | tf_op jit(solution)/shard_map/ppermute | solution.py:584

commit v11 on v10

--- a/solution.py
+++ b/solution.py
@@ -104,8 +104,7 @@
         for k, (source, target) in enumerate(
             (
                 (ids_in, ids), (stored_in, stored), (decay_in, decay),
-                (own_in.at[: half // 2], own.at[: half // 2]),
-                (own_in.at[half // 2 :], own.at[half // 2 :]), (middle, key_w),
+                (middle, key_w), (own_in, own),
             )
         )
     ]
@@ -131,17 +130,12 @@
             ctl_o[r : r + 1, :] = jnp.where(
                 low, cum[2 * p : 2 * p + 1, CHUNK - 1 :], cum[2 * p + 1 : 2 * p + 2, CHUNK - 1 :]
             )
+    copies[3].wait()
+    key_w_o[...] = jnp.transpose(key_w[...].astype(f32)).astype(bf16)
     first = lax.axis_index("dp") * half
-    for k in range(2):
-        copies[3 + k].wait()
-        piece = own.at[k * half // 2 : (k + 1) * half // 2]
-        for i in range(n // CHUNK):
-            rows = picked_rows(slots[:, chunk(i)], first + k * half // 2, piece)
-            if k:
-                rows += part_o[chunk(i), :].astype(f32)
-            part_o[chunk(i), :] = rows.astype(bf16)
-    copies[5].wait()
-    key_w_o[...] = jnp.transpose(key_w[...].astype(f32)).astype(bf16)
+    copies[4].wait()
+    for i in range(n // CHUNK):
+        part_o[chunk(i), :] = picked_rows(slots[:, chunk(i)], first, own).astype(bf16)
 
 
 def summary_kernel(
@@ -287,20 +281,21 @@
 
 
 def candidate_kernel(
-    order, owned, id_rows, stored, own, peer, query_w, pair_w, val_w_o, *quarters
+    orders, owned, id_rows, stored, own, peer, query_w, pair_w, val_w_o, *quarters
 ):
     half, width = own.shape
     ids = id_rows[...]
     ids = (ids * float(LANES) + pltpu.roll(ids, LANES // 2, 1)).astype(i32)
     step = LANES // owned
     dp = lax.axis_index("dp")
-    for start in range(0, len(order), 2 * step):
+    for start in range(0, len(orders[0]), 2 * step):
         tiles = []
         for first in (start, start + step):
             tile = None
             for k in range(step):
-                j = order[first + k]
-                slots = stored_slots(ids[j : j + 1], stored[...])
+                one, two = (order[first + k] for order in orders)
+                row = jnp.where(dp == 0, ids[one : one + 1], ids[two : two + 1])
+                slots = stored_slots(row, stored[...])
                 if k:
                     moved = pltpu.roll(slots, k * owned, 1)
                     slots = jnp.where(iota((1, LANES), 1) >= k * owned, moved, tile)
@@ -583,6 +578,12 @@
     def swap(value, mask):
         return lax.ppermute(value, "seq", [(j, j ^ mask) for j in range(seq)])
 
+    def swap_by_core(value, masks):
+        pairs = [
+            (2 * j + core, 2 * (j ^ mask) + core) for j in range(seq) for core, mask in enumerate(masks)
+        ]
+        return lax.ppermute(value, ("seq", "dp"), pairs)
+
     peer = lax.ppermute(item_embedding_table, "dp", [(0, 1), (1, 0)])
     far_ids = swap(candidate_item_index, seq // 2)
     scale = head_score_scale.reshape(1, heads)
@@ -649,11 +650,13 @@
             after=[early[-1][1]],
         )
     got = swap(pay, 1 << (bits - 1))
-    order = [t + 4 * reversed_bits(k, bits - 2) for t in range(4) for k in range(seq // 4)]
-    order = [2 * (j % (seq // 2)) + j // (seq // 2) for j in order]
+    orders = []
+    for turn in ((0, 1, 2, 3), (0, 2, 1, 3)):
+        order = [t + 4 * reversed_bits(k, bits - 2) for t in turn for k in range(seq // 4)]
+        orders.append([2 * (j % (seq // 2)) + j // (seq // 2) for j in order])
     work = cands * 2 * half * width
     val_w, *quarters = call(
-        lambda *refs: candidate_kernel(order, owned, *refs), "candidates",
+        lambda *refs: candidate_kernel(orders, owned, *refs), "candidates",
         [
             every[0], stored, item_embedding_table, peer, candidate_query_weight,
             candidate_key_value_weight,
@@ -677,12 +680,12 @@
         spaces=[ANY, VMEM, VMEM, VMEM, VMEM],
         flops=2 * n * half * width,
     )
-    gots = [swap(pay, 3), swap(pay_b, 2)]
+    gots = [swap(pay, 3), swap_by_core(pay_b, (2, 1))]
     (pay,) = call(
         send_kernel, "send", [here, scale, quarters[1], key_two, val_two],
         [shape((message, LANES), bf16)], buffers, after=[pay, pay_b], flops=20 * work,
     )
-    gots.append(swap(pay, 1))
+    gots.append(swap_by_core(pay, (1, 2)))
     mean, logs = call(
         keep_kernel, "keep", [here, scale, quarters[0], key_two, val_two],
         [shape((width, LANES), f32), shape((heads, LANES), f32)], buffers, after=[pay], flops=8 * work,

time: 51.3 us -> 51.1 us (level)
    ppermute x0 -> x2, waiting for transfers between devices: none -> 2.71 us  [swap_by_core(): return lax.ppermute(value, ('seq', 'dp'), pairs)]
    ppermute x8 -> x6, waiting for transfers between devices: 7.99 us -> 5.45 us  [swap(): return lax.ppermute(value, 'seq', [(j, j ^ mask) for j in range(seq)])]
    ppermute x0 -> x2, starting transfers between devices: none -> 1.23 us  [swap_by_core(): return lax.ppermute(value, ('seq', 'dp'), pairs)]
    ppermute x8 -> x6, starting transfers between devices: 12.3 us -> 11.1 us  [swap(): return lax.ppermute(value, 'seq', [(j, j ^ mask) for j in range(seq)])]
  transfers between devices with their start and end apart: 9 -> 9, of which waited for: 4 -> 5; matrix products, arithmetic and copies ran while one was open for 0% -> 0% of each run, Pallas kernels for 30% -> 30%
where the time goes in v11:
time: 51.1 us; the launch traced here: 50.9 us
  Pallas kernels  28.4 us (56%)
  starting transfers between devices  12.8 us (25%)
  waiting for transfers between devices  8.16 us (16%)
  between operations  1.42 us (3%)
    pallas_call x12, Pallas kernels, call(): pl.pallas_call(body, name=name, in_specs=[SMEM] * len(scalars) + [space]...  28.4 us
    ppermute x6, starting transfers between devices, swap(): return lax.ppermute(value, 'seq', [(j, j ^ mask) for j in range(seq)])  11.1 us
    ppermute x6, waiting for transfers between devices, swap(): return lax.ppermute(value, 'seq', [(j, j ^ mask) for j in range(seq)])  5.45 us
    ppermute x2, waiting for transfers between devices, swap_by_core(): return lax.ppermute(value, ('seq', 'dp'), pairs)  2.71 us
    ppermute x2, starting transfers between devices, swap_by_core(): return lax.ppermute(value, ('seq', 'dp'), pairs)  1.23 us
  transfers between devices with their start and end apart: 9, of which 5 were waited for; matrix products, arithmetic and copies ran while one was open for 0% of the time, Pallas kernels for 30%

profile of v11, /device:TPU:0, one launch (start us, length us, event | category | flops | bytes accessed | tf_op | source)
XLA Modules:
  0.0 50.9 jit_solution(15892312272710026389)
XLA Ops:
  0.6 0.5 %collective-permute-start = (bf16[2048,512]{1,0:T(8,128)(2,1)}, bf16[2048,512]{1,0:T(8,128)(2,1)S(1)}, u32[]{:S(2)}, u32[]{:S(2)}) collective-permute-start(bf16[2048,512]{1,0:T(8,128)(2,1)} %refs_2_.1), channel_id=1, source_target_pairs={{0,1},{1,0},{2,3},{3,2},{4,5},{5,4},{6,7},{7,6},{8,9},{9,8},{10,11... | collective-permute-start | bytes 6291464 | tf_op jit(solution)/shard_map/ppermute | solution.py:587
  1.1 3.7 %collective-permute-start.1 = (s32[1,64]{1,0:T(1,128)}, s32[1,64]{1,0:T(1,128)S(1)}, u32[]{:S(2)}, u32[]{:S(2)}) collective-permute-start(s32[1,64]{1,0:T(1,128)} %param.15), channel_id=1, source_target_pairs={{0,8},{2,10},{4,12},{6,14},{8,0},{10,2},{12,4},{14,6},{1,9},{3,11}... | collective-permute-start | bytes 776 | tf_op jit(solution)/shard_map/ppermute | solution.py:579
  4.8 0.0 copy-start.8
  4.8 0.0 copy-start
  4.8 4.3 %own_rows.1 = (bf16[1024,512]{1,0:T(8,128)(2,1)S(1)}, f32[1,1024]{1,0:T(1,128)S(1)}, f32[4,8,256]{2,1,0:T(8,128)S(1)}, f32[1024,16]{1,0:T(8,128)S(1)}, f32[16,12...) custom-call(s32[1,1024]{1,0:T(1,128)} %refs_0_.2, s32[32,128]{1,0:T(8,128)} %bitcast.5, f32[8,1024]{1,0:T(8,128)} %bitcast.11, ...), custom_call_target="tpu_custom_call" | custom-call | flops 2147483648 | tf_op jit(solution)/shard_map/own_rows/pallas_call | solution.py:535
  9.8 0.0 collective-permute-done.1
  9.8 0.0 copy-done.8
  9.9 0.1 add_convert_fusion.refs_6_
  9.9 0.0 collective-permute-done.refs_2_.refs_3_
  9.9 0.0 copy-done
  9.9 4.4 %summary.1 = (bf16[1024,512]{1,0:T(8,128)(2,1)S(1)}, bf16[512,1024]{1,0:T(8,128)(2,1)S(1)}, bf16[1024,512]{1,0:T(8,128)(2,1)S(1)}, f32[4,256,128]{2,1,0:T(8,128)...) custom-call(s32[1]{0:T(128)S(6)} %copy.14.refs_0_, bf16[1024,512]{1,0:T(8,128)(2,1)S(1)} %get-tuple-element.40.refs_1_, ...), custom_call_target="tpu_custom_call" | custom-call | flops 2147483648 | tf_op jit(solution)/shard_map/summary/pallas_call | solution.py:535
  14.4 1.6 %collective-permute-start.2 = (bf16[272,128]{1,0:T(8,128)(2,1)S(1)}, bf16[272,128]{1,0:T(8,128)(2,1)S(1)}, u32[]{:S(2)}, u32[]{:S(2)}) collective-permute-start(bf16[272,128]{1,0:T(8,128)(2,1)S(1)} %get-tuple-element.51.refs_0_), channel_id=1, source_target_pairs={{0,2},{2,0},{4,6},{6,4},{8,10},{10,8},{12,14},{14,12},{1,3},{3,1},... | collective-permute-start | bytes 208904 | tf_op jit(solution)/shard_map/ppermute | solution.py:579
  15.9 2.7 %local_a.1 = (bf16[1024,256]{1,0:T(8,128)(2,1)S(1)}, f32[1024,256]{1,0:T(8,128)S(1)}) custom-call(bf16[1024,512]{1,0:T(8,128)(2,1)S(1)} %get-tuple-element.46.refs_0_.refs_2_, bf16[512,1024]{1,0:T(8,128)(2,1)S(1)} %get-tuple-element.47.refs_1_, bf16[1024,512]{1,0:T(8,128)(2,1)S(1)} %get-tuple-element.48.refs_2_, ...), custom_call_target="tpu_custom_call" | custom-call | flops 1073741824 | tf_op jit(solution)/shard_map/local_a/pallas_call | solution.py:535
  18.6 0.1 collective-permute-done.2.refs_1_
  18.7 0.1 join.2
  18.8 1.7 %collective-permute-start.3 = (bf16[272,128]{1,0:T(8,128)(2,1)S(1)}, bf16[272,128]{1,0:T(8,128)(2,1)S(1)}, u32[]{:S(2)}, u32[]{:S(2)}) collective-permute-start(bf16[272,128]{1,0:T(8,128)(2,1)S(1)} %get-tuple-element.57.refs_0_), channel_id=1, source_target_pairs={{0,4},{2,6},{4,0},{6,2},{8,12},{10,14},{12,8},{14,10},{1,5},{3,7},... | collective-permute-start | bytes 208904 | tf_op jit(solution)/shard_map/ppermute | solution.py:579
  20.4 0.0 copy-start.2
  20.4 0.0 copy-start.3
  20.4 0.0 copy-start.4
  20.4 0.0 copy-start.6
  20.4 2.7 %local_b.1 = (bf16[1024,256]{1,0:T(8,128)(2,1)S(1)}, f32[1024,256]{1,0:T(8,128)S(1)}) custom-call(bf16[1024,512]{1,0:T(8,128)(2,1)S(1)} %get-tuple-element.46.refs_0_.refs_2_, bf16[512,1024]{1,0:T(8,128)(2,1)S(1)} %get-tuple-element.47.refs_1_, bf16[1024,512]{1,0:T(8,128)(2,1)S(1)} %get-tuple-element.48.refs_2_, ...), custom_call_target="tpu_custom_call" | custom-call | flops 1073741824 | tf_op jit(solution)/shard_map/local_b/pallas_call | solution.py:535
  23.1 0.2 collective-permute-done.3.refs_1_
  23.3 0.1 join.3
  23.4 0.4 collective-permute-start.4
  23.8 0.0 copy-done.2
  23.8 0.0 copy-done.3
  23.8 0.0 copy-done.4
  23.8 0.0 copy-done.6
  23.8 0.0 copy-start.5
  23.8 0.0 copy-start.7
  23.8 3.6 %candidates.1 = (bf16[512,512]{1,0:T(8,128)(2,1)S(1)}, bf16[512,128]{1,0:T(8,128)(2,1)S(1)}, bf16[512,128]{1,0:T(8,128)(2,1)S(1)}, bf16[512,128]{1,0:T(8,128)(2,1)S(1)}, bf16[512,128]{1,0:T(8,128)(2,1)S(1)}) custom-call(f32[8,128]{1,0:T(8,128)S(1)} %get-tuple-element.62.refs_0_, s32[32,128]{1,0:T(8,128)S(1)} %bitcast.6, bf16[2048,512]{1,0:T(8,128)(2,1)S(1)} %copy-done.2, ...), custom_call_target="tpu_custom_call" | custom-call | flops 2147483648 | tf_op jit(solution)/shard_map/candidates/pallas_call | solution.py:535
  27.4 1.3 %collective-permute-done.4.refs_9_ = bf16[272,128]{1,0:T(8,128)(2,1)S(1)} collective-permute-done((bf16[272,128]{1,0:T(8,128)(2,1)S(1)}, bf16[272,128]{1,0:T(8,128)(2,1)S(1)}, u32[]{:S(2)}, u32[]{:S(2)}) %collective-permute-start.4) | collective-permute-done | bytes 69664 | tf_op jit(solution)/shard_map/ppermute | solution.py:579
  28.7 0.0 copy-done.5
  28.7 0.0 copy-done.7
  28.7 5.9 %finish.1 = (f32[1024,512]{1,0:T(8,128)}, bf16[1024,512]{1,0:T(8,128)(2,1)S(1)}, bf16[512,1024]{1,0:T(8,128)(2,1)S(1)}, bf16[544,128]{1,0:T(8,128)(2,1)S(1)}, bf16[544,128]{1,0:T(8,128)(2,1)S(1)}) custom-call(s32[8,128]{1,0:T(8,128)S(1)} %get-tuple-element.45.refs_0_, f32[1,8]{1,0:T(1,128)S(1)} %bitcast.7, ...), custom_call_target="tpu_custom_call" | custom-call | flops 2147483648 | tf_op jit(solution)/shard_map/finish/pallas_call | solution.py:535
  34.6 2.4 %collective-permute-start.5 = (bf16[544,128]{1,0:T(8,128)(2,1)S(1)}, bf16[544,128]{1,0:T(8,128)(2,1)S(1)}, u32[]{:S(2)}, u32[]{:S(2)}) collective-permute-start(bf16[544,128]{1,0:T(8,128)(2,1)S(1)} %get-tuple-element.71.refs_5_), channel_id=1, source_target_pairs={{0,6},{2,4},{4,2},{6,0},{8,14},{10,12},{12,10},{14,8},{1,7},{3,5},... | collective-permute-start | bytes 417800 | tf_op jit(solution)/shard_map/ppermute | solution.py:579
  37.0 0.6 %collective-permute-start.6 = (bf16[544,128]{1,0:T(8,128)(2,1)S(1)}, bf16[544,128]{1,0:T(8,128)(2,1)S(1)}, u32[]{:S(2)}, u32[]{:S(2)}) collective-permute-start(bf16[544,128]{1,0:T(8,128)(2,1)S(1)} %get-tuple-element.72.refs_6_), channel_id=1, source_target_pairs={{0,4},{1,3},{2,6},{3,1},{4,0},{5,7},{6,2},{7,5},{8,12},{9,11},{10,... | collective-permute-start | bytes 417800 | tf_op jit(solution)/shard_map/ppermute | solution.py:585
  37.6 1.8 %send.1.refs_5_ = bf16[544,128]{1,0:T(8,128)(2,1)S(1)} custom-call(s32[8,128]{1,0:T(8,128)S(1)} %get-tuple-element.45.refs_0_, f32[1,8]{1,0:T(1,128)S(1)} %bitcast.8, bf16[512,128]{1,0:T(8,128)(2,1)S(1)} %get-tuple-element.70.refs_2_, bf16[1024,512]{1,0:T(8,128)(2,1)S(1)} %get-tuple-element.68.refs_3_, bf16[512,1024]{1,0:T(8,128)(2,1)S(1)} %get-tuple-element.69.refs_4_, ...), custom_call_target="tpu_custom_call" | custom-call | flops 21474836480 | tf_op jit(solution)/shard_map/send/pallas_call | solution.py:535
  39.4 0.6 %collective-permute-start.7 = (bf16[544,128]{1,0:T(8,128)(2,1)S(1)}, bf16[544,128]{1,0:T(8,128)(2,1)S(1)}, u32[]{:S(2)}, u32[]{:S(2)}) collective-permute-start(bf16[544,128]{1,0:T(8,128)(2,1)S(1)} %send.1.refs_5_), channel_id=1, source_target_pairs={{0,2},{1,5},{2,0},{3,7},{4,6},{5,1},{6,4},{7,3},{8,10},{9,13},{10,... | collective-permute-start | bytes 417800 | tf_op jit(solution)/shard_map/ppermute | solution.py:585
  40.0 1.8 %keep.1 = (f32[512,128]{1,0:T(8,128)S(1)}, f32[8,128]{1,0:T(8,128)S(1)}) custom-call(s32[8,128]{1,0:T(8,128)S(1)} %get-tuple-element.45.refs_0_, f32[1,8]{1,0:T(1,128)S(1)} %bitcast.9, bf16[512,128]{1,0:T(8,128)(2,1)S(1)} %get-tuple-element.67.refs_2_, bf16[1024,512]{1,0:T(8,128)(2,1)S(1)} %get-tuple-element.68.refs_3_, ...), custom_call_target="tpu_custom_call" | custom-call | flops 8589934592 | tf_op jit(solution)/shard_map/keep/pallas_call | solution.py:535
  41.8 2.7 %collective-permute-done.7.refs_4_ = bf16[544,128]{1,0:T(8,128)(2,1)S(1)} collective-permute-done((bf16[544,128]{1,0:T(8,128)(2,1)S(1)}, bf16[544,128]{1,0:T(8,128)(2,1)S(1)}, u32[]{:S(2)}, u32[]{:S(2)}) %collective-permute-start.7) | collective-permute-done | bytes 139296 | tf_op jit(solution)/shard_map/ppermute | solution.py:585
  44.5 0.0 collective-permute-done.5.refs_2_
  44.5 0.0 collective-permute-done.6.refs_3_
  44.5 0.1 fold.1
  44.7 1.4 %collective-permute-start.8 = (bf16[272,128]{1,0:T(8,128)(2,1)S(1)}, bf16[272,128]{1,0:T(8,128)(2,1)S(1)}, u32[]{:S(2)}, u32[]{:S(2)}) collective-permute-start(bf16[272,128]{1,0:T(8,128)(2,1)S(1)} %get-tuple-element.77), channel_id=1, source_target_pairs={{0,8},{2,10},{4,12},{6,14},{8,0},{10,2},{12,4},{14,6},{1,9},{3,11}... | collective-permute-start | bytes 208904 | tf_op jit(solution)/shard_map/ppermute | solution.py:579
  46.1 3.9 %collective-permute-done.8.refs_2_ = bf16[272,128]{1,0:T(8,128)(2,1)S(1)} collective-permute-done((bf16[272,128]{1,0:T(8,128)(2,1)S(1)}, bf16[272,128]{1,0:T(8,128)(2,1)S(1)}, u32[]{:S(2)}, u32[]{:S(2)}) %collective-permute-start.8) | collective-permute-done | bytes 69664 | tf_op jit(solution)/shard_map/ppermute | solution.py:579
  49.9 0.0 copy-done.1
  49.9 1.0 %last.1 = f32[64,512]{1,0:T(8,128)} custom-call(f32[512,64]{1,0:T(8,128)S(1)} %get-tuple-element.75.refs_0_, f32[8,64]{1,0:T(8,128)S(1)} %get-tuple-element.76.refs_1_, bf16[272,128]{1,0:T(8,128)(2,1)S(1)} %collective-permute-done.8.refs_2_, bf16[512,512]{1,0:T(8,128)(2,1)S(1)} %copy-done.1), custom_call_target="tpu_custom_call" | custom-call | tf_op jit(solution)/shard_map/last/pallas_call | solution.py:535
  (2 shorter events, 0.0 us)
Async XLA Ops:
  0.6 9.3 %collective-permute-start = (bf16[2048,512]{1,0:T(8,128)(2,1)}, bf16[2048,512]{1,0:T(8,128)(2,1)S(1)}, u32[]{:S(2)}, u32[]{:S(2)}) collective-permute-start(bf16[2048,512]{1,0:T(8,128)(2,1)} %refs_2_.1), channel_id=1, source_target_pairs={{0,1},{1,0},{2,3},{3,2},{4,5},{5,4},{6,7},{7,6},{8,9},{9,8},{10,11... | collective-permute-start | bytes 6291464 | tf_op jit(solution)/shard_map/ppermute | solution.py:587
  1.1 8.7 %collective-permute-start.1 = (s32[1,64]{1,0:T(1,128)}, s32[1,64]{1,0:T(1,128)S(1)}, u32[]{:S(2)}, u32[]{:S(2)}) collective-permute-start(s32[1,64]{1,0:T(1,128)} %param.15), channel_id=1, source_target_pairs={{0,8},{2,10},{4,12},{6,14},{8,0},{10,2},{12,4},{14,6},{1,9},{3,11}... | collective-permute-start | bytes 776 | tf_op jit(solution)/shard_map/ppermute | solution.py:579
  4.8 5.0 %copy-start.8 = (s32[1,64]{1,0:T(1,128)S(1)}, s32[1,64]{1,0:T(1,128)}, u32[]{:S(2)}) copy-start(s32[1,64]{1,0:T(1,128)} %param.15) | copy-start | bytes 772
  4.8 5.1 %copy-start = (bf16[512,1536]{1,0:T(8,128)(2,1)S(1)}, bf16[512,1536]{1,0:T(8,128)(2,1)}, u32[]{:S(2)}) copy-start(bf16[512,1536]{1,0:T(8,128)(2,1)} %refs_5_.4) | copy-start | bytes 4718596
  14.4 4.4 %collective-permute-start.2 = (bf16[272,128]{1,0:T(8,128)(2,1)S(1)}, bf16[272,128]{1,0:T(8,128)(2,1)S(1)}, u32[]{:S(2)}, u32[]{:S(2)}) collective-permute-start(bf16[272,128]{1,0:T(8,128)(2,1)S(1)} %get-tuple-element.51.refs_0_), channel_id=1, source_target_pairs={{0,2},{2,0},{4,6},{6,4},{8,10},{10,8},{12,14},{14,12},{1,3},{3,1},... | collective-permute-start | bytes 208904 | tf_op jit(solution)/shard_map/ppermute | solution.py:579
  18.8 4.5 %collective-permute-start.3 = (bf16[272,128]{1,0:T(8,128)(2,1)S(1)}, bf16[272,128]{1,0:T(8,128)(2,1)S(1)}, u32[]{:S(2)}, u32[]{:S(2)}) collective-permute-start(bf16[272,128]{1,0:T(8,128)(2,1)S(1)} %get-tuple-element.57.refs_0_), channel_id=1, source_target_pairs={{0,4},{2,6},{4,0},{6,2},{8,12},{10,14},{12,8},{14,10},{1,5},{3,7},... | collective-permute-start | bytes 208904 | tf_op jit(solution)/shard_map/ppermute | solution.py:579
  20.4 3.4 %copy-start.2 = (bf16[2048,512]{1,0:T(8,128)(2,1)S(1)}, bf16[2048,512]{1,0:T(8,128)(2,1)}, u32[]{:S(2)}) copy-start(bf16[2048,512]{1,0:T(8,128)(2,1)} %refs_2_.1) | copy-start | bytes 6291460
  20.4 3.4 %copy-start.3 = (bf16[512,1024]{1,0:T(8,128)(2,1)S(1)}, bf16[512,1024]{1,0:T(8,128)(2,1)}, u32[]{:S(2)}) copy-start(bf16[512,1024]{1,0:T(8,128)(2,1)} %refs_13_.1) | copy-start | bytes 3145732
  20.4 3.4 %copy-start.4 = (bf16[512,512]{1,0:T(8,128)(2,1)S(1)}, bf16[512,512]{1,0:T(8,128)(2,1)}, u32[]{:S(2)}) copy-start(bf16[512,512]{1,0:T(8,128)(2,1)} %refs_4_.3) | copy-start | bytes 1572868
  20.4 3.4 %copy-start.6 = (s32[4096]{0:T(1024)S(1)}, s32[4096]{0:T(1024)}, u32[]{:S(2)}) copy-start(s32[4096]{0:T(1024)} %param.16) | copy-start | bytes 49156
  23.4 5.3 %collective-permute-start.4 = (bf16[272,128]{1,0:T(8,128)(2,1)S(1)}, bf16[272,128]{1,0:T(8,128)(2,1)S(1)}, u32[]{:S(2)}, u32[]{:S(2)}) collective-permute-start(bf16[272,128]{1,0:T(8,128)(2,1)S(1)} %get-tuple-element.59), channel_id=1, source_target_pairs={{0,8},{2,10},{4,12},{6,14},{8,0},{10,2},{12,4},{14,6},{1,9},{3,11}... | collective-permute-start | bytes 208904 | tf_op jit(solution)/shard_map/ppermute | solution.py:579
  23.8 4.9 %copy-start.5 = (bf16[512,512]{1,0:T(8,128)(2,1)S(1)}, bf16[512,512]{1,0:T(8,128)(2,1)}, u32[]{:S(2)}) copy-start(bf16[512,512]{1,0:T(8,128)(2,1)} %refs_12_.1) | copy-start | bytes 1572868
  23.8 4.8 %copy-start.7 = (f32[8]{0:T(128)S(1)}, f32[8]{0:T(128)}, u32[]{:S(2)}) copy-start(f32[8]{0:T(128)} %param.18) | copy-start | bytes 100
  34.6 9.9 %collective-permute-start.5 = (bf16[544,128]{1,0:T(8,128)(2,1)S(1)}, bf16[544,128]{1,0:T(8,128)(2,1)S(1)}, u32[]{:S(2)}, u32[]{:S(2)}) collective-permute-start(bf16[544,128]{1,0:T(8,128)(2,1)S(1)} %get-tuple-element.71.refs_5_), channel_id=1, source_target_pairs={{0,6},{2,4},{4,2},{6,0},{8,14},{10,12},{12,10},{14,8},{1,7},{3,5},... | collective-permute-start | bytes 417800 | tf_op jit(solution)/shard_map/ppermute | solution.py:579
  37.0 7.5 %collective-permute-start.6 = (bf16[544,128]{1,0:T(8,128)(2,1)S(1)}, bf16[544,128]{1,0:T(8,128)(2,1)S(1)}, u32[]{:S(2)}, u32[]{:S(2)}) collective-permute-start(bf16[544,128]{1,0:T(8,128)(2,1)S(1)} %get-tuple-element.72.refs_6_), channel_id=1, source_target_pairs={{0,4},{1,3},{2,6},{3,1},{4,0},{5,7},{6,2},{7,5},{8,12},{9,11},{10,... | collective-permute-start | bytes 417800 | tf_op jit(solution)/shard_map/ppermute | solution.py:585
  39.4 5.1 %collective-permute-start.7 = (bf16[544,128]{1,0:T(8,128)(2,1)S(1)}, bf16[544,128]{1,0:T(8,128)(2,1)S(1)}, u32[]{:S(2)}, u32[]{:S(2)}) collective-permute-start(bf16[544,128]{1,0:T(8,128)(2,1)S(1)} %send.1.refs_5_), channel_id=1, source_target_pairs={{0,2},{1,5},{2,0},{3,7},{4,6},{5,1},{6,4},{7,3},{8,10},{9,13},{10,... | collective-permute-start | bytes 417800 | tf_op jit(solution)/shard_map/ppermute | solution.py:585
  40.0 9.9 %copy-start.1 = (bf16[512,512]{1,0:T(8,128)(2,1)S(1)}, bf16[512,512]{1,0:T(8,128)(2,1)}, u32[]{:S(2)}) copy-start(bf16[512,512]{1,0:T(8,128)(2,1)} %refs_3_.3) | copy-start | bytes 1572868
  44.7 5.3 %collective-permute-start.8 = (bf16[272,128]{1,0:T(8,128)(2,1)S(1)}, bf16[272,128]{1,0:T(8,128)(2,1)S(1)}, u32[]{:S(2)}, u32[]{:S(2)}) collective-permute-start(bf16[272,128]{1,0:T(8,128)(2,1)S(1)} %get-tuple-element.77), channel_id=1, source_target_pairs={{0,8},{2,10},{4,12},{6,14},{8,0},{10,2},{12,4},{14,6},{1,9},{3,11}... | collective-permute-start | bytes 208904 | tf_op jit(solution)/shard_map/ppermute | solution.py:579

commit v12 on v11

--- a/solution.py
+++ b/solution.py
@@ -683,7 +683,7 @@
     gots = [swap(pay, 3), swap_by_core(pay_b, (2, 1))]
     (pay,) = call(
         send_kernel, "send", [here, scale, quarters[1], key_two, val_two],
-        [shape((message, LANES), bf16)], buffers, after=[pay, pay_b], flops=20 * work,
+        [shape((message, LANES), bf16)], buffers, after=[pay], flops=8 * work,
     )
     gots.append(swap_by_core(pay, (1, 2)))
     mean, logs = call(

time: 51.1 us -> 51.7 us (1.012)
  waiting for transfers between devices: 8.16 us -> 8.83 us
    ppermute x6, waiting for transfers between devices: 5.45 us -> 6.19 us  [swap(): return lax.ppermute(value, 'seq', [(j, j ^ mask) for j in range(seq)])]
  transfers between devices with their start and end apart: 9 -> 9, of which waited for: 5 -> 6; matrix products, arithmetic and copies ran while one was open for 0% -> 0% of each run, Pallas kernels for 30% -> 29%
where the time goes in v12:
time: 51.7 us; the launch traced here: 51.6 us
  Pallas kernels  28.4 us (55%)
  starting transfers between devices  12.8 us (25%)
  waiting for transfers between devices  8.83 us (17%)
  between operations  1.42 us (3%)
    pallas_call x12, Pallas kernels, call(): pl.pallas_call(body, name=name, in_specs=[SMEM] * len(scalars) + [space]...  28.4 us
    ppermute x6, starting transfers between devices, swap(): return lax.ppermute(value, 'seq', [(j, j ^ mask) for j in range(seq)])  11.1 us
    ppermute x6, waiting for transfers between devices, swap(): return lax.ppermute(value, 'seq', [(j, j ^ mask) for j in range(seq)])  6.19 us
    ppermute x2, waiting for transfers between devices, swap_by_core(): return lax.ppermute(value, ('seq', 'dp'), pairs)  2.64 us
    ppermute x2, starting transfers between devices, swap_by_core(): return lax.ppermute(value, ('seq', 'dp'), pairs)  1.23 us
  transfers between devices with their start and end apart: 9, of which 6 were waited for; matrix products, arithmetic and copies ran while one was open for 0% of the time, Pallas kernels for 29%

profile of v12, /device:TPU:0, one launch (start us, length us, event | category | flops | bytes accessed | tf_op | source)
XLA Modules:
  0.0 51.6 jit_solution(10321569770025838194)
XLA Ops:
  0.6 0.5 %collective-permute-start = (bf16[2048,512]{1,0:T(8,128)(2,1)}, bf16[2048,512]{1,0:T(8,128)(2,1)S(1)}, u32[]{:S(2)}, u32[]{:S(2)}) collective-permute-start(bf16[2048,512]{1,0:T(8,128)(2,1)} %refs_2_.1), channel_id=1, source_target_pairs={{0,1},{1,0},{2,3},{3,2},{4,5},{5,4},{6,7},{7,6},{8,9},{9,8},{10,11... | collective-permute-start | bytes 6291464 | tf_op jit(solution)/shard_map/ppermute | solution.py:587
  1.1 3.7 %collective-permute-start.1 = (s32[1,64]{1,0:T(1,128)}, s32[1,64]{1,0:T(1,128)S(1)}, u32[]{:S(2)}, u32[]{:S(2)}) collective-permute-start(s32[1,64]{1,0:T(1,128)} %param.15), channel_id=1, source_target_pairs={{0,8},{2,10},{4,12},{6,14},{8,0},{10,2},{12,4},{14,6},{1,9},{3,11}... | collective-permute-start | bytes 776 | tf_op jit(solution)/shard_map/ppermute | solution.py:579
  4.8 0.0 copy-start.8
  4.8 4.3 %own_rows.1 = (bf16[1024,512]{1,0:T(8,128)(2,1)S(1)}, f32[1,1024]{1,0:T(1,128)S(1)}, f32[4,8,256]{2,1,0:T(8,128)S(1)}, f32[1024,16]{1,0:T(8,128)S(1)}, f32[16,12...) custom-call(s32[1,1024]{1,0:T(1,128)} %refs_0_.2, s32[32,128]{1,0:T(8,128)} %bitcast.5, f32[8,1024]{1,0:T(8,128)} %bitcast.11, ...), custom_call_target="tpu_custom_call" | custom-call | flops 2147483648 | tf_op jit(solution)/shard_map/own_rows/pallas_call | solution.py:535
  9.8 0.0 collective-permute-done.1
  9.8 0.0 copy-done.8
  9.9 0.1 add_convert_fusion.refs_6_
  9.9 0.0 collective-permute-done.refs_2_.refs_3_
  9.9 0.0 copy-done
  9.9 4.4 %summary.1 = (bf16[1024,512]{1,0:T(8,128)(2,1)S(1)}, bf16[512,1024]{1,0:T(8,128)(2,1)S(1)}, bf16[1024,512]{1,0:T(8,128)(2,1)S(1)}, f32[4,256,128]{2,1,0:T(8,128)...) custom-call(s32[1]{0:T(128)S(6)} %copy.14.refs_0_, bf16[1024,512]{1,0:T(8,128)(2,1)S(1)} %get-tuple-element.40.refs_1_, ...), custom_call_target="tpu_custom_call" | custom-call | flops 2147483648 | tf_op jit(solution)/shard_map/summary/pallas_call | solution.py:535
  14.4 1.6 %collective-permute-start.2 = (bf16[272,128]{1,0:T(8,128)(2,1)S(1)}, bf16[272,128]{1,0:T(8,128)(2,1)S(1)}, u32[]{:S(2)}, u32[]{:S(2)}) collective-permute-start(bf16[272,128]{1,0:T(8,128)(2,1)S(1)} %get-tuple-element.51.refs_0_), channel_id=1, source_target_pairs={{0,2},{2,0},{4,6},{6,4},{8,10},{10,8},{12,14},{14,12},{1,3},{3,1},... | collective-permute-start | bytes 208904 | tf_op jit(solution)/shard_map/ppermute | solution.py:579
  15.9 2.7 %local_a.1 = (bf16[1024,256]{1,0:T(8,128)(2,1)S(1)}, f32[1024,256]{1,0:T(8,128)S(1)}) custom-call(bf16[1024,512]{1,0:T(8,128)(2,1)S(1)} %get-tuple-element.46.refs_0_.refs_2_, bf16[512,1024]{1,0:T(8,128)(2,1)S(1)} %get-tuple-element.47.refs_1_, bf16[1024,512]{1,0:T(8,128)(2,1)S(1)} %get-tuple-element.48.refs_2_, ...), custom_call_target="tpu_custom_call" | custom-call | flops 1073741824 | tf_op jit(solution)/shard_map/local_a/pallas_call | solution.py:535
  18.6 0.1 collective-permute-done.2.refs_1_
  18.7 0.1 join.2
  18.8 1.7 %collective-permute-start.3 = (bf16[272,128]{1,0:T(8,128)(2,1)S(1)}, bf16[272,128]{1,0:T(8,128)(2,1)S(1)}, u32[]{:S(2)}, u32[]{:S(2)}) collective-permute-start(bf16[272,128]{1,0:T(8,128)(2,1)S(1)} %get-tuple-element.57.refs_0_), channel_id=1, source_target_pairs={{0,4},{2,6},{4,0},{6,2},{8,12},{10,14},{12,8},{14,10},{1,5},{3,7},... | collective-permute-start | bytes 208904 | tf_op jit(solution)/shard_map/ppermute | solution.py:579
  20.4 0.0 copy-start.2
  20.4 0.0 copy-start.3
  20.4 0.0 copy-start.4
  20.4 0.0 copy-start.6
  20.4 2.7 %local_b.1 = (bf16[1024,256]{1,0:T(8,128)(2,1)S(1)}, f32[1024,256]{1,0:T(8,128)S(1)}) custom-call(bf16[1024,512]{1,0:T(8,128)(2,1)S(1)} %get-tuple-element.46.refs_0_.refs_2_, bf16[512,1024]{1,0:T(8,128)(2,1)S(1)} %get-tuple-element.47.refs_1_, bf16[1024,512]{1,0:T(8,128)(2,1)S(1)} %get-tuple-element.48.refs_2_, ...), custom_call_target="tpu_custom_call" | custom-call | flops 1073741824 | tf_op jit(solution)/shard_map/local_b/pallas_call | solution.py:535
  23.1 0.2 collective-permute-done.3.refs_1_
  23.3 0.1 join.3
  23.4 0.4 collective-permute-start.4
  23.8 0.0 copy-done.2
  23.8 0.0 copy-done.3
  23.8 0.0 copy-done.4
  23.8 0.0 copy-done.6
  23.8 0.0 copy-start.5
  23.8 0.0 copy-start.7
  23.8 3.6 %candidates.1 = (bf16[512,512]{1,0:T(8,128)(2,1)S(1)}, bf16[512,128]{1,0:T(8,128)(2,1)S(1)}, bf16[512,128]{1,0:T(8,128)(2,1)S(1)}, bf16[512,128]{1,0:T(8,128)(2,1)S(1)}, bf16[512,128]{1,0:T(8,128)(2,1)S(1)}) custom-call(f32[8,128]{1,0:T(8,128)S(1)} %get-tuple-element.62.refs_0_, s32[32,128]{1,0:T(8,128)S(1)} %bitcast.6, bf16[2048,512]{1,0:T(8,128)(2,1)S(1)} %copy-done.2, ...), custom_call_target="tpu_custom_call" | custom-call | flops 2147483648 | tf_op jit(solution)/shard_map/candidates/pallas_call | solution.py:535
  27.4 1.3 %collective-permute-done.4.refs_9_ = bf16[272,128]{1,0:T(8,128)(2,1)S(1)} collective-permute-done((bf16[272,128]{1,0:T(8,128)(2,1)S(1)}, bf16[272,128]{1,0:T(8,128)(2,1)S(1)}, u32[]{:S(2)}, u32[]{:S(2)}) %collective-permute-start.4) | collective-permute-done | bytes 69664 | tf_op jit(solution)/shard_map/ppermute | solution.py:579
  28.7 0.0 copy-done.5
  28.7 0.0 copy-done.7
  28.7 5.9 %finish.1 = (f32[1024,512]{1,0:T(8,128)}, bf16[1024,512]{1,0:T(8,128)(2,1)S(1)}, bf16[512,1024]{1,0:T(8,128)(2,1)S(1)}, bf16[544,128]{1,0:T(8,128)(2,1)S(1)}, bf16[544,128]{1,0:T(8,128)(2,1)S(1)}) custom-call(s32[8,128]{1,0:T(8,128)S(1)} %get-tuple-element.45.refs_0_, f32[1,8]{1,0:T(1,128)S(1)} %bitcast.7, ...), custom_call_target="tpu_custom_call" | custom-call | flops 2147483648 | tf_op jit(solution)/shard_map/finish/pallas_call | solution.py:535
  34.6 2.4 %collective-permute-start.5 = (bf16[544,128]{1,0:T(8,128)(2,1)S(1)}, bf16[544,128]{1,0:T(8,128)(2,1)S(1)}, u32[]{:S(2)}, u32[]{:S(2)}) collective-permute-start(bf16[544,128]{1,0:T(8,128)(2,1)S(1)} %get-tuple-element.71.refs_5_), channel_id=1, source_target_pairs={{0,6},{2,4},{4,2},{6,0},{8,14},{10,12},{12,10},{14,8},{1,7},{3,5},... | collective-permute-start | bytes 417800 | tf_op jit(solution)/shard_map/ppermute | solution.py:579
  37.0 1.8 %send.1.refs_5_ = bf16[544,128]{1,0:T(8,128)(2,1)S(1)} custom-call(s32[8,128]{1,0:T(8,128)S(1)} %get-tuple-element.45.refs_0_, f32[1,8]{1,0:T(1,128)S(1)} %bitcast.8, bf16[512,128]{1,0:T(8,128)(2,1)S(1)} %get-tuple-element.70.refs_2_, bf16[1024,512]{1,0:T(8,128)(2,1)S(1)} %get-tuple-element.68.refs_3_, bf16[512,1024]{1,0:T(8,128)(2,1)S(1)} %get-tuple-element.69.refs_4_, ...), custom_call_target="tpu_custom_call" | custom-call | flops 8589934592 | tf_op jit(solution)/shard_map/send/pallas_call | solution.py:535
  38.8 0.6 %collective-permute-start.7 = (bf16[544,128]{1,0:T(8,128)(2,1)S(1)}, bf16[544,128]{1,0:T(8,128)(2,1)S(1)}, u32[]{:S(2)}, u32[]{:S(2)}) collective-permute-start(bf16[544,128]{1,0:T(8,128)(2,1)S(1)} %send.1.refs_5_), channel_id=1, source_target_pairs={{0,2},{1,5},{2,0},{3,7},{4,6},{5,1},{6,4},{7,3},{8,10},{9,13},{10,... | collective-permute-start | bytes 417800 | tf_op jit(solution)/shard_map/ppermute | solution.py:585
  39.4 0.6 %collective-permute-start.6 = (bf16[544,128]{1,0:T(8,128)(2,1)S(1)}, bf16[544,128]{1,0:T(8,128)(2,1)S(1)}, u32[]{:S(2)}, u32[]{:S(2)}) collective-permute-start(bf16[544,128]{1,0:T(8,128)(2,1)S(1)} %get-tuple-element.74), channel_id=1, source_target_pairs={{0,4},{1,3},{2,6},{3,1},{4,0},{5,7},{6,2},{7,5},{8,12},{9,11},{10,... | collective-permute-start | bytes 417800 | tf_op jit(solution)/shard_map/ppermute | solution.py:585
  40.0 0.0 copy-start.1
  40.0 1.8 %keep.1 = (f32[512,128]{1,0:T(8,128)S(1)}, f32[8,128]{1,0:T(8,128)S(1)}) custom-call(s32[8,128]{1,0:T(8,128)S(1)} %get-tuple-element.45.refs_0_, f32[1,8]{1,0:T(1,128)S(1)} %bitcast.9, bf16[512,128]{1,0:T(8,128)(2,1)S(1)} %get-tuple-element.67.refs_2_, bf16[1024,512]{1,0:T(8,128)(2,1)S(1)} %get-tuple-element.68.refs_3_, ...), custom_call_target="tpu_custom_call" | custom-call | flops 8589934592 | tf_op jit(solution)/shard_map/keep/pallas_call | solution.py:535
  41.8 2.1 %collective-permute-done.7.refs_4_ = bf16[544,128]{1,0:T(8,128)(2,1)S(1)} collective-permute-done((bf16[544,128]{1,0:T(8,128)(2,1)S(1)}, bf16[544,128]{1,0:T(8,128)(2,1)S(1)}, u32[]{:S(2)}, u32[]{:S(2)}) %collective-permute-start.7) | collective-permute-done | bytes 139296 | tf_op jit(solution)/shard_map/ppermute | solution.py:585
  43.9 0.5 collective-permute-done.6.refs_3_
  44.4 0.0 collective-permute-done.5.refs_2_
  44.4 0.2 fold.1
  44.6 1.4 %collective-permute-start.8 = (bf16[272,128]{1,0:T(8,128)(2,1)S(1)}, bf16[272,128]{1,0:T(8,128)(2,1)S(1)}, u32[]{:S(2)}, u32[]{:S(2)}) collective-permute-start(bf16[272,128]{1,0:T(8,128)(2,1)S(1)} %get-tuple-element.77), channel_id=1, source_target_pairs={{0,8},{2,10},{4,12},{6,14},{8,0},{10,2},{12,4},{14,6},{1,9},{3,11}... | collective-permute-start | bytes 208904 | tf_op jit(solution)/shard_map/ppermute | solution.py:579
  46.0 4.6 %collective-permute-done.8.refs_2_ = bf16[272,128]{1,0:T(8,128)(2,1)S(1)} collective-permute-done((bf16[272,128]{1,0:T(8,128)(2,1)S(1)}, bf16[272,128]{1,0:T(8,128)(2,1)S(1)}, u32[]{:S(2)}, u32[]{:S(2)}) %collective-permute-start.8) | collective-permute-done | bytes 69664 | tf_op jit(solution)/shard_map/ppermute | solution.py:579
  50.6 0.0 copy-done.1
  50.6 1.0 %last.1 = f32[64,512]{1,0:T(8,128)} custom-call(f32[512,64]{1,0:T(8,128)S(1)} %get-tuple-element.75.refs_0_, f32[8,64]{1,0:T(8,128)S(1)} %get-tuple-element.76.refs_1_, bf16[272,128]{1,0:T(8,128)(2,1)S(1)} %collective-permute-done.8.refs_2_, bf16[512,512]{1,0:T(8,128)(2,1)S(1)} %copy-done.1), custom_call_target="tpu_custom_call" | custom-call | tf_op jit(solution)/shard_map/last/pallas_call | solution.py:535
  (2 shorter events, 0.0 us)
Async XLA Ops:
  0.6 9.3 %collective-permute-start = (bf16[2048,512]{1,0:T(8,128)(2,1)}, bf16[2048,512]{1,0:T(8,128)(2,1)S(1)}, u32[]{:S(2)}, u32[]{:S(2)}) collective-permute-start(bf16[2048,512]{1,0:T(8,128)(2,1)} %refs_2_.1), channel_id=1, source_target_pairs={{0,1},{1,0},{2,3},{3,2},{4,5},{5,4},{6,7},{7,6},{8,9},{9,8},{10,11... | collective-permute-start | bytes 6291464 | tf_op jit(solution)/shard_map/ppermute | solution.py:587
  1.1 8.7 %collective-permute-start.1 = (s32[1,64]{1,0:T(1,128)}, s32[1,64]{1,0:T(1,128)S(1)}, u32[]{:S(2)}, u32[]{:S(2)}) collective-permute-start(s32[1,64]{1,0:T(1,128)} %param.15), channel_id=1, source_target_pairs={{0,8},{2,10},{4,12},{6,14},{8,0},{10,2},{12,4},{14,6},{1,9},{3,11}... | collective-permute-start | bytes 776 | tf_op jit(solution)/shard_map/ppermute | solution.py:579
  4.8 5.0 %copy-start.8 = (s32[1,64]{1,0:T(1,128)S(1)}, s32[1,64]{1,0:T(1,128)}, u32[]{:S(2)}) copy-start(s32[1,64]{1,0:T(1,128)} %param.15) | copy-start | bytes 772
  4.8 5.1 %copy-start = (bf16[512,1536]{1,0:T(8,128)(2,1)S(1)}, bf16[512,1536]{1,0:T(8,128)(2,1)}, u32[]{:S(2)}) copy-start(bf16[512,1536]{1,0:T(8,128)(2,1)} %refs_5_.4) | copy-start | bytes 4718596
  14.4 4.4 %collective-permute-start.2 = (bf16[272,128]{1,0:T(8,128)(2,1)S(1)}, bf16[272,128]{1,0:T(8,128)(2,1)S(1)}, u32[]{:S(2)}, u32[]{:S(2)}) collective-permute-start(bf16[272,128]{1,0:T(8,128)(2,1)S(1)} %get-tuple-element.51.refs_0_), channel_id=1, source_target_pairs={{0,2},{2,0},{4,6},{6,4},{8,10},{10,8},{12,14},{14,12},{1,3},{3,1},... | collective-permute-start | bytes 208904 | tf_op jit(solution)/shard_map/ppermute | solution.py:579
  18.8 4.5 %collective-permute-start.3 = (bf16[272,128]{1,0:T(8,128)(2,1)S(1)}, bf16[272,128]{1,0:T(8,128)(2,1)S(1)}, u32[]{:S(2)}, u32[]{:S(2)}) collective-permute-start(bf16[272,128]{1,0:T(8,128)(2,1)S(1)} %get-tuple-element.57.refs_0_), channel_id=1, source_target_pairs={{0,4},{2,6},{4,0},{6,2},{8,12},{10,14},{12,8},{14,10},{1,5},{3,7},... | collective-permute-start | bytes 208904 | tf_op jit(solution)/shard_map/ppermute | solution.py:579
  20.4 3.4 %copy-start.2 = (bf16[2048,512]{1,0:T(8,128)(2,1)S(1)}, bf16[2048,512]{1,0:T(8,128)(2,1)}, u32[]{:S(2)}) copy-start(bf16[2048,512]{1,0:T(8,128)(2,1)} %refs_2_.1) | copy-start | bytes 6291460
  20.4 3.4 %copy-start.3 = (bf16[512,1024]{1,0:T(8,128)(2,1)S(1)}, bf16[512,1024]{1,0:T(8,128)(2,1)}, u32[]{:S(2)}) copy-start(bf16[512,1024]{1,0:T(8,128)(2,1)} %refs_13_.1) | copy-start | bytes 3145732
  20.4 3.4 %copy-start.4 = (bf16[512,512]{1,0:T(8,128)(2,1)S(1)}, bf16[512,512]{1,0:T(8,128)(2,1)}, u32[]{:S(2)}) copy-start(bf16[512,512]{1,0:T(8,128)(2,1)} %refs_4_.3) | copy-start | bytes 1572868
  20.4 3.4 %copy-start.6 = (s32[4096]{0:T(1024)S(1)}, s32[4096]{0:T(1024)}, u32[]{:S(2)}) copy-start(s32[4096]{0:T(1024)} %param.16) | copy-start | bytes 49156
  23.4 5.3 %collective-permute-start.4 = (bf16[272,128]{1,0:T(8,128)(2,1)S(1)}, bf16[272,128]{1,0:T(8,128)(2,1)S(1)}, u32[]{:S(2)}, u32[]{:S(2)}) collective-permute-start(bf16[272,128]{1,0:T(8,128)(2,1)S(1)} %get-tuple-element.59), channel_id=1, source_target_pairs={{0,8},{2,10},{4,12},{6,14},{8,0},{10,2},{12,4},{14,6},{1,9},{3,11}... | collective-permute-start | bytes 208904 | tf_op jit(solution)/shard_map/ppermute | solution.py:579
  23.8 4.9 %copy-start.5 = (bf16[512,512]{1,0:T(8,128)(2,1)S(1)}, bf16[512,512]{1,0:T(8,128)(2,1)}, u32[]{:S(2)}) copy-start(bf16[512,512]{1,0:T(8,128)(2,1)} %refs_12_.1) | copy-start | bytes 1572868
  23.8 4.8 %copy-start.7 = (f32[8]{0:T(128)S(1)}, f32[8]{0:T(128)}, u32[]{:S(2)}) copy-start(f32[8]{0:T(128)} %param.18) | copy-start | bytes 100
  34.6 9.9 %collective-permute-start.5 = (bf16[544,128]{1,0:T(8,128)(2,1)S(1)}, bf16[544,128]{1,0:T(8,128)(2,1)S(1)}, u32[]{:S(2)}, u32[]{:S(2)}) collective-permute-start(bf16[544,128]{1,0:T(8,128)(2,1)S(1)} %get-tuple-element.71.refs_5_), channel_id=1, source_target_pairs={{0,6},{2,4},{4,2},{6,0},{8,14},{10,12},{12,10},{14,8},{1,7},{3,5},... | collective-permute-start | bytes 417800 | tf_op jit(solution)/shard_map/ppermute | solution.py:579
  38.8 5.2 %collective-permute-start.7 = (bf16[544,128]{1,0:T(8,128)(2,1)S(1)}, bf16[544,128]{1,0:T(8,128)(2,1)S(1)}, u32[]{:S(2)}, u32[]{:S(2)}) collective-permute-start(bf16[544,128]{1,0:T(8,128)(2,1)S(1)} %send.1.refs_5_), channel_id=1, source_target_pairs={{0,2},{1,5},{2,0},{3,7},{4,6},{5,1},{6,4},{7,3},{8,10},{9,13},{10,... | collective-permute-start | bytes 417800 | tf_op jit(solution)/shard_map/ppermute | solution.py:585
  39.4 5.1 %collective-permute-start.6 = (bf16[544,128]{1,0:T(8,128)(2,1)S(1)}, bf16[544,128]{1,0:T(8,128)(2,1)S(1)}, u32[]{:S(2)}, u32[]{:S(2)}) collective-permute-start(bf16[544,128]{1,0:T(8,128)(2,1)S(1)} %get-tuple-element.74), channel_id=1, source_target_pairs={{0,4},{1,3},{2,6},{3,1},{4,0},{5,7},{6,2},{7,5},{8,12},{9,11},{10,... | collective-permute-start | bytes 417800 | tf_op jit(solution)/shard_map/ppermute | solution.py:585
  40.0 10.6 %copy-start.1 = (bf16[512,512]{1,0:T(8,128)(2,1)S(1)}, bf16[512,512]{1,0:T(8,128)(2,1)}, u32[]{:S(2)}) copy-start(bf16[512,512]{1,0:T(8,128)(2,1)} %refs_3_.3) | copy-start | bytes 1572868
  44.6 6.0 %collective-permute-start.8 = (bf16[272,128]{1,0:T(8,128)(2,1)S(1)}, bf16[272,128]{1,0:T(8,128)(2,1)S(1)}, u32[]{:S(2)}, u32[]{:S(2)}) collective-permute-start(bf16[272,128]{1,0:T(8,128)(2,1)S(1)} %get-tuple-element.77), channel_id=1, source_target_pairs={{0,8},{2,10},{4,12},{6,14},{8,0},{10,2},{12,4},{14,6},{1,9},{3,11}... | collective-permute-start | bytes 208904 | tf_op jit(solution)/shard_map/ppermute | solution.py:579

commit v13 on v11

--- a/solution.py
+++ b/solution.py
@@ -238,7 +238,11 @@
         logs_o[...] = jnp.where(upper, prefix_logs + other_logs, prefix_logs)
 
 
-def local_kernel(first, emb, key, val, crow, ccol, weight, query_o, intra_o):
+def local_kernel(first, emb, key, val, crow, ccol, weight, *refs):
+    if len(refs) > 2:
+        pair_w, *refs, val_w_o = refs
+        val_w_o[...] = jnp.transpose(pair_w[:, val_w_o.shape[1] :].astype(f32)).astype(bf16)
+    query_o, intra_o = refs
     n, width = query_o.shape
     heads = ccol.shape[1] // 2
     ones, lanes = same_head(), head_spread(heads, first // 64, width // 64)
@@ -281,7 +285,7 @@
 
 
 def candidate_kernel(
-    orders, owned, id_rows, stored, own, peer, query_w, pair_w, val_w_o, *quarters
+    orders, owned, id_rows, stored, own, peer, query_w, *quarters
 ):
     half, width = own.shape
     ids = id_rows[...]
@@ -306,7 +310,6 @@
         query = jnp.transpose(dot(found.astype(bf16), query_w[...])).astype(bf16)
         for k in (0, 1):
             quarters[start // step + k][...] = query[:, pair_cut(k)]
-    val_w_o[...] = jnp.transpose(pair_w[:, width:].astype(f32)).astype(bf16)
 
 
 def attend(alive_count, scale, queries, key, val, buffers, emit):
@@ -624,11 +627,12 @@
         flops=2 * n * half * width,
     )
 
-    def local(first, name, after):
+    def local(first, name, after, more=()):
         return call(
             lambda *refs: local_kernel(first, *refs), name,
-            [emb, key, val, crow, ccol, history_query_key_value_weight],
-            [shape((n, width // 2), bf16), shape((n, width // 2), f32)],
+            [emb, key, val, crow, ccol, history_query_key_value_weight, *more],
+            [shape((n, width // 2), bf16), shape((n, width // 2), f32)]
+            + [shape((width, width), bf16)] * len(more),
             after=after, flops=2 * n * half * width // 2,
         )
 
@@ -637,7 +641,7 @@
     for bit in range(bits - 1):
         got = swap(pay, 1 << bit)
         if bit == 1:
-            early.append(local(width // 2, "local_b", [prefix]))
+            early.append(local(width // 2, "local_b", [prefix], [candidate_key_value_weight]))
         count = 2 << bit
         final = bit == bits - 2
         pay, prefix, logs, *every = call(
@@ -655,15 +659,14 @@
         order = [t + 4 * reversed_bits(k, bits - 2) for t in turn for k in range(seq // 4)]
         orders.append([2 * (j % (seq // 2)) + j // (seq // 2) for j in order])
     work = cands * 2 * half * width
-    val_w, *quarters = call(
+    quarters = call(
         lambda *refs: candidate_kernel(orders, owned, *refs), "candidates",
         [
             every[0], stored, item_embedding_table, peer, candidate_query_weight,
-            candidate_key_value_weight,
         ],
-        [shape((width, width), bf16)] + [shape((width, LANES), bf16)] * 4, flops=2 * work,
-    )
-    (query_a, intra_a), (query_b, intra_b) = early
+        [shape((width, LANES), bf16)] * 4, flops=2 * work,
+    )
+    (query_a, intra_a), (query_b, intra_b, val_w) = early
     buffers = [pltpu.VMEM((n, 2 * LANES), f32)] * 2
     message = width + log_pad(heads)
     hist, key_two, val_two, pay, pay_b = call(

time: 51.1 us -> 51.1 us (level)
  transfers between devices with their start and end apart: 9 -> 9, of which waited for: 5 -> 4; matrix products, arithmetic and copies ran while one was open for 0% -> 0% of each run, Pallas kernels for 30% -> 30%
where the time goes in v13:
time: 51.1 us; the launch traced here: 50.9 us
  Pallas kernels  28.5 us (56%)
  starting transfers between devices  12.8 us (25%)
  waiting for transfers between devices  8.09 us (16%)
  between operations  1.41 us (3%)
    pallas_call x12, Pallas kernels, call(): pl.pallas_call(body, name=name, in_specs=[SMEM] * len(scalars) + [space]...  28.5 us
    ppermute x6, starting transfers between devices, swap(): return lax.ppermute(value, 'seq', [(j, j ^ mask) for j in range(seq)])  11.1 us
    ppermute x6, waiting for transfers between devices, swap(): return lax.ppermute(value, 'seq', [(j, j ^ mask) for j in range(seq)])  5.37 us
    ppermute x2, waiting for transfers between devices, swap_by_core(): return lax.ppermute(value, ('seq', 'dp'), pairs)  2.72 us
    ppermute x2, starting transfers between devices, swap_by_core(): return lax.ppermute(value, ('seq', 'dp'), pairs)  1.21 us
  transfers between devices with their start and end apart: 9, of which 4 were waited for; matrix products, arithmetic and copies ran while one was open for 0% of the time, Pallas kernels for 30%

profile of v13, /device:TPU:0, one launch (start us, length us, event | category | flops | bytes accessed | tf_op | source)
XLA Modules:
  0.0 50.9 jit_solution(9497359875409183983)
XLA Ops:
  0.6 0.5 %collective-permute-start = (bf16[2048,512]{1,0:T(8,128)(2,1)}, bf16[2048,512]{1,0:T(8,128)(2,1)S(1)}, u32[]{:S(2)}, u32[]{:S(2)}) collective-permute-start(bf16[2048,512]{1,0:T(8,128)(2,1)} %refs_2_.1), channel_id=1, source_target_pairs={{0,1},{1,0},{2,3},{3,2},{4,5},{5,4},{6,7},{7,6},{8,9},{9,8},{10,11... | collective-permute-start | bytes 6291464 | tf_op jit(solution)/shard_map/ppermute | solution.py:590
  1.1 3.7 %collective-permute-start.1 = (s32[1,64]{1,0:T(1,128)}, s32[1,64]{1,0:T(1,128)S(1)}, u32[]{:S(2)}, u32[]{:S(2)}) collective-permute-start(s32[1,64]{1,0:T(1,128)} %param.15), channel_id=1, source_target_pairs={{0,8},{2,10},{4,12},{6,14},{8,0},{10,2},{12,4},{14,6},{1,9},{3,11}... | collective-permute-start | bytes 776 | tf_op jit(solution)/shard_map/ppermute | solution.py:582
  4.8 0.0 copy-start.8
  4.8 0.0 copy-start
  4.8 4.3 %own_rows.1 = (bf16[1024,512]{1,0:T(8,128)(2,1)S(1)}, f32[1,1024]{1,0:T(1,128)S(1)}, f32[4,8,256]{2,1,0:T(8,128)S(1)}, f32[1024,16]{1,0:T(8,128)S(1)}, f32[16,12...) custom-call(s32[1,1024]{1,0:T(1,128)} %refs_0_.2, s32[32,128]{1,0:T(8,128)} %bitcast.5, f32[8,1024]{1,0:T(8,128)} %bitcast.11, ...), custom_call_target="tpu_custom_call" | custom-call | flops 2147483648 | tf_op jit(solution)/shard_map/own_rows/pallas_call | solution.py:538
  9.8 0.0 collective-permute-done.1
  9.8 0.0 copy-done.8
  9.9 0.1 add_convert_fusion.refs_6_
  9.9 0.0 collective-permute-done.refs_2_.refs_3_
  9.9 0.0 copy-done
  9.9 4.4 %summary.1 = (bf16[1024,512]{1,0:T(8,128)(2,1)S(1)}, bf16[512,1024]{1,0:T(8,128)(2,1)S(1)}, bf16[1024,512]{1,0:T(8,128)(2,1)S(1)}, f32[4,256,128]{2,1,0:T(8,128)...) custom-call(s32[1]{0:T(128)S(6)} %copy.14.refs_0_, bf16[1024,512]{1,0:T(8,128)(2,1)S(1)} %get-tuple-element.40.refs_1_, ...), custom_call_target="tpu_custom_call" | custom-call | flops 2147483648 | tf_op jit(solution)/shard_map/summary/pallas_call | solution.py:538
  14.4 1.6 %collective-permute-start.2 = (bf16[272,128]{1,0:T(8,128)(2,1)S(1)}, bf16[272,128]{1,0:T(8,128)(2,1)S(1)}, u32[]{:S(2)}, u32[]{:S(2)}) collective-permute-start(bf16[272,128]{1,0:T(8,128)(2,1)S(1)} %get-tuple-element.51.refs_0_), channel_id=1, source_target_pairs={{0,2},{2,0},{4,6},{6,4},{8,10},{10,8},{12,14},{14,12},{1,3},{3,1},... | collective-permute-start | bytes 208904 | tf_op jit(solution)/shard_map/ppermute | solution.py:582
  15.9 0.0 copy-start.1
  15.9 2.7 %local_a.1 = (bf16[1024,256]{1,0:T(8,128)(2,1)S(1)}, f32[1024,256]{1,0:T(8,128)S(1)}) custom-call(bf16[1024,512]{1,0:T(8,128)(2,1)S(1)} %get-tuple-element.46.refs_0_.refs_2_, bf16[512,1024]{1,0:T(8,128)(2,1)S(1)} %get-tuple-element.47.refs_1_, bf16[1024,512]{1,0:T(8,128)(2,1)S(1)} %get-tuple-element.48.refs_2_, ...), custom_call_target="tpu_custom_call" | custom-call | flops 1073741824 | tf_op jit(solution)/shard_map/local_a/pallas_call | solution.py:538
  18.6 0.1 collective-permute-done.2.refs_1_
  18.7 0.1 join.2
  18.8 1.7 %collective-permute-start.3 = (bf16[272,128]{1,0:T(8,128)(2,1)S(1)}, bf16[272,128]{1,0:T(8,128)(2,1)S(1)}, u32[]{:S(2)}, u32[]{:S(2)}) collective-permute-start(bf16[272,128]{1,0:T(8,128)(2,1)S(1)} %get-tuple-element.57.refs_0_), channel_id=1, source_target_pairs={{0,4},{2,6},{4,0},{6,2},{8,12},{10,14},{12,8},{14,10},{1,5},{3,7},... | collective-permute-start | bytes 208904 | tf_op jit(solution)/shard_map/ppermute | solution.py:582
  20.4 0.0 copy-done.1
  20.4 0.0 copy-start.3
  20.4 0.0 copy-start.4
  20.4 0.0 copy-start.6
  20.5 2.9 %local_b.1 = (bf16[1024,256]{1,0:T(8,128)(2,1)S(1)}, f32[1024,256]{1,0:T(8,128)S(1)}, bf16[512,512]{1,0:T(8,128)(2,1)S(1)}) custom-call(bf16[1024,512]{1,0:T(8,128)(2,1)S(1)} %get-tuple-element.46.refs_0_.refs_2_, bf16[512,1024]{1,0:T(8,128)(2,1)S(1)} %get-tuple-element.47.refs_1_, bf16[1024,512]{1,0:T(8,128)(2,1)S(1)} %get-tuple-element.48.refs_2_, ...), custom_call_target="tpu_custom_call" | custom-call | flops 1073741824 | tf_op jit(solution)/shard_map/local_b/pallas_call | solution.py:538
  23.3 0.0 collective-permute-done.3.refs_1_
  23.3 0.1 join.3
  23.4 0.4 collective-permute-start.4
  23.8 0.0 copy-done.3
  23.8 0.0 copy-done.4
  23.8 0.0 copy-done.6
  23.8 0.0 copy-start.7
  23.8 3.5 %candidates.1 = (bf16[512,128]{1,0:T(8,128)(2,1)S(1)}, bf16[512,128]{1,0:T(8,128)(2,1)S(1)}, bf16[512,128]{1,0:T(8,128)(2,1)S(1)}, bf16[512,128]{1,0:T(8,128)(2,1)S(1)}) custom-call(f32[8,128]{1,0:T(8,128)S(1)} %get-tuple-element.63.refs_0_, s32[32,128]{1,0:T(8,128)S(1)} %bitcast.6, bf16[2048,512]{1,0:T(8,128)(2,1)S(1)} %copy-done.3, ...), custom_call_target="tpu_custom_call" | custom-call | flops 2147483648 | tf_op jit(solution)/shard_map/candidates/pallas_call | solution.py:538
  27.3 1.3 %collective-permute-done.4.refs_9_ = bf16[272,128]{1,0:T(8,128)(2,1)S(1)} collective-permute-done((bf16[272,128]{1,0:T(8,128)(2,1)S(1)}, bf16[272,128]{1,0:T(8,128)(2,1)S(1)}, u32[]{:S(2)}, u32[]{:S(2)}) %collective-permute-start.4) | collective-permute-done | bytes 69664 | tf_op jit(solution)/shard_map/ppermute | solution.py:582
  28.7 0.0 copy-done.5
  28.7 0.0 copy-done.7
  28.7 5.9 %finish.1 = (f32[1024,512]{1,0:T(8,128)}, bf16[1024,512]{1,0:T(8,128)(2,1)S(1)}, bf16[512,1024]{1,0:T(8,128)(2,1)S(1)}, bf16[544,128]{1,0:T(8,128)(2,1)S(1)}, bf16[544,128]{1,0:T(8,128)(2,1)S(1)}) custom-call(s32[8,128]{1,0:T(8,128)S(1)} %get-tuple-element.45.refs_0_, f32[1,8]{1,0:T(1,128)S(1)} %bitcast.7, ...), custom_call_target="tpu_custom_call" | custom-call | flops 2147483648 | tf_op jit(solution)/shard_map/finish/pallas_call | solution.py:538
  34.6 2.4 %collective-permute-start.5 = (bf16[544,128]{1,0:T(8,128)(2,1)S(1)}, bf16[544,128]{1,0:T(8,128)(2,1)S(1)}, u32[]{:S(2)}, u32[]{:S(2)}) collective-permute-start(bf16[544,128]{1,0:T(8,128)(2,1)S(1)} %get-tuple-element.71.refs_5_), channel_id=1, source_target_pairs={{0,6},{2,4},{4,2},{6,0},{8,14},{10,12},{12,10},{14,8},{1,7},{3,5},... | collective-permute-start | bytes 417800 | tf_op jit(solution)/shard_map/ppermute | solution.py:582
  37.0 0.6 %collective-permute-start.6 = (bf16[544,128]{1,0:T(8,128)(2,1)S(1)}, bf16[544,128]{1,0:T(8,128)(2,1)S(1)}, u32[]{:S(2)}, u32[]{:S(2)}) collective-permute-start(bf16[544,128]{1,0:T(8,128)(2,1)S(1)} %get-tuple-element.72.refs_6_), channel_id=1, source_target_pairs={{0,4},{1,3},{2,6},{3,1},{4,0},{5,7},{6,2},{7,5},{8,12},{9,11},{10,... | collective-permute-start | bytes 417800 | tf_op jit(solution)/shard_map/ppermute | solution.py:588
  37.6 1.8 %send.1.refs_5_ = bf16[544,128]{1,0:T(8,128)(2,1)S(1)} custom-call(s32[8,128]{1,0:T(8,128)S(1)} %get-tuple-element.45.refs_0_, f32[1,8]{1,0:T(1,128)S(1)} %bitcast.8, bf16[512,128]{1,0:T(8,128)(2,1)S(1)} %get-tuple-element.70.refs_2_, bf16[1024,512]{1,0:T(8,128)(2,1)S(1)} %get-tuple-element.68.refs_3_, bf16[512,1024]{1,0:T(8,128)(2,1)S(1)} %get-tuple-element.69.refs_4_, ...), custom_call_target="tpu_custom_call" | custom-call | flops 21474836480 | tf_op jit(solution)/shard_map/send/pallas_call | solution.py:538
  39.4 0.6 %collective-permute-start.7 = (bf16[544,128]{1,0:T(8,128)(2,1)S(1)}, bf16[544,128]{1,0:T(8,128)(2,1)S(1)}, u32[]{:S(2)}, u32[]{:S(2)}) collective-permute-start(bf16[544,128]{1,0:T(8,128)(2,1)S(1)} %send.1.refs_5_), channel_id=1, source_target_pairs={{0,2},{1,5},{2,0},{3,7},{4,6},{5,1},{6,4},{7,3},{8,10},{9,13},{10,... | collective-permute-start | bytes 417800 | tf_op jit(solution)/shard_map/ppermute | solution.py:588
  40.0 0.0 copy-start.2
  40.0 1.8 %keep.1 = (f32[512,128]{1,0:T(8,128)S(1)}, f32[8,128]{1,0:T(8,128)S(1)}) custom-call(s32[8,128]{1,0:T(8,128)S(1)} %get-tuple-element.45.refs_0_, f32[1,8]{1,0:T(1,128)S(1)} %bitcast.9, bf16[512,128]{1,0:T(8,128)(2,1)S(1)} %get-tuple-element.67.refs_2_, bf16[1024,512]{1,0:T(8,128)(2,1)S(1)} %get-tuple-element.68.refs_3_, ...), custom_call_target="tpu_custom_call" | custom-call | flops 8589934592 | tf_op jit(solution)/shard_map/keep/pallas_call | solution.py:538
  41.8 2.7 %collective-permute-done.7.refs_4_ = bf16[544,128]{1,0:T(8,128)(2,1)S(1)} collective-permute-done((bf16[544,128]{1,0:T(8,128)(2,1)S(1)}, bf16[544,128]{1,0:T(8,128)(2,1)S(1)}, u32[]{:S(2)}, u32[]{:S(2)}) %collective-permute-start.7) | collective-permute-done | bytes 139296 | tf_op jit(solution)/shard_map/ppermute | solution.py:588
  44.5 0.0 collective-permute-done.5.refs_2_
  44.5 0.0 collective-permute-done.6.refs_3_
  44.5 0.1 fold.1
  44.7 1.4 %collective-permute-start.8 = (bf16[272,128]{1,0:T(8,128)(2,1)S(1)}, bf16[272,128]{1,0:T(8,128)(2,1)S(1)}, u32[]{:S(2)}, u32[]{:S(2)}) collective-permute-start(bf16[272,128]{1,0:T(8,128)(2,1)S(1)} %get-tuple-element.77), channel_id=1, source_target_pairs={{0,8},{2,10},{4,12},{6,14},{8,0},{10,2},{12,4},{14,6},{1,9},{3,11}... | collective-permute-start | bytes 208904 | tf_op jit(solution)/shard_map/ppermute | solution.py:582
  46.0 3.9 %collective-permute-done.8.refs_2_ = bf16[272,128]{1,0:T(8,128)(2,1)S(1)} collective-permute-done((bf16[272,128]{1,0:T(8,128)(2,1)S(1)}, bf16[272,128]{1,0:T(8,128)(2,1)S(1)}, u32[]{:S(2)}, u32[]{:S(2)}) %collective-permute-start.8) | collective-permute-done | bytes 69664 | tf_op jit(solution)/shard_map/ppermute | solution.py:582
  49.9 0.0 copy-done.2
  49.9 1.0 %last.1 = f32[64,512]{1,0:T(8,128)} custom-call(f32[512,64]{1,0:T(8,128)S(1)} %get-tuple-element.75.refs_0_, f32[8,64]{1,0:T(8,128)S(1)} %get-tuple-element.76.refs_1_, bf16[272,128]{1,0:T(8,128)(2,1)S(1)} %collective-permute-done.8.refs_2_, bf16[512,512]{1,0:T(8,128)(2,1)S(1)} %copy-done.2), custom_call_target="tpu_custom_call" | custom-call | tf_op jit(solution)/shard_map/last/pallas_call | solution.py:538
  (2 shorter events, 0.0 us)
Async XLA Ops:
  0.6 9.3 %collective-permute-start = (bf16[2048,512]{1,0:T(8,128)(2,1)}, bf16[2048,512]{1,0:T(8,128)(2,1)S(1)}, u32[]{:S(2)}, u32[]{:S(2)}) collective-permute-start(bf16[2048,512]{1,0:T(8,128)(2,1)} %refs_2_.1), channel_id=1, source_target_pairs={{0,1},{1,0},{2,3},{3,2},{4,5},{5,4},{6,7},{7,6},{8,9},{9,8},{10,11... | collective-permute-start | bytes 6291464 | tf_op jit(solution)/shard_map/ppermute | solution.py:590
  1.1 8.7 %collective-permute-start.1 = (s32[1,64]{1,0:T(1,128)}, s32[1,64]{1,0:T(1,128)S(1)}, u32[]{:S(2)}, u32[]{:S(2)}) collective-permute-start(s32[1,64]{1,0:T(1,128)} %param.15), channel_id=1, source_target_pairs={{0,8},{2,10},{4,12},{6,14},{8,0},{10,2},{12,4},{14,6},{1,9},{3,11}... | collective-permute-start | bytes 776 | tf_op jit(solution)/shard_map/ppermute | solution.py:582
  4.8 5.0 %copy-start.8 = (s32[1,64]{1,0:T(1,128)S(1)}, s32[1,64]{1,0:T(1,128)}, u32[]{:S(2)}) copy-start(s32[1,64]{1,0:T(1,128)} %param.15) | copy-start | bytes 772
  4.8 5.1 %copy-start = (bf16[512,1536]{1,0:T(8,128)(2,1)S(1)}, bf16[512,1536]{1,0:T(8,128)(2,1)}, u32[]{:S(2)}) copy-start(bf16[512,1536]{1,0:T(8,128)(2,1)} %refs_5_.3) | copy-start | bytes 4718596
  14.4 4.4 %collective-permute-start.2 = (bf16[272,128]{1,0:T(8,128)(2,1)S(1)}, bf16[272,128]{1,0:T(8,128)(2,1)S(1)}, u32[]{:S(2)}, u32[]{:S(2)}) collective-permute-start(bf16[272,128]{1,0:T(8,128)(2,1)S(1)} %get-tuple-element.51.refs_0_), channel_id=1, source_target_pairs={{0,2},{2,0},{4,6},{6,4},{8,10},{10,8},{12,14},{14,12},{1,3},{3,1},... | collective-permute-start | bytes 208904 | tf_op jit(solution)/shard_map/ppermute | solution.py:582
  15.9 4.5 %copy-start.1 = (bf16[512,1024]{1,0:T(8,128)(2,1)S(1)}, bf16[512,1024]{1,0:T(8,128)(2,1)}, u32[]{:S(2)}) copy-start(bf16[512,1024]{1,0:T(8,128)(2,1)} %refs_13_.1) | copy-start | bytes 3145732
  18.8 4.5 %collective-permute-start.3 = (bf16[272,128]{1,0:T(8,128)(2,1)S(1)}, bf16[272,128]{1,0:T(8,128)(2,1)S(1)}, u32[]{:S(2)}, u32[]{:S(2)}) collective-permute-start(bf16[272,128]{1,0:T(8,128)(2,1)S(1)} %get-tuple-element.57.refs_0_), channel_id=1, source_target_pairs={{0,4},{2,6},{4,0},{6,2},{8,12},{10,14},{12,8},{14,10},{1,5},{3,7},... | collective-permute-start | bytes 208904 | tf_op jit(solution)/shard_map/ppermute | solution.py:582
  20.4 3.3 %copy-start.3 = (bf16[2048,512]{1,0:T(8,128)(2,1)S(1)}, bf16[2048,512]{1,0:T(8,128)(2,1)}, u32[]{:S(2)}) copy-start(bf16[2048,512]{1,0:T(8,128)(2,1)} %refs_2_.1) | copy-start | bytes 6291460
  20.4 3.3 %copy-start.4 = (bf16[512,512]{1,0:T(8,128)(2,1)S(1)}, bf16[512,512]{1,0:T(8,128)(2,1)}, u32[]{:S(2)}) copy-start(bf16[512,512]{1,0:T(8,128)(2,1)} %refs_4_.3) | copy-start | bytes 1572868
  20.4 3.3 %copy-start.6 = (s32[4096]{0:T(1024)S(1)}, s32[4096]{0:T(1024)}, u32[]{:S(2)}) copy-start(s32[4096]{0:T(1024)} %param.16) | copy-start | bytes 49156
  23.4 5.3 %collective-permute-start.4 = (bf16[272,128]{1,0:T(8,128)(2,1)S(1)}, bf16[272,128]{1,0:T(8,128)(2,1)S(1)}, u32[]{:S(2)}, u32[]{:S(2)}) collective-permute-start(bf16[272,128]{1,0:T(8,128)(2,1)S(1)} %get-tuple-element.59), channel_id=1, source_target_pairs={{0,8},{2,10},{4,12},{6,14},{8,0},{10,2},{12,4},{14,6},{1,9},{3,11}... | collective-permute-start | bytes 208904 | tf_op jit(solution)/shard_map/ppermute | solution.py:582
  23.8 4.9 %copy-start.5 = (bf16[512,512]{1,0:T(8,128)(2,1)S(1)}, bf16[512,512]{1,0:T(8,128)(2,1)}, u32[]{:S(2)}) copy-start(bf16[512,512]{1,0:T(8,128)(2,1)} %refs_12_.1) | copy-start | bytes 1572868
  23.8 4.9 %copy-start.7 = (f32[8]{0:T(128)S(1)}, f32[8]{0:T(128)}, u32[]{:S(2)}) copy-start(f32[8]{0:T(128)} %param.18) | copy-start | bytes 100
  34.6 9.9 %collective-permute-start.5 = (bf16[544,128]{1,0:T(8,128)(2,1)S(1)}, bf16[544,128]{1,0:T(8,128)(2,1)S(1)}, u32[]{:S(2)}, u32[]{:S(2)}) collective-permute-start(bf16[544,128]{1,0:T(8,128)(2,1)S(1)} %get-tuple-element.71.refs_5_), channel_id=1, source_target_pairs={{0,6},{2,4},{4,2},{6,0},{8,14},{10,12},{12,10},{14,8},{1,7},{3,5},... | collective-permute-start | bytes 417800 | tf_op jit(solution)/shard_map/ppermute | solution.py:582
  37.0 7.5 %collective-permute-start.6 = (bf16[544,128]{1,0:T(8,128)(2,1)S(1)}, bf16[544,128]{1,0:T(8,128)(2,1)S(1)}, u32[]{:S(2)}, u32[]{:S(2)}) collective-permute-start(bf16[544,128]{1,0:T(8,128)(2,1)S(1)} %get-tuple-element.72.refs_6_), channel_id=1, source_target_pairs={{0,4},{1,3},{2,6},{3,1},{4,0},{5,7},{6,2},{7,5},{8,12},{9,11},{10,... | collective-permute-start | bytes 417800 | tf_op jit(solution)/shard_map/ppermute | solution.py:588
  39.4 5.1 %collective-permute-start.7 = (bf16[544,128]{1,0:T(8,128)(2,1)S(1)}, bf16[544,128]{1,0:T(8,128)(2,1)S(1)}, u32[]{:S(2)}, u32[]{:S(2)}) collective-permute-start(bf16[544,128]{1,0:T(8,128)(2,1)S(1)} %send.1.refs_5_), channel_id=1, source_target_pairs={{0,2},{1,5},{2,0},{3,7},{4,6},{5,1},{6,4},{7,3},{8,10},{9,13},{10,... | collective-permute-start | bytes 417800 | tf_op jit(solution)/shard_map/ppermute | solution.py:588
  40.0 9.9 %copy-start.2 = (bf16[512,512]{1,0:T(8,128)(2,1)S(1)}, bf16[512,512]{1,0:T(8,128)(2,1)}, u32[]{:S(2)}) copy-start(bf16[512,512]{1,0:T(8,128)(2,1)} %refs_3_.3) | copy-start | bytes 1572868
  44.7 5.3 %collective-permute-start.8 = (bf16[272,128]{1,0:T(8,128)(2,1)S(1)}, bf16[272,128]{1,0:T(8,128)(2,1)S(1)}, u32[]{:S(2)}, u32[]{:S(2)}) collective-permute-start(bf16[272,128]{1,0:T(8,128)(2,1)S(1)} %get-tuple-element.77), channel_id=1, source_target_pairs={{0,8},{2,10},{4,12},{6,14},{8,0},{10,2},{12,4},{14,6},{1,9},{3,11}... | collective-permute-start | bytes 208904 | tf_op jit(solution)/shard_map/ppermute | solution.py:582

commit v14 on v13

--- a/solution.py
+++ b/solution.py
@@ -314,8 +314,9 @@
 
 def attend(alive_count, scale, queries, key, val, buffers, emit):
     n, width = key.shape
-    blocks = range(0, n, KEYS)
-    ones = jnp.ones((16, KEYS), bf16)
+    keys = KEYS // 2 if len(queries) == 1 else KEYS
+    blocks = range(0, n, keys)
+    ones = jnp.ones((16, keys), bf16)
     heads = width // 64
     if len(queries) == 1:
         units = [[(h, 0), (h + 1, 0)] for h in range(0, heads, 2)]
@@ -331,10 +332,10 @@
         return jnp.concatenate(parts, axis=1)
 
     def store(u, block, weights, peak):
-        values = dot(key[block : block + KEYS, pair_cut(units[u][0][0] // 2)], weights)
-        values = jnp.where(iota((KEYS, 1), 0) < alive_count - block, values, DEAD)
-        buffers[u % 2][block : block + KEYS, :] = values
-        top = jnp.max(values.reshape(KEYS // 8, 8, 2 * LANES), axis=0)
+        values = dot(key[block : block + keys, pair_cut(units[u][0][0] // 2)], weights)
+        values = jnp.where(iota((keys, 1), 0) < alive_count - block, values, DEAD)
+        buffers[u % 2][block : block + keys, :] = values
+        top = jnp.max(values.reshape(keys // 8, 8, 2 * LANES), axis=0)
         return top if peak is None else jnp.maximum(peak, top)
 
     peak, weights = None, weights_of(units[0])
@@ -353,9 +354,9 @@
         for block in blocks:
             if more:
                 following = store(u + 1, block, weights, following)
-            gap = buffers[u % 2][block : block + KEYS, :] - peak
+            gap = buffers[u % 2][block : block + keys, :] - peak
             probs = jnp.exp2(gap * factor).astype(bf16)
-            side = [val[first : first + rows, block : block + KEYS], ones]
+            side = [val[first : first + rows, block : block + keys], ones]
             part = dot(jnp.concatenate(side, axis=0), probs)
             sums = part if sums is None else sums + part
         total = sums[rows : rows + 1]

time: 51.1 us -> 51 us (level)
  no operation moved by 1% of the time
where the time goes in v14:
time: 51 us; the launch traced here: 50.8 us
  Pallas kernels  28.3 us (55%)
  starting transfers between devices  12.8 us (25%)
  waiting for transfers between devices  8.19 us (16%)
  between operations  1.41 us (3%)
    pallas_call x12, Pallas kernels, call(): pl.pallas_call(body, name=name, in_specs=[SMEM] * len(scalars) + [space]...  28.3 us
    ppermute x6, starting transfers between devices, swap(): return lax.ppermute(value, 'seq', [(j, j ^ mask) for j in range(seq)])  11.1 us
    ppermute x6, waiting for transfers between devices, swap(): return lax.ppermute(value, 'seq', [(j, j ^ mask) for j in range(seq)])  5.37 us
    ppermute x2, waiting for transfers between devices, swap_by_core(): return lax.ppermute(value, ('seq', 'dp'), pairs)  2.81 us
    ppermute x2, starting transfers between devices, swap_by_core(): return lax.ppermute(value, ('seq', 'dp'), pairs)  1.21 us
  transfers between devices with their start and end apart: 9, of which 4 were waited for; matrix products, arithmetic and copies ran while one was open for 0% of the time, Pallas kernels for 30%

profile of v14, /device:TPU:0, one launch (start us, length us, event | category | flops | bytes accessed | tf_op | source)
XLA Modules:
  0.0 50.8 jit_solution(2268941416455008486)
XLA Ops:
  0.6 0.5 %collective-permute-start = (bf16[2048,512]{1,0:T(8,128)(2,1)}, bf16[2048,512]{1,0:T(8,128)(2,1)S(1)}, u32[]{:S(2)}, u32[]{:S(2)}) collective-permute-start(bf16[2048,512]{1,0:T(8,128)(2,1)} %refs_2_.1), channel_id=1, source_target_pairs={{0,1},{1,0},{2,3},{3,2},{4,5},{5,4},{6,7},{7,6},{8,9},{9,8},{10,11... | collective-permute-start | bytes 6291464 | tf_op jit(solution)/shard_map/ppermute | solution.py:591
  1.1 3.7 %collective-permute-start.1 = (s32[1,64]{1,0:T(1,128)}, s32[1,64]{1,0:T(1,128)S(1)}, u32[]{:S(2)}, u32[]{:S(2)}) collective-permute-start(s32[1,64]{1,0:T(1,128)} %param.15), channel_id=1, source_target_pairs={{0,8},{2,10},{4,12},{6,14},{8,0},{10,2},{12,4},{14,6},{1,9},{3,11}... | collective-permute-start | bytes 776 | tf_op jit(solution)/shard_map/ppermute | solution.py:583
  4.8 0.0 copy-start.8
  4.8 0.0 copy-start
  4.8 4.3 %own_rows.1 = (bf16[1024,512]{1,0:T(8,128)(2,1)S(1)}, f32[1,1024]{1,0:T(1,128)S(1)}, f32[4,8,256]{2,1,0:T(8,128)S(1)}, f32[1024,16]{1,0:T(8,128)S(1)}, f32[16,12...) custom-call(s32[1,1024]{1,0:T(1,128)} %refs_0_.2, s32[32,128]{1,0:T(8,128)} %bitcast.5, f32[8,1024]{1,0:T(8,128)} %bitcast.11, ...), custom_call_target="tpu_custom_call" | custom-call | flops 2147483648 | tf_op jit(solution)/shard_map/own_rows/pallas_call | solution.py:539
  9.8 0.0 collective-permute-done.1
  9.8 0.0 copy-done.8
  9.9 0.1 add_convert_fusion.refs_6_
  9.9 0.0 collective-permute-done.refs_2_.refs_3_
  9.9 0.0 copy-done
  9.9 4.4 %summary.1 = (bf16[1024,512]{1,0:T(8,128)(2,1)S(1)}, bf16[512,1024]{1,0:T(8,128)(2,1)S(1)}, bf16[1024,512]{1,0:T(8,128)(2,1)S(1)}, f32[4,256,128]{2,1,0:T(8,128)...) custom-call(s32[1]{0:T(128)S(6)} %copy.14.refs_0_, bf16[1024,512]{1,0:T(8,128)(2,1)S(1)} %get-tuple-element.40.refs_1_, ...), custom_call_target="tpu_custom_call" | custom-call | flops 2147483648 | tf_op jit(solution)/shard_map/summary/pallas_call | solution.py:539
  14.4 1.6 %collective-permute-start.2 = (bf16[272,128]{1,0:T(8,128)(2,1)S(1)}, bf16[272,128]{1,0:T(8,128)(2,1)S(1)}, u32[]{:S(2)}, u32[]{:S(2)}) collective-permute-start(bf16[272,128]{1,0:T(8,128)(2,1)S(1)} %get-tuple-element.51.refs_0_), channel_id=1, source_target_pairs={{0,2},{2,0},{4,6},{6,4},{8,10},{10,8},{12,14},{14,12},{1,3},{3,1},... | collective-permute-start | bytes 208904 | tf_op jit(solution)/shard_map/ppermute | solution.py:583
  15.9 0.0 copy-start.1
  15.9 2.7 %local_a.1 = (bf16[1024,256]{1,0:T(8,128)(2,1)S(1)}, f32[1024,256]{1,0:T(8,128)S(1)}) custom-call(bf16[1024,512]{1,0:T(8,128)(2,1)S(1)} %get-tuple-element.46.refs_0_.refs_2_, bf16[512,1024]{1,0:T(8,128)(2,1)S(1)} %get-tuple-element.47.refs_1_, bf16[1024,512]{1,0:T(8,128)(2,1)S(1)} %get-tuple-element.48.refs_2_, ...), custom_call_target="tpu_custom_call" | custom-call | flops 1073741824 | tf_op jit(solution)/shard_map/local_a/pallas_call | solution.py:539
  18.6 0.1 collective-permute-done.2.refs_1_
  18.7 0.1 join.2
  18.8 1.7 %collective-permute-start.3 = (bf16[272,128]{1,0:T(8,128)(2,1)S(1)}, bf16[272,128]{1,0:T(8,128)(2,1)S(1)}, u32[]{:S(2)}, u32[]{:S(2)}) collective-permute-start(bf16[272,128]{1,0:T(8,128)(2,1)S(1)} %get-tuple-element.57.refs_0_), channel_id=1, source_target_pairs={{0,4},{2,6},{4,0},{6,2},{8,12},{10,14},{12,8},{14,10},{1,5},{3,7},... | collective-permute-start | bytes 208904 | tf_op jit(solution)/shard_map/ppermute | solution.py:583
  20.4 0.0 copy-done.1
  20.4 0.0 copy-start.3
  20.4 0.0 copy-start.4
  20.4 0.0 copy-start.6
  20.5 2.9 %local_b.1 = (bf16[1024,256]{1,0:T(8,128)(2,1)S(1)}, f32[1024,256]{1,0:T(8,128)S(1)}, bf16[512,512]{1,0:T(8,128)(2,1)S(1)}) custom-call(bf16[1024,512]{1,0:T(8,128)(2,1)S(1)} %get-tuple-element.46.refs_0_.refs_2_, bf16[512,1024]{1,0:T(8,128)(2,1)S(1)} %get-tuple-element.47.refs_1_, bf16[1024,512]{1,0:T(8,128)(2,1)S(1)} %get-tuple-element.48.refs_2_, ...), custom_call_target="tpu_custom_call" | custom-call | flops 1073741824 | tf_op jit(solution)/shard_map/local_b/pallas_call | solution.py:539
  23.3 0.0 collective-permute-done.3.refs_1_
  23.3 0.1 join.3
  23.4 0.4 collective-permute-start.4
  23.8 0.0 copy-done.3
  23.8 0.0 copy-done.4
  23.8 0.0 copy-done.6
  23.8 0.0 copy-start.5
  23.8 0.0 copy-start.7
  23.8 3.5 %candidates.1 = (bf16[512,128]{1,0:T(8,128)(2,1)S(1)}, bf16[512,128]{1,0:T(8,128)(2,1)S(1)}, bf16[512,128]{1,0:T(8,128)(2,1)S(1)}, bf16[512,128]{1,0:T(8,128)(2,1)S(1)}) custom-call(f32[8,128]{1,0:T(8,128)S(1)} %get-tuple-element.63.refs_0_, s32[32,128]{1,0:T(8,128)S(1)} %bitcast.6, bf16[2048,512]{1,0:T(8,128)(2,1)S(1)} %copy-done.3, ...), custom_call_target="tpu_custom_call" | custom-call | flops 2147483648 | tf_op jit(solution)/shard_map/candidates/pallas_call | solution.py:539
  27.3 1.3 %collective-permute-done.4.refs_9_ = bf16[272,128]{1,0:T(8,128)(2,1)S(1)} collective-permute-done((bf16[272,128]{1,0:T(8,128)(2,1)S(1)}, bf16[272,128]{1,0:T(8,128)(2,1)S(1)}, u32[]{:S(2)}, u32[]{:S(2)}) %collective-permute-start.4) | collective-permute-done | bytes 69664 | tf_op jit(solution)/shard_map/ppermute | solution.py:583
  28.7 0.0 copy-done.5
  28.7 0.0 copy-done.7
  28.7 5.9 %finish.1 = (f32[1024,512]{1,0:T(8,128)}, bf16[1024,512]{1,0:T(8,128)(2,1)S(1)}, bf16[512,1024]{1,0:T(8,128)(2,1)S(1)}, bf16[544,128]{1,0:T(8,128)(2,1)S(1)}, bf16[544,128]{1,0:T(8,128)(2,1)S(1)}) custom-call(s32[8,128]{1,0:T(8,128)S(1)} %get-tuple-element.45.refs_0_, f32[1,8]{1,0:T(1,128)S(1)} %bitcast.7, ...), custom_call_target="tpu_custom_call" | custom-call | flops 2147483648 | tf_op jit(solution)/shard_map/finish/pallas_call | solution.py:539
  34.6 2.4 %collective-permute-start.5 = (bf16[544,128]{1,0:T(8,128)(2,1)S(1)}, bf16[544,128]{1,0:T(8,128)(2,1)S(1)}, u32[]{:S(2)}, u32[]{:S(2)}) collective-permute-start(bf16[544,128]{1,0:T(8,128)(2,1)S(1)} %get-tuple-element.71.refs_5_), channel_id=1, source_target_pairs={{0,6},{2,4},{4,2},{6,0},{8,14},{10,12},{12,10},{14,8},{1,7},{3,5},... | collective-permute-start | bytes 417800 | tf_op jit(solution)/shard_map/ppermute | solution.py:583
  37.0 0.6 %collective-permute-start.6 = (bf16[544,128]{1,0:T(8,128)(2,1)S(1)}, bf16[544,128]{1,0:T(8,128)(2,1)S(1)}, u32[]{:S(2)}, u32[]{:S(2)}) collective-permute-start(bf16[544,128]{1,0:T(8,128)(2,1)S(1)} %get-tuple-element.72.refs_6_), channel_id=1, source_target_pairs={{0,4},{1,3},{2,6},{3,1},{4,0},{5,7},{6,2},{7,5},{8,12},{9,11},{10,... | collective-permute-start | bytes 417800 | tf_op jit(solution)/shard_map/ppermute | solution.py:589
  37.6 1.7 %send.1.refs_5_ = bf16[544,128]{1,0:T(8,128)(2,1)S(1)} custom-call(s32[8,128]{1,0:T(8,128)S(1)} %get-tuple-element.45.refs_0_, f32[1,8]{1,0:T(1,128)S(1)} %bitcast.8, bf16[512,128]{1,0:T(8,128)(2,1)S(1)} %get-tuple-element.70.refs_2_, bf16[1024,512]{1,0:T(8,128)(2,1)S(1)} %get-tuple-element.68.refs_3_, bf16[512,1024]{1,0:T(8,128)(2,1)S(1)} %get-tuple-element.69.refs_4_, ...), custom_call_target="tpu_custom_call" | custom-call | flops 21474836480 | tf_op jit(solution)/shard_map/send/pallas_call | solution.py:539
  39.3 0.6 %collective-permute-start.7 = (bf16[544,128]{1,0:T(8,128)(2,1)S(1)}, bf16[544,128]{1,0:T(8,128)(2,1)S(1)}, u32[]{:S(2)}, u32[]{:S(2)}) collective-permute-start(bf16[544,128]{1,0:T(8,128)(2,1)S(1)} %send.1.refs_5_), channel_id=1, source_target_pairs={{0,2},{1,5},{2,0},{3,7},{4,6},{5,1},{6,4},{7,3},{8,10},{9,13},{10,... | collective-permute-start | bytes 417800 | tf_op jit(solution)/shard_map/ppermute | solution.py:589
  39.9 1.7 %keep.1 = (f32[512,128]{1,0:T(8,128)S(1)}, f32[8,128]{1,0:T(8,128)S(1)}) custom-call(s32[8,128]{1,0:T(8,128)S(1)} %get-tuple-element.45.refs_0_, f32[1,8]{1,0:T(1,128)S(1)} %bitcast.9, bf16[512,128]{1,0:T(8,128)(2,1)S(1)} %get-tuple-element.67.refs_2_, bf16[1024,512]{1,0:T(8,128)(2,1)S(1)} %get-tuple-element.68.refs_3_, ...), custom_call_target="tpu_custom_call" | custom-call | flops 8589934592 | tf_op jit(solution)/shard_map/keep/pallas_call | solution.py:539
  41.6 2.8 %collective-permute-done.7.refs_4_ = bf16[544,128]{1,0:T(8,128)(2,1)S(1)} collective-permute-done((bf16[544,128]{1,0:T(8,128)(2,1)S(1)}, bf16[544,128]{1,0:T(8,128)(2,1)S(1)}, u32[]{:S(2)}, u32[]{:S(2)}) %collective-permute-start.7) | collective-permute-done | bytes 139296 | tf_op jit(solution)/shard_map/ppermute | solution.py:589
  44.4 0.0 collective-permute-done.5.refs_2_
  44.4 0.0 collective-permute-done.6.refs_3_
  44.4 0.1 fold.1
  44.6 1.4 %collective-permute-start.8 = (bf16[272,128]{1,0:T(8,128)(2,1)S(1)}, bf16[272,128]{1,0:T(8,128)(2,1)S(1)}, u32[]{:S(2)}, u32[]{:S(2)}) collective-permute-start(bf16[272,128]{1,0:T(8,128)(2,1)S(1)} %get-tuple-element.77), channel_id=1, source_target_pairs={{0,8},{2,10},{4,12},{6,14},{8,0},{10,2},{12,4},{14,6},{1,9},{3,11}... | collective-permute-start | bytes 208904 | tf_op jit(solution)/shard_map/ppermute | solution.py:583
  46.0 3.9 %collective-permute-done.8.refs_2_ = bf16[272,128]{1,0:T(8,128)(2,1)S(1)} collective-permute-done((bf16[272,128]{1,0:T(8,128)(2,1)S(1)}, bf16[272,128]{1,0:T(8,128)(2,1)S(1)}, u32[]{:S(2)}, u32[]{:S(2)}) %collective-permute-start.8) | collective-permute-done | bytes 69664 | tf_op jit(solution)/shard_map/ppermute | solution.py:583
  49.9 0.0 copy-done.2
  49.9 1.0 %last.1 = f32[64,512]{1,0:T(8,128)} custom-call(f32[512,64]{1,0:T(8,128)S(1)} %get-tuple-element.75.refs_0_, f32[8,64]{1,0:T(8,128)S(1)} %get-tuple-element.76.refs_1_, bf16[272,128]{1,0:T(8,128)(2,1)S(1)} %collective-permute-done.8.refs_2_, bf16[512,512]{1,0:T(8,128)(2,1)S(1)} %copy-done.2), custom_call_target="tpu_custom_call" | custom-call | tf_op jit(solution)/shard_map/last/pallas_call | solution.py:539
  (2 shorter events, 0.0 us)
Async XLA Ops:
  0.6 9.3 %collective-permute-start = (bf16[2048,512]{1,0:T(8,128)(2,1)}, bf16[2048,512]{1,0:T(8,128)(2,1)S(1)}, u32[]{:S(2)}, u32[]{:S(2)}) collective-permute-start(bf16[2048,512]{1,0:T(8,128)(2,1)} %refs_2_.1), channel_id=1, source_target_pairs={{0,1},{1,0},{2,3},{3,2},{4,5},{5,4},{6,7},{7,6},{8,9},{9,8},{10,11... | collective-permute-start | bytes 6291464 | tf_op jit(solution)/shard_map/ppermute | solution.py:591
  1.1 8.7 %collective-permute-start.1 = (s32[1,64]{1,0:T(1,128)}, s32[1,64]{1,0:T(1,128)S(1)}, u32[]{:S(2)}, u32[]{:S(2)}) collective-permute-start(s32[1,64]{1,0:T(1,128)} %param.15), channel_id=1, source_target_pairs={{0,8},{2,10},{4,12},{6,14},{8,0},{10,2},{12,4},{14,6},{1,9},{3,11}... | collective-permute-start | bytes 776 | tf_op jit(solution)/shard_map/ppermute | solution.py:583
  4.8 5.0 %copy-start.8 = (s32[1,64]{1,0:T(1,128)S(1)}, s32[1,64]{1,0:T(1,128)}, u32[]{:S(2)}) copy-start(s32[1,64]{1,0:T(1,128)} %param.15) | copy-start | bytes 772
  4.8 5.1 %copy-start = (bf16[512,1536]{1,0:T(8,128)(2,1)S(1)}, bf16[512,1536]{1,0:T(8,128)(2,1)}, u32[]{:S(2)}) copy-start(bf16[512,1536]{1,0:T(8,128)(2,1)} %refs_5_.3) | copy-start | bytes 4718596
  14.4 4.4 %collective-permute-start.2 = (bf16[272,128]{1,0:T(8,128)(2,1)S(1)}, bf16[272,128]{1,0:T(8,128)(2,1)S(1)}, u32[]{:S(2)}, u32[]{:S(2)}) collective-permute-start(bf16[272,128]{1,0:T(8,128)(2,1)S(1)} %get-tuple-element.51.refs_0_), channel_id=1, source_target_pairs={{0,2},{2,0},{4,6},{6,4},{8,10},{10,8},{12,14},{14,12},{1,3},{3,1},... | collective-permute-start | bytes 208904 | tf_op jit(solution)/shard_map/ppermute | solution.py:583
  15.9 4.5 %copy-start.1 = (bf16[512,1024]{1,0:T(8,128)(2,1)S(1)}, bf16[512,1024]{1,0:T(8,128)(2,1)}, u32[]{:S(2)}) copy-start(bf16[512,1024]{1,0:T(8,128)(2,1)} %refs_13_.1) | copy-start | bytes 3145732
  18.8 4.5 %collective-permute-start.3 = (bf16[272,128]{1,0:T(8,128)(2,1)S(1)}, bf16[272,128]{1,0:T(8,128)(2,1)S(1)}, u32[]{:S(2)}, u32[]{:S(2)}) collective-permute-start(bf16[272,128]{1,0:T(8,128)(2,1)S(1)} %get-tuple-element.57.refs_0_), channel_id=1, source_target_pairs={{0,4},{2,6},{4,0},{6,2},{8,12},{10,14},{12,8},{14,10},{1,5},{3,7},... | collective-permute-start | bytes 208904 | tf_op jit(solution)/shard_map/ppermute | solution.py:583
  20.4 3.3 %copy-start.3 = (bf16[2048,512]{1,0:T(8,128)(2,1)S(1)}, bf16[2048,512]{1,0:T(8,128)(2,1)}, u32[]{:S(2)}) copy-start(bf16[2048,512]{1,0:T(8,128)(2,1)} %refs_2_.1) | copy-start | bytes 6291460
  20.4 3.3 %copy-start.4 = (bf16[512,512]{1,0:T(8,128)(2,1)S(1)}, bf16[512,512]{1,0:T(8,128)(2,1)}, u32[]{:S(2)}) copy-start(bf16[512,512]{1,0:T(8,128)(2,1)} %refs_4_.3) | copy-start | bytes 1572868
  20.4 3.3 %copy-start.6 = (s32[4096]{0:T(1024)S(1)}, s32[4096]{0:T(1024)}, u32[]{:S(2)}) copy-start(s32[4096]{0:T(1024)} %param.16) | copy-start | bytes 49156
  23.4 5.3 %collective-permute-start.4 = (bf16[272,128]{1,0:T(8,128)(2,1)S(1)}, bf16[272,128]{1,0:T(8,128)(2,1)S(1)}, u32[]{:S(2)}, u32[]{:S(2)}) collective-permute-start(bf16[272,128]{1,0:T(8,128)(2,1)S(1)} %get-tuple-element.59), channel_id=1, source_target_pairs={{0,8},{2,10},{4,12},{6,14},{8,0},{10,2},{12,4},{14,6},{1,9},{3,11}... | collective-permute-start | bytes 208904 | tf_op jit(solution)/shard_map/ppermute | solution.py:583
  23.8 4.9 %copy-start.5 = (bf16[512,512]{1,0:T(8,128)(2,1)S(1)}, bf16[512,512]{1,0:T(8,128)(2,1)}, u32[]{:S(2)}) copy-start(bf16[512,512]{1,0:T(8,128)(2,1)} %refs_12_.1) | copy-start | bytes 1572868
  23.8 4.9 %copy-start.7 = (f32[8]{0:T(128)S(1)}, f32[8]{0:T(128)}, u32[]{:S(2)}) copy-start(f32[8]{0:T(128)} %param.18) | copy-start | bytes 100
  34.6 9.8 %collective-permute-start.5 = (bf16[544,128]{1,0:T(8,128)(2,1)S(1)}, bf16[544,128]{1,0:T(8,128)(2,1)S(1)}, u32[]{:S(2)}, u32[]{:S(2)}) collective-permute-start(bf16[544,128]{1,0:T(8,128)(2,1)S(1)} %get-tuple-element.71.refs_5_), channel_id=1, source_target_pairs={{0,6},{2,4},{4,2},{6,0},{8,14},{10,12},{12,10},{14,8},{1,7},{3,5},... | collective-permute-start | bytes 417800 | tf_op jit(solution)/shard_map/ppermute | solution.py:583
  37.0 7.4 %collective-permute-start.6 = (bf16[544,128]{1,0:T(8,128)(2,1)S(1)}, bf16[544,128]{1,0:T(8,128)(2,1)S(1)}, u32[]{:S(2)}, u32[]{:S(2)}) collective-permute-start(bf16[544,128]{1,0:T(8,128)(2,1)S(1)} %get-tuple-element.72.refs_6_), channel_id=1, source_target_pairs={{0,4},{1,3},{2,6},{3,1},{4,0},{5,7},{6,2},{7,5},{8,12},{9,11},{10,... | collective-permute-start | bytes 417800 | tf_op jit(solution)/shard_map/ppermute | solution.py:589
  39.3 5.1 %collective-permute-start.7 = (bf16[544,128]{1,0:T(8,128)(2,1)S(1)}, bf16[544,128]{1,0:T(8,128)(2,1)S(1)}, u32[]{:S(2)}, u32[]{:S(2)}) collective-permute-start(bf16[544,128]{1,0:T(8,128)(2,1)S(1)} %send.1.refs_5_), channel_id=1, source_target_pairs={{0,2},{1,5},{2,0},{3,7},{4,6},{5,1},{6,4},{7,3},{8,10},{9,13},{10,... | collective-permute-start | bytes 417800 | tf_op jit(solution)/shard_map/ppermute | solution.py:589
  39.9 9.9 %copy-start.2 = (bf16[512,512]{1,0:T(8,128)(2,1)S(1)}, bf16[512,512]{1,0:T(8,128)(2,1)}, u32[]{:S(2)}) copy-start(bf16[512,512]{1,0:T(8,128)(2,1)} %refs_3_.3) | copy-start | bytes 1572868
  44.6 5.3 %collective-permute-start.8 = (bf16[272,128]{1,0:T(8,128)(2,1)S(1)}, bf16[272,128]{1,0:T(8,128)(2,1)S(1)}, u32[]{:S(2)}, u32[]{:S(2)}) collective-permute-start(bf16[272,128]{1,0:T(8,128)(2,1)S(1)} %get-tuple-element.77), channel_id=1, source_target_pairs={{0,8},{2,10},{4,12},{6,14},{8,0},{10,2},{12,4},{14,6},{1,9},{3,11}... | collective-permute-start | bytes 208904 | tf_op jit(solution)/shard_map/ppermute | solution.py:583
